TPU v7x, 128 devices: a whole 4x4x4 slice. The times are simulated.
128 devices in a mesh: row: 8 (over y, z_hi), col: 8 (over z_lo, x), dp: 2 (over core).
Axes of the slice: x: 4, y: 4, z: 4 (z_hi: 2, z_lo: 2; z = z_hi * 2 + z_lo), core: 2. Of those that a mesh axis runs over, the one named last changes fastest.
Arguments:
- tokens: bfloat16 [2048, 4096], P(('col', 'dp'), 'row'), may hold values from -6 to 6
- grad_out: bfloat16 [2048, 4096], P(('col', 'dp'), 'row'), may hold values from -6 to 6
- gate_pre: bfloat16 [2048, 16384], P(('row', 'dp'), 'col'), may hold values from -8 to 8
- up_pre: bfloat16 [2048, 16384], P(('row', 'dp'), 'col'), may hold values from -6 to 6
- w_gate: bfloat16 [4096, 16384], P('row', 'col'), may hold values from -0.09375 to 0.09375
- w_up: bfloat16 [4096, 16384], P('row', 'col'), may hold values from -0.09375 to 0.09375
- w_down: bfloat16 [16384, 4096], P('col', 'row'), may hold values from -0.046875 to 0.046875
Outputs:
- grad_tokens: bfloat16 [2048, 4096], P(('col', 'dp'), 'row')
- grad_gate: bfloat16 [4096, 16384], P('row', 'col')
- grad_up: bfloat16 [4096, 16384], P('row', 'col')
- grad_down: bfloat16 [16384, 4096], P('col', 'row')
All inputs are finite; a program needn't handle non-finite values.
Results may differ from a plain program's by a relative error of at most 0.0051.
Values may be sent and summed in bfloat16 or wider, within the bound.
No kernel may reach another device: no remote copies, remote signals or barrier semaphores. Data moves between devices by JAX's collectives and lax.ppermute only.
A program may use at most 128 MiB of HBM per device.

v0:
```python
import functools

import jax
import jax.numpy as jnp
import numpy as np
from jax import lax
from jax.experimental import pallas as pl
from jax.experimental.pallas import tpu as pltpu
from jax.sharding import Mesh, PartitionSpec as P


COL = ("zl", "x")
BF = jnp.bfloat16
F32 = jnp.float32
SWAP = [(0, 1), (1, 0)]
STEP = 256


def ring(shift):
    return [(i, (i + shift) % 4) for i in range(4)]


def along_y(x, shift):
    return lax.ppermute(x, "y", ring(shift))


def to_pair(x):
    return lax.ppermute(x, "zh", SWAP)


def across_col(x):
    return lax.all_to_all(x, COL, 0, 0, tiled=True)


def gather_col(x):
    many = jnp.broadcast_to(x[None], (8,) + x.shape)
    whole = across_col(many)
    return whole.reshape(8 * x.shape[0], x.shape[1])


def inner_rows(left, right):
    return lax.dot_general(left, right, (((0,), (0,)), ((), ())), preferred_element_type=F32)


def times_transposed(left, right):
    return lax.dot_general(left, right, (((1,), (1,)), ((), ())), preferred_element_type=F32)


def place(where, p, rows):
    return pl.ds(pl.multiple_of(where[p] * rows, rows), rows)


def hidden_kernel(where, *refs):
    gates, ups = refs[:8], refs[8:16]
    hidden, slope, active = refs[16:]
    rows = gates[0].shape[0]
    for p in range(8):
        g = gates[p][...].astype(F32)
        u = ups[p][...].astype(F32)
        s = jax.nn.sigmoid(g)
        here = place(where, p, rows)
        act = g * s
        hidden[here, :] = (act * u).astype(BF)
        slope[here, :] = u * s * (1.0 + g * (1.0 - s))
        active[here, :] = act


def hidden_of(where, gates, ups):
    rows, width = gates[0].shape
    total = 8 * rows
    piece = pl.BlockSpec((rows, STEP), lambda c, w: (0, c))
    full = pl.BlockSpec((total, STEP), lambda c, w: (0, c))
    return pl.pallas_call(
        hidden_kernel,
        out_shape=(
            jax.ShapeDtypeStruct((total, width), BF),
            jax.ShapeDtypeStruct((total, width), F32),
            jax.ShapeDtypeStruct((total, width), F32),
        ),
        grid_spec=pltpu.PrefetchScalarGridSpec(
            num_scalar_prefetch=1,
            grid=(width // STEP,),
            in_specs=[piece] * 16,
            out_specs=(full, full, full),
        ),
        cost_estimate=pl.CostEstimate(
            flops=total * width * 10, bytes_accessed=total * width * 14, transcendentals=total * width * 2
        ),
    )(where, *gates, *ups)


def back_kernel(factor, where, *refs):
    ds = refs[:8]
    slope, active, w_gate, w_up, tok, grad_gate, grad_up, back, d_gate, d_up, total = refs[8:]
    rows = ds[0].shape[0]
    c = pl.program_id(0)
    for p in range(8):
        d = ds[p][...].astype(F32)
        here = place(where, p, rows)
        d_gate[here, :] = (d * slope[here, :]).astype(BF)
        d_up[here, :] = (d * active[here, :]).astype(BF)
    dg, du = d_gate[...], d_up[...]
    more = times_transposed(dg, w_gate[...]) + times_transposed(du, w_up[...])
    grad_gate[...] = (jnp.dot(tok[...], dg, preferred_element_type=F32) * factor).astype(BF)
    grad_up[...] = (jnp.dot(tok[...], du, preferred_element_type=F32) * factor).astype(BF)

    @pl.when(c == 0)
    def _():
        total[...] = more

    @pl.when(c > 0)
    def _():
        total[...] += more

    @pl.when(c == pl.num_programs(0) - 1)
    def _():
        back[...] = total[...].astype(BF)


def back_of(where, ds, slope, active, w_gate, w_up, tok, factor):
    rows, width = ds[0].shape
    depth = w_gate.shape[0]
    total = 8 * rows
    piece = pl.BlockSpec((rows, STEP), lambda c, w: (0, c))
    weight = pl.BlockSpec((depth, STEP), lambda c, w: (0, c))
    full = pl.BlockSpec((total, STEP), lambda c, w: (0, c))
    return pl.pallas_call(
        functools.partial(back_kernel, factor),
        out_shape=(
            jax.ShapeDtypeStruct((depth, width), BF),
            jax.ShapeDtypeStruct((depth, width), BF),
            jax.ShapeDtypeStruct((total, depth), BF),
        ),
        grid_spec=pltpu.PrefetchScalarGridSpec(
            num_scalar_prefetch=1,
            grid=(width // STEP,),
            in_specs=[piece] * 8 + [full, full, weight, weight, pl.BlockSpec((depth, total), lambda c, w: (0, 0))],
            out_specs=(weight, weight, pl.BlockSpec((total, depth), lambda c, w: (0, 0))),
            scratch_shapes=[
                pltpu.VMEM((total, STEP), BF),
                pltpu.VMEM((total, STEP), BF),
                pltpu.VMEM((total, depth), F32),
            ],
        ),
        cost_estimate=pl.CostEstimate(
            flops=8 * total * width * depth, bytes_accessed=total * width * 14, transcendentals=0
        ),
    )(where, *ds, slope, active, w_gate, w_up, tok)


def local(tokens, grad_out, gate_pre, up_pre, w_gate, w_up, w_down):
    rows, width = tokens.shape
    factor = float(1.0 / np.sqrt(np.float32(16 * rows)))
    y, zh = lax.axis_index("y"), lax.axis_index("zh")
    p = lax.iota(jnp.int32, 8)
    where = lax.rem(y + p // 2, 4) * 2 + lax.rem(zh + p, 2)
    where_too = lax.rem(2 * y + (p & 6), 8) + (zh ^ (p & 1))

    out_all = gather_col(grad_out)

    g3, g1 = along_y(gate_pre, 1), along_y(gate_pre, -1)
    u3, u1 = along_y(up_pre, 1), along_y(up_pre, -1)
    g2, u2 = along_y(g3, 1), along_y(u1, -1)
    gates = [v for g in (gate_pre, g1, g2, g3) for v in (g, to_pair(g))]
    ups = [v for u in (up_pre, u1, u2, u3) for v in (u, to_pair(u))]

    def part(k):
        here = lax.dynamic_slice_in_dim(out_all, lax.rem(y + k, 4) * (2 * rows), 2 * rows, 0)
        return times_transposed(here, w_down).astype(BF if k else F32)

    recv = [along_y(part(k), k) for k in (2, 1, 3)]
    total = part(0) + sum(r.astype(F32) for r in recv)
    total = total.reshape(2, rows, -1)
    theirs = lax.dynamic_index_in_dim(total, 1 - zh, 0, keepdims=False).astype(BF)
    mine = lax.dynamic_index_in_dim(total, zh, 0, keepdims=False)
    d00 = (mine + to_pair(theirs).astype(F32)).astype(BF)
    d30, d10 = along_y(d00, 1), along_y(d00, -1)
    d01 = to_pair(d00)
    d31, d11 = along_y(d01, 1), along_y(d01, -1)
    d20, d21 = along_y(d30, 1), along_y(d11, -1)
    ds = [d00, d01, d10, d11, d20, d21, d30, d31]

    tok_all = gather_col(tokens)

    def both_cores(own):
        other = lax.ppermute(own, "core", SWAP)
        return (own.astype(F32) + other.astype(F32)).astype(BF)

    hidden, slope, active = hidden_of(where, gates, ups)
    down = (inner_rows(hidden, out_all) * factor).astype(BF)
    grad_down = both_cores(down)
    gate, up, back = back_of(where_too, ds, slope, active, w_gate, w_up, tok_all.T, factor)
    back_recv = across_col(back.reshape(8, rows, width))
    grad_gate = both_cores(gate)
    grad_up = both_cores(up)
    grad_tokens = jnp.sum(back_recv.astype(F32), axis=0).astype(BF)
    return grad_tokens, grad_gate, grad_up, grad_down


def solution(mesh):
    fine = Mesh(mesh.devices.reshape(4, 2, 2, 4, 2), ("y", "zh", "zl", "x", "core"))
    row, col = ("y", "zh"), COL
    act = P(col + ("core",), row)
    pre = P(row + ("core",), col)
    up = P(row, col)
    down = P(col, row)

    return jax.shard_map(
        local,
        mesh=fine,
        in_specs=(act, act, pre, pre, up, up, down),
        out_specs=(act, up, up, down),
        check_vma=False,
    )
```

profile of v0, /device:TPU:0, one launch (start us, length us, event | category | flops | bytes accessed | tf_op | source)
XLA Modules:
  0.0 279.0 jit_solution(6578202779402808443)
XLA Ops:
  0.6 0.0 copy-start
  0.6 2.1 broadcast_in_dim.4
  2.8 5.8 %all-to-all-start = ((bf16[8,128,512]{2,1,0:T(8,128)(2,1)}), bf16[8,128,512]{2,1,0:T(8,128)(2,1)S(1)}, u32[]{:S(2)}, u32[]{:S(2)}) async-start(bf16[8,128,512]{2,1,0:T(8,128)(2,1)} %broadcast_in_dim.4), calls=%async_computation | async-start | bytes 2097152 | tf_op jit(solution)/shard_map/all_to_all | solution.py:32
  8.5 15.7 %all-to-all-done = bf16[8,128,512]{2,1,0:T(8,128)(2,1)S(1)} async-done(((bf16[8,128,512]{2,1,0:T(8,128)(2,1)}), bf16[8,128,512]{2,1,0:T(8,128)(2,1)S(1)}, u32[]{:S(2)}, u32[]{:S(2)}) %all-to-all-start) | async-done | bytes 1048608 | tf_op jit(solution)/shard_map/all_to_all | solution.py:32
  24.2 1.7 convolution_convert_fusion
  25.9 3.0 %collective-permute-start.2 = (bf16[256,2048]{1,0:T(8,128)(2,1)}, bf16[256,2048]{1,0:T(8,128)(2,1)}, u32[]{:S(2)}, u32[]{:S(2)}) collective-permute-start(bf16[256,2048]{1,0:T(8,128)(2,1)} %convolution_convert_fusion), channel_id=1, source_target_pairs={{0,96},{32,0},{64,32},{96,64},{1,97},{33,1},{65,33},{97,65},{2,98}... | collective-permute-start | bytes 3145736 | tf_op jit(solution)/shard_map/ppermute | solution.py:24
  29.0 1.7 convolution_convert_fusion.1
  30.7 1.7 convolution_convert_fusion.2
  32.4 2.2 collective-permute-start
  34.6 3.6 %collective-permute-start.11 = (bf16[128,2048]{1,0:T(8,128)(2,1)}, bf16[128,2048]{1,0:T(8,128)(2,1)}, u32[]{:S(2)}, u32[]{:S(2)}) collective-permute-start(bf16[128,2048]{1,0:T(8,128)(2,1)} %refs_0_.1), channel_id=1, source_target_pairs={{0,16},{16,0},{1,17},{17,1},{2,18},{18,2},{3,19},{19,3},{4,20},{20... | collective-permute-start | bytes 1572872 | tf_op jit(solution)/shard_map/ppermute | solution.py:28
  38.2 1.1 collective-permute-start.12
  39.2 36.1 %collective-permute-done.2 = bf16[256,2048]{1,0:T(8,128)(2,1)} collective-permute-done((bf16[256,2048]{1,0:T(8,128)(2,1)}, bf16[256,2048]{1,0:T(8,128)(2,1)}, u32[]{:S(2)}, u32[]{:S(2)}) %collective-permute-start.2) | collective-permute-done | bytes 1048608 | tf_op jit(solution)/shard_map/ppermute | solution.py:24
  75.3 0.0 collective-permute-start.14
  75.3 4.8 %collective-permute-done.1 = bf16[256,2048]{1,0:T(8,128)(2,1)} collective-permute-done((bf16[256,2048]{1,0:T(8,128)(2,1)}, bf16[256,2048]{1,0:T(8,128)(2,1)}, u32[]{:S(2)}, u32[]{:S(2)}) %collective-permute-start.1) | collective-permute-done | bytes 1048608 | tf_op jit(solution)/shard_map/ppermute | solution.py:24
  80.1 3.6 %collective-permute-start.18 = (bf16[128,2048]{1,0:T(8,128)(2,1)}, bf16[128,2048]{1,0:T(8,128)(2,1)}, u32[]{:S(2)}, u32[]{:S(2)}) collective-permute-start(bf16[128,2048]{1,0:T(8,128)(2,1)} %refs_8_.1), channel_id=1, source_target_pairs={{0,16},{16,0},{1,17},{17,1},{2,18},{18,2},{3,19},{19,3},{4,20},{20... | collective-permute-start | bytes 1572872 | tf_op jit(solution)/shard_map/ppermute | solution.py:28
  83.7 2.6 add_add_fusion
  86.3 0.0 copy-start.2
  86.3 1.3 copy-done.2
  87.6 0.9 fusion.1
  88.5 0.0 collective-permute-start.3
  88.5 2.1 collective-permute-start.23
  90.6 1.2 collective-permute-done.14.refs_6_
  91.8 3.6 %collective-permute-start.13 = (bf16[128,2048]{1,0:T(8,128)(2,1)}, bf16[128,2048]{1,0:T(8,128)(2,1)}, u32[]{:S(2)}, u32[]{:S(2)}) collective-permute-start(bf16[128,2048]{1,0:T(8,128)(2,1)} %collective-permute-done.12.refs_2_), channel_id=1, source_target_pairs={{0,16},{16,0},{1,17},{17,1},{2,18},{18,2},{3,19},{19,3},{4,20},{20... | collective-permute-start | bytes 1572872 | tf_op jit(solution)/shard_map/ppermute | solution.py:28
  95.4 0.1 copy.12
  95.5 1.1 broadcast_in_dim.5
  96.6 4.2 %all-to-all-start.1 = ((bf16[8,128,512]{1,2,0:T(8,128)(2,1)}), bf16[8,128,512]{1,2,0:T(8,128)(2,1)}, u32[]{:S(2)}, u32[]{:S(2)}) async-start(bf16[8,128,512]{1,2,0:T(8,128)(2,1)} %broadcast_in_dim.5), calls=%async_computation.1 | async-start | bytes 2097152 | tf_op jit(solution)/shard_map/all_to_all | solution.py:32
  100.9 0.1 collective-permute-start.15
  101.0 0.1 collective-permute-start.17
  101.1 14.4 %collective-permute-done.3 = bf16[128,2048]{1,0:T(8,128)(2,1)} collective-permute-done((bf16[128,2048]{1,0:T(8,128)(2,1)}, bf16[128,2048]{1,0:T(8,128)(2,1)}, u32[]{:S(2)}, u32[]{:S(2)}) %collective-permute-start.3) | collective-permute-done | bytes 524320 | tf_op jit(solution)/shard_map/ppermute | solution.py:28
  115.5 1.9 fusion.refs_0_
  117.4 4.0 %collective-permute-start.20 = (bf16[128,2048]{1,0:T(8,128)(2,1)}, bf16[128,2048]{1,0:T(8,128)(2,1)S(1)}, u32[]{:S(2)}, u32[]{:S(2)}) collective-permute-start(bf16[128,2048]{1,0:T(8,128)(2,1)} %collective-permute-done.19.refs_10_), channel_id=1, source_target_pairs={{0,16},{16,0},{1,17},{17,1},{2,18},{18,2},{3,19},{19,3},{4,20},{20... | collective-permute-start | bytes 1572872 | tf_op jit(solution)/shard_map/ppermute | solution.py:28
  121.4 5.3 %collective-permute-done.13.refs_3_ = bf16[128,2048]{1,0:T(8,128)(2,1)} collective-permute-done((bf16[128,2048]{1,0:T(8,128)(2,1)}, bf16[128,2048]{1,0:T(8,128)(2,1)}, u32[]{:S(2)}, u32[]{:S(2)}) %collective-permute-start.13) | collective-permute-done | bytes 524320 | tf_op jit(solution)/shard_map/ppermute | solution.py:28
  126.7 4.0 %collective-permute-start.4 = (bf16[128,2048]{1,0:T(8,128)(2,1)}, bf16[128,2048]{1,0:T(8,128)(2,1)}, u32[]{:S(2)}, u32[]{:S(2)}) collective-permute-start(bf16[128,2048]{1,0:T(8,128)(2,1)} %fusion.refs_0_), channel_id=1, source_target_pairs={{0,16},{16,0},{1,17},{17,1},{2,18},{18,2},{3,19},{19,3},{4,20},{20... | collective-permute-start | bytes 1572872 | tf_op jit(solution)/shard_map/ppermute | solution.py:28
  130.7 0.0 collective-permute-start.24
  130.7 10.0 %collective-permute-done.17.refs_7_ = bf16[128,2048]{1,0:T(8,128)(2,1)} collective-permute-done((bf16[128,2048]{1,0:T(8,128)(2,1)}, bf16[128,2048]{1,0:T(8,128)(2,1)}, u32[]{:S(2)}, u32[]{:S(2)}) %collective-permute-start.17) | collective-permute-done | bytes 524320 | tf_op jit(solution)/shard_map/ppermute | solution.py:28
  140.8 4.0 %collective-permute-start.16 = (bf16[128,2048]{1,0:T(8,128)(2,1)}, bf16[128,2048]{1,0:T(8,128)(2,1)S(1)}, u32[]{:S(2)}, u32[]{:S(2)}) collective-permute-start(bf16[128,2048]{1,0:T(8,128)(2,1)} %collective-permute-done.15.refs_4_), channel_id=1, source_target_pairs={{0,16},{16,0},{1,17},{17,1},{2,18},{18,2},{3,19},{19,3},{4,20},{20... | collective-permute-start | bytes 1572872 | tf_op jit(solution)/shard_map/ppermute | solution.py:28
  144.8 0.0 collective-permute-start.22
  144.8 7.2 %collective-permute-done.20.refs_11_ = bf16[128,2048]{1,0:T(8,128)(2,1)S(1)} collective-permute-done((bf16[128,2048]{1,0:T(8,128)(2,1)}, bf16[128,2048]{1,0:T(8,128)(2,1)S(1)}, u32[]{:S(2)}, u32[]{:S(2)}) %collective-permute-start.20) | collective-permute-done | bytes 524320 | tf_op jit(solution)/shard_map/ppermute | solution.py:28
  152.0 11.2 %collective-permute-done.4.refs_1_ = bf16[128,2048]{1,0:T(8,128)(2,1)} collective-permute-done((bf16[128,2048]{1,0:T(8,128)(2,1)}, bf16[128,2048]{1,0:T(8,128)(2,1)}, u32[]{:S(2)}, u32[]{:S(2)}) %collective-permute-start.4) | collective-permute-done | bytes 524320 | tf_op jit(solution)/shard_map/ppermute | solution.py:28
  163.2 0.5 fusion.18.where
  163.8 0.5 fusion.15.where
  164.3 2.4 bitcast_bitcast_fusion.refs_12_
  166.6 7.8 %collective-permute-done.24.refs_15_ = bf16[128,2048]{1,0:T(8,128)(2,1)S(1)} collective-permute-done((bf16[128,2048]{1,0:T(8,128)(2,1)}, bf16[128,2048]{1,0:T(8,128)(2,1)S(1)}, u32[]{:S(2)}, u32[]{:S(2)}) %collective-permute-start.24) | collective-permute-done | bytes 524320 | tf_op jit(solution)/shard_map/ppermute | solution.py:28
  174.5 11.2 %collective-permute-done.16.refs_5_ = bf16[128,2048]{1,0:T(8,128)(2,1)S(1)} collective-permute-done((bf16[128,2048]{1,0:T(8,128)(2,1)}, bf16[128,2048]{1,0:T(8,128)(2,1)S(1)}, u32[]{:S(2)}, u32[]{:S(2)}) %collective-permute-start.16) | collective-permute-done | bytes 524320 | tf_op jit(solution)/shard_map/ppermute | solution.py:28
  185.7 6.5 %collective-permute-done.22.refs_13_ = bf16[128,2048]{1,0:T(8,128)(2,1)S(1)} collective-permute-done((bf16[128,2048]{1,0:T(8,128)(2,1)}, bf16[128,2048]{1,0:T(8,128)(2,1)S(1)}, u32[]{:S(2)}, u32[]{:S(2)}) %collective-permute-start.22) | collective-permute-done | bytes 524320 | tf_op jit(solution)/shard_map/ppermute | solution.py:28
  192.2 0.0 copy-start.8
  192.2 0.8 copy-done.8
  193.0 13.1 %shard_map.102 = (bf16[1024,2048]{1,0:T(8,128)(2,1)}, f32[1024,2048]{1,0:T(8,128)}, f32[1024,2048]{1,0:T(8,128)}) custom-call(s32[8]{0:T(128)} %fusion.18.where, bf16[128,2048]{1,0:T(8,128)(2,1)} %refs_0_.1, bf16[128,2048]{1,0:T(8,128)(2,1)} %collective-permute-done.11.refs_1_, bf16[128,2048]{1,0:T(8,128)(2,1)} %collective-permute-done.12.refs_2_, ...), custom_call_target="tpu_custom_call" | custom-call | flops 20971520 | bytes 29360128 | tf_op jit(solution)/shard_map/pallas_call | solution.py:73
  206.1 0.5 collective-permute-start.5
  206.6 1.6 collective-permute-start.10
  208.2 0.0 collective-permute-start.8
  208.2 3.2 %collective-permute-start.9 = (bf16[128,2048]{1,0:T(8,128)(2,1)}, bf16[128,2048]{1,0:T(8,128)(2,1)}, u32[]{:S(2)}, u32[]{:S(2)}) collective-permute-start(bf16[128,2048]{1,0:T(8,128)(2,1)} %collective-permute-done.6.refs_3_), channel_id=1, source_target_pairs={{0,96},{32,0},{64,32},{96,64},{1,97},{33,1},{65,33},{97,65},{2,98}... | collective-permute-start | bytes 1572872 | tf_op jit(solution)/shard_map/ppermute | solution.py:24
  211.5 5.9 %multiply_convert_fusion = bf16[2048,512]{1,0:T(8,128)(2,1)} fusion(bf16[1024,2048]{1,0:T(8,128)(2,1)} %get-tuple-element.15, bf16[1024,512]{1,0:T(8,128)(2,1)S(1)} %bitcast.28), kind=kOutput, calls=%fused_computation.1 | convolution fusion | flops 2149580800 | bytes 7340032 | tf_op jit(solution)/shard_map/dot_general | solution.py:42
  217.4 3.9 %collective-permute-done.5.refs_2_ = bf16[128,2048]{1,0:T(8,128)(2,1)} collective-permute-done((bf16[128,2048]{1,0:T(8,128)(2,1)}, bf16[128,2048]{1,0:T(8,128)(2,1)}, u32[]{:S(2)}, u32[]{:S(2)}) %collective-permute-start.5) | collective-permute-done | bytes 524320 | tf_op jit(solution)/shard_map/ppermute | solution.py:24
  221.3 8.6 %collective-permute-done.8.refs_4_ = bf16[128,2048]{1,0:T(8,128)(2,1)} collective-permute-done((bf16[128,2048]{1,0:T(8,128)(2,1)}, bf16[128,2048]{1,0:T(8,128)(2,1)}, u32[]{:S(2)}, u32[]{:S(2)}) %collective-permute-start.8) | collective-permute-done | bytes 524320 | tf_op jit(solution)/shard_map/ppermute | solution.py:24
  229.9 19.0 %shard_map.103 = (bf16[512,2048]{1,0:T(8,128)(2,1)}, bf16[512,2048]{1,0:T(8,128)(2,1)}, bf16[1024,512]{1,0:T(8,128)(2,1)}) custom-call(s32[8]{0:T(128)} %fusion.15.where, bf16[128,2048]{1,0:T(8,128)(2,1)} %fusion.refs_0_, bf16[128,2048]{1,0:T(8,128)(2,1)} %collective-permute-done.4.refs_1_, bf16[128,2048]{1,0:T(8,128)(2,1)} %collective-permute-done.5.refs_2_, ...), custom_call_target="tpu_custom_call" | custom-call | flops 8589934592 | bytes 29360128 | tf_op jit(solution)/shard_map/pallas_call | solution.py:127
  248.8 0.1 collective-permute-start.25
  248.9 0.5 collective-permute-start.26
  249.4 4.5 %all-to-all-start.2 = ((bf16[8,128,512]{2,1,0:T(8,128)(2,1)}), bf16[8,128,512]{2,1,0:T(8,128)(2,1)S(1)}, u32[]{:S(2)}, u32[]{:S(2)}) async-start(bf16[8,128,512]{2,1,0:T(8,128)(2,1)} %bitcast.29), calls=%async_computation.2 | async-start | bytes 2097152 | tf_op jit(solution)/shard_map/all_to_all | solution.py:32
  253.9 3.5 %add_convert_fusion = bf16[2048,512]{1,0:T(8,128)(2,1)} fusion(bf16[2048,512]{1,0:T(8,128)(2,1)S(1)} %collective-permute-done.27, bf16[2048,512]{1,0:T(8,128)(2,1)} %multiply_convert_fusion), kind=kLoop, calls=%fused_computation | loop fusion | flops 4194304 | bytes 6291456 | tf_op jit(solution)/shard_map/convert_element_type | solution.py:187
  257.4 12.5 %all-to-all-done.2 = bf16[8,128,512]{2,1,0:T(8,128)(2,1)S(1)} async-done(((bf16[8,128,512]{2,1,0:T(8,128)(2,1)}), bf16[8,128,512]{2,1,0:T(8,128)(2,1)S(1)}, u32[]{:S(2)}, u32[]{:S(2)}) %all-to-all-start.2) | async-done | bytes 1048608 | tf_op jit(solution)/shard_map/all_to_all | solution.py:32
  269.9 0.8 reduce_sum.12
  270.7 4.6 %add_convert_fusion.2 = bf16[512,2048]{1,0:T(8,128)(2,1)} fusion(bf16[512,2048]{1,0:T(8,128)(2,1)} %collective-permute-done.25, bf16[512,2048]{1,0:T(8,128)(2,1)} %get-tuple-element.13), kind=kLoop, calls=%fused_computation.3 | loop fusion | flops 4194304 | bytes 6291456 | tf_op jit(solution)/shard_map/convert_element_type | solution.py:187
  275.3 3.7 %add_convert_fusion.1 = bf16[512,2048]{1,0:T(8,128)(2,1)} fusion(bf16[512,2048]{1,0:T(8,128)(2,1)} %collective-permute-done.26, bf16[512,2048]{1,0:T(8,128)(2,1)S(1)} %copy-done.4), kind=kLoop, calls=%fused_computation.2 | loop fusion | flops 4194304 | bytes 6291456 | tf_op jit(solution)/shard_map/convert_element_type | solution.py:187
  (37 shorter events, 0.1 us)
Async XLA Ops:
  0.6 23.6 %copy-start = (bf16[2048,512]{1,0:T(8,128)(2,1)S(1)}, bf16[2048,512]{1,0:T(8,128)(2,1)}, u32[]{:S(2)}) copy-start(bf16[2048,512]{1,0:T(8,128)(2,1)} %param.13) | copy-start | bytes 6291460
  2.8 21.5 %all-to-all-start = ((bf16[8,128,512]{2,1,0:T(8,128)(2,1)}), bf16[8,128,512]{2,1,0:T(8,128)(2,1)S(1)}, u32[]{:S(2)}, u32[]{:S(2)}) async-start(bf16[8,128,512]{2,1,0:T(8,128)(2,1)} %broadcast_in_dim.4), calls=%async_computation | async-start | bytes 2097152 | tf_op jit(solution)/shard_map/all_to_all | solution.py:32
  25.9 49.3 %collective-permute-start.2 = (bf16[256,2048]{1,0:T(8,128)(2,1)}, bf16[256,2048]{1,0:T(8,128)(2,1)}, u32[]{:S(2)}, u32[]{:S(2)}) collective-permute-start(bf16[256,2048]{1,0:T(8,128)(2,1)} %convolution_convert_fusion), channel_id=1, source_target_pairs={{0,96},{32,0},{64,32},{96,64},{1,97},{33,1},{65,33},{97,65},{2,98}... | collective-permute-start | bytes 3145736 | tf_op jit(solution)/shard_map/ppermute | solution.py:24
  30.7 49.4 %collective-permute-start.1 = (bf16[256,2048]{1,0:T(8,128)(2,1)}, bf16[256,2048]{1,0:T(8,128)(2,1)}, u32[]{:S(2)}, u32[]{:S(2)}) collective-permute-start(bf16[256,2048]{1,0:T(8,128)(2,1)} %convolution_convert_fusion.1), channel_id=1, source_target_pairs={{0,32},{32,64},{64,96},{96,0},{1,33},{33,65},{65,97},{97,1},{2,34}... | collective-permute-start | bytes 3145736 | tf_op jit(solution)/shard_map/ppermute | solution.py:24
  32.4 51.3 %collective-permute-start = (bf16[256,2048]{1,0:T(8,128)(2,1)}, bf16[256,2048]{1,0:T(8,128)(2,1)}, u32[]{:S(2)}, u32[]{:S(2)}) collective-permute-start(bf16[256,2048]{1,0:T(8,128)(2,1)} %convolution_convert_fusion.2), channel_id=1, source_target_pairs={{0,64},{32,96},{64,0},{96,32},{1,65},{33,97},{65,1},{97,33},{2,66}... | collective-permute-start | bytes 3145736 | tf_op jit(solution)/shard_map/ppermute | solution.py:24
  34.6 53.9 %collective-permute-start.11 = (bf16[128,2048]{1,0:T(8,128)(2,1)}, bf16[128,2048]{1,0:T(8,128)(2,1)}, u32[]{:S(2)}, u32[]{:S(2)}) collective-permute-start(bf16[128,2048]{1,0:T(8,128)(2,1)} %refs_0_.1), channel_id=1, source_target_pairs={{0,16},{16,0},{1,17},{17,1},{2,18},{18,2},{3,19},{19,3},{4,20},{20... | collective-permute-start | bytes 1572872 | tf_op jit(solution)/shard_map/ppermute | solution.py:28
  38.2 50.3 %collective-permute-start.12 = (bf16[128,2048]{1,0:T(8,128)(2,1)}, bf16[128,2048]{1,0:T(8,128)(2,1)}, u32[]{:S(2)}, u32[]{:S(2)}) collective-permute-start(bf16[128,2048]{1,0:T(8,128)(2,1)} %refs_0_.1), channel_id=1, source_target_pairs={{0,96},{32,0},{64,32},{96,64},{1,97},{33,1},{65,33},{97,65},{2,98}... | collective-permute-start | bytes 1572872 | tf_op jit(solution)/shard_map/ppermute | solution.py:24
  39.2 56.2 %copy-start.9 = (bf16[128,512]{1,0:T(8,128)(2,1)S(1)}, bf16[128,512]{1,0:T(8,128)(2,1)}, u32[]{:S(2)}) copy-start(bf16[128,512]{1,0:T(8,128)(2,1)} %param.7) | copy-start | bytes 393220
  75.3 16.5 %collective-permute-start.14 = (bf16[128,2048]{1,0:T(8,128)(2,1)}, bf16[128,2048]{1,0:T(8,128)(2,1)}, u32[]{:S(2)}, u32[]{:S(2)}) collective-permute-start(bf16[128,2048]{1,0:T(8,128)(2,1)} %refs_0_.1), channel_id=1, source_target_pairs={{0,32},{32,64},{64,96},{96,0},{1,33},{33,65},{65,97},{97,1},{2,34}... | collective-permute-start | bytes 1572872 | tf_op jit(solution)/shard_map/ppermute | solution.py:24
  80.1 20.8 %collective-permute-start.18 = (bf16[128,2048]{1,0:T(8,128)(2,1)}, bf16[128,2048]{1,0:T(8,128)(2,1)}, u32[]{:S(2)}, u32[]{:S(2)}) collective-permute-start(bf16[128,2048]{1,0:T(8,128)(2,1)} %refs_8_.1), channel_id=1, source_target_pairs={{0,16},{16,0},{1,17},{17,1},{2,18},{18,2},{3,19},{19,3},{4,20},{20... | collective-permute-start | bytes 1572872 | tf_op jit(solution)/shard_map/ppermute | solution.py:28
  83.7 17.3 %collective-permute-start.19 = (bf16[128,2048]{1,0:T(8,128)(2,1)}, bf16[128,2048]{1,0:T(8,128)(2,1)}, u32[]{:S(2)}, u32[]{:S(2)}) collective-permute-start(bf16[128,2048]{1,0:T(8,128)(2,1)} %refs_8_.1), channel_id=1, source_target_pairs={{0,96},{32,0},{64,32},{96,64},{1,97},{33,1},{65,33},{97,65},{2,98}... | collective-permute-start | bytes 1572872 | tf_op jit(solution)/shard_map/ppermute | solution.py:24
  86.3 1.3 copy-start.2
  88.5 27.0 %copy-start.3 = (f32[256,2048]{1,0:T(8,128)S(1)}, f32[256,2048]{1,0:T(8,128)}, u32[]{:S(2)}) copy-start(f32[256,2048]{1,0:T(8,128)} %copy-done.2) | copy-start | bytes 6291460
  88.5 27.0 %collective-permute-start.3 = (bf16[128,2048]{1,0:T(8,128)(2,1)}, bf16[128,2048]{1,0:T(8,128)(2,1)}, u32[]{:S(2)}, u32[]{:S(2)}) collective-permute-start(bf16[128,2048]{1,0:T(8,128)(2,1)} %fusion.1), channel_id=1, source_target_pairs={{0,16},{16,0},{1,17},{17,1},{2,18},{18,2},{3,19},{19,3},{4,20},{20... | collective-permute-start | bytes 1572872 | tf_op jit(solution)/shard_map/ppermute | solution.py:28
  88.5 28.9 %collective-permute-start.23 = (bf16[128,2048]{1,0:T(8,128)(2,1)}, bf16[128,2048]{1,0:T(8,128)(2,1)}, u32[]{:S(2)}, u32[]{:S(2)}) collective-permute-start(bf16[128,2048]{1,0:T(8,128)(2,1)} %refs_8_.1), channel_id=1, source_target_pairs={{0,32},{32,64},{64,96},{96,0},{1,33},{33,65},{65,97},{97,1},{2,34}... | collective-permute-start | bytes 1572872 | tf_op jit(solution)/shard_map/ppermute | solution.py:24
  91.8 34.9 %collective-permute-start.13 = (bf16[128,2048]{1,0:T(8,128)(2,1)}, bf16[128,2048]{1,0:T(8,128)(2,1)}, u32[]{:S(2)}, u32[]{:S(2)}) collective-permute-start(bf16[128,2048]{1,0:T(8,128)(2,1)} %collective-permute-done.12.refs_2_), channel_id=1, source_target_pairs={{0,16},{16,0},{1,17},{17,1},{2,18},{18,2},{3,19},{19,3},{4,20},{20... | collective-permute-start | bytes 1572872 | tf_op jit(solution)/shard_map/ppermute | solution.py:28
  96.6 67.7 %all-to-all-start.1 = ((bf16[8,128,512]{1,2,0:T(8,128)(2,1)}), bf16[8,128,512]{1,2,0:T(8,128)(2,1)}, u32[]{:S(2)}, u32[]{:S(2)}) async-start(bf16[8,128,512]{1,2,0:T(8,128)(2,1)} %broadcast_in_dim.5), calls=%async_computation.1 | async-start | bytes 2097152 | tf_op jit(solution)/shard_map/all_to_all | solution.py:32
  100.9 29.8 %collective-permute-start.15 = (bf16[128,2048]{1,0:T(8,128)(2,1)}, bf16[128,2048]{1,0:T(8,128)(2,1)}, u32[]{:S(2)}, u32[]{:S(2)}) collective-permute-start(bf16[128,2048]{1,0:T(8,128)(2,1)} %collective-permute-done.14.refs_6_), channel_id=1, source_target_pairs={{0,32},{32,64},{64,96},{96,0},{1,33},{33,65},{65,97},{97,1},{2,34}... | collective-permute-start | bytes 1572872 | tf_op jit(solution)/shard_map/ppermute | solution.py:24
  101.0 39.8 %collective-permute-start.17 = (bf16[128,2048]{1,0:T(8,128)(2,1)}, bf16[128,2048]{1,0:T(8,128)(2,1)}, u32[]{:S(2)}, u32[]{:S(2)}) collective-permute-start(bf16[128,2048]{1,0:T(8,128)(2,1)} %collective-permute-done.14.refs_6_), channel_id=1, source_target_pairs={{0,16},{16,0},{1,17},{17,1},{2,18},{18,2},{3,19},{19,3},{4,20},{20... | collective-permute-start | bytes 1572872 | tf_op jit(solution)/shard_map/ppermute | solution.py:28
  115.5 29.3 %collective-permute-start.21 = (bf16[128,2048]{1,0:T(8,128)(2,1)}, bf16[128,2048]{1,0:T(8,128)(2,1)}, u32[]{:S(2)}, u32[]{:S(2)}) collective-permute-start(bf16[128,2048]{1,0:T(8,128)(2,1)} %collective-permute-done.19.refs_10_), channel_id=1, source_target_pairs={{0,96},{32,0},{64,32},{96,64},{1,97},{33,1},{65,33},{97,65},{2,98}... | collective-permute-start | bytes 1572872 | tf_op jit(solution)/shard_map/ppermute | solution.py:24
  117.4 34.6 %collective-permute-start.20 = (bf16[128,2048]{1,0:T(8,128)(2,1)}, bf16[128,2048]{1,0:T(8,128)(2,1)S(1)}, u32[]{:S(2)}, u32[]{:S(2)}) collective-permute-start(bf16[128,2048]{1,0:T(8,128)(2,1)} %collective-permute-done.19.refs_10_), channel_id=1, source_target_pairs={{0,16},{16,0},{1,17},{17,1},{2,18},{18,2},{3,19},{19,3},{4,20},{20... | collective-permute-start | bytes 1572872 | tf_op jit(solution)/shard_map/ppermute | solution.py:28
  126.7 36.5 %collective-permute-start.4 = (bf16[128,2048]{1,0:T(8,128)(2,1)}, bf16[128,2048]{1,0:T(8,128)(2,1)}, u32[]{:S(2)}, u32[]{:S(2)}) collective-permute-start(bf16[128,2048]{1,0:T(8,128)(2,1)} %fusion.refs_0_), channel_id=1, source_target_pairs={{0,16},{16,0},{1,17},{17,1},{2,18},{18,2},{3,19},{19,3},{4,20},{20... | collective-permute-start | bytes 1572872 | tf_op jit(solution)/shard_map/ppermute | solution.py:28
  130.7 43.8 %collective-permute-start.24 = (bf16[128,2048]{1,0:T(8,128)(2,1)}, bf16[128,2048]{1,0:T(8,128)(2,1)S(1)}, u32[]{:S(2)}, u32[]{:S(2)}) collective-permute-start(bf16[128,2048]{1,0:T(8,128)(2,1)} %collective-permute-done.23.refs_14_), channel_id=1, source_target_pairs={{0,16},{16,0},{1,17},{17,1},{2,18},{18,2},{3,19},{19,3},{4,20},{20... | collective-permute-start | bytes 1572872 | tf_op jit(solution)/shard_map/ppermute | solution.py:28
  140.8 44.9 %collective-permute-start.16 = (bf16[128,2048]{1,0:T(8,128)(2,1)}, bf16[128,2048]{1,0:T(8,128)(2,1)S(1)}, u32[]{:S(2)}, u32[]{:S(2)}) collective-permute-start(bf16[128,2048]{1,0:T(8,128)(2,1)} %collective-permute-done.15.refs_4_), channel_id=1, source_target_pairs={{0,16},{16,0},{1,17},{17,1},{2,18},{18,2},{3,19},{19,3},{4,20},{20... | collective-permute-start | bytes 1572872 | tf_op jit(solution)/shard_map/ppermute | solution.py:28
  144.8 47.4 %collective-permute-start.22 = (bf16[128,2048]{1,0:T(8,128)(2,1)}, bf16[128,2048]{1,0:T(8,128)(2,1)S(1)}, u32[]{:S(2)}, u32[]{:S(2)}) collective-permute-start(bf16[128,2048]{1,0:T(8,128)(2,1)} %collective-permute-done.21.refs_12_), channel_id=1, source_target_pairs={{0,16},{16,0},{1,17},{17,1},{2,18},{18,2},{3,19},{19,3},{4,20},{20... | collective-permute-start | bytes 1572872 | tf_op jit(solution)/shard_map/ppermute | solution.py:28
  152.0 40.2 %copy-start.5 = (bf16[128,2048]{1,0:T(8,128)(2,1)}, bf16[128,2048]{1,0:T(8,128)(2,1)S(1)}, u32[]{:S(2)}) copy-start(bf16[128,2048]{1,0:T(8,128)(2,1)S(1)} %collective-permute-done.20.refs_11_) | copy-start | bytes 1572868
  152.0 56.2 %collective-permute-start.7 = (bf16[128,2048]{1,0:T(8,128)(2,1)}, bf16[128,2048]{1,0:T(8,128)(2,1)}, u32[]{:S(2)}, u32[]{:S(2)}) collective-permute-start(bf16[128,2048]{1,0:T(8,128)(2,1)} %fusion.refs_0_), channel_id=1, source_target_pairs={{0,32},{32,64},{64,96},{96,0},{1,33},{33,65},{65,97},{97,1},{2,34}... | collective-permute-start | bytes 1572872 | tf_op jit(solution)/shard_map/ppermute | solution.py:24
  163.2 45.0 %collective-permute-start.6 = (bf16[128,2048]{1,0:T(8,128)(2,1)}, bf16[128,2048]{1,0:T(8,128)(2,1)}, u32[]{:S(2)}, u32[]{:S(2)}) collective-permute-start(bf16[128,2048]{1,0:T(8,128)(2,1)} %collective-permute-done.4.refs_1_), channel_id=1, source_target_pairs={{0,96},{32,0},{64,32},{96,64},{1,97},{33,1},{65,33},{97,65},{2,98}... | collective-permute-start | bytes 1572872 | tf_op jit(solution)/shard_map/ppermute | solution.py:24
  174.5 17.7 %copy-start.6 = (bf16[128,2048]{1,0:T(8,128)(2,1)}, bf16[128,2048]{1,0:T(8,128)(2,1)S(1)}, u32[]{:S(2)}) copy-start(bf16[128,2048]{1,0:T(8,128)(2,1)S(1)} %collective-permute-done.24.refs_15_) | copy-start | bytes 1572868
  185.7 6.5 %copy-start.7 = (bf16[128,2048]{1,0:T(8,128)(2,1)}, bf16[128,2048]{1,0:T(8,128)(2,1)S(1)}, u32[]{:S(2)}) copy-start(bf16[128,2048]{1,0:T(8,128)(2,1)S(1)} %collective-permute-done.16.refs_5_) | copy-start | bytes 1572868
  192.2 0.8 copy-start.8
  206.1 15.2 %collective-permute-start.5 = (bf16[128,2048]{1,0:T(8,128)(2,1)}, bf16[128,2048]{1,0:T(8,128)(2,1)}, u32[]{:S(2)}, u32[]{:S(2)}) collective-permute-start(bf16[128,2048]{1,0:T(8,128)(2,1)} %fusion.refs_0_), channel_id=1, source_target_pairs={{0,96},{32,0},{64,32},{96,64},{1,97},{33,1},{65,33},{97,65},{2,98}... | collective-permute-start | bytes 1572872 | tf_op jit(solution)/shard_map/ppermute | solution.py:24
  206.6 23.2 %collective-permute-start.10 = (bf16[128,2048]{1,0:T(8,128)(2,1)}, bf16[128,2048]{1,0:T(8,128)(2,1)}, u32[]{:S(2)}, u32[]{:S(2)}) collective-permute-start(bf16[128,2048]{1,0:T(8,128)(2,1)} %collective-permute-done.4.refs_1_), channel_id=1, source_target_pairs={{0,32},{32,64},{64,96},{96,0},{1,33},{33,65},{65,97},{97,1},{2,34}... | collective-permute-start | bytes 1572872 | tf_op jit(solution)/shard_map/ppermute | solution.py:24
  208.2 21.7 %collective-permute-start.8 = (bf16[128,2048]{1,0:T(8,128)(2,1)}, bf16[128,2048]{1,0:T(8,128)(2,1)}, u32[]{:S(2)}, u32[]{:S(2)}) collective-permute-start(bf16[128,2048]{1,0:T(8,128)(2,1)} %collective-permute-done.7.refs_6_), channel_id=1, source_target_pairs={{0,32},{32,64},{64,96},{96,0},{1,33},{33,65},{65,97},{97,1},{2,34}... | collective-permute-start | bytes 1572872 | tf_op jit(solution)/shard_map/ppermute | solution.py:24
  208.2 21.6 %collective-permute-start.9 = (bf16[128,2048]{1,0:T(8,128)(2,1)}, bf16[128,2048]{1,0:T(8,128)(2,1)}, u32[]{:S(2)}, u32[]{:S(2)}) collective-permute-start(bf16[128,2048]{1,0:T(8,128)(2,1)} %collective-permute-done.6.refs_3_), channel_id=1, source_target_pairs={{0,96},{32,0},{64,32},{96,64},{1,97},{33,1},{65,33},{97,65},{2,98}... | collective-permute-start | bytes 1572872 | tf_op jit(solution)/shard_map/ppermute | solution.py:24
  217.3 36.6 %collective-permute-start.27 = (bf16[2048,512]{1,0:T(8,128)(2,1)}, bf16[2048,512]{1,0:T(8,128)(2,1)S(1)}, u32[]{:S(2)}, u32[]{:S(2)}) collective-permute-start(bf16[2048,512]{1,0:T(8,128)(2,1)} %multiply_convert_fusion), channel_id=1, source_target_pairs={{0,1},{1,0},{2,3},{3,2},{4,5},{5,4},{6,7},{7,6},{8,9},{9,8},{10,11... | collective-permute-start | bytes 6291464 | tf_op jit(solution)/shard_map/ppermute | solution.py:186
  248.8 21.9 %collective-permute-start.25 = (bf16[512,2048]{1,0:T(8,128)(2,1)}, bf16[512,2048]{1,0:T(8,128)(2,1)}, u32[]{:S(2)}, u32[]{:S(2)}) collective-permute-start(bf16[512,2048]{1,0:T(8,128)(2,1)} %get-tuple-element.13), channel_id=1, source_target_pairs={{0,1},{1,0},{2,3},{3,2},{4,5},{5,4},{6,7},{7,6},{8,9},{9,8},{10,11... | collective-permute-start | bytes 6291464 | tf_op jit(solution)/shard_map/ppermute | solution.py:186
  248.9 26.4 %collective-permute-start.26 = (bf16[512,2048]{1,0:T(8,128)(2,1)}, bf16[512,2048]{1,0:T(8,128)(2,1)}, u32[]{:S(2)}, u32[]{:S(2)}) collective-permute-start(bf16[512,2048]{1,0:T(8,128)(2,1)} %get-tuple-element.14), channel_id=1, source_target_pairs={{0,1},{1,0},{2,3},{3,2},{4,5},{5,4},{6,7},{7,6},{8,9},{9,8},{10,11... | collective-permute-start | bytes 6291464 | tf_op jit(solution)/shard_map/ppermute | solution.py:186
  249.4 20.4 %all-to-all-start.2 = ((bf16[8,128,512]{2,1,0:T(8,128)(2,1)}), bf16[8,128,512]{2,1,0:T(8,128)(2,1)S(1)}, u32[]{:S(2)}, u32[]{:S(2)}) async-start(bf16[8,128,512]{2,1,0:T(8,128)(2,1)} %bitcast.29), calls=%async_computation.2 | async-start | bytes 2097152 | tf_op jit(solution)/shard_map/all_to_all | solution.py:32
  270.7 4.6 %copy-start.4 = (bf16[512,2048]{1,0:T(8,128)(2,1)S(1)}, bf16[512,2048]{1,0:T(8,128)(2,1)}, u32[]{:S(2)}) copy-start(bf16[512,2048]{1,0:T(8,128)(2,1)} %get-tuple-element.14) | copy-start | bytes 6291460
  270.7 8.3 %copy-start.1 = (bf16[2048,512]{1,0:T(8,128)(2,1)S(1)}, bf16[2048,512]{1,0:T(8,128)(2,1)}, u32[]{:S(2)}) copy-start(bf16[2048,512]{1,0:T(8,128)(2,1)} %param.13) | copy-start | bytes 6291460
where the time goes:
time: 281 us; the launch traced here: 279 us
  waiting for transfers between devices  157 us (56%)
  starting transfers between devices  51.7 us (18%)
  Pallas kernels  32.1 us (11%)
  other arithmetic  15.6 us (6%)
  matrix products  13.6 us (5%)
  local copies, waits for them, and re-layouts  8.69 us (3%)
    ppermute x10, waiting for transfers between devices, to_pair(): return lax.ppermute(x, 'zh', SWAP)  73.7 us
    ppermute x15, waiting for transfers between devices, along_y(): return lax.ppermute(x, 'y', ring(shift))  54.6 us
    all_to_all x3, waiting for transfers between devices, across_col(): return lax.all_to_all(x, COL, 0, 0, tiled=True)  28.2 us
    ppermute x10, starting transfers between devices, to_pair(): return lax.ppermute(x, 'zh', SWAP)  22.9 us
    pallas_call x1, Pallas kernels, back_of(): pl.pallas_call(functools.partial(back_kernel, factor), out_shape=(jax.Sha...  19 us
    all_to_all x3, starting transfers between devices, across_col(): return lax.all_to_all(x, COL, 0, 0, tiled=True)  14.5 us
    ppermute x15, starting transfers between devices, along_y(): return lax.ppermute(x, 'y', ring(shift))  13.8 us
    pallas_call x1, Pallas kernels, hidden_of(): pl.pallas_call(hidden_kernel, out_shape=(jax.ShapeDtypeStruct((total, wid...  13.1 us
  transfers between devices with their start and end apart: 31, of which 15 were waited for; matrix products, arithmetic and copies ran while one was open for 10% of the time, Pallas kernels for 12%

commit v1 on v0

--- a/solution.py
+++ b/solution.py
@@ -13,7 +13,7 @@
 BF = jnp.bfloat16
 F32 = jnp.float32
 SWAP = [(0, 1), (1, 0)]
-STEP = 256
+STEP = 512
 
 
 def ring(shift):
@@ -50,26 +50,27 @@
     return pl.ds(pl.multiple_of(where[p] * rows, rows), rows)
 
 
-def hidden_kernel(where, *refs):
-    gates, ups = refs[:8], refs[8:16]
-    hidden, slope, active = refs[16:]
+def hidden_kernel(at, *refs):
+    gates, ups = refs[:2], refs[2:4]
+    hidden, slope, active = refs[-3:]
     rows = gates[0].shape[0]
-    for p in range(8):
-        g = gates[p][...].astype(F32)
-        u = ups[p][...].astype(F32)
+    for j in range(2):
+        g = gates[j][...].astype(F32)
+        u = ups[j][...].astype(F32)
         s = jax.nn.sigmoid(g)
-        here = place(where, p, rows)
+        here = place(at, 1 + j, rows)
         act = g * s
         hidden[here, :] = (act * u).astype(BF)
         slope[here, :] = u * s * (1.0 + g * (1.0 - s))
         active[here, :] = act
 
 
-def hidden_of(where, gates, ups):
+def hidden_of(at, gates, ups, before):
     rows, width = gates[0].shape
     total = 8 * rows
     piece = pl.BlockSpec((rows, STEP), lambda c, w: (0, c))
-    full = pl.BlockSpec((total, STEP), lambda c, w: (0, c))
+    pair = pl.BlockSpec((2 * rows, STEP), lambda c, w: (w[0], c))
+    kept = [pl.BlockSpec(memory_space=pl.ANY)] * len(before)
     return pl.pallas_call(
         hidden_kernel,
         out_shape=(
@@ -80,13 +81,14 @@
         grid_spec=pltpu.PrefetchScalarGridSpec(
             num_scalar_prefetch=1,
             grid=(width // STEP,),
-            in_specs=[piece] * 16,
-            out_specs=(full, full, full),
-        ),
+            in_specs=[piece] * 4 + kept,
+            out_specs=(pair, pair, pair),
+        ),
+        input_output_aliases={5 + i: i for i in range(len(before))},
         cost_estimate=pl.CostEstimate(
-            flops=total * width * 10, bytes_accessed=total * width * 14, transcendentals=total * width * 2
-        ),
-    )(where, *gates, *ups)
+            flops=2 * rows * width * 10, bytes_accessed=2 * rows * width * 14, transcendentals=2 * rows * width * 2
+        ),
+    )(at, *gates, *ups, *before)
 
 
 def back_kernel(factor, where, *refs):
@@ -154,7 +156,6 @@
     y, zh = lax.axis_index("y"), lax.axis_index("zh")
     p = lax.iota(jnp.int32, 8)
     where = lax.rem(y + p // 2, 4) * 2 + lax.rem(zh + p, 2)
-    where_too = lax.rem(2 * y + (p & 6), 8) + (zh ^ (p & 1))
 
     out_all = gather_col(grad_out)
 
@@ -180,16 +181,24 @@
     d20, d21 = along_y(d30, 1), along_y(d11, -1)
     ds = [d00, d01, d10, d11, d20, d21, d30, d31]
 
-    tok_all = gather_col(tokens)
+    tok_near = lax.ppermute(tokens, "zl", SWAP)
+    zl = lax.axis_index("zl")
+    tok_pair = jnp.stack([jnp.where(zl == 0, tokens, tok_near), jnp.where(zl == 0, tok_near, tokens)])
+    tok_all = lax.all_to_all(jnp.broadcast_to(tok_pair[None], (4,) + tok_pair.shape), "x", 0, 0, tiled=True)
+    tok_turned = tok_all.transpose(3, 1, 0, 2).reshape(width, 8 * rows)
 
     def both_cores(own):
         other = lax.ppermute(own, "core", SWAP)
         return (own.astype(F32) + other.astype(F32)).astype(BF)
 
-    hidden, slope, active = hidden_of(where, gates, ups)
+    kept = ()
+    for k in (0, 3, 1, 2):
+        at = jnp.stack([lax.rem(y + k, 4), zh, 1 - zh]).astype(jnp.int32)
+        kept = hidden_of(at, gates[2 * k : 2 * k + 2], ups[2 * k : 2 * k + 2], kept)
+    hidden, slope, active = kept
     down = (inner_rows(hidden, out_all) * factor).astype(BF)
     grad_down = both_cores(down)
-    gate, up, back = back_of(where_too, ds, slope, active, w_gate, w_up, tok_all.T, factor)
+    gate, up, back = back_of(where, ds, slope, active, w_gate, w_up, tok_turned, factor)
     back_recv = across_col(back.reshape(8, rows, width))
     grad_gate = both_cores(gate)
     grad_up = both_cores(up)

time: 281 us -> 271 us (0.964)
  waiting for transfers between devices: 157 us -> 125 us
  starting transfers between devices: 51.7 us -> 63.5 us
  Pallas kernels: 32.1 us -> 40.9 us
    ppermute x10, waiting for transfers between devices: 73.7 us -> 20.3 us  [to_pair(): return lax.ppermute(x, 'zh', SWAP)]
    ppermute x0 -> x1, waiting for transfers between devices: none -> 14.4 us  [local(): tok_near = lax.ppermute(tokens, 'zl', SWAP)]
    ppermute x15, starting transfers between devices: 13.8 us -> 28.1 us  [along_y(): return lax.ppermute(x, 'y', ring(shift))]
    pallas_call x1 -> x4, Pallas kernels: 13.1 us -> 22.5 us  [hidden_of(): pl.pallas_call(hidden_kernel, out_shape=(jax.ShapeDtypeStruct((total, wid...]
    ppermute x15, waiting for transfers between devices: 54.6 us -> 61.7 us  [along_y(): return lax.ppermute(x, 'y', ring(shift))]
    all_to_all x3 -> x2, starting transfers between devices: 14.5 us -> 9.32 us  [across_col(): return lax.all_to_all(x, COL, 0, 0, tiled=True)]
    all_to_all x0 -> x1, starting transfers between devices: none -> 3.52 us  [local(): lax.all_to_all(jnp.broadcast_to(tok_pair[None], (4,) + tok_pair.shape), '...]
    all_to_all x3 -> x2, waiting for transfers between devices: 28.2 us -> 28.4 us  [across_col(): return lax.all_to_all(x, COL, 0, 0, tiled=True)]
  transfers between devices with their start and end apart: 31 -> 32, of which waited for: 15 -> 15; matrix products, arithmetic and copies ran while one was open for 10% -> 11% of each run, Pallas kernels for 12% -> 15%
where the time goes in v1:
time: 271 us; the launch traced here: 270 us
  waiting for transfers between devices  125 us (46%)
  starting transfers between devices  63.5 us (23%)
  Pallas kernels  40.9 us (15%)
  other arithmetic  18 us (7%)
  matrix products  13.6 us (5%)
  local copies, waits for them, and re-layouts  8.13 us (3%)
    ppermute x15, waiting for transfers between devices, along_y(): return lax.ppermute(x, 'y', ring(shift))  61.7 us
    all_to_all x2, waiting for transfers between devices, across_col(): return lax.all_to_all(x, COL, 0, 0, tiled=True)  28.4 us
    ppermute x15, starting transfers between devices, along_y(): return lax.ppermute(x, 'y', ring(shift))  28.1 us
    pallas_call x4, Pallas kernels, hidden_of(): pl.pallas_call(hidden_kernel, out_shape=(jax.ShapeDtypeStruct((total, wid...  22.5 us
    ppermute x10, starting transfers between devices, to_pair(): return lax.ppermute(x, 'zh', SWAP)  21.9 us
    ppermute x10, waiting for transfers between devices, to_pair(): return lax.ppermute(x, 'zh', SWAP)  20.3 us
    pallas_call x1, Pallas kernels, back_of(): pl.pallas_call(functools.partial(back_kernel, factor), out_shape=(jax.Sha...  18.4 us
    ppermute x1, waiting for transfers between devices, local(): tok_near = lax.ppermute(tokens, 'zl', SWAP)  14.4 us
  transfers between devices with their start and end apart: 32, of which 15 were waited for; matrix products, arithmetic and copies ran while one was open for 11% of the time, Pallas kernels for 15%

profile of v1, /device:TPU:0, one launch (start us, length us, event | category | flops | bytes accessed | tf_op | source)
XLA Modules:
  0.0 269.9 jit_solution(4883004527451720402)
XLA Ops:
  0.6 2.1 broadcast_in_dim.4
  2.8 5.8 %all-to-all-start = ((bf16[8,128,512]{2,1,0:T(8,128)(2,1)}), bf16[8,128,512]{2,1,0:T(8,128)(2,1)S(1)}, u32[]{:S(2)}, u32[]{:S(2)}) async-start(bf16[8,128,512]{2,1,0:T(8,128)(2,1)} %broadcast_in_dim.4), calls=%async_computation | async-start | bytes 2097152 | tf_op jit(solution)/shard_map/all_to_all | solution.py:32
  8.5 15.7 %all-to-all-done = bf16[8,128,512]{2,1,0:T(8,128)(2,1)S(1)} async-done(((bf16[8,128,512]{2,1,0:T(8,128)(2,1)}), bf16[8,128,512]{2,1,0:T(8,128)(2,1)S(1)}, u32[]{:S(2)}, u32[]{:S(2)}) %all-to-all-start) | async-done | bytes 1048608 | tf_op jit(solution)/shard_map/all_to_all | solution.py:32
  24.2 1.7 convolution_convert_fusion.2
  25.9 3.2 %collective-permute-start = (bf16[256,2048]{1,0:T(8,128)(2,1)}, bf16[256,2048]{1,0:T(8,128)(2,1)}, u32[]{:S(2)}, u32[]{:S(2)}) collective-permute-start(bf16[256,2048]{1,0:T(8,128)(2,1)} %convolution_convert_fusion.2), channel_id=1, source_target_pairs={{0,64},{32,96},{64,0},{96,32},{1,65},{33,97},{65,1},{97,33},{2,66}... | collective-permute-start | bytes 3145736 | tf_op jit(solution)/shard_map/ppermute | solution.py:24
  29.1 1.7 convolution_convert_fusion.1
  30.9 0.7 collective-permute-start.1
  31.5 1.7 convolution_convert_fusion
  33.2 2.6 collective-permute-start.2
  35.8 3.6 %collective-permute-start.23 = (bf16[128,2048]{1,0:T(8,128)(2,1)}, bf16[128,2048]{1,0:T(8,128)(2,1)}, u32[]{:S(2)}, u32[]{:S(2)}) collective-permute-start(bf16[128,2048]{1,0:T(8,128)(2,1)} %refs_0_.1), channel_id=1, source_target_pairs={{0,16},{16,0},{1,17},{17,1},{2,18},{18,2},{3,19},{19,3},{4,20},{20... | collective-permute-start | bytes 1572872 | tf_op jit(solution)/shard_map/ppermute | solution.py:28
  39.4 14.5 %collective-permute-done = bf16[256,2048]{1,0:T(8,128)(2,1)} collective-permute-done((bf16[256,2048]{1,0:T(8,128)(2,1)}, bf16[256,2048]{1,0:T(8,128)(2,1)}, u32[]{:S(2)}, u32[]{:S(2)}) %collective-permute-start) | collective-permute-done | bytes 1048608 | tf_op jit(solution)/shard_map/ppermute | solution.py:24
  53.8 21.7 %collective-permute-done.1 = bf16[256,2048]{1,0:T(8,128)(2,1)} collective-permute-done((bf16[256,2048]{1,0:T(8,128)(2,1)}, bf16[256,2048]{1,0:T(8,128)(2,1)}, u32[]{:S(2)}, u32[]{:S(2)}) %collective-permute-start.1) | collective-permute-done | bytes 1048608 | tf_op jit(solution)/shard_map/ppermute | solution.py:24
  75.5 2.6 add_add_fusion
  78.1 1.3 copy-done.2
  79.5 3.7 %collective-permute-start.3 = (bf16[128,2048]{1,0:T(8,128)(2,1)S(1)}, bf16[128,2048]{1,0:T(8,128)(2,1)}, u32[]{:S(2)}, u32[]{:S(2)}) collective-permute-start(bf16[128,2048]{1,0:T(8,128)(2,1)S(1)} %fusion.1), channel_id=1, source_target_pairs={{0,16},{16,0},{1,17},{17,1},{2,18},{18,2},{3,19},{19,3},{4,20},{20... | collective-permute-start | bytes 1572872 | tf_op jit(solution)/shard_map/ppermute | solution.py:28
  83.2 1.1 collective-permute-start.24
  84.3 14.4 %collective-permute-done.25 = bf16[128,512]{1,0:T(8,128)(2,1)S(1)} collective-permute-done((bf16[128,512]{1,0:T(8,128)(2,1)S(1)}, bf16[128,512]{1,0:T(8,128)(2,1)S(1)}, u32[]{:S(2)}, u32[]{:S(2)}) %collective-permute-start.25) | collective-permute-done | bytes 131104 | tf_op jit(solution)/shard_map/ppermute | solution.py:184
  98.7 2.5 collective-permute-start.14
  101.2 3.2 %collective-permute-start.17 = (bf16[128,2048]{1,0:T(8,128)(2,1)}, bf16[128,2048]{1,0:T(8,128)(2,1)}, u32[]{:S(2)}, u32[]{:S(2)}) collective-permute-start(bf16[128,2048]{1,0:T(8,128)(2,1)} %refs_0_.1), channel_id=1, source_target_pairs={{0,96},{32,0},{64,32},{96,64},{1,97},{33,1},{65,33},{97,65},{2,98}... | collective-permute-start | bytes 1572872 | tf_op jit(solution)/shard_map/ppermute | solution.py:24
  104.5 1.2 collective-permute-start.20
  105.6 2.3 fusion.refs_0_
  107.9 2.1 collective-permute-done.24.refs_3_
  110.0 2.5 collective-permute-start.12
  112.5 1.7 collective-permute-done.14.refs_2_
  114.2 1.8 collective-permute-start.19
  116.5 2.1 collective-permute-start.15
  118.6 6.9 %collective-permute-done.17.refs_0_ = bf16[128,2048]{1,0:T(8,128)(2,1)} collective-permute-done((bf16[128,2048]{1,0:T(8,128)(2,1)}, bf16[128,2048]{1,0:T(8,128)(2,1)}, u32[]{:S(2)}, u32[]{:S(2)}) %collective-permute-start.17) | collective-permute-done | bytes 524320 | tf_op jit(solution)/shard_map/ppermute | solution.py:24
  125.5 1.2 collective-permute-start.22
  126.7 2.4 collective-permute-start.4
  129.3 1.5 broadcast_in_dim.5
  130.8 3.5 %all-to-all-start.1 = ((bf16[4,2,128,512]{2,1,3,0:T(2,128)(2,1)}), bf16[4,2,128,512]{2,1,3,0:T(2,128)(2,1)S(1)}, u32[]{:S(2)}, u32[]{:S(2)}) async-start(bf16[4,2,128,512]{2,1,3,0:T(2,128)(2,1)} %broadcast_in_dim.5), calls=%async_computation.1 | async-start | bytes 2097152 | tf_op jit(solution)/shard_map/all_to_all | solution.py:187
  134.3 9.5 %collective-permute-done.22.refs_3_ = bf16[128,2048]{1,0:T(8,128)(2,1)} collective-permute-done((bf16[128,2048]{1,0:T(8,128)(2,1)S(1)}, bf16[128,2048]{1,0:T(8,128)(2,1)}, u32[]{:S(2)}, u32[]{:S(2)}) %collective-permute-start.22) | collective-permute-done | bytes 524320 | tf_op jit(solution)/shard_map/ppermute | solution.py:28
  143.8 3.5 %collective-permute-start.18 = (bf16[128,2048]{1,0:T(8,128)(2,1)}, bf16[128,2048]{1,0:T(8,128)(2,1)}, u32[]{:S(2)}, u32[]{:S(2)}) collective-permute-start(bf16[128,2048]{1,0:T(8,128)(2,1)} %collective-permute-done.17.refs_0_), channel_id=1, source_target_pairs={{0,16},{16,0},{1,17},{17,1},{2,18},{18,2},{3,19},{19,3},{4,20},{20... | collective-permute-start | bytes 1572872 | tf_op jit(solution)/shard_map/ppermute | solution.py:28
  147.4 3.5 %collective-permute-start.16 = (bf16[128,2048]{1,0:T(8,128)(2,1)}, bf16[128,2048]{1,0:T(8,128)(2,1)}, u32[]{:S(2)}, u32[]{:S(2)}) collective-permute-start(bf16[128,2048]{1,0:T(8,128)(2,1)} %collective-permute-done.15.refs_2_), channel_id=1, source_target_pairs={{0,16},{16,0},{1,17},{17,1},{2,18},{18,2},{3,19},{19,3},{4,20},{20... | collective-permute-start | bytes 1572872 | tf_op jit(solution)/shard_map/ppermute | solution.py:28
  150.9 2.5 collective-permute-start.7
  153.4 1.7 collective-permute-done.4.refs_1_
  155.0 2.5 collective-permute-start.6
  157.6 0.5 fusion.16.where
  158.1 0.6 add_add_fusion.3.at
  158.7 0.7 add_add_fusion.4.at
  159.4 0.6 add_add_fusion.2.at
  160.0 0.6 add_add_fusion.1.at
  160.7 5.6 %shard_map.102 = (bf16[1024,2048]{1,0:T(8,128)(2,1)}, f32[1024,2048]{1,0:T(8,128)}, f32[1024,2048]{1,0:T(8,128)}) custom-call(s32[3]{0:T(128)} %add_add_fusion.4.at, bf16[128,2048]{1,0:T(8,128)(2,1)} %refs_0_.1, bf16[128,2048]{1,0:T(8,128)(2,1)} %collective-permute-done.23.refs_1_, bf16[128,2048]{1,0:T(8,128)(2,1)} %refs_2_.1, bf16[128,2048]{1,0:T(8,128)(2,1)} %copy-done.6), custom_call_target="tpu_custom_call" | custom-call | flops 5242880 | bytes 7340032 | tf_op jit(solution)/shard_map/pallas_call | solution.py:74
  166.3 1.4 copy.22
  167.6 1.6 reshape.25.refs_12_
  169.2 5.6 %shard_map.103 = (bf16[1024,2048]{1,0:T(8,128)(2,1)}, f32[1024,2048]{1,0:T(8,128)}, f32[1024,2048]{1,0:T(8,128)}) custom-call(s32[3]{0:T(128)} %add_add_fusion.3.at, bf16[128,2048]{1,0:T(8,128)(2,1)} %collective-permute-done.11.refs_0_, bf16[128,2048]{1,0:T(8,128)(2,1)} %copy-done.7, ...), custom_call_target="tpu_custom_call", output_to_operand_aliasing={{0}: (5, {}), {1}: (6, {}), {2}: (7, {})} | custom-call | flops 5242880 | bytes 7340032 | tf_op jit(solution)/shard_map/pallas_call | solution.py:74
  174.8 5.7 %shard_map.104 = (bf16[1024,2048]{1,0:T(8,128)(2,1)}, f32[1024,2048]{1,0:T(8,128)}, f32[1024,2048]{1,0:T(8,128)}) custom-call(s32[3]{0:T(128)} %add_add_fusion.2.at, bf16[128,2048]{1,0:T(8,128)(2,1)} %collective-permute-done.17.refs_0_, ...), custom_call_target="tpu_custom_call", output_to_operand_aliasing={{0}: (5, {}), {1}: (6, {}), {2}: (7, {})} | custom-call | flops 5242880 | bytes 7340032 | tf_op jit(solution)/shard_map/pallas_call | solution.py:74
  180.5 7.1 %collective-permute-done.16.refs_3_ = bf16[128,2048]{1,0:T(8,128)(2,1)} collective-permute-done((bf16[128,2048]{1,0:T(8,128)(2,1)}, bf16[128,2048]{1,0:T(8,128)(2,1)}, u32[]{:S(2)}, u32[]{:S(2)}) %collective-permute-start.16) | collective-permute-done | bytes 524320 | tf_op jit(solution)/shard_map/ppermute | solution.py:28
  187.6 5.6 %shard_map.105 = (bf16[1024,2048]{1,0:T(8,128)(2,1)}, f32[1024,2048]{1,0:T(8,128)}, f32[1024,2048]{1,0:T(8,128)}) custom-call(s32[3]{0:T(128)} %add_add_fusion.1.at, bf16[128,2048]{1,0:T(8,128)(2,1)} %collective-permute-done.12.refs_0_, ...), custom_call_target="tpu_custom_call", output_to_operand_aliasing={{0}: (5, {}), {1}: (6, {}), {2}: (7, {})} | custom-call | flops 5242880 | bytes 7340032 | tf_op jit(solution)/shard_map/pallas_call | solution.py:74
  193.2 3.1 %collective-permute-start.5 = (bf16[128,2048]{1,0:T(8,128)(2,1)}, bf16[128,2048]{1,0:T(8,128)(2,1)}, u32[]{:S(2)}, u32[]{:S(2)}) collective-permute-start(bf16[128,2048]{1,0:T(8,128)(2,1)} %fusion.refs_0_), channel_id=1, source_target_pairs={{0,96},{32,0},{64,32},{96,64},{1,97},{33,1},{65,33},{97,65},{2,98}... | collective-permute-start | bytes 1572872 | tf_op jit(solution)/shard_map/ppermute | solution.py:24
  196.3 0.5 collective-permute-start.8
  196.8 2.8 %collective-permute-start.9 = (bf16[128,2048]{1,0:T(8,128)(2,1)}, bf16[128,2048]{1,0:T(8,128)(2,1)}, u32[]{:S(2)}, u32[]{:S(2)}) collective-permute-start(bf16[128,2048]{1,0:T(8,128)(2,1)} %collective-permute-done.6.refs_3_), channel_id=1, source_target_pairs={{0,96},{32,0},{64,32},{96,64},{1,97},{33,1},{65,33},{97,65},{2,98}... | collective-permute-start | bytes 1572872 | tf_op jit(solution)/shard_map/ppermute | solution.py:24
  199.6 5.9 %multiply_convert_fusion = bf16[2048,512]{1,0:T(8,128)(2,1)} fusion(bf16[1024,2048]{1,0:T(8,128)(2,1)} %get-tuple-element.33, bf16[1024,512]{1,0:T(8,128)(2,1)S(1)} %bitcast.32), kind=kOutput, calls=%fused_computation.1 | convolution fusion | flops 2149580800 | bytes 7340032 | tf_op jit(solution)/shard_map/dot_general | solution.py:42
  205.5 3.4 %collective-permute-done.5.refs_2_ = bf16[128,2048]{1,0:T(8,128)(2,1)} collective-permute-done((bf16[128,2048]{1,0:T(8,128)(2,1)}, bf16[128,2048]{1,0:T(8,128)(2,1)}, u32[]{:S(2)}, u32[]{:S(2)}) %collective-permute-start.5) | collective-permute-done | bytes 524320 | tf_op jit(solution)/shard_map/ppermute | solution.py:24
  208.9 3.7 %collective-permute-done.10.refs_7_ = bf16[128,2048]{1,0:T(8,128)(2,1)} collective-permute-done((bf16[128,2048]{1,0:T(8,128)(2,1)}, bf16[128,2048]{1,0:T(8,128)(2,1)}, u32[]{:S(2)}, u32[]{:S(2)}) %collective-permute-start.10) | collective-permute-done | bytes 524320 | tf_op jit(solution)/shard_map/ppermute | solution.py:24
  212.6 9.4 %collective-permute-done.8.refs_4_ = bf16[128,2048]{1,0:T(8,128)(2,1)} collective-permute-done((bf16[128,2048]{1,0:T(8,128)(2,1)}, bf16[128,2048]{1,0:T(8,128)(2,1)}, u32[]{:S(2)}, u32[]{:S(2)}) %collective-permute-start.8) | collective-permute-done | bytes 524320 | tf_op jit(solution)/shard_map/ppermute | solution.py:24
  222.0 18.4 %shard_map.106 = (bf16[512,2048]{1,0:T(8,128)(2,1)}, bf16[512,2048]{1,0:T(8,128)(2,1)}, bf16[1024,512]{1,0:T(8,128)(2,1)}) custom-call(s32[8]{0:T(128)} %fusion.16.where, bf16[128,2048]{1,0:T(8,128)(2,1)} %fusion.refs_0_, bf16[128,2048]{1,0:T(8,128)(2,1)} %collective-permute-done.4.refs_1_, bf16[128,2048]{1,0:T(8,128)(2,1)} %collective-permute-done.5.refs_2_, ...), custom_call_target="tpu_custom_call" | custom-call | flops 8589934592 | bytes 29360128 | tf_op jit(solution)/shard_map/pallas_call | solution.py:129
  240.5 0.5 collective-permute-start.26
  241.0 3.6 %all-to-all-start.2 = ((bf16[8,128,512]{2,1,0:T(8,128)(2,1)}), bf16[8,128,512]{2,1,0:T(8,128)(2,1)S(1)}, u32[]{:S(2)}, u32[]{:S(2)}) async-start(bf16[8,128,512]{2,1,0:T(8,128)(2,1)} %bitcast.34), calls=%async_computation.2 | async-start | bytes 2097152 | tf_op jit(solution)/shard_map/all_to_all | solution.py:32
  244.6 3.5 %add_convert_fusion = bf16[2048,512]{1,0:T(8,128)(2,1)} fusion(bf16[2048,512]{1,0:T(8,128)(2,1)S(1)} %collective-permute-done.28, bf16[2048,512]{1,0:T(8,128)(2,1)} %multiply_convert_fusion), kind=kLoop, calls=%fused_computation | loop fusion | flops 4194304 | bytes 6291456 | tf_op jit(solution)/shard_map/convert_element_type | solution.py:192
  248.1 12.7 %all-to-all-done.2 = bf16[8,128,512]{2,1,0:T(8,128)(2,1)S(1)} async-done(((bf16[8,128,512]{2,1,0:T(8,128)(2,1)}), bf16[8,128,512]{2,1,0:T(8,128)(2,1)S(1)}, u32[]{:S(2)}, u32[]{:S(2)}) %all-to-all-start.2) | async-done | bytes 1048608 | tf_op jit(solution)/shard_map/all_to_all | solution.py:32
  260.8 0.8 reduce_sum.12
  261.6 4.6 %add_convert_fusion.1 = bf16[512,2048]{1,0:T(8,128)(2,1)} fusion(bf16[512,2048]{1,0:T(8,128)(2,1)} %collective-permute-done.27, bf16[512,2048]{1,0:T(8,128)(2,1)} %get-tuple-element.32), kind=kLoop, calls=%fused_computation.2 | loop fusion | flops 4194304 | bytes 6291456 | tf_op jit(solution)/shard_map/convert_element_type | solution.py:192
  266.2 3.7 %add_convert_fusion.2 = bf16[512,2048]{1,0:T(8,128)(2,1)} fusion(bf16[512,2048]{1,0:T(8,128)(2,1)} %collective-permute-done.26, bf16[512,2048]{1,0:T(8,128)(2,1)S(1)} %copy-done.3), kind=kLoop, calls=%fused_computation.3 | loop fusion | flops 4194304 | bytes 6291456 | tf_op jit(solution)/shard_map/convert_element_type | solution.py:192
  (46 shorter events, 0.9 us)
Async XLA Ops:
  0.6 23.6 %copy-start = (bf16[2048,512]{1,0:T(8,128)(2,1)S(1)}, bf16[2048,512]{1,0:T(8,128)(2,1)}, u32[]{:S(2)}) copy-start(bf16[2048,512]{1,0:T(8,128)(2,1)} %param.13) | copy-start | bytes 6291460
  2.8 21.5 %all-to-all-start = ((bf16[8,128,512]{2,1,0:T(8,128)(2,1)}), bf16[8,128,512]{2,1,0:T(8,128)(2,1)S(1)}, u32[]{:S(2)}, u32[]{:S(2)}) async-start(bf16[8,128,512]{2,1,0:T(8,128)(2,1)} %broadcast_in_dim.4), calls=%async_computation | async-start | bytes 2097152 | tf_op jit(solution)/shard_map/all_to_all | solution.py:32
  25.9 27.9 %collective-permute-start = (bf16[256,2048]{1,0:T(8,128)(2,1)}, bf16[256,2048]{1,0:T(8,128)(2,1)}, u32[]{:S(2)}, u32[]{:S(2)}) collective-permute-start(bf16[256,2048]{1,0:T(8,128)(2,1)} %convolution_convert_fusion.2), channel_id=1, source_target_pairs={{0,64},{32,96},{64,0},{96,32},{1,65},{33,97},{65,1},{97,33},{2,66}... | collective-permute-start | bytes 3145736 | tf_op jit(solution)/shard_map/ppermute | solution.py:24
  30.9 44.7 %collective-permute-start.1 = (bf16[256,2048]{1,0:T(8,128)(2,1)}, bf16[256,2048]{1,0:T(8,128)(2,1)}, u32[]{:S(2)}, u32[]{:S(2)}) collective-permute-start(bf16[256,2048]{1,0:T(8,128)(2,1)} %convolution_convert_fusion.1), channel_id=1, source_target_pairs={{0,32},{32,64},{64,96},{96,0},{1,33},{33,65},{65,97},{97,1},{2,34}... | collective-permute-start | bytes 3145736 | tf_op jit(solution)/shard_map/ppermute | solution.py:24
  33.2 42.3 %collective-permute-start.2 = (bf16[256,2048]{1,0:T(8,128)(2,1)}, bf16[256,2048]{1,0:T(8,128)(2,1)}, u32[]{:S(2)}, u32[]{:S(2)}) collective-permute-start(bf16[256,2048]{1,0:T(8,128)(2,1)} %convolution_convert_fusion), channel_id=1, source_target_pairs={{0,96},{32,0},{64,32},{96,64},{1,97},{33,1},{65,33},{97,65},{2,98}... | collective-permute-start | bytes 3145736 | tf_op jit(solution)/shard_map/ppermute | solution.py:24
  35.8 65.4 %collective-permute-start.23 = (bf16[128,2048]{1,0:T(8,128)(2,1)}, bf16[128,2048]{1,0:T(8,128)(2,1)}, u32[]{:S(2)}, u32[]{:S(2)}) collective-permute-start(bf16[128,2048]{1,0:T(8,128)(2,1)} %refs_0_.1), channel_id=1, source_target_pairs={{0,16},{16,0},{1,17},{17,1},{2,18},{18,2},{3,19},{19,3},{4,20},{20... | collective-permute-start | bytes 1572872 | tf_op jit(solution)/shard_map/ppermute | solution.py:28
  39.4 61.9 %collective-permute-start.11 = (bf16[128,2048]{1,0:T(8,128)(2,1)}, bf16[128,2048]{1,0:T(8,128)(2,1)}, u32[]{:S(2)}, u32[]{:S(2)}) collective-permute-start(bf16[128,2048]{1,0:T(8,128)(2,1)} %refs_0_.1), channel_id=1, source_target_pairs={{0,32},{32,64},{64,96},{96,0},{1,33},{33,65},{65,97},{97,1},{2,34}... | collective-permute-start | bytes 1572872 | tf_op jit(solution)/shard_map/ppermute | solution.py:24
  39.4 43.8 %copy-start.8 = (bf16[128,512]{1,0:T(8,128)(2,1)S(1)}, bf16[128,512]{1,0:T(8,128)(2,1)}, u32[]{:S(2)}) copy-start(bf16[128,512]{1,0:T(8,128)(2,1)} %param.7) | copy-start | bytes 393220
  78.1 1.3 copy-start.2
  79.5 25.0 %collective-permute-start.3 = (bf16[128,2048]{1,0:T(8,128)(2,1)S(1)}, bf16[128,2048]{1,0:T(8,128)(2,1)}, u32[]{:S(2)}, u32[]{:S(2)}) collective-permute-start(bf16[128,2048]{1,0:T(8,128)(2,1)S(1)} %fusion.1), channel_id=1, source_target_pairs={{0,16},{16,0},{1,17},{17,1},{2,18},{18,2},{3,19},{19,3},{4,20},{20... | collective-permute-start | bytes 1572872 | tf_op jit(solution)/shard_map/ppermute | solution.py:28
  83.2 15.5 %collective-permute-start.25 = (bf16[128,512]{1,0:T(8,128)(2,1)S(1)}, bf16[128,512]{1,0:T(8,128)(2,1)S(1)}, u32[]{:S(2)}, u32[]{:S(2)}) collective-permute-start(bf16[128,512]{1,0:T(8,128)(2,1)S(1)} %copy-done.8), channel_id=1, source_target_pairs={{0,8},{8,0},{1,9},{9,1},{2,10},{10,2},{3,11},{11,3},{4,12},{12,4},... | collective-permute-start | bytes 393224 | tf_op jit(solution)/shard_map/ppermute | solution.py:184
  83.2 26.8 %collective-permute-start.24 = (bf16[128,2048]{1,0:T(8,128)(2,1)}, bf16[128,2048]{1,0:T(8,128)(2,1)S(1)}, u32[]{:S(2)}, u32[]{:S(2)}) collective-permute-start(bf16[128,2048]{1,0:T(8,128)(2,1)} %refs_2_.1), channel_id=1, source_target_pairs={{0,16},{16,0},{1,17},{17,1},{2,18},{18,2},{3,19},{19,3},{4,20},{20... | collective-permute-start | bytes 1572872 | tf_op jit(solution)/shard_map/ppermute | solution.py:28
  98.7 15.5 %collective-permute-start.14 = (bf16[128,2048]{1,0:T(8,128)(2,1)}, bf16[128,2048]{1,0:T(8,128)(2,1)S(1)}, u32[]{:S(2)}, u32[]{:S(2)}) collective-permute-start(bf16[128,2048]{1,0:T(8,128)(2,1)} %refs_2_.1), channel_id=1, source_target_pairs={{0,96},{32,0},{64,32},{96,64},{1,97},{33,1},{65,33},{97,65},{2,98}... | collective-permute-start | bytes 1572872 | tf_op jit(solution)/shard_map/ppermute | solution.py:24
  101.2 15.2 %collective-permute-start.21 = (bf16[128,2048]{1,0:T(8,128)(2,1)}, bf16[128,2048]{1,0:T(8,128)(2,1)S(1)}, u32[]{:S(2)}, u32[]{:S(2)}) collective-permute-start(bf16[128,2048]{1,0:T(8,128)(2,1)} %refs_2_.1), channel_id=1, source_target_pairs={{0,32},{32,64},{64,96},{96,0},{1,33},{33,65},{65,97},{97,1},{2,34}... | collective-permute-start | bytes 1572872 | tf_op jit(solution)/shard_map/ppermute | solution.py:24
  101.2 24.3 %collective-permute-start.17 = (bf16[128,2048]{1,0:T(8,128)(2,1)}, bf16[128,2048]{1,0:T(8,128)(2,1)}, u32[]{:S(2)}, u32[]{:S(2)}) collective-permute-start(bf16[128,2048]{1,0:T(8,128)(2,1)} %refs_0_.1), channel_id=1, source_target_pairs={{0,96},{32,0},{64,32},{96,64},{1,97},{33,1},{65,33},{97,65},{2,98}... | collective-permute-start | bytes 1572872 | tf_op jit(solution)/shard_map/ppermute | solution.py:24
  104.5 22.2 %collective-permute-start.20 = (bf16[128,2048]{1,0:T(8,128)(2,1)}, bf16[128,2048]{1,0:T(8,128)(2,1)S(1)}, u32[]{:S(2)}, u32[]{:S(2)}) collective-permute-start(bf16[128,2048]{1,0:T(8,128)(2,1)} %collective-permute-done.11.refs_0_), channel_id=1, source_target_pairs={{0,16},{16,0},{1,17},{17,1},{2,18},{18,2},{3,19},{19,3},{4,20},{20... | collective-permute-start | bytes 1572872 | tf_op jit(solution)/shard_map/ppermute | solution.py:28
  110.0 19.1 %copy-start.6 = (bf16[128,2048]{1,0:T(8,128)(2,1)}, bf16[128,2048]{1,0:T(8,128)(2,1)S(1)}, u32[]{:S(2)}) copy-start(bf16[128,2048]{1,0:T(8,128)(2,1)S(1)} %collective-permute-done.24.refs_3_) | copy-start | bytes 1572868
  110.0 37.3 %collective-permute-start.12 = (bf16[128,2048]{1,0:T(8,128)(2,1)}, bf16[128,2048]{1,0:T(8,128)(2,1)}, u32[]{:S(2)}, u32[]{:S(2)}) collective-permute-start(bf16[128,2048]{1,0:T(8,128)(2,1)} %collective-permute-done.11.refs_0_), channel_id=1, source_target_pairs={{0,32},{32,64},{64,96},{96,0},{1,33},{33,65},{65,97},{97,1},{2,34}... | collective-permute-start | bytes 1572872 | tf_op jit(solution)/shard_map/ppermute | solution.py:24
  114.2 16.6 %copy-start.4 = (bf16[128,2048]{1,0:T(8,128)(2,1)}, bf16[128,2048]{1,0:T(8,128)(2,1)S(1)}, u32[]{:S(2)}) copy-start(bf16[128,2048]{1,0:T(8,128)(2,1)S(1)} %collective-permute-done.14.refs_2_) | copy-start | bytes 1572868
  114.2 36.7 %collective-permute-start.19 = (bf16[128,2048]{1,0:T(8,128)(2,1)S(1)}, bf16[128,2048]{1,0:T(8,128)(2,1)}, u32[]{:S(2)}, u32[]{:S(2)}) collective-permute-start(bf16[128,2048]{1,0:T(8,128)(2,1)S(1)} %collective-permute-done.14.refs_2_), channel_id=1, source_target_pairs={{0,16},{16,0},{1,17},{17,1},{2,18},{18,2},{3,19},{19,3},{4,20},{20... | collective-permute-start | bytes 1572872 | tf_op jit(solution)/shard_map/ppermute | solution.py:28
  116.5 14.3 %copy-start.5 = (bf16[128,2048]{1,0:T(8,128)(2,1)}, bf16[128,2048]{1,0:T(8,128)(2,1)S(1)}, u32[]{:S(2)}) copy-start(bf16[128,2048]{1,0:T(8,128)(2,1)S(1)} %collective-permute-done.21.refs_2_) | copy-start | bytes 1572868
  116.5 30.9 %collective-permute-start.15 = (bf16[128,2048]{1,0:T(8,128)(2,1)S(1)}, bf16[128,2048]{1,0:T(8,128)(2,1)}, u32[]{:S(2)}, u32[]{:S(2)}) collective-permute-start(bf16[128,2048]{1,0:T(8,128)(2,1)S(1)} %collective-permute-done.14.refs_2_), channel_id=1, source_target_pairs={{0,96},{32,0},{64,32},{96,64},{1,97},{33,1},{65,33},{97,65},{2,98}... | collective-permute-start | bytes 1572872 | tf_op jit(solution)/shard_map/ppermute | solution.py:24
  125.5 18.3 %collective-permute-start.22 = (bf16[128,2048]{1,0:T(8,128)(2,1)S(1)}, bf16[128,2048]{1,0:T(8,128)(2,1)}, u32[]{:S(2)}, u32[]{:S(2)}) collective-permute-start(bf16[128,2048]{1,0:T(8,128)(2,1)S(1)} %collective-permute-done.21.refs_2_), channel_id=1, source_target_pairs={{0,16},{16,0},{1,17},{17,1},{2,18},{18,2},{3,19},{19,3},{4,20},{20... | collective-permute-start | bytes 1572872 | tf_op jit(solution)/shard_map/ppermute | solution.py:28
  126.7 4.1 %copy-start.7 = (bf16[128,2048]{1,0:T(8,128)(2,1)}, bf16[128,2048]{1,0:T(8,128)(2,1)S(1)}, u32[]{:S(2)}) copy-start(bf16[128,2048]{1,0:T(8,128)(2,1)S(1)} %collective-permute-done.20.refs_1_) | copy-start | bytes 1572868
  126.7 28.4 %collective-permute-start.4 = (bf16[128,2048]{1,0:T(8,128)(2,1)}, bf16[128,2048]{1,0:T(8,128)(2,1)}, u32[]{:S(2)}, u32[]{:S(2)}) collective-permute-start(bf16[128,2048]{1,0:T(8,128)(2,1)} %fusion.refs_0_), channel_id=1, source_target_pairs={{0,16},{16,0},{1,17},{17,1},{2,18},{18,2},{3,19},{19,3},{4,20},{20... | collective-permute-start | bytes 1572872 | tf_op jit(solution)/shard_map/ppermute | solution.py:28
  130.8 35.5 %all-to-all-start.1 = ((bf16[4,2,128,512]{2,1,3,0:T(2,128)(2,1)}), bf16[4,2,128,512]{2,1,3,0:T(2,128)(2,1)S(1)}, u32[]{:S(2)}, u32[]{:S(2)}) async-start(bf16[4,2,128,512]{2,1,3,0:T(2,128)(2,1)} %broadcast_in_dim.5), calls=%async_computation.1 | async-start | bytes 2097152 | tf_op jit(solution)/shard_map/all_to_all | solution.py:187
  143.8 31.0 %collective-permute-start.18 = (bf16[128,2048]{1,0:T(8,128)(2,1)}, bf16[128,2048]{1,0:T(8,128)(2,1)}, u32[]{:S(2)}, u32[]{:S(2)}) collective-permute-start(bf16[128,2048]{1,0:T(8,128)(2,1)} %collective-permute-done.17.refs_0_), channel_id=1, source_target_pairs={{0,16},{16,0},{1,17},{17,1},{2,18},{18,2},{3,19},{19,3},{4,20},{20... | collective-permute-start | bytes 1572872 | tf_op jit(solution)/shard_map/ppermute | solution.py:28
  147.3 33.2 %collective-permute-start.13 = (bf16[128,2048]{1,0:T(8,128)(2,1)}, bf16[128,2048]{1,0:T(8,128)(2,1)}, u32[]{:S(2)}, u32[]{:S(2)}) collective-permute-start(bf16[128,2048]{1,0:T(8,128)(2,1)} %collective-permute-done.12.refs_0_), channel_id=1, source_target_pairs={{0,16},{16,0},{1,17},{17,1},{2,18},{18,2},{3,19},{19,3},{4,20},{20... | collective-permute-start | bytes 1572872 | tf_op jit(solution)/shard_map/ppermute | solution.py:28
  147.4 40.2 %collective-permute-start.16 = (bf16[128,2048]{1,0:T(8,128)(2,1)}, bf16[128,2048]{1,0:T(8,128)(2,1)}, u32[]{:S(2)}, u32[]{:S(2)}) collective-permute-start(bf16[128,2048]{1,0:T(8,128)(2,1)} %collective-permute-done.15.refs_2_), channel_id=1, source_target_pairs={{0,16},{16,0},{1,17},{17,1},{2,18},{18,2},{3,19},{19,3},{4,20},{20... | collective-permute-start | bytes 1572872 | tf_op jit(solution)/shard_map/ppermute | solution.py:28
  150.9 45.4 %collective-permute-start.7 = (bf16[128,2048]{1,0:T(8,128)(2,1)}, bf16[128,2048]{1,0:T(8,128)(2,1)}, u32[]{:S(2)}, u32[]{:S(2)}) collective-permute-start(bf16[128,2048]{1,0:T(8,128)(2,1)} %fusion.refs_0_), channel_id=1, source_target_pairs={{0,32},{32,64},{64,96},{96,0},{1,33},{33,65},{65,97},{97,1},{2,34}... | collective-permute-start | bytes 1572872 | tf_op jit(solution)/shard_map/ppermute | solution.py:24
  155.0 41.8 %collective-permute-start.6 = (bf16[128,2048]{1,0:T(8,128)(2,1)}, bf16[128,2048]{1,0:T(8,128)(2,1)}, u32[]{:S(2)}, u32[]{:S(2)}) collective-permute-start(bf16[128,2048]{1,0:T(8,128)(2,1)} %collective-permute-done.4.refs_1_), channel_id=1, source_target_pairs={{0,96},{32,0},{64,32},{96,64},{1,97},{33,1},{65,33},{97,65},{2,98}... | collective-permute-start | bytes 1572872 | tf_op jit(solution)/shard_map/ppermute | solution.py:24
  193.2 15.7 %collective-permute-start.5 = (bf16[128,2048]{1,0:T(8,128)(2,1)}, bf16[128,2048]{1,0:T(8,128)(2,1)}, u32[]{:S(2)}, u32[]{:S(2)}) collective-permute-start(bf16[128,2048]{1,0:T(8,128)(2,1)} %fusion.refs_0_), channel_id=1, source_target_pairs={{0,96},{32,0},{64,32},{96,64},{1,97},{33,1},{65,33},{97,65},{2,98}... | collective-permute-start | bytes 1572872 | tf_op jit(solution)/shard_map/ppermute | solution.py:24
  196.3 16.3 %collective-permute-start.10 = (bf16[128,2048]{1,0:T(8,128)(2,1)}, bf16[128,2048]{1,0:T(8,128)(2,1)}, u32[]{:S(2)}, u32[]{:S(2)}) collective-permute-start(bf16[128,2048]{1,0:T(8,128)(2,1)} %collective-permute-done.4.refs_1_), channel_id=1, source_target_pairs={{0,32},{32,64},{64,96},{96,0},{1,33},{33,65},{65,97},{97,1},{2,34}... | collective-permute-start | bytes 1572872 | tf_op jit(solution)/shard_map/ppermute | solution.py:24
  196.3 25.7 %collective-permute-start.8 = (bf16[128,2048]{1,0:T(8,128)(2,1)}, bf16[128,2048]{1,0:T(8,128)(2,1)}, u32[]{:S(2)}, u32[]{:S(2)}) collective-permute-start(bf16[128,2048]{1,0:T(8,128)(2,1)} %collective-permute-done.7.refs_6_), channel_id=1, source_target_pairs={{0,32},{32,64},{64,96},{96,0},{1,33},{33,65},{65,97},{97,1},{2,34}... | collective-permute-start | bytes 1572872 | tf_op jit(solution)/shard_map/ppermute | solution.py:24
  196.8 25.2 %collective-permute-start.9 = (bf16[128,2048]{1,0:T(8,128)(2,1)}, bf16[128,2048]{1,0:T(8,128)(2,1)}, u32[]{:S(2)}, u32[]{:S(2)}) collective-permute-start(bf16[128,2048]{1,0:T(8,128)(2,1)} %collective-permute-done.6.refs_3_), channel_id=1, source_target_pairs={{0,96},{32,0},{64,32},{96,64},{1,97},{33,1},{65,33},{97,65},{2,98}... | collective-permute-start | bytes 1572872 | tf_op jit(solution)/shard_map/ppermute | solution.py:24
  205.5 39.1 %collective-permute-start.28 = (bf16[2048,512]{1,0:T(8,128)(2,1)}, bf16[2048,512]{1,0:T(8,128)(2,1)S(1)}, u32[]{:S(2)}, u32[]{:S(2)}) collective-permute-start(bf16[2048,512]{1,0:T(8,128)(2,1)} %multiply_convert_fusion), channel_id=1, source_target_pairs={{0,1},{1,0},{2,3},{3,2},{4,5},{5,4},{6,7},{7,6},{8,9},{9,8},{10,11... | collective-permute-start | bytes 6291464 | tf_op jit(solution)/shard_map/ppermute | solution.py:191
  240.4 21.2 %collective-permute-start.27 = (bf16[512,2048]{1,0:T(8,128)(2,1)}, bf16[512,2048]{1,0:T(8,128)(2,1)}, u32[]{:S(2)}, u32[]{:S(2)}) collective-permute-start(bf16[512,2048]{1,0:T(8,128)(2,1)} %get-tuple-element.32), channel_id=1, source_target_pairs={{0,1},{1,0},{2,3},{3,2},{4,5},{5,4},{6,7},{7,6},{8,9},{9,8},{10,11... | collective-permute-start | bytes 6291464 | tf_op jit(solution)/shard_map/ppermute | solution.py:191
  240.5 25.7 %collective-permute-start.26 = (bf16[512,2048]{1,0:T(8,128)(2,1)}, bf16[512,2048]{1,0:T(8,128)(2,1)}, u32[]{:S(2)}, u32[]{:S(2)}) collective-permute-start(bf16[512,2048]{1,0:T(8,128)(2,1)} %get-tuple-element.31), channel_id=1, source_target_pairs={{0,1},{1,0},{2,3},{3,2},{4,5},{5,4},{6,7},{7,6},{8,9},{9,8},{10,11... | collective-permute-start | bytes 6291464 | tf_op jit(solution)/shard_map/ppermute | solution.py:191
  241.0 19.7 %all-to-all-start.2 = ((bf16[8,128,512]{2,1,0:T(8,128)(2,1)}), bf16[8,128,512]{2,1,0:T(8,128)(2,1)S(1)}, u32[]{:S(2)}, u32[]{:S(2)}) async-start(bf16[8,128,512]{2,1,0:T(8,128)(2,1)} %bitcast.34), calls=%async_computation.2 | async-start | bytes 2097152 | tf_op jit(solution)/shard_map/all_to_all | solution.py:32
  261.6 4.6 %copy-start.3 = (bf16[512,2048]{1,0:T(8,128)(2,1)S(1)}, bf16[512,2048]{1,0:T(8,128)(2,1)}, u32[]{:S(2)}) copy-start(bf16[512,2048]{1,0:T(8,128)(2,1)} %get-tuple-element.31) | copy-start | bytes 6291460
  261.6 8.3 %copy-start.1 = (bf16[2048,512]{1,0:T(8,128)(2,1)S(1)}, bf16[2048,512]{1,0:T(8,128)(2,1)}, u32[]{:S(2)}) copy-start(bf16[2048,512]{1,0:T(8,128)(2,1)} %param.13) | copy-start | bytes 6291460

commit v2 on v1

--- a/solution.py
+++ b/solution.py
@@ -14,6 +14,7 @@
 F32 = jnp.float32
 SWAP = [(0, 1), (1, 0)]
 STEP = 512
+NARROW = 256
 
 
 def ring(shift):
@@ -65,10 +66,14 @@
         active[here, :] = act
 
 
-def hidden_of(at, gates, ups, before):
-    rows, width = gates[0].shape
+def piece_of(rows, which):
+    return pl.BlockSpec((rows, STEP), lambda c, w: (which, c))
+
+
+def hidden_of(at, rows, gates, ups, before):
+    width = gates[0].shape[1]
     total = 8 * rows
-    piece = pl.BlockSpec((rows, STEP), lambda c, w: (0, c))
+    pieces = [piece_of(rows, 0)] * 2 + [piece_of(rows, u.shape[0] // rows - 1) for u in ups]
     pair = pl.BlockSpec((2 * rows, STEP), lambda c, w: (w[0], c))
     kept = [pl.BlockSpec(memory_space=pl.ANY)] * len(before)
     return pl.pallas_call(
@@ -81,7 +86,7 @@
         grid_spec=pltpu.PrefetchScalarGridSpec(
             num_scalar_prefetch=1,
             grid=(width // STEP,),
-            in_specs=[piece] * 4 + kept,
+            in_specs=pieces + kept,
             out_specs=(pair, pair, pair),
         ),
         input_output_aliases={5 + i: i for i in range(len(before))},
@@ -91,9 +96,10 @@
     )(at, *gates, *ups, *before)
 
 
-def back_kernel(factor, where, *refs):
-    ds = refs[:8]
-    slope, active, w_gate, w_up, tok, grad_gate, grad_up, back, d_gate, d_up, total = refs[8:]
+def back_kernel(factor, first, where, *refs):
+    ds, refs = refs[:8], refs[8:]
+    slope, active, w_gate, w_up, tok = refs[:5]
+    grad_gate, grad_up, back, d_gate, d_up, total = refs[-6:]
     rows = ds[0].shape[0]
     c = pl.program_id(0)
     for p in range(8):
@@ -108,7 +114,7 @@
 
     @pl.when(c == 0)
     def _():
-        total[...] = more
+        total[...] = more if first else refs[5][...] + more
 
     @pl.when(c > 0)
     def _():
@@ -116,38 +122,44 @@
 
     @pl.when(c == pl.num_programs(0) - 1)
     def _():
-        back[...] = total[...].astype(BF)
-
-
-def back_of(where, ds, slope, active, w_gate, w_up, tok, factor):
-    rows, width = ds[0].shape
-    depth = w_gate.shape[0]
+        back[...] = total[...].astype(back.dtype)
+
+
+def back_of(where, half, ds, slope, active, w_gate, w_up, tok, factor, before):
+    rows, part = ds[0].shape
+    depth, width = w_gate.shape
     total = 8 * rows
-    piece = pl.BlockSpec((rows, STEP), lambda c, w: (0, c))
-    weight = pl.BlockSpec((depth, STEP), lambda c, w: (0, c))
-    full = pl.BlockSpec((total, STEP), lambda c, w: (0, c))
+    steps = part // NARROW
+    piece = pl.BlockSpec((rows, NARROW), lambda c, w: (0, c))
+    weight = pl.BlockSpec((depth, NARROW), lambda c, w: (0, c + half * steps))
+    full = pl.BlockSpec((total, NARROW), lambda c, w: (0, c + half * steps))
+    whole = pl.BlockSpec((total, depth), lambda c, w: (0, 0))
+    kept = [whole] + [pl.BlockSpec(memory_space=pl.ANY)] * 2 if before else []
     return pl.pallas_call(
-        functools.partial(back_kernel, factor),
+        functools.partial(back_kernel, factor, not before),
         out_shape=(
             jax.ShapeDtypeStruct((depth, width), BF),
             jax.ShapeDtypeStruct((depth, width), BF),
-            jax.ShapeDtypeStruct((total, depth), BF),
+            jax.ShapeDtypeStruct((total, depth), BF if before else F32),
         ),
         grid_spec=pltpu.PrefetchScalarGridSpec(
             num_scalar_prefetch=1,
-            grid=(width // STEP,),
-            in_specs=[piece] * 8 + [full, full, weight, weight, pl.BlockSpec((depth, total), lambda c, w: (0, 0))],
-            out_specs=(weight, weight, pl.BlockSpec((total, depth), lambda c, w: (0, 0))),
+            grid=(steps,),
+            in_specs=[piece] * 8
+            + [full, full, weight, weight, pl.BlockSpec((depth, total), lambda c, w: (0, 0))]
+            + kept,
+            out_specs=(weight, weight, whole),
             scratch_shapes=[
-                pltpu.VMEM((total, STEP), BF),
-                pltpu.VMEM((total, STEP), BF),
+                pltpu.VMEM((total, NARROW), BF),
+                pltpu.VMEM((total, NARROW), BF),
                 pltpu.VMEM((total, depth), F32),
             ],
         ),
+        input_output_aliases={15: 0, 16: 1} if before else {},
         cost_estimate=pl.CostEstimate(
-            flops=8 * total * width * depth, bytes_accessed=total * width * 14, transcendentals=0
-        ),
-    )(where, *ds, slope, active, w_gate, w_up, tok)
+            flops=8 * total * part * depth, bytes_accessed=total * part * 14, transcendentals=0
+        ),
+    )(where, *ds, slope, active, w_gate, w_up, tok, *before)
 
 
 def local(tokens, grad_out, gate_pre, up_pre, w_gate, w_up, w_down):
@@ -159,27 +171,34 @@
 
     out_all = gather_col(grad_out)
 
-    g3, g1 = along_y(gate_pre, 1), along_y(gate_pre, -1)
-    u3, u1 = along_y(up_pre, 1), along_y(up_pre, -1)
-    g2, u2 = along_y(g3, 1), along_y(u1, -1)
-    gates = [v for g in (gate_pre, g1, g2, g3) for v in (g, to_pair(g))]
-    ups = [v for u in (up_pre, u1, u2, u3) for v in (u, to_pair(u))]
-
-    def part(k):
+    both = jnp.concatenate([gate_pre, up_pre], axis=0)
+    both3, both1 = along_y(both, 1), along_y(both, -1)
+    g2 = along_y(both3[:rows], 1)
+    u2 = along_y(both1[rows:], -1)
+    paired = {k: (v, to_pair(v)) for k, v in ((0, both), (3, both3), (1, both1))}
+    saved = {k: (v, v) for k, v in paired.items()}
+    saved[2] = ((g2, to_pair(g2)), (u2, to_pair(u2)))
+
+    part_rows = w_down.shape[0] // 2
+
+    def part(h, k):
         here = lax.dynamic_slice_in_dim(out_all, lax.rem(y + k, 4) * (2 * rows), 2 * rows, 0)
-        return times_transposed(here, w_down).astype(BF if k else F32)
-
-    recv = [along_y(part(k), k) for k in (2, 1, 3)]
-    total = part(0) + sum(r.astype(F32) for r in recv)
-    total = total.reshape(2, rows, -1)
-    theirs = lax.dynamic_index_in_dim(total, 1 - zh, 0, keepdims=False).astype(BF)
-    mine = lax.dynamic_index_in_dim(total, zh, 0, keepdims=False)
-    d00 = (mine + to_pair(theirs).astype(F32)).astype(BF)
-    d30, d10 = along_y(d00, 1), along_y(d00, -1)
-    d01 = to_pair(d00)
-    d31, d11 = along_y(d01, 1), along_y(d01, -1)
-    d20, d21 = along_y(d30, 1), along_y(d11, -1)
-    ds = [d00, d01, d10, d11, d20, d21, d30, d31]
+        return times_transposed(here, w_down[h * part_rows : (h + 1) * part_rows]).astype(BF if k else F32)
+
+    def gathered(h):
+        recv = [along_y(part(h, k), k) for k in (2, 1, 3)]
+        total = part(h, 0) + sum(r.astype(F32) for r in recv)
+        total = total.reshape(2, rows, -1)
+        theirs = lax.dynamic_index_in_dim(total, 1 - zh, 0, keepdims=False).astype(BF)
+        mine = lax.dynamic_index_in_dim(total, zh, 0, keepdims=False)
+        d00 = (mine + to_pair(theirs).astype(F32)).astype(BF)
+        d30, d10 = along_y(d00, 1), along_y(d00, -1)
+        d01 = to_pair(d00)
+        d31, d11 = along_y(d01, 1), along_y(d01, -1)
+        d20, d21 = along_y(d30, 1), along_y(d11, -1)
+        return [d00, d01, d10, d11, d20, d21, d30, d31]
+
+    halves = [gathered(h) for h in (0, 1)]
 
     tok_near = lax.ppermute(tokens, "zl", SWAP)
     zl = lax.axis_index("zl")
@@ -194,11 +213,14 @@
     kept = ()
     for k in (0, 3, 1, 2):
         at = jnp.stack([lax.rem(y + k, 4), zh, 1 - zh]).astype(jnp.int32)
-        kept = hidden_of(at, gates[2 * k : 2 * k + 2], ups[2 * k : 2 * k + 2], kept)
+        kept = hidden_of(at, rows, *saved[k], kept)
     hidden, slope, active = kept
     down = (inner_rows(hidden, out_all) * factor).astype(BF)
     grad_down = both_cores(down)
-    gate, up, back = back_of(where, ds, slope, active, w_gate, w_up, tok_turned, factor)
+    before = ()
+    for h in (0, 1):
+        gate, up, back = back_of(where, h, halves[h], slope, active, w_gate, w_up, tok_turned, factor, before)
+        before = (back, gate, up)
     back_recv = across_col(back.reshape(8, rows, width))
     grad_gate = both_cores(gate)
     grad_up = both_cores(up)

time: 271 us -> 272 us (level)
  waiting for transfers between devices: 125 us -> 106 us
  matrix products: 13.6 us -> 22.8 us
  Pallas kernels: 40.9 us -> 46.7 us
  local copies, waits for them, and re-layouts: 8.13 us -> 11.7 us
    ppermute x15 -> x22, waiting for transfers between devices: 61.7 us -> 26.4 us  [along_y(): return lax.ppermute(x, 'y', ring(shift))]
    ppermute x10 -> x9, waiting for transfers between devices: 20.3 us -> 55 us  [to_pair(): return lax.ppermute(x, 'zh', SWAP)]
    all_to_all x2, waiting for transfers between devices: 28.4 us -> 16.1 us  [across_col(): return lax.all_to_all(x, COL, 0, 0, tiled=True)]
    dot_general x4 -> x8, matrix products: 7.74 us -> 16.6 us  [times_transposed(): lax.dot_general(left, right, (((1,), (1,)), ((), ())), preferred_element_...]
    ppermute x10 -> x9, starting transfers between devices: 21.9 us -> 14.6 us  [to_pair(): return lax.ppermute(x, 'zh', SWAP)]
    ppermute x1, waiting for transfers between devices: 14.4 us -> 8.35 us  [local(): tok_near = lax.ppermute(tokens, 'zl', SWAP)]
    pallas_call x1 -> x2, Pallas kernels: 18.4 us -> 24.2 us  [back_of(): pl.pallas_call(functools.partial(back_kernel, factor, not before), out_sh...]
    ppermute x15 -> x22, starting transfers between devices: 28.1 us -> 32.5 us  [along_y(): return lax.ppermute(x, 'y', ring(shift))]
  transfers between devices with their start and end apart: 32 -> 38, of which waited for: 15 -> 8; matrix products, arithmetic and copies ran while one was open for 11% -> 16% of each run, Pallas kernels for 15% -> 17%
where the time goes in v2:
time: 272 us; the launch traced here: 270 us
  waiting for transfers between devices  106 us (39%)
  starting transfers between devices  64 us (24%)
  Pallas kernels  46.7 us (17%)
  matrix products  22.8 us (8%)
  other arithmetic  18.1 us (7%)
  local copies, waits for them, and re-layouts  11.7 us (4%)
    ppermute x9, waiting for transfers between devices, to_pair(): return lax.ppermute(x, 'zh', SWAP)  55 us
    ppermute x22, starting transfers between devices, along_y(): return lax.ppermute(x, 'y', ring(shift))  32.5 us
    ppermute x22, waiting for transfers between devices, along_y(): return lax.ppermute(x, 'y', ring(shift))  26.4 us
    pallas_call x2, Pallas kernels, back_of(): pl.pallas_call(functools.partial(back_kernel, factor, not before), out_sh...  24.2 us
    pallas_call x4, Pallas kernels, hidden_of(): pl.pallas_call(hidden_kernel, out_shape=(jax.ShapeDtypeStruct((total, wid...  22.5 us
    dot_general x8, matrix products, times_transposed(): lax.dot_general(left, right, (((1,), (1,)), ((), ())), preferred_element_...  16.6 us
    all_to_all x2, waiting for transfers between devices, across_col(): return lax.all_to_all(x, COL, 0, 0, tiled=True)  16.1 us
    ppermute x9, starting transfers between devices, to_pair(): return lax.ppermute(x, 'zh', SWAP)  14.6 us
  transfers between devices with their start and end apart: 38, of which 8 were waited for; matrix products, arithmetic and copies ran while one was open for 16% of the time, Pallas kernels for 17%

profile of v2, /device:TPU:0, one launch (start us, length us, event | category | flops | bytes accessed | tf_op | source)
XLA Modules:
  0.0 270.2 jit_solution(6051907801597242002)
XLA Ops:
  0.7 2.1 broadcast_in_dim.4
  2.7 5.8 %all-to-all-start = ((bf16[8,128,512]{2,1,0:T(8,128)(2,1)}), bf16[8,128,512]{2,1,0:T(8,128)(2,1)}, u32[]{:S(2)}, u32[]{:S(2)}) async-start(bf16[8,128,512]{2,1,0:T(8,128)(2,1)} %broadcast_in_dim.4), calls=%async_computation | async-start | bytes 2097152 | tf_op jit(solution)/shard_map/all_to_all | solution.py:33
  8.5 2.0 collective-permute-start.20
  10.6 3.7 %collective-permute-start.19 = (bf16[256,2048]{1,0:T(8,128)(2,1)S(1)}, bf16[256,2048]{1,0:T(8,128)(2,1)}, u32[]{:S(2)}, u32[]{:S(2)}) collective-permute-start(bf16[256,2048]{1,0:T(8,128)(2,1)S(1)} %constant_dynamic-update-slice_fusion.refs_0_.refs_2_), channel_id=1, source_target_pairs={{0,16},{16,0},{1,17},{17,1},{2,18},{18,2},{3,19},{19,3},{4,20},{20... | collective-permute-start | bytes 3145736 | tf_op jit(solution)/shard_map/ppermute | solution.py:29
  14.3 1.6 collective-permute-start.11
  15.9 1.7 collective-permute-start.14
  18.1 8.3 %collective-permute-done.20 = bf16[128,512]{1,0:T(8,128)(2,1)} collective-permute-done((bf16[128,512]{1,0:T(8,128)(2,1)S(1)}, bf16[128,512]{1,0:T(8,128)(2,1)}, u32[]{:S(2)}, u32[]{:S(2)}) %collective-permute-start.20) | collective-permute-done | bytes 131104 | tf_op jit(solution)/shard_map/ppermute | solution.py:203
  26.4 0.9 select_bitcast_fusion.1
  27.3 1.9 convolution_convert_fusion.2
  29.3 3.3 %collective-permute-start.21 = (bf16[256,1024]{1,0:T(8,128)(2,1)S(1)}, bf16[256,1024]{1,0:T(8,128)(2,1)S(1)}, u32[]{:S(2)}, u32[]{:S(2)}) collective-permute-start(bf16[256,1024]{1,0:T(8,128)(2,1)S(1)} %convolution_convert_fusion.2), channel_id=1, source_target_pairs={{0,64},{32,96},{64,0},{96,32},{1,65},{33,97},{65,1},{97,33},{2,66}... | collective-permute-start | bytes 1572872 | tf_op jit(solution)/shard_map/ppermute | solution.py:25
  32.6 1.8 convolution_convert_fusion.1
  34.4 0.7 collective-permute-start.22
  35.1 2.2 convolution_convert_fusion.5
  37.3 2.2 convolution_convert_fusion
  39.6 11.9 %collective-permute-done.11.refs_0_.refs_2_ = bf16[256,2048]{1,0:T(8,128)(2,1)S(1)} collective-permute-done((bf16[256,2048]{1,0:T(8,128)(2,1)S(1)}, bf16[256,2048]{1,0:T(8,128)(2,1)S(1)}, u32[]{:S(2)}, u32[]{:S(2)}) %collective-permute-start.11) | collective-permute-done | bytes 1048608 | tf_op jit(solution)/shard_map/ppermute | solution.py:25
  51.5 2.4 convolution_convert_fusion.4
  53.9 3.3 %collective-permute-start = (bf16[256,1024]{1,0:T(8,128)(2,1)}, bf16[256,1024]{1,0:T(8,128)(2,1)}, u32[]{:S(2)}, u32[]{:S(2)}) collective-permute-start(bf16[256,1024]{1,0:T(8,128)(2,1)} %convolution_convert_fusion.5), channel_id=1, source_target_pairs={{0,64},{32,96},{64,0},{96,32},{1,65},{33,97},{65,1},{97,33},{2,66}... | collective-permute-start | bytes 1572872 | tf_op jit(solution)/shard_map/ppermute | solution.py:25
  57.1 2.2 convolution_convert_fusion.3
  59.4 1.3 collective-permute-start.1
  60.6 13.3 %collective-permute-done.22 = bf16[256,1024]{1,0:T(8,128)(2,1)S(1)} collective-permute-done((bf16[256,1024]{1,0:T(8,128)(2,1)S(1)}, bf16[256,1024]{1,0:T(8,128)(2,1)S(1)}, u32[]{:S(2)}, u32[]{:S(2)}) %collective-permute-start.22) | collective-permute-done | bytes 524320 | tf_op jit(solution)/shard_map/ppermute | solution.py:25
  73.9 0.8 copy-done.14
  74.7 0.7 pad_maximum_fusion
  75.4 1.1 copy.23
  76.5 1.5 broadcast_in_dim.5
  78.1 4.2 %all-to-all-start.1 = ((bf16[4,2,128,512]{2,1,3,0:T(2,128)(2,1)}), bf16[4,2,128,512]{2,1,3,0:T(2,128)(2,1)}, u32[]{:S(2)}, u32[]{:S(2)}) async-start(bf16[4,2,128,512]{2,1,3,0:T(2,128)(2,1)} %broadcast_in_dim.5), calls=%async_computation.1 | async-start | bytes 2097152 | tf_op jit(solution)/shard_map/all_to_all | solution.py:206
  82.4 1.3 collective-permute-start.12
  83.8 1.9 add_add_fusion
  85.8 3.5 %collective-permute-start.17 = (bf16[256,2048]{1,0:T(8,128)(2,1)S(1)}, bf16[256,2048]{1,0:T(8,128)(2,1)S(1)}, u32[]{:S(2)}, u32[]{:S(2)}) collective-permute-start(bf16[256,2048]{1,0:T(8,128)(2,1)S(1)} %collective-permute-done.14.refs_0_.refs_2_), channel_id=1, source_target_pairs={{0,16},{16,0},{1,17},{17,1},{2,18},{18,2},{3,19},{19,3},{4,20},{20... | collective-permute-start | bytes 3145736 | tf_op jit(solution)/shard_map/ppermute | solution.py:29
  89.4 2.9 %collective-permute-start.15 = (bf16[128,2048]{1,0:T(8,128)(2,1)S(1)}, bf16[128,2048]{1,0:T(8,128)(2,1)}, u32[]{:S(2)}, u32[]{:S(2)}) collective-permute-start(bf16[128,2048]{1,0:T(8,128)(2,1)S(1)} %slice.23), channel_id=1, source_target_pairs={{0,96},{32,0},{64,32},{96,64},{1,97},{33,1},{65,33},{97,65},{2,98}... | collective-permute-start | bytes 1572872 | tf_op jit(solution)/shard_map/ppermute | solution.py:25
  92.4 1.9 add_add_fusion.1
  94.4 1.1 collective-permute-done.12.refs_0_
  95.5 2.4 collective-permute-start.3
  97.9 43.5 %collective-permute-done.24 = bf16[128,1024]{1,0:T(8,128)(2,1)S(1)} collective-permute-done((bf16[128,1024]{1,0:T(8,128)(2,1)S(1)}, bf16[128,1024]{1,0:T(8,128)(2,1)S(1)}, u32[]{:S(2)}, u32[]{:S(2)}) %collective-permute-start.24) | collective-permute-done | bytes 262176 | tf_op jit(solution)/shard_map/ppermute | solution.py:29
  141.4 0.8 fusion.14.refs_0_
  142.2 3.5 %collective-permute-start.25 = (bf16[128,1024]{1,0:T(8,128)(2,1)}, bf16[128,1024]{1,0:T(8,128)(2,1)}, u32[]{:S(2)}, u32[]{:S(2)}) collective-permute-start(bf16[128,1024]{1,0:T(8,128)(2,1)} %fusion.14.refs_0_), channel_id=1, source_target_pairs={{0,16},{16,0},{1,17},{17,1},{2,18},{18,2},{3,19},{19,3},{4,20},{20... | collective-permute-start | bytes 786440 | tf_op jit(solution)/shard_map/ppermute | solution.py:29
  146.3 0.7 collective-permute-done.3
  147.1 10.7 %collective-permute-done.25.refs_1_ = bf16[128,1024]{1,0:T(8,128)(2,1)} collective-permute-done((bf16[128,1024]{1,0:T(8,128)(2,1)}, bf16[128,1024]{1,0:T(8,128)(2,1)}, u32[]{:S(2)}, u32[]{:S(2)}) %collective-permute-start.25) | collective-permute-done | bytes 262176 | tf_op jit(solution)/shard_map/ppermute | solution.py:29
  158.0 3.0 %collective-permute-start.26 = (bf16[128,1024]{1,0:T(8,128)(2,1)}, bf16[128,1024]{1,0:T(8,128)(2,1)S(1)}, u32[]{:S(2)}, u32[]{:S(2)}) collective-permute-start(bf16[128,1024]{1,0:T(8,128)(2,1)} %fusion.14.refs_0_), channel_id=1, source_target_pairs={{0,96},{32,0},{64,32},{96,64},{1,97},{33,1},{65,33},{97,65},{2,98}... | collective-permute-start | bytes 786440 | tf_op jit(solution)/shard_map/ppermute | solution.py:25
  161.0 1.3 collective-permute-start.4
  162.4 0.8 copy-done.11
  163.2 0.9 collective-permute-start.27
  165.4 0.7 add_add_fusion.2.at
  166.0 2.6 copy.24
  168.6 1.6 reshape.29.refs_12_
  170.2 5.7 %shard_map.102 = (bf16[1024,2048]{1,0:T(8,128)(2,1)}, f32[1024,2048]{1,0:T(8,128)}, f32[1024,2048]{1,0:T(8,128)}) custom-call(s32[3]{0:T(128)} %add_add_fusion.5.at, bf16[256,2048]{1,0:T(8,128)(2,1)} %copy-done.4, bf16[256,2048]{1,0:T(8,128)(2,1)} %collective-permute-done.19.refs_1_.refs_3_, bf16[256,2048]{1,0:T(8,128)(2,1)} %copy-done.4, ...), custom_call_target="tpu_custom_call" | custom-call | flops 5242880 | bytes 7340032 | tf_op jit(solution)/shard_map/pallas_call | solution.py:79
  175.9 5.6 %shard_map.103 = (bf16[1024,2048]{1,0:T(8,128)(2,1)}, f32[1024,2048]{1,0:T(8,128)}, f32[1024,2048]{1,0:T(8,128)}) custom-call(s32[3]{0:T(128)} %add_add_fusion.4.at, bf16[256,2048]{1,0:T(8,128)(2,1)} %copy-done.3, bf16[256,2048]{1,0:T(8,128)(2,1)} %copy-done.6, ...), custom_call_target="tpu_custom_call", output_to_operand_aliasing={{0}: (5, {}), {1}: (6, {}), {2}: (7, {})} | custom-call | flops 5242880 | bytes 7340032 | tf_op jit(solution)/shard_map/pallas_call | solution.py:79
  181.4 5.6 %shard_map.104 = (bf16[1024,2048]{1,0:T(8,128)(2,1)}, f32[1024,2048]{1,0:T(8,128)}, f32[1024,2048]{1,0:T(8,128)}) custom-call(s32[3]{0:T(128)} %add_add_fusion.3.at, bf16[256,2048]{1,0:T(8,128)(2,1)} %copy-done.2, bf16[256,2048]{1,0:T(8,128)(2,1)} %copy-done.5, ...), custom_call_target="tpu_custom_call", output_to_operand_aliasing={{0}: (5, {}), {1}: (6, {}), {2}: (7, {})} | custom-call | flops 5242880 | bytes 7340032 | tf_op jit(solution)/shard_map/pallas_call | solution.py:79
  187.1 1.3 collective-permute-start.7
  188.3 5.6 %shard_map.105 = (bf16[1024,2048]{1,0:T(8,128)(2,1)}, f32[1024,2048]{1,0:T(8,128)}, f32[1024,2048]{1,0:T(8,128)}) custom-call(s32[3]{0:T(128)} %add_add_fusion.2.at, bf16[128,2048]{1,0:T(8,128)(2,1)} %copy-done.10, bf16[128,2048]{1,0:T(8,128)(2,1)} %copy-done.11, ...), custom_call_target="tpu_custom_call", output_to_operand_aliasing={{0}: (5, {}), {1}: (6, {}), {2}: (7, {})} | custom-call | flops 5242880 | bytes 7340032 | tf_op jit(solution)/shard_map/pallas_call | solution.py:79
  194.1 1.0 collective-permute-start.29
  195.0 2.9 %collective-permute-start.6 = (bf16[128,1024]{1,0:T(8,128)(2,1)S(1)}, bf16[128,1024]{1,0:T(8,128)(2,1)S(1)}, u32[]{:S(2)}, u32[]{:S(2)}) collective-permute-start(bf16[128,1024]{1,0:T(8,128)(2,1)S(1)} %collective-permute-done.4.refs_1_), channel_id=1, source_target_pairs={{0,96},{32,0},{64,32},{96,64},{1,97},{33,1},{65,33},{97,65},{2,98}... | collective-permute-start | bytes 786440 | tf_op jit(solution)/shard_map/ppermute | solution.py:25
  198.0 1.4 collective-permute-start.30
  199.4 6.2 %multiply_convert_fusion = bf16[2048,512]{1,0:T(8,128)(2,1)} fusion(bf16[1024,2048]{1,0:T(8,128)(2,1)} %get-tuple-element.39, bf16[1024,512]{1,0:T(8,128)(2,1)} %bitcast), kind=kOutput, calls=%fused_computation.1 | convolution fusion | flops 2149580800 | bytes 7340032 | tf_op jit(solution)/shard_map/dot_general | solution.py:43
  205.6 0.9 collective-permute-start.5
  206.5 1.2 collective-permute-start.10
  208.4 2.9 %collective-permute-start.9 = (bf16[128,1024]{1,0:T(8,128)(2,1)S(1)}, bf16[128,1024]{1,0:T(8,128)(2,1)S(1)}, u32[]{:S(2)}, u32[]{:S(2)}) collective-permute-start(bf16[128,1024]{1,0:T(8,128)(2,1)S(1)} %collective-permute-done.6.refs_3_), channel_id=1, source_target_pairs={{0,96},{32,0},{64,32},{96,64},{1,97},{33,1},{65,33},{97,65},{2,98}... | collective-permute-start | bytes 786440 | tf_op jit(solution)/shard_map/ppermute | solution.py:25
  211.3 11.9 %shard_map.106 = (bf16[512,2048]{1,0:T(8,128)(2,1)}, bf16[512,2048]{1,0:T(8,128)(2,1)}, f32[1024,512]{1,0:T(8,128)}) custom-call(s32[8]{0:T(128)} %fusion.37.where, bf16[128,1024]{1,0:T(8,128)(2,1)} %fusion.14.refs_0_, bf16[128,1024]{1,0:T(8,128)(2,1)} %collective-permute-done.25.refs_1_, bf16[128,1024]{1,0:T(8,128)(2,1)} %copy-done.25, ...), custom_call_target="tpu_custom_call" | custom-call | flops 4294967296 | bytes 14680064 | tf_op jit(solution)/shard_map/pallas_call | solution.py:138
  224.3 12.3 %shard_map.107 = (bf16[512,2048]{1,0:T(8,128)(2,1)}, bf16[512,2048]{1,0:T(8,128)(2,1)}, bf16[1024,512]{1,0:T(8,128)(2,1)}) custom-call(s32[8]{0:T(128)} %fusion.37.where, bf16[128,1024]{1,0:T(8,128)(2,1)} %copy-done.9, bf16[128,1024]{1,0:T(8,128)(2,1)} %copy-done.18, bf16[128,1024]{1,0:T(8,128)(2,1)} %copy-done.21, ...), custom_call_target="tpu_custom_call", output_to_operand_aliasing={{0}: (15, {}), {1}: (16, {})} | custom-call | flops 4294967296 | bytes 14680064 | tf_op jit(solution)/shard_map/pallas_call | solution.py:138
  236.7 4.7 %all-to-all-start.2 = ((bf16[8,128,512]{2,1,0:T(8,128)(2,1)}), bf16[8,128,512]{2,1,0:T(8,128)(2,1)S(1)}, u32[]{:S(2)}, u32[]{:S(2)}) async-start(bf16[8,128,512]{2,1,0:T(8,128)(2,1)} %bitcast.33), calls=%async_computation.2 | async-start | bytes 2097152 | tf_op jit(solution)/shard_map/all_to_all | solution.py:33
  241.5 16.1 %all-to-all-done.2 = bf16[8,128,512]{2,1,0:T(8,128)(2,1)S(1)} async-done(((bf16[8,128,512]{2,1,0:T(8,128)(2,1)}), bf16[8,128,512]{2,1,0:T(8,128)(2,1)S(1)}, u32[]{:S(2)}, u32[]{:S(2)}) %all-to-all-start.2) | async-done | bytes 1048608 | tf_op jit(solution)/shard_map/all_to_all | solution.py:33
  257.6 0.8 reduce_sum.12
  258.4 4.3 %add_convert_fusion = bf16[2048,512]{1,0:T(8,128)(2,1)} fusion(bf16[2048,512]{1,0:T(8,128)(2,1)} %collective-permute-done.34, bf16[2048,512]{1,0:T(8,128)(2,1)} %multiply_convert_fusion), kind=kLoop, calls=%fused_computation | loop fusion | flops 4194304 | bytes 6291456 | tf_op jit(solution)/shard_map/convert_element_type | solution.py:211
  262.7 3.7 %add_convert_fusion.1 = bf16[512,2048]{1,0:T(8,128)(2,1)} fusion(bf16[512,2048]{1,0:T(8,128)(2,1)} %collective-permute-done.33, bf16[512,2048]{1,0:T(8,128)(2,1)S(1)} %copy-done.1), kind=kLoop, calls=%fused_computation.2 | loop fusion | flops 4194304 | bytes 6291456 | tf_op jit(solution)/shard_map/convert_element_type | solution.py:211
  266.4 3.8 %add_convert_fusion.2 = bf16[512,2048]{1,0:T(8,128)(2,1)} fusion(bf16[512,2048]{1,0:T(8,128)(2,1)} %collective-permute-done.32, bf16[512,2048]{1,0:T(8,128)(2,1)S(1)} %copy-done), kind=kLoop, calls=%fused_computation.3 | loop fusion | flops 4194304 | bytes 6291456 | tf_op jit(solution)/shard_map/convert_element_type | solution.py:211
  (111 shorter events, 5.1 us)
Async XLA Ops:
  0.6 7.9 %copy-start.29 = (bf16[128,512]{1,0:T(8,128)(2,1)S(1)}, bf16[128,512]{1,0:T(8,128)(2,1)}, u32[]{:S(2)}) copy-start(bf16[128,512]{1,0:T(8,128)(2,1)} %param.7) | copy-start | bytes 393220
  0.6 9.9 %copy-start.16 = (bf16[128,2048]{1,0:T(8,128)(2,1)S(1)}, bf16[128,2048]{1,0:T(8,128)(2,1)}, u32[]{:S(2)}) copy-start(bf16[128,2048]{1,0:T(8,128)(2,1)} %param.9) | copy-start | bytes 1572868
  0.7 9.9 %copy-start.17 = (bf16[128,2048]{1,0:T(8,128)(2,1)S(1)}, bf16[128,2048]{1,0:T(8,128)(2,1)}, u32[]{:S(2)}) copy-start(bf16[128,2048]{1,0:T(8,128)(2,1)} %param.10) | copy-start | bytes 1572868
  2.7 24.6 %all-to-all-start = ((bf16[8,128,512]{2,1,0:T(8,128)(2,1)}), bf16[8,128,512]{2,1,0:T(8,128)(2,1)}, u32[]{:S(2)}, u32[]{:S(2)}) async-start(bf16[8,128,512]{2,1,0:T(8,128)(2,1)} %broadcast_in_dim.4), calls=%async_computation | async-start | bytes 2097152 | tf_op jit(solution)/shard_map/all_to_all | solution.py:33
  8.5 17.9 %collective-permute-start.20 = (bf16[128,512]{1,0:T(8,128)(2,1)S(1)}, bf16[128,512]{1,0:T(8,128)(2,1)}, u32[]{:S(2)}, u32[]{:S(2)}) collective-permute-start(bf16[128,512]{1,0:T(8,128)(2,1)S(1)} %copy-done.29), channel_id=1, source_target_pairs={{0,8},{8,0},{1,9},{9,1},{2,10},{10,2},{3,11},{11,3},{4,12},{12,4},... | collective-permute-start | bytes 393224 | tf_op jit(solution)/shard_map/ppermute | solution.py:203
  10.6 23.7 %copy-start.4 = (bf16[256,2048]{1,0:T(8,128)(2,1)}, bf16[256,2048]{1,0:T(8,128)(2,1)S(1)}, u32[]{:S(2)}) copy-start(bf16[256,2048]{1,0:T(8,128)(2,1)S(1)} %constant_dynamic-update-slice_fusion.refs_0_.refs_2_) | copy-start | bytes 3145732
  10.6 75.1 %collective-permute-start.19 = (bf16[256,2048]{1,0:T(8,128)(2,1)S(1)}, bf16[256,2048]{1,0:T(8,128)(2,1)}, u32[]{:S(2)}, u32[]{:S(2)}) collective-permute-start(bf16[256,2048]{1,0:T(8,128)(2,1)S(1)} %constant_dynamic-update-slice_fusion.refs_0_.refs_2_), channel_id=1, source_target_pairs={{0,16},{16,0},{1,17},{17,1},{2,18},{18,2},{3,19},{19,3},{4,20},{20... | collective-permute-start | bytes 3145736 | tf_op jit(solution)/shard_map/ppermute | solution.py:29
  14.3 37.2 %collective-permute-start.11 = (bf16[256,2048]{1,0:T(8,128)(2,1)S(1)}, bf16[256,2048]{1,0:T(8,128)(2,1)S(1)}, u32[]{:S(2)}, u32[]{:S(2)}) collective-permute-start(bf16[256,2048]{1,0:T(8,128)(2,1)S(1)} %constant_dynamic-update-slice_fusion.refs_0_.refs_2_), channel_id=1, source_target_pairs={{0,32},{32,64},{64,96},{96,0},{1,33},{33,65},{65,97},{97,1},{2,34}... | collective-permute-start | bytes 3145736 | tf_op jit(solution)/shard_map/ppermute | solution.py:25
  15.9 38.0 %collective-permute-start.14 = (bf16[256,2048]{1,0:T(8,128)(2,1)S(1)}, bf16[256,2048]{1,0:T(8,128)(2,1)S(1)}, u32[]{:S(2)}, u32[]{:S(2)}) collective-permute-start(bf16[256,2048]{1,0:T(8,128)(2,1)S(1)} %constant_dynamic-update-slice_fusion.refs_0_.refs_2_), channel_id=1, source_target_pairs={{0,96},{32,0},{64,32},{96,64},{1,97},{33,1},{65,33},{97,65},{2,98}... | collective-permute-start | bytes 3145736 | tf_op jit(solution)/shard_map/ppermute | solution.py:25
  27.3 7.8 %copy-start.7 = (bf16[2048,512]{1,0:T(8,128)(2,1)S(1)}, bf16[2048,512]{1,0:T(8,128)(2,1)}, u32[]{:S(2)}) copy-start(bf16[2048,512]{1,0:T(8,128)(2,1)} %param.13) | copy-start | bytes 6291460
  29.3 30.1 %collective-permute-start.21 = (bf16[256,1024]{1,0:T(8,128)(2,1)S(1)}, bf16[256,1024]{1,0:T(8,128)(2,1)S(1)}, u32[]{:S(2)}, u32[]{:S(2)}) collective-permute-start(bf16[256,1024]{1,0:T(8,128)(2,1)S(1)} %convolution_convert_fusion.2), channel_id=1, source_target_pairs={{0,64},{32,96},{64,0},{96,32},{1,65},{33,97},{65,1},{97,33},{2,66}... | collective-permute-start | bytes 1572872 | tf_op jit(solution)/shard_map/ppermute | solution.py:25
  34.4 39.5 %collective-permute-start.22 = (bf16[256,1024]{1,0:T(8,128)(2,1)S(1)}, bf16[256,1024]{1,0:T(8,128)(2,1)S(1)}, u32[]{:S(2)}, u32[]{:S(2)}) collective-permute-start(bf16[256,1024]{1,0:T(8,128)(2,1)S(1)} %convolution_convert_fusion.1), channel_id=1, source_target_pairs={{0,32},{32,64},{64,96},{96,0},{1,33},{33,65},{65,97},{97,1},{2,34}... | collective-permute-start | bytes 1572872 | tf_op jit(solution)/shard_map/ppermute | solution.py:25
  51.5 34.2 %copy-start.3 = (bf16[256,2048]{1,0:T(8,128)(2,1)}, bf16[256,2048]{1,0:T(8,128)(2,1)S(1)}, u32[]{:S(2)}) copy-start(bf16[256,2048]{1,0:T(8,128)(2,1)S(1)} %collective-permute-done.11.refs_0_.refs_2_) | copy-start | bytes 3145732
  51.5 31.0 %collective-permute-start.23 = (bf16[256,1024]{1,0:T(8,128)(2,1)}, bf16[256,1024]{1,0:T(8,128)(2,1)}, u32[]{:S(2)}, u32[]{:S(2)}) collective-permute-start(bf16[256,1024]{1,0:T(8,128)(2,1)} %convolution_convert_fusion), channel_id=1, source_target_pairs={{0,96},{32,0},{64,32},{96,64},{1,97},{33,1},{65,33},{97,65},{2,98}... | collective-permute-start | bytes 1572872 | tf_op jit(solution)/shard_map/ppermute | solution.py:25
  53.9 31.9 %copy-start.2 = (bf16[256,2048]{1,0:T(8,128)(2,1)}, bf16[256,2048]{1,0:T(8,128)(2,1)S(1)}, u32[]{:S(2)}) copy-start(bf16[256,2048]{1,0:T(8,128)(2,1)S(1)} %collective-permute-done.14.refs_0_.refs_2_) | copy-start | bytes 3145732
  53.9 31.9 %collective-permute-start = (bf16[256,1024]{1,0:T(8,128)(2,1)}, bf16[256,1024]{1,0:T(8,128)(2,1)}, u32[]{:S(2)}, u32[]{:S(2)}) collective-permute-start(bf16[256,1024]{1,0:T(8,128)(2,1)} %convolution_convert_fusion.5), channel_id=1, source_target_pairs={{0,64},{32,96},{64,0},{96,32},{1,65},{33,97},{65,1},{97,33},{2,66}... | collective-permute-start | bytes 1572872 | tf_op jit(solution)/shard_map/ppermute | solution.py:25
  59.4 14.5 %copy-start.12 = (bf16[256,1024]{1,0:T(8,128)(2,1)}, bf16[256,1024]{1,0:T(8,128)(2,1)S(1)}, u32[]{:S(2)}) copy-start(bf16[256,1024]{1,0:T(8,128)(2,1)S(1)} %collective-permute-done.21) | copy-start | bytes 1572868
  59.4 30.0 %collective-permute-start.1 = (bf16[256,1024]{1,0:T(8,128)(2,1)}, bf16[256,1024]{1,0:T(8,128)(2,1)}, u32[]{:S(2)}, u32[]{:S(2)}) collective-permute-start(bf16[256,1024]{1,0:T(8,128)(2,1)} %convolution_convert_fusion.4), channel_id=1, source_target_pairs={{0,32},{32,64},{64,96},{96,0},{1,33},{33,65},{65,97},{97,1},{2,34}... | collective-permute-start | bytes 1572872 | tf_op jit(solution)/shard_map/ppermute | solution.py:25
  73.9 18.4 %collective-permute-start.2 = (bf16[256,1024]{1,0:T(8,128)(2,1)}, bf16[256,1024]{1,0:T(8,128)(2,1)}, u32[]{:S(2)}, u32[]{:S(2)}) collective-permute-start(bf16[256,1024]{1,0:T(8,128)(2,1)} %convolution_convert_fusion.3), channel_id=1, source_target_pairs={{0,96},{32,0},{64,32},{96,64},{1,97},{33,1},{65,33},{97,65},{2,98}... | collective-permute-start | bytes 1572872 | tf_op jit(solution)/shard_map/ppermute | solution.py:25
  78.1 88.0 %all-to-all-start.1 = ((bf16[4,2,128,512]{2,1,3,0:T(2,128)(2,1)}), bf16[4,2,128,512]{2,1,3,0:T(2,128)(2,1)}, u32[]{:S(2)}, u32[]{:S(2)}) async-start(bf16[4,2,128,512]{2,1,3,0:T(2,128)(2,1)} %broadcast_in_dim.5), calls=%async_computation.1 | async-start | bytes 2097152 | tf_op jit(solution)/shard_map/all_to_all | solution.py:206
  82.3 1.5 copy-start.13
  82.3 1.4 copy-start.15
  82.4 10.0 %copy-start.8 = (bf16[2048,512]{1,0:T(8,128)(2,1)S(1)}, bf16[2048,512]{1,0:T(8,128)(2,1)}, u32[]{:S(2)}) copy-start(bf16[2048,512]{1,0:T(8,128)(2,1)} %param.13) | copy-start | bytes 6291460
  82.4 13.1 %collective-permute-start.12 = (bf16[128,2048]{1,0:T(8,128)(2,1)S(1)}, bf16[128,2048]{1,0:T(8,128)(2,1)S(1)}, u32[]{:S(2)}, u32[]{:S(2)}) collective-permute-start(bf16[128,2048]{1,0:T(8,128)(2,1)S(1)} %slice.22), channel_id=1, source_target_pairs={{0,32},{32,64},{64,96},{96,0},{1,33},{33,65},{65,97},{97,1},{2,34}... | collective-permute-start | bytes 1572872 | tf_op jit(solution)/shard_map/ppermute | solution.py:25
  85.7 72.3 %collective-permute-start.18 = (bf16[256,2048]{1,0:T(8,128)(2,1)S(1)}, bf16[256,2048]{1,0:T(8,128)(2,1)S(1)}, u32[]{:S(2)}, u32[]{:S(2)}) collective-permute-start(bf16[256,2048]{1,0:T(8,128)(2,1)S(1)} %collective-permute-done.11.refs_0_.refs_2_), channel_id=1, source_target_pairs={{0,16},{16,0},{1,17},{17,1},{2,18},{18,2},{3,19},{19,3},{4,20},{20... | collective-permute-start | bytes 3145736 | tf_op jit(solution)/shard_map/ppermute | solution.py:29
  85.8 75.2 %collective-permute-start.17 = (bf16[256,2048]{1,0:T(8,128)(2,1)S(1)}, bf16[256,2048]{1,0:T(8,128)(2,1)S(1)}, u32[]{:S(2)}, u32[]{:S(2)}) collective-permute-start(bf16[256,2048]{1,0:T(8,128)(2,1)S(1)} %collective-permute-done.14.refs_0_.refs_2_), channel_id=1, source_target_pairs={{0,16},{16,0},{1,17},{17,1},{2,18},{18,2},{3,19},{19,3},{4,20},{20... | collective-permute-start | bytes 3145736 | tf_op jit(solution)/shard_map/ppermute | solution.py:29
  89.4 52.8 %collective-permute-start.15 = (bf16[128,2048]{1,0:T(8,128)(2,1)S(1)}, bf16[128,2048]{1,0:T(8,128)(2,1)}, u32[]{:S(2)}, u32[]{:S(2)}) collective-permute-start(bf16[128,2048]{1,0:T(8,128)(2,1)S(1)} %slice.23), channel_id=1, source_target_pairs={{0,96},{32,0},{64,32},{96,64},{1,97},{33,1},{65,33},{97,65},{2,98}... | collective-permute-start | bytes 1572872 | tf_op jit(solution)/shard_map/ppermute | solution.py:25
  92.3 49.1 %collective-permute-start.24 = (bf16[128,1024]{1,0:T(8,128)(2,1)S(1)}, bf16[128,1024]{1,0:T(8,128)(2,1)S(1)}, u32[]{:S(2)}, u32[]{:S(2)}) collective-permute-start(bf16[128,1024]{1,0:T(8,128)(2,1)S(1)} %fusion.17), channel_id=1, source_target_pairs={{0,16},{16,0},{1,17},{17,1},{2,18},{18,2},{3,19},{19,3},{4,20},{20... | collective-permute-start | bytes 786440 | tf_op jit(solution)/shard_map/ppermute | solution.py:29
  95.5 66.9 %copy-start.10 = (bf16[128,2048]{1,0:T(8,128)(2,1)}, bf16[128,2048]{1,0:T(8,128)(2,1)S(1)}, u32[]{:S(2)}) copy-start(bf16[128,2048]{1,0:T(8,128)(2,1)S(1)} %collective-permute-done.12.refs_0_) | copy-start | bytes 1572868
  95.5 51.5 %collective-permute-start.3 = (bf16[128,1024]{1,0:T(8,128)(2,1)S(1)}, bf16[128,1024]{1,0:T(8,128)(2,1)S(1)}, u32[]{:S(2)}, u32[]{:S(2)}) collective-permute-start(bf16[128,1024]{1,0:T(8,128)(2,1)S(1)} %fusion.16), channel_id=1, source_target_pairs={{0,16},{16,0},{1,17},{17,1},{2,18},{18,2},{3,19},{19,3},{4,20},{20... | collective-permute-start | bytes 786440 | tf_op jit(solution)/shard_map/ppermute | solution.py:29
  141.4 21.0 %collective-permute-start.13 = (bf16[128,2048]{1,0:T(8,128)(2,1)S(1)}, bf16[128,2048]{1,0:T(8,128)(2,1)S(1)}, u32[]{:S(2)}, u32[]{:S(2)}) collective-permute-start(bf16[128,2048]{1,0:T(8,128)(2,1)S(1)} %collective-permute-done.12.refs_0_), channel_id=1, source_target_pairs={{0,16},{16,0},{1,17},{17,1},{2,18},{18,2},{3,19},{19,3},{4,20},{20... | collective-permute-start | bytes 1572872 | tf_op jit(solution)/shard_map/ppermute | solution.py:29
  142.2 15.6 %collective-permute-start.25 = (bf16[128,1024]{1,0:T(8,128)(2,1)}, bf16[128,1024]{1,0:T(8,128)(2,1)}, u32[]{:S(2)}, u32[]{:S(2)}) collective-permute-start(bf16[128,1024]{1,0:T(8,128)(2,1)} %fusion.14.refs_0_), channel_id=1, source_target_pairs={{0,16},{16,0},{1,17},{17,1},{2,18},{18,2},{3,19},{19,3},{4,20},{20... | collective-permute-start | bytes 786440 | tf_op jit(solution)/shard_map/ppermute | solution.py:29
  147.0 40.1 %collective-permute-start.16 = (bf16[128,2048]{1,0:T(8,128)(2,1)}, bf16[128,2048]{1,0:T(8,128)(2,1)}, u32[]{:S(2)}, u32[]{:S(2)}) collective-permute-start(bf16[128,2048]{1,0:T(8,128)(2,1)} %collective-permute-done.15.refs_2_), channel_id=1, source_target_pairs={{0,16},{16,0},{1,17},{17,1},{2,18},{18,2},{3,19},{19,3},{4,20},{20... | collective-permute-start | bytes 1572872 | tf_op jit(solution)/shard_map/ppermute | solution.py:29
  147.1 58.5 %copy-start.9 = (bf16[128,1024]{1,0:T(8,128)(2,1)}, bf16[128,1024]{1,0:T(8,128)(2,1)S(1)}, u32[]{:S(2)}) copy-start(bf16[128,1024]{1,0:T(8,128)(2,1)S(1)} %fusion.15.refs_0_) | copy-start | bytes 786436
  157.8 36.2 %collective-permute-start.28 = (bf16[128,1024]{1,0:T(8,128)(2,1)}, bf16[128,1024]{1,0:T(8,128)(2,1)}, u32[]{:S(2)}, u32[]{:S(2)}) collective-permute-start(bf16[128,1024]{1,0:T(8,128)(2,1)} %fusion.14.refs_0_), channel_id=1, source_target_pairs={{0,32},{32,64},{64,96},{96,0},{1,33},{33,65},{65,97},{97,1},{2,34}... | collective-permute-start | bytes 786440 | tf_op jit(solution)/shard_map/ppermute | solution.py:25
  158.0 3.1 %copy-start.6 = (bf16[256,2048]{1,0:T(8,128)(2,1)}, bf16[256,2048]{1,0:T(8,128)(2,1)S(1)}, u32[]{:S(2)}) copy-start(bf16[256,2048]{1,0:T(8,128)(2,1)S(1)} %collective-permute-done.18.refs_1_.refs_3_) | copy-start | bytes 3145732
  158.0 36.0 %collective-permute-start.26 = (bf16[128,1024]{1,0:T(8,128)(2,1)}, bf16[128,1024]{1,0:T(8,128)(2,1)S(1)}, u32[]{:S(2)}, u32[]{:S(2)}) collective-permute-start(bf16[128,1024]{1,0:T(8,128)(2,1)} %fusion.14.refs_0_), channel_id=1, source_target_pairs={{0,96},{32,0},{64,32},{96,64},{1,97},{33,1},{65,33},{97,65},{2,98}... | collective-permute-start | bytes 786440 | tf_op jit(solution)/shard_map/ppermute | solution.py:25
  161.0 9.2 %copy-start.5 = (bf16[256,2048]{1,0:T(8,128)(2,1)}, bf16[256,2048]{1,0:T(8,128)(2,1)S(1)}, u32[]{:S(2)}) copy-start(bf16[256,2048]{1,0:T(8,128)(2,1)S(1)} %collective-permute-done.17.refs_1_.refs_3_) | copy-start | bytes 3145732
  161.0 34.0 %collective-permute-start.4 = (bf16[128,1024]{1,0:T(8,128)(2,1)S(1)}, bf16[128,1024]{1,0:T(8,128)(2,1)S(1)}, u32[]{:S(2)}, u32[]{:S(2)}) collective-permute-start(bf16[128,1024]{1,0:T(8,128)(2,1)S(1)} %fusion.15.refs_0_), channel_id=1, source_target_pairs={{0,16},{16,0},{1,17},{17,1},{2,18},{18,2},{3,19},{19,3},{4,20},{20... | collective-permute-start | bytes 786440 | tf_op jit(solution)/shard_map/ppermute | solution.py:29
  163.2 34.8 %collective-permute-start.27 = (bf16[128,1024]{1,0:T(8,128)(2,1)}, bf16[128,1024]{1,0:T(8,128)(2,1)}, u32[]{:S(2)}, u32[]{:S(2)}) collective-permute-start(bf16[128,1024]{1,0:T(8,128)(2,1)} %collective-permute-done.25.refs_1_), channel_id=1, source_target_pairs={{0,96},{32,0},{64,32},{96,64},{1,97},{33,1},{65,33},{97,65},{2,98}... | collective-permute-start | bytes 786440 | tf_op jit(solution)/shard_map/ppermute | solution.py:25
  187.1 18.5 %collective-permute-start.7 = (bf16[128,1024]{1,0:T(8,128)(2,1)S(1)}, bf16[128,1024]{1,0:T(8,128)(2,1)S(1)}, u32[]{:S(2)}, u32[]{:S(2)}) collective-permute-start(bf16[128,1024]{1,0:T(8,128)(2,1)S(1)} %fusion.15.refs_0_), channel_id=1, source_target_pairs={{0,32},{32,64},{64,96},{96,0},{1,33},{33,65},{65,97},{97,1},{2,34}... | collective-permute-start | bytes 786440 | tf_op jit(solution)/shard_map/ppermute | solution.py:25
  193.9 13.8 %collective-permute-start.31 = (bf16[128,1024]{1,0:T(8,128)(2,1)}, bf16[128,1024]{1,0:T(8,128)(2,1)S(1)}, u32[]{:S(2)}, u32[]{:S(2)}) collective-permute-start(bf16[128,1024]{1,0:T(8,128)(2,1)} %collective-permute-done.25.refs_1_), channel_id=1, source_target_pairs={{0,32},{32,64},{64,96},{96,0},{1,33},{33,65},{65,97},{97,1},{2,34}... | collective-permute-start | bytes 786440 | tf_op jit(solution)/shard_map/ppermute | solution.py:25
  194.0 1.0 copy-start.25
  194.1 12.5 %collective-permute-start.29 = (bf16[128,1024]{1,0:T(8,128)(2,1)}, bf16[128,1024]{1,0:T(8,128)(2,1)S(1)}, u32[]{:S(2)}, u32[]{:S(2)}) collective-permute-start(bf16[128,1024]{1,0:T(8,128)(2,1)} %collective-permute-done.28.refs_6_), channel_id=1, source_target_pairs={{0,32},{32,64},{64,96},{96,0},{1,33},{33,65},{65,97},{97,1},{2,34}... | collective-permute-start | bytes 786440 | tf_op jit(solution)/shard_map/ppermute | solution.py:25
  195.0 11.5 %copy-start.18 = (bf16[128,1024]{1,0:T(8,128)(2,1)}, bf16[128,1024]{1,0:T(8,128)(2,1)S(1)}, u32[]{:S(2)}) copy-start(bf16[128,1024]{1,0:T(8,128)(2,1)S(1)} %collective-permute-done.4.refs_1_) | copy-start | bytes 786436
  195.0 13.4 %collective-permute-start.6 = (bf16[128,1024]{1,0:T(8,128)(2,1)S(1)}, bf16[128,1024]{1,0:T(8,128)(2,1)S(1)}, u32[]{:S(2)}, u32[]{:S(2)}) collective-permute-start(bf16[128,1024]{1,0:T(8,128)(2,1)S(1)} %collective-permute-done.4.refs_1_), channel_id=1, source_target_pairs={{0,96},{32,0},{64,32},{96,64},{1,97},{33,1},{65,33},{97,65},{2,98}... | collective-permute-start | bytes 786440 | tf_op jit(solution)/shard_map/ppermute | solution.py:25
  198.0 10.4 %collective-permute-start.30 = (bf16[128,1024]{1,0:T(8,128)(2,1)}, bf16[128,1024]{1,0:T(8,128)(2,1)S(1)}, u32[]{:S(2)}, u32[]{:S(2)}) collective-permute-start(bf16[128,1024]{1,0:T(8,128)(2,1)} %collective-permute-done.27.refs_3_), channel_id=1, source_target_pairs={{0,96},{32,0},{64,32},{96,64},{1,97},{33,1},{65,33},{97,65},{2,98}... | collective-permute-start | bytes 786440 | tf_op jit(solution)/shard_map/ppermute | solution.py:25
  205.6 17.7 %copy-start.19 = (bf16[128,1024]{1,0:T(8,128)(2,1)}, bf16[128,1024]{1,0:T(8,128)(2,1)S(1)}, u32[]{:S(2)}) copy-start(bf16[128,1024]{1,0:T(8,128)(2,1)S(1)} %collective-permute-done.7.refs_6_) | copy-start | bytes 786436
  205.6 17.7 %collective-permute-start.5 = (bf16[128,1024]{1,0:T(8,128)(2,1)S(1)}, bf16[128,1024]{1,0:T(8,128)(2,1)S(1)}, u32[]{:S(2)}, u32[]{:S(2)}) collective-permute-start(bf16[128,1024]{1,0:T(8,128)(2,1)S(1)} %fusion.15.refs_0_), channel_id=1, source_target_pairs={{0,96},{32,0},{64,32},{96,64},{1,97},{33,1},{65,33},{97,65},{2,98}... | collective-permute-start | bytes 786440 | tf_op jit(solution)/shard_map/ppermute | solution.py:25
  206.5 4.8 %copy-start.27 = (bf16[128,1024]{1,0:T(8,128)(2,1)}, bf16[128,1024]{1,0:T(8,128)(2,1)S(1)}, u32[]{:S(2)}) copy-start(bf16[128,1024]{1,0:T(8,128)(2,1)S(1)} %collective-permute-done.29.refs_4_) | copy-start | bytes 786436
  206.5 16.8 %collective-permute-start.10 = (bf16[128,1024]{1,0:T(8,128)(2,1)S(1)}, bf16[128,1024]{1,0:T(8,128)(2,1)S(1)}, u32[]{:S(2)}, u32[]{:S(2)}) collective-permute-start(bf16[128,1024]{1,0:T(8,128)(2,1)S(1)} %collective-permute-done.4.refs_1_), channel_id=1, source_target_pairs={{0,32},{32,64},{64,96},{96,0},{1,33},{33,65},{65,97},{97,1},{2,34}... | collective-permute-start | bytes 786440 | tf_op jit(solution)/shard_map/ppermute | solution.py:25
  207.8 3.6 %copy-start.26 = (bf16[128,1024]{1,0:T(8,128)(2,1)}, bf16[128,1024]{1,0:T(8,128)(2,1)S(1)}, u32[]{:S(2)}) copy-start(bf16[128,1024]{1,0:T(8,128)(2,1)S(1)} %collective-permute-done.31.refs_7_) | copy-start | bytes 786436
  207.8 15.6 %collective-permute-start.8 = (bf16[128,1024]{1,0:T(8,128)(2,1)S(1)}, bf16[128,1024]{1,0:T(8,128)(2,1)S(1)}, u32[]{:S(2)}, u32[]{:S(2)}) collective-permute-start(bf16[128,1024]{1,0:T(8,128)(2,1)S(1)} %collective-permute-done.7.refs_6_), channel_id=1, source_target_pairs={{0,32},{32,64},{64,96},{96,0},{1,33},{33,65},{65,97},{97,1},{2,34}... | collective-permute-start | bytes 786440 | tf_op jit(solution)/shard_map/ppermute | solution.py:25
  208.4 14.9 %copy-start.20 = (bf16[128,1024]{1,0:T(8,128)(2,1)}, bf16[128,1024]{1,0:T(8,128)(2,1)S(1)}, u32[]{:S(2)}) copy-start(bf16[128,1024]{1,0:T(8,128)(2,1)S(1)} %collective-permute-done.6.refs_3_) | copy-start | bytes 786436
  208.4 50.0 %collective-permute-start.34 = (bf16[2048,512]{1,0:T(8,128)(2,1)}, bf16[2048,512]{1,0:T(8,128)(2,1)}, u32[]{:S(2)}, u32[]{:S(2)}) collective-permute-start(bf16[2048,512]{1,0:T(8,128)(2,1)} %multiply_convert_fusion), channel_id=1, source_target_pairs={{0,1},{1,0},{2,3},{3,2},{4,5},{5,4},{6,7},{7,6},{8,9},{9,8},{10,11... | collective-permute-start | bytes 6291464 | tf_op jit(solution)/shard_map/ppermute | solution.py:210
  208.4 2.9 %copy-start.28 = (bf16[128,1024]{1,0:T(8,128)(2,1)}, bf16[128,1024]{1,0:T(8,128)(2,1)S(1)}, u32[]{:S(2)}) copy-start(bf16[128,1024]{1,0:T(8,128)(2,1)S(1)} %collective-permute-done.30.refs_5_) | copy-start | bytes 786436
  208.4 14.9 %collective-permute-start.9 = (bf16[128,1024]{1,0:T(8,128)(2,1)S(1)}, bf16[128,1024]{1,0:T(8,128)(2,1)S(1)}, u32[]{:S(2)}, u32[]{:S(2)}) collective-permute-start(bf16[128,1024]{1,0:T(8,128)(2,1)S(1)} %collective-permute-done.6.refs_3_), channel_id=1, source_target_pairs={{0,96},{32,0},{64,32},{96,64},{1,97},{33,1},{65,33},{97,65},{2,98}... | collective-permute-start | bytes 786440 | tf_op jit(solution)/shard_map/ppermute | solution.py:25
  223.3 0.9 copy-start.23
  223.3 0.9 copy-start.24
  236.6 4.8 %copy-start = (bf16[512,2048]{1,0:T(8,128)(2,1)S(1)}, bf16[512,2048]{1,0:T(8,128)(2,1)}, u32[]{:S(2)}) copy-start(bf16[512,2048]{1,0:T(8,128)(2,1)} %get-tuple-element.37) | copy-start | bytes 6291460
  236.6 26.1 %collective-permute-start.33 = (bf16[512,2048]{1,0:T(8,128)(2,1)}, bf16[512,2048]{1,0:T(8,128)(2,1)}, u32[]{:S(2)}, u32[]{:S(2)}) collective-permute-start(bf16[512,2048]{1,0:T(8,128)(2,1)} %get-tuple-element.38), channel_id=1, source_target_pairs={{0,1},{1,0},{2,3},{3,2},{4,5},{5,4},{6,7},{7,6},{8,9},{9,8},{10,11... | collective-permute-start | bytes 6291464 | tf_op jit(solution)/shard_map/ppermute | solution.py:210
  236.7 20.9 %all-to-all-start.2 = ((bf16[8,128,512]{2,1,0:T(8,128)(2,1)}), bf16[8,128,512]{2,1,0:T(8,128)(2,1)S(1)}, u32[]{:S(2)}, u32[]{:S(2)}) async-start(bf16[8,128,512]{2,1,0:T(8,128)(2,1)} %bitcast.33), calls=%async_computation.2 | async-start | bytes 2097152 | tf_op jit(solution)/shard_map/all_to_all | solution.py:33
  241.4 25.0 %collective-permute-start.32 = (bf16[512,2048]{1,0:T(8,128)(2,1)S(1)}, bf16[512,2048]{1,0:T(8,128)(2,1)}, u32[]{:S(2)}, u32[]{:S(2)}) collective-permute-start(bf16[512,2048]{1,0:T(8,128)(2,1)S(1)} %copy-done), channel_id=1, source_target_pairs={{0,1},{1,0},{2,3},{3,2},{4,5},{5,4},{6,7},{7,6},{8,9},{9,8},{10,11... | collective-permute-start | bytes 6291464 | tf_op jit(solution)/shard_map/ppermute | solution.py:210
  258.4 4.3 %copy-start.1 = (bf16[512,2048]{1,0:T(8,128)(2,1)S(1)}, bf16[512,2048]{1,0:T(8,128)(2,1)}, u32[]{:S(2)}) copy-start(bf16[512,2048]{1,0:T(8,128)(2,1)} %get-tuple-element.38) | copy-start | bytes 6291460
  (4 other events, 3.1 us)

commit v3 on v2

--- a/solution.py
+++ b/solution.py
@@ -51,15 +51,15 @@
     return pl.ds(pl.multiple_of(where[p] * rows, rows), rows)
 
 
-def hidden_kernel(at, *refs):
+def hidden_kernel(spots, *refs):
     gates, ups = refs[:2], refs[2:4]
     hidden, slope, active = refs[-3:]
     rows = gates[0].shape[0]
     for j in range(2):
         g = gates[j][...].astype(F32)
         u = ups[j][...].astype(F32)
-        s = jax.nn.sigmoid(g)
-        here = place(at, 1 + j, rows)
+        s = 0.5 * jnp.tanh(0.5 * g) + 0.5
+        here = place(spots, 4 + j, rows)
         act = g * s
         hidden[here, :] = (act * u).astype(BF)
         slope[here, :] = u * s * (1.0 + g * (1.0 - s))
@@ -70,11 +70,11 @@
     return pl.BlockSpec((rows, STEP), lambda c, w: (which, c))
 
 
-def hidden_of(at, rows, gates, ups, before):
+def hidden_of(spots, k, rows, gates, ups, before):
     width = gates[0].shape[1]
     total = 8 * rows
     pieces = [piece_of(rows, 0)] * 2 + [piece_of(rows, u.shape[0] // rows - 1) for u in ups]
-    pair = pl.BlockSpec((2 * rows, STEP), lambda c, w: (w[0], c))
+    pair = pl.BlockSpec((2 * rows, STEP), lambda c, w: (w[k], c))
     kept = [pl.BlockSpec(memory_space=pl.ANY)] * len(before)
     return pl.pallas_call(
         hidden_kernel,
@@ -93,18 +93,18 @@
         cost_estimate=pl.CostEstimate(
             flops=2 * rows * width * 10, bytes_accessed=2 * rows * width * 14, transcendentals=2 * rows * width * 2
         ),
-    )(at, *gates, *ups, *before)
-
-
-def back_kernel(factor, first, where, *refs):
-    ds, refs = refs[:8], refs[8:]
+    )(spots, *gates, *ups, *before)
+
+
+def back_kernel(factor, first, spots, *refs):
+    ds, refs = refs[:5], refs[5:]
     slope, active, w_gate, w_up, tok = refs[:5]
     grad_gate, grad_up, back, d_gate, d_up, total = refs[-6:]
-    rows = ds[0].shape[0]
     c = pl.program_id(0)
-    for p in range(8):
-        d = ds[p][...].astype(F32)
-        here = place(where, p, rows)
+    for ref, k, skip in zip(ds, (0, 1, 3, 2, 2), (0, 0, 0, 0, 1)):
+        d = ref[...].astype(F32)
+        rows = d.shape[0]
+        here = pl.ds(pl.multiple_of(spots[k] * ds[0].shape[0] + skip * rows, rows), rows)
         d_gate[here, :] = (d * slope[here, :]).astype(BF)
         d_up[here, :] = (d * active[here, :]).astype(BF)
     dg, du = d_gate[...], d_up[...]
@@ -125,12 +125,12 @@
         back[...] = total[...].astype(back.dtype)
 
 
-def back_of(where, half, ds, slope, active, w_gate, w_up, tok, factor, before):
+def back_of(spots, half, ds, slope, active, w_gate, w_up, tok, factor, before):
     rows, part = ds[0].shape
     depth, width = w_gate.shape
-    total = 8 * rows
+    total = 4 * rows
     steps = part // NARROW
-    piece = pl.BlockSpec((rows, NARROW), lambda c, w: (0, c))
+    pieces = [pl.BlockSpec((d.shape[0], NARROW), lambda c, w: (0, c)) for d in ds]
     weight = pl.BlockSpec((depth, NARROW), lambda c, w: (0, c + half * steps))
     full = pl.BlockSpec((total, NARROW), lambda c, w: (0, c + half * steps))
     whole = pl.BlockSpec((total, depth), lambda c, w: (0, 0))
@@ -145,7 +145,7 @@
         grid_spec=pltpu.PrefetchScalarGridSpec(
             num_scalar_prefetch=1,
             grid=(steps,),
-            in_specs=[piece] * 8
+            in_specs=pieces
             + [full, full, weight, weight, pl.BlockSpec((depth, total), lambda c, w: (0, 0))]
             + kept,
             out_specs=(weight, weight, whole),
@@ -155,19 +155,19 @@
                 pltpu.VMEM((total, depth), F32),
             ],
         ),
-        input_output_aliases={15: 0, 16: 1} if before else {},
+        input_output_aliases={12: 0, 13: 1} if before else {},
         cost_estimate=pl.CostEstimate(
             flops=8 * total * part * depth, bytes_accessed=total * part * 14, transcendentals=0
         ),
-    )(where, *ds, slope, active, w_gate, w_up, tok, *before)
+    )(spots, *ds, slope, active, w_gate, w_up, tok, *before)
 
 
 def local(tokens, grad_out, gate_pre, up_pre, w_gate, w_up, w_down):
     rows, width = tokens.shape
     factor = float(1.0 / np.sqrt(np.float32(16 * rows)))
     y, zh = lax.axis_index("y"), lax.axis_index("zh")
-    p = lax.iota(jnp.int32, 8)
-    where = lax.rem(y + p // 2, 4) * 2 + lax.rem(zh + p, 2)
+    p = lax.iota(jnp.int32, 6)
+    spots = jnp.where(p < 4, lax.rem(y + p, 4), jnp.where(p == 4, zh, 1 - zh))
 
     out_all = gather_col(grad_out)
 
@@ -181,22 +181,14 @@
 
     part_rows = w_down.shape[0] // 2
 
-    def part(h, k):
-        here = lax.dynamic_slice_in_dim(out_all, lax.rem(y + k, 4) * (2 * rows), 2 * rows, 0)
-        return times_transposed(here, w_down[h * part_rows : (h + 1) * part_rows]).astype(BF if k else F32)
-
     def gathered(h):
-        recv = [along_y(part(h, k), k) for k in (2, 1, 3)]
-        total = part(h, 0) + sum(r.astype(F32) for r in recv)
-        total = total.reshape(2, rows, -1)
-        theirs = lax.dynamic_index_in_dim(total, 1 - zh, 0, keepdims=False).astype(BF)
-        mine = lax.dynamic_index_in_dim(total, zh, 0, keepdims=False)
-        d00 = (mine + to_pair(theirs).astype(F32)).astype(BF)
-        d30, d10 = along_y(d00, 1), along_y(d00, -1)
-        d01 = to_pair(d00)
-        d31, d11 = along_y(d01, 1), along_y(d01, -1)
-        d20, d21 = along_y(d30, 1), along_y(d11, -1)
-        return [d00, d01, d10, d11, d20, d21, d30, d31]
+        part = times_transposed(out_all, w_down[h * part_rows : (h + 1) * part_rows]).astype(BF)
+        recv = lax.all_to_all(part.reshape(4, 2 * rows, part_rows), "y", 0, 0, tiled=True)
+        total = jnp.sum(recv.astype(F32), axis=0)
+        mine = total.astype(BF)
+        d = (total + to_pair(mine).astype(F32)).astype(BF)
+        d3, d1 = along_y(d, 1), along_y(d, -1)
+        return [d, d1, d3, along_y(d3[:rows], 1), along_y(d1[rows:], -1)]
 
     halves = [gathered(h) for h in (0, 1)]
 
@@ -212,14 +204,13 @@
 
     kept = ()
     for k in (0, 3, 1, 2):
-        at = jnp.stack([lax.rem(y + k, 4), zh, 1 - zh]).astype(jnp.int32)
-        kept = hidden_of(at, rows, *saved[k], kept)
+        kept = hidden_of(spots, k, rows, *saved[k], kept)
     hidden, slope, active = kept
     down = (inner_rows(hidden, out_all) * factor).astype(BF)
     grad_down = both_cores(down)
     before = ()
     for h in (0, 1):
-        gate, up, back = back_of(where, h, halves[h], slope, active, w_gate, w_up, tok_turned, factor, before)
+        gate, up, back = back_of(spots, h, halves[h], slope, active, w_gate, w_up, tok_turned, factor, before)
         before = (back, gate, up)
     back_recv = across_col(back.reshape(8, rows, width))
     grad_gate = both_cores(gate)

time: 272 us -> 262 us (0.963)
  waiting for transfers between devices: 106 us -> 84.2 us
  blocking collectives: 0 us -> 21.3 us
  matrix products: 22.8 us -> 12.4 us
  starting transfers between devices: 64 us -> 54.9 us
  other arithmetic: 18.1 us -> 23.1 us
  local copies, waits for them, and re-layouts: 11.7 us -> 15.4 us
    ppermute x9 -> x7, waiting for transfers between devices: 55 us -> 32.8 us  [to_pair(): return lax.ppermute(x, 'zh', SWAP)]
    all_to_all x0 -> x1, blocking collectives: none -> 21.3 us  [across_col(): return lax.all_to_all(x, COL, 0, 0, tiled=True)]
    all_to_all x0 -> x2, waiting for transfers between devices: none -> 19.4 us  [gathered(): lax.all_to_all(part.reshape(4, 2 * rows, part_rows), 'y', 0, 0, tiled=True)]
    ppermute x22 -> x12, starting transfers between devices: 32.5 us -> 18.5 us  [along_y(): return lax.ppermute(x, 'y', ring(shift))]
    ppermute x22 -> x12, waiting for transfers between devices: 26.4 us -> 12.9 us  [along_y(): return lax.ppermute(x, 'y', ring(shift))]
    dot_general x8 -> x2, matrix products: 16.6 us -> 6.43 us  [times_transposed(): lax.dot_general(left, right, (((1,), (1,)), ((), ())), preferred_element_...]
    all_to_all x0 -> x2, starting transfers between devices: none -> 9.05 us  [gathered(): lax.all_to_all(part.reshape(4, 2 * rows, part_rows), 'y', 0, 0, tiled=True)]
    all_to_all x2 -> x1, starting transfers between devices: 10.4 us -> 3.56 us  [across_col(): return lax.all_to_all(x, COL, 0, 0, tiled=True)]
  transfers between devices with their start and end apart: 38 -> 27, of which waited for: 8 -> 7; matrix products, arithmetic and copies ran while one was open for 16% -> 16% of each run, Pallas kernels for 17% -> 18%
where the time goes in v3:
time: 262 us; the launch traced here: 260 us
  waiting for transfers between devices  84.2 us (32%)
  starting transfers between devices  54.9 us (21%)
  Pallas kernels  47.4 us (18%)
  other arithmetic  23.1 us (9%)
  blocking collectives  21.3 us (8%)
  local copies, waits for them, and re-layouts  15.4 us (6%)
  matrix products  12.4 us (5%)
    ppermute x7, waiting for transfers between devices, to_pair(): return lax.ppermute(x, 'zh', SWAP)  32.8 us
    pallas_call x2, Pallas kernels, back_of(): pl.pallas_call(functools.partial(back_kernel, factor, not before), out_sh...  24.7 us
    pallas_call x4, Pallas kernels, hidden_of(): pl.pallas_call(hidden_kernel, out_shape=(jax.ShapeDtypeStruct((total, wid...  22.7 us
    all_to_all x1, blocking collectives, across_col(): return lax.all_to_all(x, COL, 0, 0, tiled=True)  21.3 us
    all_to_all x2, waiting for transfers between devices, gathered(): lax.all_to_all(part.reshape(4, 2 * rows, part_rows), 'y', 0, 0, tiled=True)  19.4 us
    ppermute x7, starting transfers between devices, to_pair(): return lax.ppermute(x, 'zh', SWAP)  18.9 us
    ppermute x12, starting transfers between devices, along_y(): return lax.ppermute(x, 'y', ring(shift))  18.5 us
    ppermute x12, waiting for transfers between devices, along_y(): return lax.ppermute(x, 'y', ring(shift))  12.9 us
  transfers between devices with their start and end apart: 27, of which 7 were waited for; matrix products, arithmetic and copies ran while one was open for 16% of the time, Pallas kernels for 18%

profile of v3, /device:TPU:0, one launch (start us, length us, event | category | flops | bytes accessed | tf_op | source)
XLA Modules:
  0.0 259.6 jit_solution(12183504793409204676)
XLA Ops:
  0.6 1.1 broadcast_in_dim.22
  1.8 21.3 %all_to_all.25 = bf16[8,128,512]{2,1,0:T(8,128)(2,1)S(1)} all-to-all(bf16[8,128,512]{2,1,0:T(8,128)(2,1)S(1)} %broadcast_in_dim.22), channel_id=1, replica_groups=mesh['y'=4,'zh'=2,'zl'=2,'x'=4,'core'=2] {'zl','x'}, dimensions={0} | all-to-all | bytes 2097152 | tf_op jit(solution)/shard_map/all_to_all | solution.py:33
  23.1 2.6 %convolution_convert_fusion = bf16[1024,1024]{1,0:T(8,128)(2,1)} fusion(bf16[1024,512]{1,0:T(8,128)(2,1)S(1)} %bitcast.15, bf16[2048,512]{1,0:T(8,128)(2,1)S(1)} %copy-done.20), kind=kOutput, calls=%fused_computation.6 | convolution fusion | flops 1074790400 | bytes 4194304 | tf_op jit(solution)/shard_map/dot_general | solution.py:47
  25.7 4.6 %all-to-all-start.3 = ((bf16[4,256,1024]{2,1,0:T(8,128)(2,1)}), bf16[4,256,1024]{2,1,0:T(8,128)(2,1)S(1)}, u32[]{:S(2)}, u32[]{:S(2)}) async-start(bf16[4,256,1024]{2,1,0:T(8,128)(2,1)} %bitcast.14), calls=%async_computation.3 | async-start | bytes 4194304 | tf_op jit(solution)/shard_map/all_to_all | solution.py:186
  30.3 0.8 constant_dynamic-update-slice_fusion.1
  31.1 0.8 constant_dynamic-update-slice_fusion.refs_0_.refs_2_
  31.9 2.0 collective-permute-start.5
  34.0 1.2 collective-permute-start.8
  35.2 3.8 %convolution_convert_fusion.1 = bf16[1024,1024]{1,0:T(8,128)(2,1)} fusion(bf16[1024,512]{1,0:T(8,128)(2,1)S(1)} %bitcast.16, bf16[2048,512]{1,0:T(8,128)(2,1)} %param.13), kind=kOutput, calls=%fused_computation.7 | convolution fusion | flops 1074790400 | bytes 4194304 | tf_op jit(solution)/shard_map/dot_general | solution.py:47
  39.0 19.0 %all-to-all-done.3 = bf16[4,256,1024]{2,1,0:T(8,128)(2,1)S(1)} async-done(((bf16[4,256,1024]{2,1,0:T(8,128)(2,1)}), bf16[4,256,1024]{2,1,0:T(8,128)(2,1)S(1)}, u32[]{:S(2)}, u32[]{:S(2)}) %all-to-all-start.3) | async-done | bytes 2097184 | tf_op jit(solution)/shard_map/all_to_all | solution.py:186
  58.1 1.3 copy-done.2
  59.4 4.5 %all-to-all-start.1 = ((bf16[4,256,1024]{2,1,0:T(8,128)(2,1)}), bf16[4,256,1024]{2,1,0:T(8,128)(2,1)}, u32[]{:S(2)}, u32[]{:S(2)}) async-start(bf16[4,256,1024]{2,1,0:T(8,128)(2,1)} %bitcast.13), calls=%async_computation.1 | async-start | bytes 4194304 | tf_op jit(solution)/shard_map/all_to_all | solution.py:186
  63.8 3.7 %collective-permute-start.13 = (bf16[256,2048]{1,0:T(8,128)(2,1)}, bf16[256,2048]{1,0:T(8,128)(2,1)S(1)}, u32[]{:S(2)}, u32[]{:S(2)}) collective-permute-start(bf16[256,2048]{1,0:T(8,128)(2,1)} %constant_dynamic-update-slice_fusion.refs_0_.refs_2_), channel_id=1, source_target_pairs={{0,16},{16,0},{1,17},{17,1},{2,18},{18,2},{3,19},{19,3},{4,20},{20... | collective-permute-start | bytes 3145736 | tf_op jit(solution)/shard_map/ppermute | solution.py:29
  67.5 11.5 %collective-permute-done.8.refs_0_.refs_2_ = bf16[256,2048]{1,0:T(8,128)(2,1)S(1)} collective-permute-done((bf16[256,2048]{1,0:T(8,128)(2,1)}, bf16[256,2048]{1,0:T(8,128)(2,1)S(1)}, u32[]{:S(2)}, u32[]{:S(2)}) %collective-permute-start.8) | collective-permute-done | bytes 1048608 | tf_op jit(solution)/shard_map/ppermute | solution.py:25
  79.0 0.9 slice.35
  79.9 1.2 collective-permute-start.9
  81.1 1.9 slice.34
  83.0 0.9 collective-permute-start.6
  83.8 3.6 %collective-permute-start.12 = (bf16[256,2048]{1,0:T(8,128)(2,1)}, bf16[256,2048]{1,0:T(8,128)(2,1)}, u32[]{:S(2)}, u32[]{:S(2)}) collective-permute-start(bf16[256,2048]{1,0:T(8,128)(2,1)} %collective-permute-done.5.refs_0_.refs_2_), channel_id=1, source_target_pairs={{0,16},{16,0},{1,17},{17,1},{2,18},{18,2},{3,19},{19,3},{4,20},{20... | collective-permute-start | bytes 3145736 | tf_op jit(solution)/shard_map/ppermute | solution.py:29
  87.4 7.0 %collective-permute-done.14 = bf16[128,512]{1,0:T(8,128)(2,1)S(1)} collective-permute-done((bf16[128,512]{1,0:T(8,128)(2,1)S(1)}, bf16[128,512]{1,0:T(8,128)(2,1)S(1)}, u32[]{:S(2)}, u32[]{:S(2)}) %collective-permute-start.14) | collective-permute-done | bytes 131104 | tf_op jit(solution)/shard_map/ppermute | solution.py:195
  94.3 1.2 collective-permute-start.11
  95.5 2.1 convert_reduce_fusion
  97.6 0.9 convert_element_type.69
  98.5 2.4 collective-permute-start.15
  100.9 0.7 pad_maximum_fusion
  101.6 1.1 copy.23
  102.7 0.4 all-to-all-done.1
  103.1 1.5 broadcast_in_dim.23
  104.7 4.3 %all-to-all-start.2 = ((bf16[4,2,128,512]{2,1,3,0:T(2,128)(2,1)}), bf16[4,2,128,512]{2,1,3,0:T(2,128)(2,1)}, u32[]{:S(2)}, u32[]{:S(2)}) async-start(bf16[4,2,128,512]{2,1,3,0:T(2,128)(2,1)} %broadcast_in_dim.23), calls=%async_computation.2 | async-start | bytes 2097152 | tf_op jit(solution)/shard_map/all_to_all | solution.py:198
  108.9 1.4 collective-permute-done.9.refs_2_
  110.3 3.6 %collective-permute-start.10 = (bf16[128,2048]{1,0:T(8,128)(2,1)}, bf16[128,2048]{1,0:T(8,128)(2,1)}, u32[]{:S(2)}, u32[]{:S(2)}) collective-permute-start(bf16[128,2048]{1,0:T(8,128)(2,1)} %collective-permute-done.9.refs_2_), channel_id=1, source_target_pairs={{0,16},{16,0},{1,17},{17,1},{2,18},{18,2},{3,19},{19,3},{4,20},{20... | collective-permute-start | bytes 1572872 | tf_op jit(solution)/shard_map/ppermute | solution.py:29
  113.9 1.1 collective-permute-start.7
  115.0 2.1 convert_reduce_fusion.1
  117.1 0.9 convert_element_type.64
  118.0 32.8 %collective-permute-done.15 = bf16[256,1024]{1,0:T(8,128)(2,1)} collective-permute-done((bf16[256,1024]{1,0:T(8,128)(2,1)}, bf16[256,1024]{1,0:T(8,128)(2,1)}, u32[]{:S(2)}, u32[]{:S(2)}) %collective-permute-start.15) | collective-permute-done | bytes 524320 | tf_op jit(solution)/shard_map/ppermute | solution.py:29
  150.8 3.4 %collective-permute-start = (bf16[256,1024]{1,0:T(8,128)(2,1)}, bf16[256,1024]{1,0:T(8,128)(2,1)}, u32[]{:S(2)}, u32[]{:S(2)}) collective-permute-start(bf16[256,1024]{1,0:T(8,128)(2,1)} %convert_element_type.64), channel_id=1, source_target_pairs={{0,16},{16,0},{1,17},{17,1},{2,18},{18,2},{3,19},{19,3},{4,20},{20... | collective-permute-start | bytes 1572872 | tf_op jit(solution)/shard_map/ppermute | solution.py:29
  154.2 2.0 add_convert_fusion.3.refs_0_
  156.2 1.8 collective-permute-start.17
  158.0 1.4 collective-permute-start.16
  159.4 0.5 compare_select_fusion.3.spots
  160.0 2.6 copy.24
  162.5 1.6 reshape.27.refs_9_
  164.1 5.7 %shard_map.102 = (bf16[1024,2048]{1,0:T(8,128)(2,1)}, f32[1024,2048]{1,0:T(8,128)}, f32[1024,2048]{1,0:T(8,128)}) custom-call(s32[6]{0:T(128)} %compare_select_fusion.3.spots, bf16[256,2048]{1,0:T(8,128)(2,1)} %constant_dynamic-update-slice_fusion.refs_0_.refs_2_, bf16[256,2048]{1,0:T(8,128)(2,1)} %copy-done.4, ...), custom_call_target="tpu_custom_call" | custom-call | flops 5242880 | bytes 7340032 | tf_op jit(solution)/shard_map/pallas_call | solution.py:79
  169.8 5.6 %shard_map.103 = (bf16[1024,2048]{1,0:T(8,128)(2,1)}, f32[1024,2048]{1,0:T(8,128)}, f32[1024,2048]{1,0:T(8,128)}) custom-call(s32[6]{0:T(128)} %compare_select_fusion.3.spots, bf16[256,2048]{1,0:T(8,128)(2,1)} %collective-permute-done.5.refs_0_.refs_2_, ...), custom_call_target="tpu_custom_call", output_to_operand_aliasing={{0}: (5, {}), {1}: (6, {}), {2}: (7, {})} | custom-call | flops 5242880 | bytes 7340032 | tf_op jit(solution)/shard_map/pallas_call | solution.py:79
  175.4 5.7 %shard_map.104 = (bf16[1024,2048]{1,0:T(8,128)(2,1)}, f32[1024,2048]{1,0:T(8,128)}, f32[1024,2048]{1,0:T(8,128)}) custom-call(s32[6]{0:T(128)} %compare_select_fusion.3.spots, bf16[256,2048]{1,0:T(8,128)(2,1)} %copy-done.3, bf16[256,2048]{1,0:T(8,128)(2,1)} %collective-permute-done.11.refs_1_.refs_3_, ...), custom_call_target="tpu_custom_call", output_to_operand_aliasing={{0}: (5, {}), {1}: (6, {}), {2}: (7, {})} | custom-call | flops 5242880 | bytes 7340032 | tf_op jit(solution)/shard_map/pallas_call | solution.py:79
  181.1 5.7 %shard_map.105 = (bf16[1024,2048]{1,0:T(8,128)(2,1)}, f32[1024,2048]{1,0:T(8,128)}, f32[1024,2048]{1,0:T(8,128)}) custom-call(s32[6]{0:T(128)} %compare_select_fusion.3.spots, bf16[128,2048]{1,0:T(8,128)(2,1)} %collective-permute-done.6.refs_0_, ...), custom_call_target="tpu_custom_call", output_to_operand_aliasing={{0}: (5, {}), {1}: (6, {}), {2}: (7, {})} | custom-call | flops 5242880 | bytes 7340032 | tf_op jit(solution)/shard_map/pallas_call | solution.py:79
  186.8 1.3 add_convert_fusion.4.refs_0_
  188.1 0.7 collective-permute-start.2
  188.8 2.6 %collective-permute-start.1 = (bf16[256,1024]{1,0:T(8,128)(2,1)S(1)}, bf16[256,1024]{1,0:T(8,128)(2,1)S(1)}, u32[]{:S(2)}, u32[]{:S(2)}) collective-permute-start(bf16[256,1024]{1,0:T(8,128)(2,1)S(1)} %add_convert_fusion.4.refs_0_), channel_id=1, source_target_pairs={{0,96},{32,0},{64,32},{96,64},{1,97},{33,1},{65,33},{97,65},{2,98}... | collective-permute-start | bytes 1572872 | tf_op jit(solution)/shard_map/ppermute | solution.py:25
  191.6 3.3 %collective-permute-start.19 = (bf16[128,1024]{1,0:T(8,128)(2,1)S(1)}, bf16[128,1024]{1,0:T(8,128)(2,1)S(1)}, u32[]{:S(2)}, u32[]{:S(2)}) collective-permute-start(bf16[128,1024]{1,0:T(8,128)(2,1)S(1)} %slice.37), channel_id=1, source_target_pairs={{0,96},{32,0},{64,32},{96,64},{1,97},{33,1},{65,33},{97,65},{2,98}... | collective-permute-start | bytes 786440 | tf_op jit(solution)/shard_map/ppermute | solution.py:25
  194.8 5.9 %multiply_convert_fusion = bf16[2048,512]{1,0:T(8,128)(2,1)} fusion(bf16[1024,2048]{1,0:T(8,128)(2,1)} %get-tuple-element.39, bf16[1024,512]{1,0:T(8,128)(2,1)S(1)} %bitcast.17), kind=kOutput, calls=%fused_computation.1 | convolution fusion | flops 2149580800 | bytes 7340032 | tf_op jit(solution)/shard_map/dot_general | solution.py:43
  201.1 3.3 %collective-permute-start.4 = (bf16[128,1024]{1,0:T(8,128)(2,1)S(1)}, bf16[128,1024]{1,0:T(8,128)(2,1)S(1)}, u32[]{:S(2)}, u32[]{:S(2)}) collective-permute-start(bf16[128,1024]{1,0:T(8,128)(2,1)S(1)} %slice.33), channel_id=1, source_target_pairs={{0,96},{32,0},{64,32},{96,64},{1,97},{33,1},{65,33},{97,65},{2,98}... | collective-permute-start | bytes 786440 | tf_op jit(solution)/shard_map/ppermute | solution.py:25
  204.4 0.7 copy-done.18
  205.1 0.1 copy-done.17
  205.2 12.1 %shard_map.106 = (bf16[512,2048]{1,0:T(8,128)(2,1)}, bf16[512,2048]{1,0:T(8,128)(2,1)}, f32[1024,512]{1,0:T(8,128)}) custom-call(s32[6]{0:T(128)} %compare_select_fusion.3.spots, bf16[256,1024]{1,0:T(8,128)(2,1)} %add_convert_fusion.3.refs_0_, bf16[256,1024]{1,0:T(8,128)(2,1)} %copy-done.9, bf16[256,1024]{1,0:T(8,128)(2,1)} %copy-done.8, ...), custom_call_target="tpu_custom_call" | custom-call | flops 4294967296 | bytes 14680064 | tf_op jit(solution)/shard_map/pallas_call | solution.py:138
  217.4 0.7 copy-done.15
  218.2 12.6 %shard_map.107 = (bf16[512,2048]{1,0:T(8,128)(2,1)}, bf16[512,2048]{1,0:T(8,128)(2,1)}, bf16[1024,512]{1,0:T(8,128)(2,1)}) custom-call(s32[6]{0:T(128)} %compare_select_fusion.3.spots, bf16[256,1024]{1,0:T(8,128)(2,1)} %copy-done.5, bf16[256,1024]{1,0:T(8,128)(2,1)} %copy-done.7, ...), custom_call_target="tpu_custom_call", output_to_operand_aliasing={{0}: (12, {}), {1}: (13, {})} | custom-call | flops 4294967296 | bytes 14680064 | tf_op jit(solution)/shard_map/pallas_call | solution.py:138
  230.8 0.5 collective-permute-start.20
  231.3 3.6 %all-to-all-start.4 = ((bf16[8,128,512]{2,1,0:T(8,128)(2,1)}), bf16[8,128,512]{2,1,0:T(8,128)(2,1)S(1)}, u32[]{:S(2)}, u32[]{:S(2)}) async-start(bf16[8,128,512]{2,1,0:T(8,128)(2,1)} %bitcast.18), calls=%async_computation.4 | async-start | bytes 2097152 | tf_op jit(solution)/shard_map/all_to_all | solution.py:33
  234.9 4.3 %add_convert_fusion = bf16[2048,512]{1,0:T(8,128)(2,1)} fusion(bf16[2048,512]{1,0:T(8,128)(2,1)} %collective-permute-done.22, bf16[2048,512]{1,0:T(8,128)(2,1)} %multiply_convert_fusion), kind=kLoop, calls=%fused_computation | loop fusion | flops 4194304 | bytes 6291456 | tf_op jit(solution)/shard_map/convert_element_type | solution.py:203
  239.2 12.1 %all-to-all-done.4 = bf16[8,128,512]{2,1,0:T(8,128)(2,1)S(1)} async-done(((bf16[8,128,512]{2,1,0:T(8,128)(2,1)}), bf16[8,128,512]{2,1,0:T(8,128)(2,1)S(1)}, u32[]{:S(2)}, u32[]{:S(2)}) %all-to-all-start.4) | async-done | bytes 1048608 | tf_op jit(solution)/shard_map/all_to_all | solution.py:33
  251.3 0.8 reduce_sum.32
  252.1 3.8 %add_convert_fusion.1 = bf16[512,2048]{1,0:T(8,128)(2,1)} fusion(bf16[512,2048]{1,0:T(8,128)(2,1)} %collective-permute-done.21, bf16[512,2048]{1,0:T(8,128)(2,1)S(1)} %copy-done.1), kind=kLoop, calls=%fused_computation.2 | loop fusion | flops 4194304 | bytes 6291456 | tf_op jit(solution)/shard_map/convert_element_type | solution.py:203
  255.9 3.7 %add_convert_fusion.2 = bf16[512,2048]{1,0:T(8,128)(2,1)} fusion(bf16[512,2048]{1,0:T(8,128)(2,1)} %collective-permute-done.20, bf16[512,2048]{1,0:T(8,128)(2,1)S(1)} %copy-done), kind=kLoop, calls=%fused_computation.3 | loop fusion | flops 4194304 | bytes 6291456 | tf_op jit(solution)/shard_map/convert_element_type | solution.py:203
  (68 shorter events, 0.6 us)
Async XLA Ops:
  0.6 22.4 %copy-start.20 = (bf16[2048,512]{1,0:T(8,128)(2,1)S(1)}, bf16[2048,512]{1,0:T(8,128)(2,1)}, u32[]{:S(2)}) copy-start(bf16[2048,512]{1,0:T(8,128)(2,1)} %param.13) | copy-start | bytes 6291460
  23.0 2.6 %copy-start.10 = (bf16[8,128,512]{2,1,0:T(8,128)(2,1)}, bf16[8,128,512]{2,1,0:T(8,128)(2,1)S(1)}, u32[]{:S(2)}) copy-start(bf16[8,128,512]{2,1,0:T(8,128)(2,1)S(1)} %all_to_all.25) | copy-start | bytes 3145732
  25.7 4.6 %copy-start.13 = (bf16[128,2048]{1,0:T(8,128)(2,1)S(1)}, bf16[128,2048]{1,0:T(8,128)(2,1)}, u32[]{:S(2)}) copy-start(bf16[128,2048]{1,0:T(8,128)(2,1)} %param.9) | copy-start | bytes 1572868
  25.7 5.5 %copy-start.14 = (bf16[128,2048]{1,0:T(8,128)(2,1)S(1)}, bf16[128,2048]{1,0:T(8,128)(2,1)}, u32[]{:S(2)}) copy-start(bf16[128,2048]{1,0:T(8,128)(2,1)} %param.10) | copy-start | bytes 1572868
  25.7 32.4 %all-to-all-start.3 = ((bf16[4,256,1024]{2,1,0:T(8,128)(2,1)}), bf16[4,256,1024]{2,1,0:T(8,128)(2,1)S(1)}, u32[]{:S(2)}, u32[]{:S(2)}) async-start(bf16[4,256,1024]{2,1,0:T(8,128)(2,1)} %bitcast.14), calls=%async_computation.3 | async-start | bytes 4194304 | tf_op jit(solution)/shard_map/all_to_all | solution.py:186
  30.3 4.9 %copy-start.11 = (bf16[8,128,512]{2,1,0:T(8,128)(2,1)S(1)}, bf16[8,128,512]{2,1,0:T(8,128)(2,1)}, u32[]{:S(2)}) copy-start(bf16[8,128,512]{2,1,0:T(8,128)(2,1)} %copy-done.10) | copy-start | bytes 3145732
  31.9 49.1 %collective-permute-start.5 = (bf16[256,2048]{1,0:T(8,128)(2,1)}, bf16[256,2048]{1,0:T(8,128)(2,1)}, u32[]{:S(2)}, u32[]{:S(2)}) collective-permute-start(bf16[256,2048]{1,0:T(8,128)(2,1)} %constant_dynamic-update-slice_fusion.refs_0_.refs_2_), channel_id=1, source_target_pairs={{0,32},{32,64},{64,96},{96,0},{1,33},{33,65},{65,97},{97,1},{2,34}... | collective-permute-start | bytes 3145736 | tf_op jit(solution)/shard_map/ppermute | solution.py:25
  34.0 45.0 %collective-permute-start.8 = (bf16[256,2048]{1,0:T(8,128)(2,1)}, bf16[256,2048]{1,0:T(8,128)(2,1)S(1)}, u32[]{:S(2)}, u32[]{:S(2)}) collective-permute-start(bf16[256,2048]{1,0:T(8,128)(2,1)} %constant_dynamic-update-slice_fusion.refs_0_.refs_2_), channel_id=1, source_target_pairs={{0,96},{32,0},{64,32},{96,64},{1,97},{33,1},{65,33},{97,65},{2,98}... | collective-permute-start | bytes 3145736 | tf_op jit(solution)/shard_map/ppermute | solution.py:25
  58.0 1.3 copy-start.2
  58.0 9.4 %copy-start.19 = (bf16[128,512]{1,0:T(8,128)(2,1)S(1)}, bf16[128,512]{1,0:T(8,128)(2,1)}, u32[]{:S(2)}) copy-start(bf16[128,512]{1,0:T(8,128)(2,1)} %param.7) | copy-start | bytes 393220
  59.4 43.8 %all-to-all-start.1 = ((bf16[4,256,1024]{2,1,0:T(8,128)(2,1)}), bf16[4,256,1024]{2,1,0:T(8,128)(2,1)}, u32[]{:S(2)}, u32[]{:S(2)}) async-start(bf16[4,256,1024]{2,1,0:T(8,128)(2,1)} %bitcast.13), calls=%async_computation.1 | async-start | bytes 4194304 | tf_op jit(solution)/shard_map/all_to_all | solution.py:186
  63.8 34.7 %collective-permute-start.13 = (bf16[256,2048]{1,0:T(8,128)(2,1)}, bf16[256,2048]{1,0:T(8,128)(2,1)S(1)}, u32[]{:S(2)}, u32[]{:S(2)}) collective-permute-start(bf16[256,2048]{1,0:T(8,128)(2,1)} %constant_dynamic-update-slice_fusion.refs_0_.refs_2_), channel_id=1, source_target_pairs={{0,16},{16,0},{1,17},{17,1},{2,18},{18,2},{3,19},{19,3},{4,20},{20... | collective-permute-start | bytes 3145736 | tf_op jit(solution)/shard_map/ppermute | solution.py:29
  67.5 26.9 %collective-permute-start.14 = (bf16[128,512]{1,0:T(8,128)(2,1)S(1)}, bf16[128,512]{1,0:T(8,128)(2,1)S(1)}, u32[]{:S(2)}, u32[]{:S(2)}) collective-permute-start(bf16[128,512]{1,0:T(8,128)(2,1)S(1)} %copy-done.19), channel_id=1, source_target_pairs={{0,8},{8,0},{1,9},{9,1},{2,10},{10,2},{3,11},{11,3},{4,12},{12,4},... | collective-permute-start | bytes 393224 | tf_op jit(solution)/shard_map/ppermute | solution.py:195
  79.0 18.6 %copy-start.3 = (bf16[256,2048]{1,0:T(8,128)(2,1)}, bf16[256,2048]{1,0:T(8,128)(2,1)S(1)}, u32[]{:S(2)}) copy-start(bf16[256,2048]{1,0:T(8,128)(2,1)S(1)} %collective-permute-done.8.refs_0_.refs_2_) | copy-start | bytes 3145732
  79.9 30.4 %collective-permute-start.9 = (bf16[128,2048]{1,0:T(8,128)(2,1)}, bf16[128,2048]{1,0:T(8,128)(2,1)}, u32[]{:S(2)}, u32[]{:S(2)}) collective-permute-start(bf16[128,2048]{1,0:T(8,128)(2,1)} %slice.35), channel_id=1, source_target_pairs={{0,96},{32,0},{64,32},{96,64},{1,97},{33,1},{65,33},{97,65},{2,98}... | collective-permute-start | bytes 1572872 | tf_op jit(solution)/shard_map/ppermute | solution.py:25
  83.0 30.9 %collective-permute-start.6 = (bf16[128,2048]{1,0:T(8,128)(2,1)}, bf16[128,2048]{1,0:T(8,128)(2,1)}, u32[]{:S(2)}, u32[]{:S(2)}) collective-permute-start(bf16[128,2048]{1,0:T(8,128)(2,1)} %slice.34), channel_id=1, source_target_pairs={{0,32},{32,64},{64,96},{96,0},{1,33},{33,65},{65,97},{97,1},{2,34}... | collective-permute-start | bytes 1572872 | tf_op jit(solution)/shard_map/ppermute | solution.py:25
  83.8 72.4 %collective-permute-start.12 = (bf16[256,2048]{1,0:T(8,128)(2,1)}, bf16[256,2048]{1,0:T(8,128)(2,1)}, u32[]{:S(2)}, u32[]{:S(2)}) collective-permute-start(bf16[256,2048]{1,0:T(8,128)(2,1)} %collective-permute-done.5.refs_0_.refs_2_), channel_id=1, source_target_pairs={{0,16},{16,0},{1,17},{17,1},{2,18},{18,2},{3,19},{19,3},{4,20},{20... | collective-permute-start | bytes 3145736 | tf_op jit(solution)/shard_map/ppermute | solution.py:29
  94.3 63.7 %collective-permute-start.11 = (bf16[256,2048]{1,0:T(8,128)(2,1)S(1)}, bf16[256,2048]{1,0:T(8,128)(2,1)}, u32[]{:S(2)}, u32[]{:S(2)}) collective-permute-start(bf16[256,2048]{1,0:T(8,128)(2,1)S(1)} %collective-permute-done.8.refs_0_.refs_2_), channel_id=1, source_target_pairs={{0,16},{16,0},{1,17},{17,1},{2,18},{18,2},{3,19},{19,3},{4,20},{20... | collective-permute-start | bytes 3145736 | tf_op jit(solution)/shard_map/ppermute | solution.py:29
  98.5 6.2 %copy-start.4 = (bf16[256,2048]{1,0:T(8,128)(2,1)}, bf16[256,2048]{1,0:T(8,128)(2,1)S(1)}, u32[]{:S(2)}) copy-start(bf16[256,2048]{1,0:T(8,128)(2,1)S(1)} %collective-permute-done.13.refs_1_.refs_3_) | copy-start | bytes 3145732
  98.5 52.3 %collective-permute-start.15 = (bf16[256,1024]{1,0:T(8,128)(2,1)}, bf16[256,1024]{1,0:T(8,128)(2,1)}, u32[]{:S(2)}, u32[]{:S(2)}) collective-permute-start(bf16[256,1024]{1,0:T(8,128)(2,1)} %convert_element_type.69), channel_id=1, source_target_pairs={{0,16},{16,0},{1,17},{17,1},{2,18},{18,2},{3,19},{19,3},{4,20},{20... | collective-permute-start | bytes 1572872 | tf_op jit(solution)/shard_map/ppermute | solution.py:29
  104.7 55.3 %all-to-all-start.2 = ((bf16[4,2,128,512]{2,1,3,0:T(2,128)(2,1)}), bf16[4,2,128,512]{2,1,3,0:T(2,128)(2,1)}, u32[]{:S(2)}, u32[]{:S(2)}) async-start(bf16[4,2,128,512]{2,1,3,0:T(2,128)(2,1)} %broadcast_in_dim.23), calls=%async_computation.2 | async-start | bytes 2097152 | tf_op jit(solution)/shard_map/all_to_all | solution.py:198
  110.3 70.8 %collective-permute-start.10 = (bf16[128,2048]{1,0:T(8,128)(2,1)}, bf16[128,2048]{1,0:T(8,128)(2,1)}, u32[]{:S(2)}, u32[]{:S(2)}) collective-permute-start(bf16[128,2048]{1,0:T(8,128)(2,1)} %collective-permute-done.9.refs_2_), channel_id=1, source_target_pairs={{0,16},{16,0},{1,17},{17,1},{2,18},{18,2},{3,19},{19,3},{4,20},{20... | collective-permute-start | bytes 1572872 | tf_op jit(solution)/shard_map/ppermute | solution.py:29
  113.9 67.2 %collective-permute-start.7 = (bf16[128,2048]{1,0:T(8,128)(2,1)}, bf16[128,2048]{1,0:T(8,128)(2,1)}, u32[]{:S(2)}, u32[]{:S(2)}) collective-permute-start(bf16[128,2048]{1,0:T(8,128)(2,1)} %collective-permute-done.6.refs_0_), channel_id=1, source_target_pairs={{0,16},{16,0},{1,17},{17,1},{2,18},{18,2},{3,19},{19,3},{4,20},{20... | collective-permute-start | bytes 1572872 | tf_op jit(solution)/shard_map/ppermute | solution.py:29
  150.8 36.0 %collective-permute-start = (bf16[256,1024]{1,0:T(8,128)(2,1)}, bf16[256,1024]{1,0:T(8,128)(2,1)}, u32[]{:S(2)}, u32[]{:S(2)}) collective-permute-start(bf16[256,1024]{1,0:T(8,128)(2,1)} %convert_element_type.64), channel_id=1, source_target_pairs={{0,16},{16,0},{1,17},{17,1},{2,18},{18,2},{3,19},{19,3},{4,20},{20... | collective-permute-start | bytes 1572872 | tf_op jit(solution)/shard_map/ppermute | solution.py:29
  156.2 35.2 %collective-permute-start.17 = (bf16[256,1024]{1,0:T(8,128)(2,1)}, bf16[256,1024]{1,0:T(8,128)(2,1)S(1)}, u32[]{:S(2)}, u32[]{:S(2)}) collective-permute-start(bf16[256,1024]{1,0:T(8,128)(2,1)} %add_convert_fusion.3.refs_0_), channel_id=1, source_target_pairs={{0,32},{32,64},{64,96},{96,0},{1,33},{33,65},{65,97},{97,1},{2,34}... | collective-permute-start | bytes 1572872 | tf_op jit(solution)/shard_map/ppermute | solution.py:25
  158.0 33.5 %collective-permute-start.16 = (bf16[256,1024]{1,0:T(8,128)(2,1)}, bf16[256,1024]{1,0:T(8,128)(2,1)S(1)}, u32[]{:S(2)}, u32[]{:S(2)}) collective-permute-start(bf16[256,1024]{1,0:T(8,128)(2,1)} %add_convert_fusion.3.refs_0_), channel_id=1, source_target_pairs={{0,96},{32,0},{64,32},{96,64},{1,97},{33,1},{65,33},{97,65},{2,98}... | collective-permute-start | bytes 1572872 | tf_op jit(solution)/shard_map/ppermute | solution.py:25
  186.8 8.0 %copy-start.12 = (bf16[8,128,512]{2,1,0:T(8,128)(2,1)S(1)}, bf16[8,128,512]{2,1,0:T(8,128)(2,1)}, u32[]{:S(2)}) copy-start(bf16[8,128,512]{2,1,0:T(8,128)(2,1)} %copy-done.10) | copy-start | bytes 3145732
  188.1 12.7 %copy-start.5 = (bf16[256,1024]{1,0:T(8,128)(2,1)}, bf16[256,1024]{1,0:T(8,128)(2,1)S(1)}, u32[]{:S(2)}) copy-start(bf16[256,1024]{1,0:T(8,128)(2,1)S(1)} %add_convert_fusion.4.refs_0_) | copy-start | bytes 1572868
  188.1 12.8 %collective-permute-start.2 = (bf16[256,1024]{1,0:T(8,128)(2,1)S(1)}, bf16[256,1024]{1,0:T(8,128)(2,1)S(1)}, u32[]{:S(2)}, u32[]{:S(2)}) collective-permute-start(bf16[256,1024]{1,0:T(8,128)(2,1)S(1)} %add_convert_fusion.4.refs_0_), channel_id=1, source_target_pairs={{0,32},{32,64},{64,96},{96,0},{1,33},{33,65},{65,97},{97,1},{2,34}... | collective-permute-start | bytes 1572872 | tf_op jit(solution)/shard_map/ppermute | solution.py:25
  188.8 12.3 %collective-permute-start.1 = (bf16[256,1024]{1,0:T(8,128)(2,1)S(1)}, bf16[256,1024]{1,0:T(8,128)(2,1)S(1)}, u32[]{:S(2)}, u32[]{:S(2)}) collective-permute-start(bf16[256,1024]{1,0:T(8,128)(2,1)S(1)} %add_convert_fusion.4.refs_0_), channel_id=1, source_target_pairs={{0,96},{32,0},{64,32},{96,64},{1,97},{33,1},{65,33},{97,65},{2,98}... | collective-permute-start | bytes 1572872 | tf_op jit(solution)/shard_map/ppermute | solution.py:25
  191.4 9.4 %copy-start.8 = (bf16[256,1024]{1,0:T(8,128)(2,1)}, bf16[256,1024]{1,0:T(8,128)(2,1)S(1)}, u32[]{:S(2)}) copy-start(bf16[256,1024]{1,0:T(8,128)(2,1)S(1)} %collective-permute-done.17.refs_2_) | copy-start | bytes 1572868
  191.4 12.9 %collective-permute-start.18 = (bf16[128,1024]{1,0:T(8,128)(2,1)S(1)}, bf16[128,1024]{1,0:T(8,128)(2,1)S(1)}, u32[]{:S(2)}, u32[]{:S(2)}) collective-permute-start(bf16[128,1024]{1,0:T(8,128)(2,1)S(1)} %slice.36), channel_id=1, source_target_pairs={{0,32},{32,64},{64,96},{96,0},{1,33},{33,65},{65,97},{97,1},{2,34}... | collective-permute-start | bytes 786440 | tf_op jit(solution)/shard_map/ppermute | solution.py:25
  191.5 9.3 %copy-start.9 = (bf16[256,1024]{1,0:T(8,128)(2,1)}, bf16[256,1024]{1,0:T(8,128)(2,1)S(1)}, u32[]{:S(2)}) copy-start(bf16[256,1024]{1,0:T(8,128)(2,1)S(1)} %collective-permute-done.16.refs_1_) | copy-start | bytes 1572868
  191.6 12.8 %collective-permute-start.19 = (bf16[128,1024]{1,0:T(8,128)(2,1)S(1)}, bf16[128,1024]{1,0:T(8,128)(2,1)S(1)}, u32[]{:S(2)}, u32[]{:S(2)}) collective-permute-start(bf16[128,1024]{1,0:T(8,128)(2,1)S(1)} %slice.37), channel_id=1, source_target_pairs={{0,96},{32,0},{64,32},{96,64},{1,97},{33,1},{65,33},{97,65},{2,98}... | collective-permute-start | bytes 786440 | tf_op jit(solution)/shard_map/ppermute | solution.py:25
  200.8 34.1 %collective-permute-start.22 = (bf16[2048,512]{1,0:T(8,128)(2,1)}, bf16[2048,512]{1,0:T(8,128)(2,1)}, u32[]{:S(2)}, u32[]{:S(2)}) collective-permute-start(bf16[2048,512]{1,0:T(8,128)(2,1)} %multiply_convert_fusion), channel_id=1, source_target_pairs={{0,1},{1,0},{2,3},{3,2},{4,5},{5,4},{6,7},{7,6},{8,9},{9,8},{10,11... | collective-permute-start | bytes 6291464 | tf_op jit(solution)/shard_map/ppermute | solution.py:202
  200.9 16.4 %copy-start.6 = (bf16[256,1024]{1,0:T(8,128)(2,1)}, bf16[256,1024]{1,0:T(8,128)(2,1)S(1)}, u32[]{:S(2)}) copy-start(bf16[256,1024]{1,0:T(8,128)(2,1)S(1)} %collective-permute-done.2.refs_2_) | copy-start | bytes 1572868
  200.9 16.4 %collective-permute-start.3 = (bf16[128,1024]{1,0:T(8,128)(2,1)S(1)}, bf16[128,1024]{1,0:T(8,128)(2,1)S(1)}, u32[]{:S(2)}, u32[]{:S(2)}) collective-permute-start(bf16[128,1024]{1,0:T(8,128)(2,1)S(1)} %slice.32), channel_id=1, source_target_pairs={{0,32},{32,64},{64,96},{96,0},{1,33},{33,65},{65,97},{97,1},{2,34}... | collective-permute-start | bytes 786440 | tf_op jit(solution)/shard_map/ppermute | solution.py:25
  201.0 16.3 %copy-start.7 = (bf16[256,1024]{1,0:T(8,128)(2,1)}, bf16[256,1024]{1,0:T(8,128)(2,1)S(1)}, u32[]{:S(2)}) copy-start(bf16[256,1024]{1,0:T(8,128)(2,1)S(1)} %collective-permute-done.1.refs_1_) | copy-start | bytes 1572868
  201.1 16.3 %collective-permute-start.4 = (bf16[128,1024]{1,0:T(8,128)(2,1)S(1)}, bf16[128,1024]{1,0:T(8,128)(2,1)S(1)}, u32[]{:S(2)}, u32[]{:S(2)}) collective-permute-start(bf16[128,1024]{1,0:T(8,128)(2,1)S(1)} %slice.33), channel_id=1, source_target_pairs={{0,96},{32,0},{64,32},{96,64},{1,97},{33,1},{65,33},{97,65},{2,98}... | collective-permute-start | bytes 786440 | tf_op jit(solution)/shard_map/ppermute | solution.py:25
  204.3 0.8 copy-start.17
  204.3 0.7 copy-start.18
  217.4 0.7 copy-start.15
  217.4 0.8 copy-start.16
  230.7 21.4 %collective-permute-start.21 = (bf16[512,2048]{1,0:T(8,128)(2,1)}, bf16[512,2048]{1,0:T(8,128)(2,1)}, u32[]{:S(2)}, u32[]{:S(2)}) collective-permute-start(bf16[512,2048]{1,0:T(8,128)(2,1)} %get-tuple-element.38), channel_id=1, source_target_pairs={{0,1},{1,0},{2,3},{3,2},{4,5},{5,4},{6,7},{7,6},{8,9},{9,8},{10,11... | collective-permute-start | bytes 6291464 | tf_op jit(solution)/shard_map/ppermute | solution.py:202
  230.8 25.1 %collective-permute-start.20 = (bf16[512,2048]{1,0:T(8,128)(2,1)}, bf16[512,2048]{1,0:T(8,128)(2,1)}, u32[]{:S(2)}, u32[]{:S(2)}) collective-permute-start(bf16[512,2048]{1,0:T(8,128)(2,1)} %get-tuple-element.37), channel_id=1, source_target_pairs={{0,1},{1,0},{2,3},{3,2},{4,5},{5,4},{6,7},{7,6},{8,9},{9,8},{10,11... | collective-permute-start | bytes 6291464 | tf_op jit(solution)/shard_map/ppermute | solution.py:202
  231.3 20.0 %all-to-all-start.4 = ((bf16[8,128,512]{2,1,0:T(8,128)(2,1)}), bf16[8,128,512]{2,1,0:T(8,128)(2,1)S(1)}, u32[]{:S(2)}, u32[]{:S(2)}) async-start(bf16[8,128,512]{2,1,0:T(8,128)(2,1)} %bitcast.18), calls=%async_computation.4 | async-start | bytes 2097152 | tf_op jit(solution)/shard_map/all_to_all | solution.py:33
  234.9 17.2 %copy-start.1 = (bf16[512,2048]{1,0:T(8,128)(2,1)S(1)}, bf16[512,2048]{1,0:T(8,128)(2,1)}, u32[]{:S(2)}) copy-start(bf16[512,2048]{1,0:T(8,128)(2,1)} %get-tuple-element.38) | copy-start | bytes 6291460
  252.1 3.8 %copy-start = (bf16[512,2048]{1,0:T(8,128)(2,1)S(1)}, bf16[512,2048]{1,0:T(8,128)(2,1)}, u32[]{:S(2)}) copy-start(bf16[512,2048]{1,0:T(8,128)(2,1)} %get-tuple-element.37) | copy-start | bytes 6291460

commit v4 on v3

v4 whole, which is shorter than its diff:
```python
import functools

import jax
import jax.numpy as jnp
import numpy as np
from jax import lax
from jax.experimental import pallas as pl
from jax.experimental.pallas import tpu as pltpu
from jax.sharding import Mesh, PartitionSpec as P


COL = ("zl", "x")
BF = jnp.bfloat16
F32 = jnp.float32
SWAP = [(0, 1), (1, 0)]
STEP = 256


def ring(shift):
    return [(i, (i + shift) % 4) for i in range(4)]


def along_y(x, shift):
    return lax.ppermute(x, "y", ring(shift))


def to_pair(x):
    return lax.ppermute(x, "zh", SWAP)


def across_col(x):
    return lax.all_to_all(x, COL, 0, 0, tiled=True)


def gather_col(x):
    many = jnp.broadcast_to(x[None], (8,) + x.shape)
    whole = across_col(many)
    return whole.reshape(8 * x.shape[0], x.shape[1])


def inner_rows(left, right):
    return lax.dot_general(left, right, (((0,), (0,)), ((), ())), preferred_element_type=F32)


def times_transposed(left, right):
    return lax.dot_general(left, right, (((1,), (1,)), ((), ())), preferred_element_type=F32)


def rows_at(block, rows):
    return pl.ds(pl.multiple_of(block * rows, rows), rows)


def back_kernel(factor, first, rows, spots, *refs):
    gates, ups, ds, refs = refs[:8], refs[8:16], refs[16:21], refs[21:]
    w_gate, w_up, tok, out = refs[:4]
    grad_gate, grad_up, grad_down, back, hidden, d_gate, d_up, total, tokens = refs[-9:]
    c = pl.program_id(0)
    flip = spots[4] == 1

    @pl.when(c == 0)
    def _():
        for b in range(8):
            tokens[:, b * rows : (b + 1) * rows] = tok[b]

    for k in range(4):
        for j in range(2):
            here = rows_at(2 * spots[k] + spots[4 + j], rows)
            g = gates[2 * k + j][...].astype(F32)
            u = ups[2 * k + j][...].astype(F32)
            if k == 2:
                low, high = ds[3][...].astype(F32), ds[4][...].astype(F32)
                d = jnp.where(flip, high, low) if j == 0 else jnp.where(flip, low, high)
            else:
                d = ds[(0, 1, None, 2)[k]][rows_at(spots[4 + j], rows), :].astype(F32)
            s = 0.5 * jnp.tanh(0.5 * g) + 0.5
            active = g * s
            hidden[here, :] = (active * u).astype(BF)
            d_gate[here, :] = (d * u * s * (1.0 + g * (1.0 - s))).astype(BF)
            d_up[here, :] = (d * active).astype(BF)
    dg, du = d_gate[...], d_up[...]
    more = times_transposed(dg, w_gate[...]) + times_transposed(du, w_up[...])
    grad_gate[...] = (jnp.dot(tokens[...], dg, preferred_element_type=F32) * factor).astype(BF)
    grad_up[...] = (jnp.dot(tokens[...], du, preferred_element_type=F32) * factor).astype(BF)
    grad_down[...] = (inner_rows(hidden[...], out[...]) * factor).astype(BF)

    @pl.when(c == 0)
    def _():
        total[...] = more if first else refs[4][...] + more

    @pl.when(c > 0)
    def _():
        total[...] += more

    @pl.when(c == pl.num_programs(0) - 1)
    def _():
        back[...] = total[...].astype(back.dtype)


def back_of(spots, half, saved, ds, w_gate, w_up, tok, out, factor, before):
    depth, width = w_gate.shape
    rows = tok.shape[2]
    part = ds[0].shape[1]
    total = 8 * rows
    steps = part // STEP
    gates = [v for k in range(4) for v in saved[k][0]]
    ups = [v for k in range(4) for v in saved[k][1]]

    def piece(v, which):
        return pl.BlockSpec((rows, STEP), lambda c, w: (which * (v.shape[0] // rows - 1), c + half * steps))

    d_specs = [pl.BlockSpec((d.shape[0], STEP), lambda c, w: (0, c)) for d in ds]
    weight = pl.BlockSpec((depth, STEP), lambda c, w: (0, c + half * steps))
    down = pl.BlockSpec((STEP, depth), lambda c, w: (c + half * steps, 0))
    whole = pl.BlockSpec((total, depth), lambda c, w: (0, 0))
    kept = [whole] + [pl.BlockSpec(memory_space=pl.ANY)] * 3 if before else []
    return pl.pallas_call(
        functools.partial(back_kernel, factor, not before, rows),
        out_shape=(
            jax.ShapeDtypeStruct((depth, width), BF),
            jax.ShapeDtypeStruct((depth, width), BF),
            jax.ShapeDtypeStruct((width, depth), BF),
            jax.ShapeDtypeStruct((total, depth), BF if before else F32),
        ),
        grid_spec=pltpu.PrefetchScalarGridSpec(
            num_scalar_prefetch=1,
            grid=(steps,),
            in_specs=[piece(v, 0) for v in gates]
            + [piece(v, 1) for v in ups]
            + d_specs
            + [weight, weight, pl.BlockSpec(tok.shape, lambda c, w: (0, 0, 0)), whole]
            + kept,
            out_specs=(weight, weight, down, whole),
            scratch_shapes=[pltpu.VMEM((total, STEP), BF)] * 3
            + [pltpu.VMEM((total, depth), F32), pltpu.VMEM((depth, total), BF)],
        ),
        input_output_aliases={27: 0, 28: 1, 29: 2} if before else {},
        cost_estimate=pl.CostEstimate(
            flops=10 * total * part * depth, bytes_accessed=total * part * 16, transcendentals=total * part
        ),
    )(spots, *gates, *ups, *ds, w_gate, w_up, tok, out, *before)


def local(tokens, grad_out, gate_pre, up_pre, w_gate, w_up, w_down):
    rows, width = tokens.shape
    factor = float(1.0 / np.sqrt(np.float32(16 * rows)))
    y, zh = lax.axis_index("y"), lax.axis_index("zh")
    p = lax.iota(jnp.int32, 6)
    spots = jnp.where(p < 4, lax.rem(y + p, 4), jnp.where(p == 4, zh, 1 - zh))

    out_all = gather_col(grad_out)

    both = jnp.concatenate([gate_pre, up_pre], axis=0)
    both3, both1 = along_y(both, 1), along_y(both, -1)
    g2 = along_y(both3[:rows], 1)
    u2 = along_y(both1[rows:], -1)
    paired = {k: (v, to_pair(v)) for k, v in ((0, both), (3, both3), (1, both1))}
    saved = {k: (v, v) for k, v in paired.items()}
    saved[2] = ((g2, to_pair(g2)), (u2, to_pair(u2)))

    part_rows = w_down.shape[0] // 2

    def gathered(h):
        part = times_transposed(out_all, w_down[h * part_rows : (h + 1) * part_rows]).astype(BF)
        recv = lax.all_to_all(part.reshape(4, 2 * rows, part_rows), "y", 0, 0, tiled=True)
        total = jnp.sum(recv.astype(F32), axis=0)
        mine = total.astype(BF)
        d = (total + to_pair(mine).astype(F32)).astype(BF)
        d3, d1 = along_y(d, 1), along_y(d, -1)
        return [d, d1, d3, along_y(d3[:rows], 1), along_y(d1[rows:], -1)]

    halves = [gathered(h) for h in (0, 1)]

    turned = tokens.T
    turned = jnp.broadcast_to(turned[None], (8, width, rows))
    tok_all = across_col(turned)

    def both_cores(own):
        other = lax.ppermute(own, "core", SWAP)
        return (own.astype(F32) + other.astype(F32)).astype(BF)

    before = ()
    for h in (0, 1):
        gate, up, down, back = back_of(
            spots, h, saved, halves[h], w_gate, w_up, tok_all, out_all, factor, before
        )
        before = (back, gate, up, down)
    back_recv = across_col(back.reshape(8, rows, width))
    grad_down = both_cores(down)
    grad_gate = both_cores(gate)
    grad_up = both_cores(up)
    grad_tokens = jnp.sum(back_recv.astype(F32), axis=0).astype(BF)
    return grad_tokens, grad_gate, grad_up, grad_down


def solution(mesh):
    fine = Mesh(mesh.devices.reshape(4, 2, 2, 4, 2), ("y", "zh", "zl", "x", "core"))
    row, col = ("y", "zh"), COL
    act = P(col + ("core",), row)
    pre = P(row + ("core",), col)
    up = P(row, col)
    down = P(col, row)

    return jax.shard_map(
        local,
        mesh=fine,
        in_specs=(act, act, pre, pre, up, up, down),
        out_specs=(act, up, up, down),
        check_vma=False,
    )
```

time: 262 us -> 283 us (1.080)
  waiting for transfers between devices: 84.2 us -> 130 us
  Pallas kernels: 47.4 us -> 31 us
  matrix products: 12.4 us -> 6.81 us
    ppermute x12, waiting for transfers between devices: 12.9 us -> 44.3 us  [along_y(): return lax.ppermute(x, 'y', ring(shift))]
    pallas_call x6 -> x2, Pallas kernels: 47.4 us -> 31 us  [back_of(): pl.pallas_call(functools.partial(back_kernel, factor, not before, rows),...]
    ppermute x7, waiting for transfers between devices: 32.8 us -> 48.6 us  [to_pair(): return lax.ppermute(x, 'zh', SWAP)]
    ppermute x1 -> x0, waiting for transfers between devices: 6.95 us -> none  [local(): tok_near = lax.ppermute(tokens, 'zl', SWAP)]
    dot_general x1 -> x0, matrix products: 5.95 us -> none  [inner_rows(): lax.dot_general(left, right, (((0,), (0,)), ((), ())), preferred_element_...]
    slice x4, local copies, waits for them, and re-layouts: 0.07 us -> 5.71 us  [gathered(): return [d, d1, d3, along_y(d3[:rows], 1), along_y(d1[rows:], -1)]]
    all_to_all x1 -> x2, starting transfers between devices: 3.56 us -> 7.93 us  [across_col(): return lax.all_to_all(x, COL, 0, 0, tiled=True)]
    all_to_all x1 -> x0, starting transfers between devices: 4.27 us -> none  [local(): lax.all_to_all(jnp.broadcast_to(tok_pair[None], (4,) + tok_pair.shape), '...]
  transfers between devices with their start and end apart: 27 -> 26, of which waited for: 7 -> 9; matrix products, arithmetic and copies ran while one was open for 16% -> 11% of each run, Pallas kernels for 18% -> 5%
where the time goes in v4:
time: 283 us; the launch traced here: 282 us
  waiting for transfers between devices  130 us (46%)
  starting transfers between devices  56.1 us (20%)
  Pallas kernels  31 us (11%)
  other arithmetic  22.1 us (8%)
  blocking collectives  21.3 us (8%)
  local copies, waits for them, and re-layouts  13.3 us (5%)
  matrix products  6.81 us (2%)
    ppermute x7, waiting for transfers between devices, to_pair(): return lax.ppermute(x, 'zh', SWAP)  48.6 us
    ppermute x12, waiting for transfers between devices, along_y(): return lax.ppermute(x, 'y', ring(shift))  44.3 us
    pallas_call x2, Pallas kernels, back_of(): pl.pallas_call(functools.partial(back_kernel, factor, not before, rows),...  31 us
    all_to_all x1, blocking collectives, across_col(): return lax.all_to_all(x, COL, 0, 0, tiled=True)  21.3 us
    all_to_all x2, waiting for transfers between devices, gathered(): lax.all_to_all(part.reshape(4, 2 * rows, part_rows), 'y', 0, 0, tiled=True)  21.2 us
    ppermute x12, starting transfers between devices, along_y(): return lax.ppermute(x, 'y', ring(shift))  20.6 us
    ppermute x7, starting transfers between devices, to_pair(): return lax.ppermute(x, 'zh', SWAP)  17.9 us
    all_to_all x2, waiting for transfers between devices, across_col(): return lax.all_to_all(x, COL, 0, 0, tiled=True)  16 us
  transfers between devices with their start and end apart: 26, of which 9 were waited for; matrix products, arithmetic and copies ran while one was open for 11% of the time, Pallas kernels for 5%

profile of v4, /device:TPU:0, one launch (start us, length us, event | category | flops | bytes accessed | tf_op | source)
XLA Modules:
  0.0 281.6 jit_solution(4734256700435110651)
XLA Ops:
  0.6 0.0 copy-start.21
  0.6 1.1 broadcast_in_dim.22
  1.8 21.3 %all_to_all.25 = bf16[8,128,512]{2,1,0:T(8,128)(2,1)S(1)} all-to-all(bf16[8,128,512]{2,1,0:T(8,128)(2,1)S(1)} %broadcast_in_dim.22), channel_id=1, replica_groups=mesh['y'=4,'zh'=2,'zl'=2,'x'=4,'core'=2] {'zl','x'}, dimensions={0} | all-to-all | bytes 2097152 | tf_op jit(solution)/shard_map/all_to_all | solution.py:32
  23.1 2.6 convolution_convert_fusion
  25.7 4.6 %all-to-all-start.3 = ((bf16[4,256,1024]{2,1,0:T(8,128)(2,1)}), bf16[4,256,1024]{2,1,0:T(8,128)(2,1)}, u32[]{:S(2)}, u32[]{:S(2)}) async-start(bf16[4,256,1024]{2,1,0:T(8,128)(2,1)} %bitcast.3), calls=%async_computation.3 | async-start | bytes 4194304 | tf_op jit(solution)/shard_map/all_to_all | solution.py:164
  30.4 4.2 %convolution_convert_fusion.1 = bf16[1024,1024]{1,0:T(8,128)(2,1)} fusion(bf16[1024,512]{1,0:T(8,128)(2,1)S(1)} %bitcast.8, bf16[2048,512]{1,0:T(8,128)(2,1)} %param.13), kind=kOutput, calls=%fused_computation.6 | convolution fusion | flops 1074790400 | bytes 4194304 | tf_op jit(solution)/shard_map/dot_general | solution.py:46
  34.6 21.2 %all-to-all-done.3 = bf16[4,256,1024]{2,1,0:T(8,128)(2,1)} async-done(((bf16[4,256,1024]{2,1,0:T(8,128)(2,1)}), bf16[4,256,1024]{2,1,0:T(8,128)(2,1)}, u32[]{:S(2)}, u32[]{:S(2)}) %all-to-all-start.3) | async-done | bytes 2097184 | tf_op jit(solution)/shard_map/all_to_all | solution.py:164
  55.8 4.4 %all-to-all-start.1 = ((bf16[4,256,1024]{2,1,0:T(8,128)(2,1)}), bf16[4,256,1024]{2,1,0:T(8,128)(2,1)}, u32[]{:S(2)}, u32[]{:S(2)}) async-start(bf16[4,256,1024]{2,1,0:T(8,128)(2,1)} %bitcast.11), calls=%async_computation.1 | async-start | bytes 4194304 | tf_op jit(solution)/shard_map/all_to_all | solution.py:164
  60.2 2.0 collective-permute-start.3
  62.2 1.3 collective-permute-start.1
  63.6 3.6 %collective-permute-start = (bf16[256,2048]{1,0:T(8,128)(2,1)S(1)}, bf16[256,2048]{1,0:T(8,128)(2,1)}, u32[]{:S(2)}, u32[]{:S(2)}) collective-permute-start(bf16[256,2048]{1,0:T(8,128)(2,1)S(1)} %constant_dynamic-update-slice_fusion.refs_0_.refs_8_), channel_id=1, source_target_pairs={{0,16},{16,0},{1,17},{17,1},{2,18},{18,2},{3,19},{19,3},{4,20},{20... | collective-permute-start | bytes 3145736 | tf_op jit(solution)/shard_map/ppermute | solution.py:28
  67.1 39.8 %collective-permute-done.3.refs_6_.refs_14_ = bf16[256,2048]{1,0:T(8,128)(2,1)S(1)} collective-permute-done((bf16[256,2048]{1,0:T(8,128)(2,1)S(1)}, bf16[256,2048]{1,0:T(8,128)(2,1)S(1)}, u32[]{:S(2)}, u32[]{:S(2)}) %collective-permute-start.3) | collective-permute-done | bytes 1048608 | tf_op jit(solution)/shard_map/ppermute | solution.py:24
  107.0 0.9 slice.32
  107.8 2.1 convert_reduce_fusion
  110.0 1.0 convert_element_type.66
  110.9 3.6 %collective-permute-start.14 = (bf16[256,1024]{1,0:T(8,128)(2,1)}, bf16[256,1024]{1,0:T(8,128)(2,1)}, u32[]{:S(2)}, u32[]{:S(2)}) collective-permute-start(bf16[256,1024]{1,0:T(8,128)(2,1)} %convert_element_type.66), channel_id=1, source_target_pairs={{0,16},{16,0},{1,17},{17,1},{2,18},{18,2},{3,19},{19,3},{4,20},{20... | collective-permute-start | bytes 1572872 | tf_op jit(solution)/shard_map/ppermute | solution.py:28
  114.5 1.0 slice.33
  115.5 3.2 %collective-permute-start.7 = (bf16[128,2048]{1,0:T(8,128)(2,1)}, bf16[128,2048]{1,0:T(8,128)(2,1)}, u32[]{:S(2)}, u32[]{:S(2)}) collective-permute-start(bf16[128,2048]{1,0:T(8,128)(2,1)} %slice.33), channel_id=1, source_target_pairs={{0,96},{32,0},{64,32},{96,64},{1,97},{33,1},{65,33},{97,65},{2,98}... | collective-permute-start | bytes 1572872 | tf_op jit(solution)/shard_map/ppermute | solution.py:24
  118.7 2.2 convert_reduce_fusion.1
  120.9 0.0 copy-start.5
  120.9 1.0 copy-done.5
  121.9 0.9 convert_element_type.61
  122.8 0.2 collective-permute-start.9
  122.9 3.4 %collective-permute-start.5 = (bf16[128,2048]{1,0:T(8,128)(2,1)}, bf16[128,2048]{1,0:T(8,128)(2,1)}, u32[]{:S(2)}, u32[]{:S(2)}) collective-permute-start(bf16[128,2048]{1,0:T(8,128)(2,1)} %collective-permute-done.4.refs_4_), channel_id=1, source_target_pairs={{0,16},{16,0},{1,17},{17,1},{2,18},{18,2},{3,19},{19,3},{4,20},{20... | collective-permute-start | bytes 1572872 | tf_op jit(solution)/shard_map/ppermute | solution.py:28
  126.3 0.2 collective-permute-done.14
  126.5 2.0 add_convert_fusion.3.refs_16_
  128.5 1.4 collective-permute-start.16
  129.9 0.1 copy.14
  130.1 1.1 broadcast_in_dim.23
  131.2 4.2 %all-to-all-start.2 = ((bf16[8,512,128]{2,1,0:T(8,128)(2,1)}), bf16[8,512,128]{2,1,0:T(8,128)(2,1)}, u32[]{:S(2)}, u32[]{:S(2)}) async-start(bf16[8,512,128]{2,1,0:T(8,128)(2,1)} %broadcast_in_dim.23), calls=%async_computation.2 | async-start | bytes 2097152 | tf_op jit(solution)/shard_map/all_to_all | solution.py:32
  135.4 4.1 %collective-permute-start.6 = (bf16[256,2048]{1,0:T(8,128)(2,1)S(1)}, bf16[256,2048]{1,0:T(8,128)(2,1)S(1)}, u32[]{:S(2)}, u32[]{:S(2)}) collective-permute-start(bf16[256,2048]{1,0:T(8,128)(2,1)S(1)} %collective-permute-done.3.refs_6_.refs_14_), channel_id=1, source_target_pairs={{0,16},{16,0},{1,17},{17,1},{2,18},{18,2},{3,19},{19,3},{4,20},{20... | collective-permute-start | bytes 3145736 | tf_op jit(solution)/shard_map/ppermute | solution.py:28
  139.5 0.1 collective-permute-start.2
  139.6 6.5 %collective-permute-done.9 = bf16[256,1024]{1,0:T(8,128)(2,1)} collective-permute-done((bf16[256,1024]{1,0:T(8,128)(2,1)}, bf16[256,1024]{1,0:T(8,128)(2,1)}, u32[]{:S(2)}, u32[]{:S(2)}) %collective-permute-start.9) | collective-permute-done | bytes 524320 | tf_op jit(solution)/shard_map/ppermute | solution.py:28
  146.2 3.9 %collective-permute-start.15 = (bf16[256,1024]{1,0:T(8,128)(2,1)}, bf16[256,1024]{1,0:T(8,128)(2,1)S(1)}, u32[]{:S(2)}, u32[]{:S(2)}) collective-permute-start(bf16[256,1024]{1,0:T(8,128)(2,1)} %add_convert_fusion.3.refs_16_), channel_id=1, source_target_pairs={{0,96},{32,0},{64,32},{96,64},{1,97},{33,1},{65,33},{97,65},{2,98}... | collective-permute-start | bytes 1572872 | tf_op jit(solution)/shard_map/ppermute | solution.py:24
  150.0 1.5 add_convert_fusion.4.refs_16_
  151.5 7.5 %collective-permute-done.5.refs_5_ = bf16[128,2048]{1,0:T(8,128)(2,1)} collective-permute-done((bf16[128,2048]{1,0:T(8,128)(2,1)}, bf16[128,2048]{1,0:T(8,128)(2,1)}, u32[]{:S(2)}, u32[]{:S(2)}) %collective-permute-start.5) | collective-permute-done | bytes 524320 | tf_op jit(solution)/shard_map/ppermute | solution.py:28
  159.0 3.2 %collective-permute-start.10 = (bf16[256,1024]{1,0:T(8,128)(2,1)S(1)}, bf16[256,1024]{1,0:T(8,128)(2,1)S(1)}, u32[]{:S(2)}, u32[]{:S(2)}) collective-permute-start(bf16[256,1024]{1,0:T(8,128)(2,1)S(1)} %add_convert_fusion.4.refs_16_), channel_id=1, source_target_pairs={{0,96},{32,0},{64,32},{96,64},{1,97},{33,1},{65,33},{97,65},{2,98}... | collective-permute-start | bytes 1572872 | tf_op jit(solution)/shard_map/ppermute | solution.py:24
  162.3 3.1 %collective-permute-start.8 = (bf16[128,2048]{1,0:T(8,128)(2,1)}, bf16[128,2048]{1,0:T(8,128)(2,1)}, u32[]{:S(2)}, u32[]{:S(2)}) collective-permute-start(bf16[128,2048]{1,0:T(8,128)(2,1)} %collective-permute-done.7.refs_12_), channel_id=1, source_target_pairs={{0,16},{16,0},{1,17},{17,1},{2,18},{18,2},{3,19},{19,3},{4,20},{20... | collective-permute-start | bytes 1572872 | tf_op jit(solution)/shard_map/ppermute | solution.py:28
  165.3 1.7 slice.36
  167.0 0.7 slice.37
  167.7 4.5 %collective-permute-done.11.refs_18_ = bf16[256,1024]{1,0:T(8,128)(2,1)S(1)} collective-permute-done((bf16[256,1024]{1,0:T(8,128)(2,1)S(1)}, bf16[256,1024]{1,0:T(8,128)(2,1)S(1)}, u32[]{:S(2)}, u32[]{:S(2)}) %collective-permute-start.11) | collective-permute-done | bytes 524320 | tf_op jit(solution)/shard_map/ppermute | solution.py:24
  172.2 0.8 copy-done.12
  173.0 2.5 collective-permute-start.18
  175.5 0.5 compare_select_fusion.3.spots
  176.1 1.7 slice.34
  177.7 1.7 slice.35
  179.4 4.8 %collective-permute-done.6.refs_7_.refs_15_ = bf16[256,2048]{1,0:T(8,128)(2,1)S(1)} collective-permute-done((bf16[256,2048]{1,0:T(8,128)(2,1)S(1)}, bf16[256,2048]{1,0:T(8,128)(2,1)S(1)}, u32[]{:S(2)}, u32[]{:S(2)}) %collective-permute-start.6) | collective-permute-done | bytes 1048608 | tf_op jit(solution)/shard_map/ppermute | solution.py:28
  184.2 29.5 %collective-permute-done.8.refs_13_ = bf16[128,2048]{1,0:T(8,128)(2,1)} collective-permute-done((bf16[128,2048]{1,0:T(8,128)(2,1)}, bf16[128,2048]{1,0:T(8,128)(2,1)}, u32[]{:S(2)}, u32[]{:S(2)}) %collective-permute-start.8) | collective-permute-done | bytes 524320 | tf_op jit(solution)/shard_map/ppermute | solution.py:28
  213.7 3.0 %collective-permute-start.13 = (bf16[128,1024]{1,0:T(8,128)(2,1)}, bf16[128,1024]{1,0:T(8,128)(2,1)S(1)}, u32[]{:S(2)}, u32[]{:S(2)}) collective-permute-start(bf16[128,1024]{1,0:T(8,128)(2,1)} %slice.35), channel_id=1, source_target_pairs={{0,96},{32,0},{64,32},{96,64},{1,97},{33,1},{65,33},{97,65},{2,98}... | collective-permute-start | bytes 786440 | tf_op jit(solution)/shard_map/ppermute | solution.py:24
  216.7 0.7 copy-done.17
  217.4 15.2 %shard_map.102 = (bf16[512,2048]{1,0:T(8,128)(2,1)}, bf16[512,2048]{1,0:T(8,128)(2,1)}, bf16[2048,512]{1,0:T(8,128)(2,1)}, f32[1024,512]{1,0:T(8,128)}) custom-call(s32[6]{0:T(128)} %compare_select_fusion.3.spots, bf16[256,2048]{1,0:T(8,128)(2,1)} %copy-done.2, bf16[256,2048]{1,0:T(8,128)(2,1)} %collective-permute-done.refs_1_.refs_9_, ...), custom_call_target="tpu_custom_call" | custom-call | flops 5368709120 | bytes 16777216 | tf_op jit(solution)/shard_map/pallas_call | solution.py:116
  232.7 0.7 copy-done.18
  233.4 0.1 copy-done.19
  233.5 15.7 %shard_map.103 = (bf16[512,2048]{1,0:T(8,128)(2,1)}, bf16[512,2048]{1,0:T(8,128)(2,1)}, bf16[2048,512]{1,0:T(8,128)(2,1)}, bf16[1024,512]{1,0:T(8,128)(2,1)}) custom-call(s32[6]{0:T(128)} %compare_select_fusion.3.spots, bf16[256,2048]{1,0:T(8,128)(2,1)} %copy-done.2, ...), custom_call_target="tpu_custom_call", output_to_operand_aliasing={{0}: (27, {}), {1}: (28, {}), {2}: (29, {})} | custom-call | flops 5368709120 | bytes 16777216 | tf_op jit(solution)/shard_map/pallas_call | solution.py:116
  249.2 0.0 copy-start.8
  249.2 0.1 collective-permute-start.19
  249.3 0.5 collective-permute-start.20
  249.8 3.7 %all-to-all-start.4 = ((bf16[8,128,512]{2,1,0:T(8,128)(2,1)}), bf16[8,128,512]{2,1,0:T(8,128)(2,1)S(1)}, u32[]{:S(2)}, u32[]{:S(2)}) async-start(bf16[8,128,512]{2,1,0:T(8,128)(2,1)} %bitcast.12), calls=%async_computation.4 | async-start | bytes 2097152 | tf_op jit(solution)/shard_map/all_to_all | solution.py:32
  253.5 0.1 collective-permute-start.21
  253.6 16.0 %all-to-all-done.4 = bf16[8,128,512]{2,1,0:T(8,128)(2,1)S(1)} async-done(((bf16[8,128,512]{2,1,0:T(8,128)(2,1)}), bf16[8,128,512]{2,1,0:T(8,128)(2,1)S(1)}, u32[]{:S(2)}, u32[]{:S(2)}) %all-to-all-start.4) | async-done | bytes 1048608 | tf_op jit(solution)/shard_map/all_to_all | solution.py:32
  269.6 0.8 reduce_sum.32
  270.4 3.8 %add_convert_fusion.2 = bf16[512,2048]{1,0:T(8,128)(2,1)} fusion(bf16[512,2048]{1,0:T(8,128)(2,1)} %collective-permute-done.19, bf16[512,2048]{1,0:T(8,128)(2,1)S(1)} %copy-done.8), kind=kLoop, calls=%fused_computation.2 | loop fusion | flops 4194304 | bytes 6291456 | tf_op jit(solution)/shard_map/convert_element_type | solution.py:179
  274.2 3.8 %add_convert_fusion.1 = bf16[512,2048]{1,0:T(8,128)(2,1)} fusion(bf16[512,2048]{1,0:T(8,128)(2,1)} %collective-permute-done.20, bf16[512,2048]{1,0:T(8,128)(2,1)S(1)} %copy-done.9), kind=kLoop, calls=%fused_computation.1 | loop fusion | flops 4194304 | bytes 6291456 | tf_op jit(solution)/shard_map/convert_element_type | solution.py:179
  278.1 3.5 %add_convert_fusion = bf16[2048,512]{1,0:T(8,128)(2,1)} fusion(bf16[2048,512]{1,0:T(8,128)(2,1)} %collective-permute-done.21, bf16[2048,512]{1,0:T(8,128)(2,1)S(1)} %copy-done.10), kind=kLoop, calls=%fused_computation | loop fusion | flops 4194304 | bytes 6291456 | tf_op jit(solution)/shard_map/convert_element_type | solution.py:179
  (59 shorter events, 0.2 us)
Async XLA Ops:
  0.6 22.4 %copy-start.21 = (bf16[2048,512]{1,0:T(8,128)(2,1)S(1)}, bf16[2048,512]{1,0:T(8,128)(2,1)}, u32[]{:S(2)}) copy-start(bf16[2048,512]{1,0:T(8,128)(2,1)} %param.13) | copy-start | bytes 6291460
  23.0 7.3 %copy-start.4 = (bf16[8,128,512]{2,1,0:T(8,128)(2,1)}, bf16[8,128,512]{2,1,0:T(8,128)(2,1)S(1)}, u32[]{:S(2)}) copy-start(bf16[8,128,512]{2,1,0:T(8,128)(2,1)S(1)} %all_to_all.25) | copy-start | bytes 3145732
  25.7 4.6 %copy-start.15 = (bf16[128,2048]{1,0:T(8,128)(2,1)S(1)}, bf16[128,2048]{1,0:T(8,128)(2,1)}, u32[]{:S(2)}) copy-start(bf16[128,2048]{1,0:T(8,128)(2,1)} %param.9) | copy-start | bytes 1572868
  25.7 4.7 %copy-start.16 = (bf16[128,2048]{1,0:T(8,128)(2,1)S(1)}, bf16[128,2048]{1,0:T(8,128)(2,1)}, u32[]{:S(2)}) copy-start(bf16[128,2048]{1,0:T(8,128)(2,1)} %param.10) | copy-start | bytes 1572868
  25.7 30.1 %all-to-all-start.3 = ((bf16[4,256,1024]{2,1,0:T(8,128)(2,1)}), bf16[4,256,1024]{2,1,0:T(8,128)(2,1)}, u32[]{:S(2)}, u32[]{:S(2)}) async-start(bf16[4,256,1024]{2,1,0:T(8,128)(2,1)} %bitcast.3), calls=%async_computation.3 | async-start | bytes 4194304 | tf_op jit(solution)/shard_map/all_to_all | solution.py:164
  30.4 33.2 %copy-start.2 = (bf16[256,2048]{1,0:T(8,128)(2,1)}, bf16[256,2048]{1,0:T(8,128)(2,1)S(1)}, u32[]{:S(2)}) copy-start(bf16[256,2048]{1,0:T(8,128)(2,1)S(1)} %constant_dynamic-update-slice_fusion.refs_0_.refs_8_) | copy-start | bytes 3145732
  55.8 62.9 %all-to-all-start.1 = ((bf16[4,256,1024]{2,1,0:T(8,128)(2,1)}), bf16[4,256,1024]{2,1,0:T(8,128)(2,1)}, u32[]{:S(2)}, u32[]{:S(2)}) async-start(bf16[4,256,1024]{2,1,0:T(8,128)(2,1)} %bitcast.11), calls=%async_computation.1 | async-start | bytes 4194304 | tf_op jit(solution)/shard_map/all_to_all | solution.py:164
  60.2 46.7 %collective-permute-start.3 = (bf16[256,2048]{1,0:T(8,128)(2,1)S(1)}, bf16[256,2048]{1,0:T(8,128)(2,1)S(1)}, u32[]{:S(2)}, u32[]{:S(2)}) collective-permute-start(bf16[256,2048]{1,0:T(8,128)(2,1)S(1)} %constant_dynamic-update-slice_fusion.refs_0_.refs_8_), channel_id=1, source_target_pairs={{0,32},{32,64},{64,96},{96,0},{1,33},{33,65},{65,97},{97,1},{2,34}... | collective-permute-start | bytes 3145736 | tf_op jit(solution)/shard_map/ppermute | solution.py:24
  62.2 52.3 %collective-permute-start.1 = (bf16[256,2048]{1,0:T(8,128)(2,1)S(1)}, bf16[256,2048]{1,0:T(8,128)(2,1)S(1)}, u32[]{:S(2)}, u32[]{:S(2)}) collective-permute-start(bf16[256,2048]{1,0:T(8,128)(2,1)S(1)} %constant_dynamic-update-slice_fusion.refs_0_.refs_8_), channel_id=1, source_target_pairs={{0,96},{32,0},{64,32},{96,64},{1,97},{33,1},{65,33},{97,65},{2,98}... | collective-permute-start | bytes 3145736 | tf_op jit(solution)/shard_map/ppermute | solution.py:24
  63.6 71.9 %collective-permute-start = (bf16[256,2048]{1,0:T(8,128)(2,1)S(1)}, bf16[256,2048]{1,0:T(8,128)(2,1)}, u32[]{:S(2)}, u32[]{:S(2)}) collective-permute-start(bf16[256,2048]{1,0:T(8,128)(2,1)S(1)} %constant_dynamic-update-slice_fusion.refs_0_.refs_8_), channel_id=1, source_target_pairs={{0,16},{16,0},{1,17},{17,1},{2,18},{18,2},{3,19},{19,3},{4,20},{20... | collective-permute-start | bytes 3145736 | tf_op jit(solution)/shard_map/ppermute | solution.py:28
  107.0 28.5 %copy-start = (bf16[256,2048]{1,0:T(8,128)(2,1)}, bf16[256,2048]{1,0:T(8,128)(2,1)S(1)}, u32[]{:S(2)}) copy-start(bf16[256,2048]{1,0:T(8,128)(2,1)S(1)} %collective-permute-done.3.refs_6_.refs_14_) | copy-start | bytes 3145732
  107.8 15.1 %collective-permute-start.4 = (bf16[128,2048]{1,0:T(8,128)(2,1)}, bf16[128,2048]{1,0:T(8,128)(2,1)}, u32[]{:S(2)}, u32[]{:S(2)}) collective-permute-start(bf16[128,2048]{1,0:T(8,128)(2,1)} %slice.32), channel_id=1, source_target_pairs={{0,32},{32,64},{64,96},{96,0},{1,33},{33,65},{65,97},{97,1},{2,34}... | collective-permute-start | bytes 1572872 | tf_op jit(solution)/shard_map/ppermute | solution.py:24
  109.9 4.6 %copy-start.6 = (f32[256,1024]{1,0:T(8,128)}, f32[256,1024]{1,0:T(8,128)S(1)}, u32[]{:S(2)}) copy-start(f32[256,1024]{1,0:T(8,128)S(1)} %convert_reduce_fusion) | copy-start | bytes 3145732
  110.9 15.6 %collective-permute-start.14 = (bf16[256,1024]{1,0:T(8,128)(2,1)}, bf16[256,1024]{1,0:T(8,128)(2,1)}, u32[]{:S(2)}, u32[]{:S(2)}) collective-permute-start(bf16[256,1024]{1,0:T(8,128)(2,1)} %convert_element_type.66), channel_id=1, source_target_pairs={{0,16},{16,0},{1,17},{17,1},{2,18},{18,2},{3,19},{19,3},{4,20},{20... | collective-permute-start | bytes 1572872 | tf_op jit(solution)/shard_map/ppermute | solution.py:28
  114.5 25.0 %copy-start.1 = (bf16[256,2048]{1,0:T(8,128)(2,1)}, bf16[256,2048]{1,0:T(8,128)(2,1)S(1)}, u32[]{:S(2)}) copy-start(bf16[256,2048]{1,0:T(8,128)(2,1)S(1)} %collective-permute-done.1.refs_2_.refs_10_) | copy-start | bytes 3145732
  115.5 24.0 %collective-permute-start.7 = (bf16[128,2048]{1,0:T(8,128)(2,1)}, bf16[128,2048]{1,0:T(8,128)(2,1)}, u32[]{:S(2)}, u32[]{:S(2)}) collective-permute-start(bf16[128,2048]{1,0:T(8,128)(2,1)} %slice.33), channel_id=1, source_target_pairs={{0,96},{32,0},{64,32},{96,64},{1,97},{33,1},{65,33},{97,65},{2,98}... | collective-permute-start | bytes 1572872 | tf_op jit(solution)/shard_map/ppermute | solution.py:24
  118.7 7.8 %copy-start.7 = (f32[256,1024]{1,0:T(8,128)S(1)}, f32[256,1024]{1,0:T(8,128)}, u32[]{:S(2)}) copy-start(f32[256,1024]{1,0:T(8,128)} %copy-done.6) | copy-start | bytes 3145732
  120.9 1.0 copy-start.5
  121.9 8.1 %copy-start.20 = (bf16[128,512]{1,0:T(8,128)(2,1)S(1)}, bf16[128,512]{1,0:T(8,128)(2,1)}, u32[]{:S(2)}) copy-start(bf16[128,512]{1,0:T(8,128)(2,1)} %param.7) | copy-start | bytes 393220
  122.8 23.4 %collective-permute-start.9 = (bf16[256,1024]{1,0:T(8,128)(2,1)}, bf16[256,1024]{1,0:T(8,128)(2,1)}, u32[]{:S(2)}, u32[]{:S(2)}) collective-permute-start(bf16[256,1024]{1,0:T(8,128)(2,1)} %convert_element_type.61), channel_id=1, source_target_pairs={{0,16},{16,0},{1,17},{17,1},{2,18},{18,2},{3,19},{19,3},{4,20},{20... | collective-permute-start | bytes 1572872 | tf_op jit(solution)/shard_map/ppermute | solution.py:28
  122.9 36.1 %collective-permute-start.5 = (bf16[128,2048]{1,0:T(8,128)(2,1)}, bf16[128,2048]{1,0:T(8,128)(2,1)}, u32[]{:S(2)}, u32[]{:S(2)}) collective-permute-start(bf16[128,2048]{1,0:T(8,128)(2,1)} %collective-permute-done.4.refs_4_), channel_id=1, source_target_pairs={{0,16},{16,0},{1,17},{17,1},{2,18},{18,2},{3,19},{19,3},{4,20},{20... | collective-permute-start | bytes 1572872 | tf_op jit(solution)/shard_map/ppermute | solution.py:28
  128.5 30.5 %collective-permute-start.16 = (bf16[256,1024]{1,0:T(8,128)(2,1)}, bf16[256,1024]{1,0:T(8,128)(2,1)}, u32[]{:S(2)}, u32[]{:S(2)}) collective-permute-start(bf16[256,1024]{1,0:T(8,128)(2,1)} %add_convert_fusion.3.refs_16_), channel_id=1, source_target_pairs={{0,32},{32,64},{64,96},{96,0},{1,33},{33,65},{65,97},{97,1},{2,34}... | collective-permute-start | bytes 1572872 | tf_op jit(solution)/shard_map/ppermute | solution.py:24
  131.2 85.5 %all-to-all-start.2 = ((bf16[8,512,128]{2,1,0:T(8,128)(2,1)}), bf16[8,512,128]{2,1,0:T(8,128)(2,1)}, u32[]{:S(2)}, u32[]{:S(2)}) async-start(bf16[8,512,128]{2,1,0:T(8,128)(2,1)} %broadcast_in_dim.23), calls=%async_computation.2 | async-start | bytes 2097152 | tf_op jit(solution)/shard_map/all_to_all | solution.py:32
  135.4 48.8 %collective-permute-start.6 = (bf16[256,2048]{1,0:T(8,128)(2,1)S(1)}, bf16[256,2048]{1,0:T(8,128)(2,1)S(1)}, u32[]{:S(2)}, u32[]{:S(2)}) collective-permute-start(bf16[256,2048]{1,0:T(8,128)(2,1)S(1)} %collective-permute-done.3.refs_6_.refs_14_), channel_id=1, source_target_pairs={{0,16},{16,0},{1,17},{17,1},{2,18},{18,2},{3,19},{19,3},{4,20},{20... | collective-permute-start | bytes 3145736 | tf_op jit(solution)/shard_map/ppermute | solution.py:28
  139.5 77.2 %collective-permute-start.2 = (bf16[256,2048]{1,0:T(8,128)(2,1)S(1)}, bf16[256,2048]{1,0:T(8,128)(2,1)}, u32[]{:S(2)}, u32[]{:S(2)}) collective-permute-start(bf16[256,2048]{1,0:T(8,128)(2,1)S(1)} %collective-permute-done.1.refs_2_.refs_10_), channel_id=1, source_target_pairs={{0,16},{16,0},{1,17},{17,1},{2,18},{18,2},{3,19},{19,3},{4,20},{20... | collective-permute-start | bytes 3145736 | tf_op jit(solution)/shard_map/ppermute | solution.py:28
  146.2 16.1 %collective-permute-start.15 = (bf16[256,1024]{1,0:T(8,128)(2,1)}, bf16[256,1024]{1,0:T(8,128)(2,1)S(1)}, u32[]{:S(2)}, u32[]{:S(2)}) collective-permute-start(bf16[256,1024]{1,0:T(8,128)(2,1)} %add_convert_fusion.3.refs_16_), channel_id=1, source_target_pairs={{0,96},{32,0},{64,32},{96,64},{1,97},{33,1},{65,33},{97,65},{2,98}... | collective-permute-start | bytes 1572872 | tf_op jit(solution)/shard_map/ppermute | solution.py:24
  151.5 7.5 %copy-start.11 = (bf16[256,1024]{1,0:T(8,128)(2,1)}, bf16[256,1024]{1,0:T(8,128)(2,1)S(1)}, u32[]{:S(2)}) copy-start(bf16[256,1024]{1,0:T(8,128)(2,1)S(1)} %add_convert_fusion.4.refs_16_) | copy-start | bytes 1572868
  159.0 13.2 %collective-permute-start.11 = (bf16[256,1024]{1,0:T(8,128)(2,1)S(1)}, bf16[256,1024]{1,0:T(8,128)(2,1)S(1)}, u32[]{:S(2)}, u32[]{:S(2)}) collective-permute-start(bf16[256,1024]{1,0:T(8,128)(2,1)S(1)} %add_convert_fusion.4.refs_16_), channel_id=1, source_target_pairs={{0,32},{32,64},{64,96},{96,0},{1,33},{33,65},{65,97},{97,1},{2,34}... | collective-permute-start | bytes 1572872 | tf_op jit(solution)/shard_map/ppermute | solution.py:24
  159.0 13.2 %collective-permute-start.10 = (bf16[256,1024]{1,0:T(8,128)(2,1)S(1)}, bf16[256,1024]{1,0:T(8,128)(2,1)S(1)}, u32[]{:S(2)}, u32[]{:S(2)}) collective-permute-start(bf16[256,1024]{1,0:T(8,128)(2,1)S(1)} %add_convert_fusion.4.refs_16_), channel_id=1, source_target_pairs={{0,96},{32,0},{64,32},{96,64},{1,97},{33,1},{65,33},{97,65},{2,98}... | collective-permute-start | bytes 1572872 | tf_op jit(solution)/shard_map/ppermute | solution.py:24
  162.3 13.3 %copy-start.14 = (bf16[256,1024]{1,0:T(8,128)(2,1)}, bf16[256,1024]{1,0:T(8,128)(2,1)S(1)}, u32[]{:S(2)}) copy-start(bf16[256,1024]{1,0:T(8,128)(2,1)S(1)} %collective-permute-done.15.refs_17_) | copy-start | bytes 1572868
  162.3 51.5 %collective-permute-start.8 = (bf16[128,2048]{1,0:T(8,128)(2,1)}, bf16[128,2048]{1,0:T(8,128)(2,1)}, u32[]{:S(2)}, u32[]{:S(2)}) collective-permute-start(bf16[128,2048]{1,0:T(8,128)(2,1)} %collective-permute-done.7.refs_12_), channel_id=1, source_target_pairs={{0,16},{16,0},{1,17},{17,1},{2,18},{18,2},{3,19},{19,3},{4,20},{20... | collective-permute-start | bytes 1572872 | tf_op jit(solution)/shard_map/ppermute | solution.py:28
  172.2 0.8 copy-start.12
  172.2 44.5 %collective-permute-start.17 = (bf16[128,1024]{1,0:T(8,128)(2,1)}, bf16[128,1024]{1,0:T(8,128)(2,1)S(1)}, u32[]{:S(2)}, u32[]{:S(2)}) collective-permute-start(bf16[128,1024]{1,0:T(8,128)(2,1)} %slice.36), channel_id=1, source_target_pairs={{0,32},{32,64},{64,96},{96,0},{1,33},{33,65},{65,97},{97,1},{2,34}... | collective-permute-start | bytes 786440 | tf_op jit(solution)/shard_map/ppermute | solution.py:24
  173.0 2.5 copy-start.13
  173.0 43.7 %collective-permute-start.18 = (bf16[128,1024]{1,0:T(8,128)(2,1)}, bf16[128,1024]{1,0:T(8,128)(2,1)}, u32[]{:S(2)}, u32[]{:S(2)}) collective-permute-start(bf16[128,1024]{1,0:T(8,128)(2,1)} %slice.37), channel_id=1, source_target_pairs={{0,96},{32,0},{64,32},{96,64},{1,97},{33,1},{65,33},{97,65},{2,98}... | collective-permute-start | bytes 786440 | tf_op jit(solution)/shard_map/ppermute | solution.py:24
  184.2 32.5 %copy-start.3 = (bf16[256,2048]{1,0:T(8,128)(2,1)}, bf16[256,2048]{1,0:T(8,128)(2,1)S(1)}, u32[]{:S(2)}) copy-start(bf16[256,2048]{1,0:T(8,128)(2,1)S(1)} %collective-permute-done.6.refs_7_.refs_15_) | copy-start | bytes 3145732
  184.2 48.4 %collective-permute-start.12 = (bf16[128,1024]{1,0:T(8,128)(2,1)}, bf16[128,1024]{1,0:T(8,128)(2,1)S(1)}, u32[]{:S(2)}, u32[]{:S(2)}) collective-permute-start(bf16[128,1024]{1,0:T(8,128)(2,1)} %slice.34), channel_id=1, source_target_pairs={{0,32},{32,64},{64,96},{96,0},{1,33},{33,65},{65,97},{97,1},{2,34}... | collective-permute-start | bytes 786440 | tf_op jit(solution)/shard_map/ppermute | solution.py:24
  213.7 18.9 %collective-permute-start.13 = (bf16[128,1024]{1,0:T(8,128)(2,1)}, bf16[128,1024]{1,0:T(8,128)(2,1)S(1)}, u32[]{:S(2)}, u32[]{:S(2)}) collective-permute-start(bf16[128,1024]{1,0:T(8,128)(2,1)} %slice.35), channel_id=1, source_target_pairs={{0,96},{32,0},{64,32},{96,64},{1,97},{33,1},{65,33},{97,65},{2,98}... | collective-permute-start | bytes 786440 | tf_op jit(solution)/shard_map/ppermute | solution.py:24
  216.7 0.7 copy-start.17
  232.7 0.7 copy-start.18
  232.7 0.8 copy-start.19
  249.2 21.2 %copy-start.8 = (bf16[512,2048]{1,0:T(8,128)(2,1)S(1)}, bf16[512,2048]{1,0:T(8,128)(2,1)}, u32[]{:S(2)}) copy-start(bf16[512,2048]{1,0:T(8,128)(2,1)} %get-tuple-element.17) | copy-start | bytes 6291460
  249.2 21.2 %collective-permute-start.19 = (bf16[512,2048]{1,0:T(8,128)(2,1)}, bf16[512,2048]{1,0:T(8,128)(2,1)}, u32[]{:S(2)}, u32[]{:S(2)}) collective-permute-start(bf16[512,2048]{1,0:T(8,128)(2,1)} %get-tuple-element.17), channel_id=1, source_target_pairs={{0,1},{1,0},{2,3},{3,2},{4,5},{5,4},{6,7},{7,6},{8,9},{9,8},{10,11... | collective-permute-start | bytes 6291464 | tf_op jit(solution)/shard_map/ppermute | solution.py:178
  249.3 24.9 %collective-permute-start.20 = (bf16[512,2048]{1,0:T(8,128)(2,1)}, bf16[512,2048]{1,0:T(8,128)(2,1)}, u32[]{:S(2)}, u32[]{:S(2)}) collective-permute-start(bf16[512,2048]{1,0:T(8,128)(2,1)} %get-tuple-element.18), channel_id=1, source_target_pairs={{0,1},{1,0},{2,3},{3,2},{4,5},{5,4},{6,7},{7,6},{8,9},{9,8},{10,11... | collective-permute-start | bytes 6291464 | tf_op jit(solution)/shard_map/ppermute | solution.py:178
  249.8 19.7 %all-to-all-start.4 = ((bf16[8,128,512]{2,1,0:T(8,128)(2,1)}), bf16[8,128,512]{2,1,0:T(8,128)(2,1)S(1)}, u32[]{:S(2)}, u32[]{:S(2)}) async-start(bf16[8,128,512]{2,1,0:T(8,128)(2,1)} %bitcast.12), calls=%async_computation.4 | async-start | bytes 2097152 | tf_op jit(solution)/shard_map/all_to_all | solution.py:32
  253.5 24.5 %collective-permute-start.21 = (bf16[2048,512]{1,0:T(8,128)(2,1)}, bf16[2048,512]{1,0:T(8,128)(2,1)}, u32[]{:S(2)}, u32[]{:S(2)}) collective-permute-start(bf16[2048,512]{1,0:T(8,128)(2,1)} %get-tuple-element.19), channel_id=1, source_target_pairs={{0,1},{1,0},{2,3},{3,2},{4,5},{5,4},{6,7},{7,6},{8,9},{9,8},{10,11... | collective-permute-start | bytes 6291464 | tf_op jit(solution)/shard_map/ppermute | solution.py:178
  270.4 3.8 %copy-start.9 = (bf16[512,2048]{1,0:T(8,128)(2,1)S(1)}, bf16[512,2048]{1,0:T(8,128)(2,1)}, u32[]{:S(2)}) copy-start(bf16[512,2048]{1,0:T(8,128)(2,1)} %get-tuple-element.18) | copy-start | bytes 6291460
  274.2 3.8 %copy-start.10 = (bf16[2048,512]{1,0:T(8,128)(2,1)S(1)}, bf16[2048,512]{1,0:T(8,128)(2,1)}, u32[]{:S(2)}) copy-start(bf16[2048,512]{1,0:T(8,128)(2,1)} %get-tuple-element.19) | copy-start | bytes 6291460

commit v5 on v3

--- a/solution.py
+++ b/solution.py
@@ -98,9 +98,19 @@
 
 def back_kernel(factor, first, spots, *refs):
     ds, refs = refs[:5], refs[5:]
-    slope, active, w_gate, w_up, tok = refs[:5]
-    grad_gate, grad_up, back, d_gate, d_up, total = refs[-6:]
+    slope, active, w_gate, w_up = refs[:4]
+    toks, refs = refs[4:8], refs[8:]
+    grad_gate, grad_up, back, d_gate, d_up, total, tokens = refs[-7:]
     c = pl.program_id(0)
+
+    @pl.when(c == 0)
+    def _():
+        depth, wide = tokens.shape[0], toks[0].shape[1]
+        for m in range(4):
+            for j in range(2):
+                here = pl.ds(pl.multiple_of(spots[6 + 2 * m + j] * wide, wide), wide)
+                tokens[:, here] = toks[m][j * depth : (j + 1) * depth, :]
+
     for ref, k, skip in zip(ds, (0, 1, 3, 2, 2), (0, 0, 0, 0, 1)):
         d = ref[...].astype(F32)
         rows = d.shape[0]
@@ -109,12 +119,12 @@
         d_up[here, :] = (d * active[here, :]).astype(BF)
     dg, du = d_gate[...], d_up[...]
     more = times_transposed(dg, w_gate[...]) + times_transposed(du, w_up[...])
-    grad_gate[...] = (jnp.dot(tok[...], dg, preferred_element_type=F32) * factor).astype(BF)
-    grad_up[...] = (jnp.dot(tok[...], du, preferred_element_type=F32) * factor).astype(BF)
+    grad_gate[...] = (jnp.dot(tokens[...], dg, preferred_element_type=F32) * factor).astype(BF)
+    grad_up[...] = (jnp.dot(tokens[...], du, preferred_element_type=F32) * factor).astype(BF)
 
     @pl.when(c == 0)
     def _():
-        total[...] = more if first else refs[5][...] + more
+        total[...] = more if first else refs[0][...] + more
 
     @pl.when(c > 0)
     def _():
@@ -125,7 +135,7 @@
         back[...] = total[...].astype(back.dtype)
 
 
-def back_of(spots, half, ds, slope, active, w_gate, w_up, tok, factor, before):
+def back_of(spots, half, ds, slope, active, w_gate, w_up, toks, factor, before):
     rows, part = ds[0].shape
     depth, width = w_gate.shape
     total = 4 * rows
@@ -146,38 +156,45 @@
             num_scalar_prefetch=1,
             grid=(steps,),
             in_specs=pieces
-            + [full, full, weight, weight, pl.BlockSpec((depth, total), lambda c, w: (0, 0))]
+            + [full, full, weight, weight]
+            + [pl.BlockSpec(t.shape, lambda c, w: (0, 0)) for t in toks]
             + kept,
             out_specs=(weight, weight, whole),
             scratch_shapes=[
                 pltpu.VMEM((total, NARROW), BF),
                 pltpu.VMEM((total, NARROW), BF),
                 pltpu.VMEM((total, depth), F32),
+                pltpu.VMEM((depth, total), BF),
             ],
         ),
-        input_output_aliases={12: 0, 13: 1} if before else {},
+        input_output_aliases={15: 0, 16: 1} if before else {},
         cost_estimate=pl.CostEstimate(
             flops=8 * total * part * depth, bytes_accessed=total * part * 14, transcendentals=0
         ),
-    )(spots, *ds, slope, active, w_gate, w_up, tok, *before)
+    )(spots, *ds, slope, active, w_gate, w_up, *toks, *before)
 
 
 def local(tokens, grad_out, gate_pre, up_pre, w_gate, w_up, w_down):
     rows, width = tokens.shape
     factor = float(1.0 / np.sqrt(np.float32(16 * rows)))
     y, zh = lax.axis_index("y"), lax.axis_index("zh")
-    p = lax.iota(jnp.int32, 6)
+    x, zl = lax.axis_index("x"), lax.axis_index("zl")
+    p = lax.iota(jnp.int32, 14)
     spots = jnp.where(p < 4, lax.rem(y + p, 4), jnp.where(p == 4, zh, 1 - zh))
+    m = p - 6
+    far = jnp.where(lax.rem(m, 2) == 0, zl, 1 - zl) * 4 + lax.rem(x + m // 2, 4)
+    spots = jnp.where(p < 6, spots, far)
 
     out_all = gather_col(grad_out)
 
     both = jnp.concatenate([gate_pre, up_pre], axis=0)
     both3, both1 = along_y(both, 1), along_y(both, -1)
-    g2 = along_y(both3[:rows], 1)
-    u2 = along_y(both1[rows:], -1)
+    low3 = both3[:rows]
+    high1 = both1[rows:]
+    g2, u2 = along_y(low3, 1), along_y(high1, -1)
     paired = {k: (v, to_pair(v)) for k, v in ((0, both), (3, both3), (1, both1))}
     saved = {k: (v, v) for k, v in paired.items()}
-    saved[2] = ((g2, to_pair(g2)), (u2, to_pair(u2)))
+    saved[2] = ((g2, along_y(paired[3][1][:rows], 1)), (u2, along_y(paired[1][1][rows:], -1)))
 
     part_rows = w_down.shape[0] // 2
 
@@ -192,11 +209,12 @@
 
     halves = [gathered(h) for h in (0, 1)]
 
-    tok_near = lax.ppermute(tokens, "zl", SWAP)
-    zl = lax.axis_index("zl")
-    tok_pair = jnp.stack([jnp.where(zl == 0, tokens, tok_near), jnp.where(zl == 0, tok_near, tokens)])
-    tok_all = lax.all_to_all(jnp.broadcast_to(tok_pair[None], (4,) + tok_pair.shape), "x", 0, 0, tiled=True)
-    tok_turned = tok_all.transpose(3, 1, 0, 2).reshape(width, 8 * rows)
+    turned = tokens.T
+    near = lax.ppermute(turned, "zl", SWAP)
+    pair = jnp.concatenate([turned, near], axis=0)
+    toks = [pair]
+    for m in (1, 2, 3):
+        toks.append(lax.ppermute(pair, "x", ring(-m)))
 
     def both_cores(own):
         other = lax.ppermute(own, "core", SWAP)
@@ -210,7 +228,7 @@
     grad_down = both_cores(down)
     before = ()
     for h in (0, 1):
-        gate, up, back = back_of(spots, h, halves[h], slope, active, w_gate, w_up, tok_turned, factor, before)
+        gate, up, back = back_of(spots, h, halves[h], slope, active, w_gate, w_up, toks, factor, before)
         before = (back, gate, up)
     back_recv = across_col(back.reshape(8, rows, width))
     grad_gate = both_cores(gate)

time: 262 us -> 293 us (1.12)
  waiting for transfers between devices: 84.2 us -> 123 us
  starting transfers between devices: 54.9 us -> 50.8 us
    ppermute x1 -> x4, waiting for transfers between devices: 6.95 us -> 37.1 us  [the longest x1 37.1 us: local(): near = lax.ppermute(turned, 'zl', SWAP)]
    ppermute x12 -> x14, waiting for transfers between devices: 12.9 us -> 22.9 us  [along_y(): return lax.ppermute(x, 'y', ring(shift))]
    ppermute x7 -> x5, waiting for transfers between devices: 32.8 us -> 23.5 us  [to_pair(): return lax.ppermute(x, 'zh', SWAP)]
    ppermute x7 -> x5, starting transfers between devices: 18.9 us -> 10.7 us  [to_pair(): return lax.ppermute(x, 'zh', SWAP)]
    all_to_all x2, waiting for transfers between devices: 19.4 us -> 27.4 us  [gathered(): lax.all_to_all(part.reshape(4, 2 * rows, part_rows), 'y', 0, 0, tiled=True)]
    all_to_all x1 -> x0, starting transfers between devices: 4.27 us -> none  [local(): lax.all_to_all(jnp.broadcast_to(tok_pair[None], (4,) + tok_pair.shape), '...]
    ppermute x1 -> x4, starting transfers between devices: 0.01 us -> 3.92 us  [the longest x3 3.42 us: local(): toks.append(lax.ppermute(pair, 'x', ring(-m)))]
    ppermute x12 -> x14, starting transfers between devices: 18.5 us -> 20.5 us  [along_y(): return lax.ppermute(x, 'y', ring(shift))]
  transfers between devices with their start and end apart: 27 -> 29, of which waited for: 7 -> 8; matrix products, arithmetic and copies ran while one was open for 16% -> 12% of each run, Pallas kernels for 18% -> 16%
where the time goes in v5:
time: 293 us; the launch traced here: 291 us
  waiting for transfers between devices  123 us (42%)
  starting transfers between devices  50.8 us (17%)
  Pallas kernels  47.9 us (16%)
  other arithmetic  22.2 us (8%)
  blocking collectives  21.3 us (7%)
  local copies, waits for them, and re-layouts  12.8 us (4%)
  matrix products  12.7 us (4%)
    ppermute x1, waiting for transfers between devices, local(): near = lax.ppermute(turned, 'zl', SWAP)  37.1 us
    all_to_all x2, waiting for transfers between devices, gathered(): lax.all_to_all(part.reshape(4, 2 * rows, part_rows), 'y', 0, 0, tiled=True)  27.4 us
    pallas_call x2, Pallas kernels, back_of(): pl.pallas_call(functools.partial(back_kernel, factor, not before), out_sh...  25.2 us
    ppermute x5, waiting for transfers between devices, to_pair(): return lax.ppermute(x, 'zh', SWAP)  23.5 us
    ppermute x14, waiting for transfers between devices, along_y(): return lax.ppermute(x, 'y', ring(shift))  22.9 us
    pallas_call x4, Pallas kernels, hidden_of(): pl.pallas_call(hidden_kernel, out_shape=(jax.ShapeDtypeStruct((total, wid...  22.7 us
    all_to_all x1, blocking collectives, across_col(): return lax.all_to_all(x, COL, 0, 0, tiled=True)  21.3 us
    ppermute x14, starting transfers between devices, along_y(): return lax.ppermute(x, 'y', ring(shift))  20.5 us
  transfers between devices with their start and end apart: 29, of which 8 were waited for; matrix products, arithmetic and copies ran while one was open for 12% of the time, Pallas kernels for 16%

profile of v5, /device:TPU:0, one launch (start us, length us, event | category | flops | bytes accessed | tf_op | source)
XLA Modules:
  0.0 291.2 jit_solution(4277784024836577682)
XLA Ops:
  0.6 1.1 broadcast_in_dim.24
  1.8 21.3 %all_to_all.20 = bf16[8,128,512]{2,1,0:T(8,128)(2,1)S(1)} all-to-all(bf16[8,128,512]{2,1,0:T(8,128)(2,1)S(1)} %broadcast_in_dim.24), channel_id=1, replica_groups=mesh['y'=4,'zh'=2,'zl'=2,'x'=4,'core'=2] {'zl','x'}, dimensions={0} | all-to-all | bytes 2097152 | tf_op jit(solution)/shard_map/all_to_all | solution.py:33
  23.1 2.6 convolution_convert_fusion
  25.7 4.6 %all-to-all-start.2 = ((bf16[4,256,1024]{2,1,0:T(8,128)(2,1)}), bf16[4,256,1024]{2,1,0:T(8,128)(2,1)S(1)}, u32[]{:S(2)}, u32[]{:S(2)}) async-start(bf16[4,256,1024]{2,1,0:T(8,128)(2,1)} %bitcast.10), calls=%async_computation.2 | async-start | bytes 4194304 | tf_op jit(solution)/shard_map/all_to_all | solution.py:203
  30.3 0.9 constant_dynamic-update-slice_fusion.1
  31.1 0.8 constant_dynamic-update-slice_fusion.refs_0_.refs_2_
  32.0 2.0 collective-permute-start.5
  34.0 1.2 collective-permute-start.9
  35.2 3.8 %convolution_convert_fusion.1 = bf16[1024,1024]{1,0:T(8,128)(2,1)} fusion(bf16[1024,512]{1,0:T(8,128)(2,1)S(1)} %bitcast.13, bf16[2048,512]{1,0:T(8,128)(2,1)} %param.13), kind=kOutput, calls=%fused_computation.7 | convolution fusion | flops 1074790400 | bytes 4194304 | tf_op jit(solution)/shard_map/dot_general | solution.py:47
  39.0 19.0 %all-to-all-done.2 = bf16[4,256,1024]{2,1,0:T(8,128)(2,1)S(1)} async-done(((bf16[4,256,1024]{2,1,0:T(8,128)(2,1)}), bf16[4,256,1024]{2,1,0:T(8,128)(2,1)S(1)}, u32[]{:S(2)}, u32[]{:S(2)}) %all-to-all-start.2) | async-done | bytes 2097184 | tf_op jit(solution)/shard_map/all_to_all | solution.py:203
  58.0 1.3 copy-done.2
  59.4 4.4 %all-to-all-start.1 = ((bf16[4,256,1024]{2,1,0:T(8,128)(2,1)}), bf16[4,256,1024]{2,1,0:T(8,128)(2,1)}, u32[]{:S(2)}, u32[]{:S(2)}) async-start(bf16[4,256,1024]{2,1,0:T(8,128)(2,1)} %bitcast.9), calls=%async_computation.1 | async-start | bytes 4194304 | tf_op jit(solution)/shard_map/all_to_all | solution.py:203
  63.8 16.5 %collective-permute-done.5.refs_0_.refs_2_ = bf16[256,2048]{1,0:T(8,128)(2,1)} collective-permute-done((bf16[256,2048]{1,0:T(8,128)(2,1)}, bf16[256,2048]{1,0:T(8,128)(2,1)}, u32[]{:S(2)}, u32[]{:S(2)}) %collective-permute-start.5) | collective-permute-done | bytes 1048608 | tf_op jit(solution)/shard_map/ppermute | solution.py:25
  80.3 3.6 %collective-permute-start.7 = (bf16[256,2048]{1,0:T(8,128)(2,1)}, bf16[256,2048]{1,0:T(8,128)(2,1)}, u32[]{:S(2)}, u32[]{:S(2)}) collective-permute-start(bf16[256,2048]{1,0:T(8,128)(2,1)} %collective-permute-done.5.refs_0_.refs_2_), channel_id=1, source_target_pairs={{0,16},{16,0},{1,17},{17,1},{2,18},{18,2},{3,19},{19,3},{4,20},{20... | collective-permute-start | bytes 3145736 | tf_op jit(solution)/shard_map/ppermute | solution.py:29
  84.0 3.4 %collective-permute-start.13 = (bf16[256,2048]{1,0:T(8,128)(2,1)}, bf16[256,2048]{1,0:T(8,128)(2,1)}, u32[]{:S(2)}, u32[]{:S(2)}) collective-permute-start(bf16[256,2048]{1,0:T(8,128)(2,1)} %constant_dynamic-update-slice_fusion.refs_0_.refs_2_), channel_id=1, source_target_pairs={{0,16},{16,0},{1,17},{17,1},{2,18},{18,2},{3,19},{19,3},{4,20},{20... | collective-permute-start | bytes 3145736 | tf_op jit(solution)/shard_map/ppermute | solution.py:29
  87.4 2.1 convert_reduce_fusion
  89.5 0.9 convert_element_type.69
  90.4 0.8 slice.44
  91.3 0.9 collective-permute-start.10
  92.2 8.4 %all-to-all-done.1 = bf16[4,256,1024]{2,1,0:T(8,128)(2,1)} async-done(((bf16[4,256,1024]{2,1,0:T(8,128)(2,1)}), bf16[4,256,1024]{2,1,0:T(8,128)(2,1)}, u32[]{:S(2)}, u32[]{:S(2)}) %all-to-all-start.1) | async-done | bytes 2097184 | tf_op jit(solution)/shard_map/all_to_all | solution.py:203
  100.5 2.1 convert_reduce_fusion.1
  102.6 0.9 convert_element_type.64
  103.5 4.7 %collective-permute-done.7.refs_1_.refs_3_ = bf16[256,2048]{1,0:T(8,128)(2,1)} collective-permute-done((bf16[256,2048]{1,0:T(8,128)(2,1)}, bf16[256,2048]{1,0:T(8,128)(2,1)}, u32[]{:S(2)}, u32[]{:S(2)}) %collective-permute-start.7) | collective-permute-done | bytes 1048608 | tf_op jit(solution)/shard_map/ppermute | solution.py:29
  108.2 3.5 %collective-permute-start = (bf16[256,1024]{1,0:T(8,128)(2,1)}, bf16[256,1024]{1,0:T(8,128)(2,1)}, u32[]{:S(2)}, u32[]{:S(2)}) collective-permute-start(bf16[256,1024]{1,0:T(8,128)(2,1)} %convert_element_type.64), channel_id=1, source_target_pairs={{0,16},{16,0},{1,17},{17,1},{2,18},{18,2},{3,19},{19,3},{4,20},{20... | collective-permute-start | bytes 1572872 | tf_op jit(solution)/shard_map/ppermute | solution.py:29
  111.7 0.1 copy.22
  111.8 18.8 %collective-permute-done.11.refs_1_.refs_3_ = bf16[256,2048]{1,0:T(8,128)(2,1)} collective-permute-done((bf16[256,2048]{1,0:T(8,128)(2,1)S(1)}, bf16[256,2048]{1,0:T(8,128)(2,1)}, u32[]{:S(2)}, u32[]{:S(2)}) %collective-permute-start.11) | collective-permute-done | bytes 1048608 | tf_op jit(solution)/shard_map/ppermute | solution.py:29
  130.7 0.5 collective-permute-start.14
  131.2 1.1 slice.42
  132.2 1.1 slice.45
  133.3 1.9 slice.43
  135.2 37.1 %collective-permute-done.14 = bf16[512,128]{1,0:T(8,128)(2,1)S(1)} collective-permute-done((bf16[512,128]{1,0:T(8,128)(2,1)S(1)}, bf16[512,128]{1,0:T(8,128)(2,1)S(1)}, u32[]{:S(2)}, u32[]{:S(2)}) %collective-permute-start.14) | collective-permute-done | bytes 131104 | tf_op jit(solution)/shard_map/ppermute | solution.py:213
  172.3 3.2 %collective-permute-start.12 = (bf16[128,2048]{1,0:T(8,128)(2,1)S(1)}, bf16[128,2048]{1,0:T(8,128)(2,1)}, u32[]{:S(2)}, u32[]{:S(2)}) collective-permute-start(bf16[128,2048]{1,0:T(8,128)(2,1)S(1)} %slice.45), channel_id=1, source_target_pairs={{0,96},{32,0},{64,32},{96,64},{1,97},{33,1},{65,33},{97,65},{2,98}... | collective-permute-start | bytes 1572872 | tf_op jit(solution)/shard_map/ppermute | solution.py:25
  175.6 2.0 add_convert_fusion.3.refs_0_
  177.6 3.2 %collective-permute-start.19 = (bf16[256,1024]{1,0:T(8,128)(2,1)}, bf16[256,1024]{1,0:T(8,128)(2,1)S(1)}, u32[]{:S(2)}, u32[]{:S(2)}) collective-permute-start(bf16[256,1024]{1,0:T(8,128)(2,1)} %add_convert_fusion.3.refs_0_), channel_id=1, source_target_pairs={{0,96},{32,0},{64,32},{96,64},{1,97},{33,1},{65,33},{97,65},{2,98}... | collective-permute-start | bytes 1572872 | tf_op jit(solution)/shard_map/ppermute | solution.py:25
  180.9 1.2 add_convert_fusion.4.refs_0_
  182.1 6.4 %collective-permute-done.6.refs_0_ = bf16[128,2048]{1,0:T(8,128)(2,1)} collective-permute-done((bf16[128,2048]{1,0:T(8,128)(2,1)S(1)}, bf16[128,2048]{1,0:T(8,128)(2,1)}, u32[]{:S(2)}, u32[]{:S(2)}) %collective-permute-start.6) | collective-permute-done | bytes 524320 | tf_op jit(solution)/shard_map/ppermute | solution.py:25
  188.4 3.2 %collective-permute-start.1 = (bf16[256,1024]{1,0:T(8,128)(2,1)S(1)}, bf16[256,1024]{1,0:T(8,128)(2,1)S(1)}, u32[]{:S(2)}, u32[]{:S(2)}) collective-permute-start(bf16[256,1024]{1,0:T(8,128)(2,1)S(1)} %add_convert_fusion.4.refs_0_), channel_id=1, source_target_pairs={{0,96},{32,0},{64,32},{96,64},{1,97},{33,1},{65,33},{97,65},{2,98}... | collective-permute-start | bytes 1572872 | tf_op jit(solution)/shard_map/ppermute | solution.py:25
  191.7 0.5 compare_select_fusion.7.spots
  192.2 5.7 %shard_map.102 = (bf16[1024,2048]{1,0:T(8,128)(2,1)}, f32[1024,2048]{1,0:T(8,128)}, f32[1024,2048]{1,0:T(8,128)}) custom-call(s32[14]{0:T(128)} %compare_select_fusion.7.spots, bf16[256,2048]{1,0:T(8,128)(2,1)} %constant_dynamic-update-slice_fusion.refs_0_.refs_2_, bf16[256,2048]{1,0:T(8,128)(2,1)} %collective-permute-done.13.refs_1_.refs_3_, ...), custom_call_target="tpu_custom_call" | custom-call | flops 5242880 | bytes 7340032 | tf_op jit(solution)/shard_map/pallas_call | solution.py:79
  197.9 5.7 %shard_map.103 = (bf16[1024,2048]{1,0:T(8,128)(2,1)}, f32[1024,2048]{1,0:T(8,128)}, f32[1024,2048]{1,0:T(8,128)}) custom-call(s32[14]{0:T(128)} %compare_select_fusion.7.spots, bf16[256,2048]{1,0:T(8,128)(2,1)} %collective-permute-done.5.refs_0_.refs_2_, ...), custom_call_target="tpu_custom_call", output_to_operand_aliasing={{0}: (5, {}), {1}: (6, {}), {2}: (7, {})} | custom-call | flops 5242880 | bytes 7340032 | tf_op jit(solution)/shard_map/pallas_call | solution.py:79
  203.6 5.7 %shard_map.104 = (bf16[1024,2048]{1,0:T(8,128)(2,1)}, f32[1024,2048]{1,0:T(8,128)}, f32[1024,2048]{1,0:T(8,128)}) custom-call(s32[14]{0:T(128)} %compare_select_fusion.7.spots, bf16[256,2048]{1,0:T(8,128)(2,1)} %copy-done.3, bf16[256,2048]{1,0:T(8,128)(2,1)} %collective-permute-done.11.refs_1_.refs_3_, ...), custom_call_target="tpu_custom_call", output_to_operand_aliasing={{0}: (5, {}), {1}: (6, {}), {2}: (7, {})} | custom-call | flops 5242880 | bytes 7340032 | tf_op jit(solution)/shard_map/pallas_call | solution.py:79
  209.3 1.6 collective-permute-start.15
  210.9 5.7 %shard_map.105 = (bf16[1024,2048]{1,0:T(8,128)(2,1)}, f32[1024,2048]{1,0:T(8,128)}, f32[1024,2048]{1,0:T(8,128)}) custom-call(s32[14]{0:T(128)} %compare_select_fusion.7.spots, bf16[128,2048]{1,0:T(8,128)(2,1)} %collective-permute-done.6.refs_0_, ...), custom_call_target="tpu_custom_call", output_to_operand_aliasing={{0}: (5, {}), {1}: (6, {}), {2}: (7, {})} | custom-call | flops 5242880 | bytes 7340032 | tf_op jit(solution)/shard_map/pallas_call | solution.py:79
  216.6 1.5 collective-permute-start.16
  218.2 0.3 collective-permute-start.17
  218.6 3.2 %collective-permute-start.22 = (bf16[128,1024]{1,0:T(8,128)(2,1)S(1)}, bf16[128,1024]{1,0:T(8,128)(2,1)S(1)}, u32[]{:S(2)}, u32[]{:S(2)}) collective-permute-start(bf16[128,1024]{1,0:T(8,128)(2,1)S(1)} %slice.47), channel_id=1, source_target_pairs={{0,96},{32,0},{64,32},{96,64},{1,97},{33,1},{65,33},{97,65},{2,98}... | collective-permute-start | bytes 786440 | tf_op jit(solution)/shard_map/ppermute | solution.py:25
  221.8 6.2 %multiply_convert_fusion = bf16[2048,512]{1,0:T(8,128)(2,1)} fusion(bf16[1024,2048]{1,0:T(8,128)(2,1)} %get-tuple-element.39, bf16[1024,512]{1,0:T(8,128)(2,1)} %bitcast.12), kind=kOutput, calls=%fused_computation.1 | convolution fusion | flops 2149580800 | bytes 7340032 | tf_op jit(solution)/shard_map/dot_general | solution.py:43
  228.0 0.7 slice.40
  229.0 0.7 copy-done.12
  229.7 3.2 %collective-permute-start.4 = (bf16[128,1024]{1,0:T(8,128)(2,1)S(1)}, bf16[128,1024]{1,0:T(8,128)(2,1)S(1)}, u32[]{:S(2)}, u32[]{:S(2)}) collective-permute-start(bf16[128,1024]{1,0:T(8,128)(2,1)S(1)} %slice.41), channel_id=1, source_target_pairs={{0,96},{32,0},{64,32},{96,64},{1,97},{33,1},{65,33},{97,65},{2,98}... | collective-permute-start | bytes 786440 | tf_op jit(solution)/shard_map/ppermute | solution.py:25
  232.9 0.7 copy-done.19
  233.6 0.7 copy-done.20
  234.3 12.4 %shard_map.106 = (bf16[512,2048]{1,0:T(8,128)(2,1)}, bf16[512,2048]{1,0:T(8,128)(2,1)}, f32[1024,512]{1,0:T(8,128)}) custom-call(s32[14]{0:T(128)} %compare_select_fusion.7.spots, bf16[256,1024]{1,0:T(8,128)(2,1)} %add_convert_fusion.3.refs_0_, bf16[256,1024]{1,0:T(8,128)(2,1)} %copy-done.9, bf16[256,1024]{1,0:T(8,128)(2,1)} %copy-done.8, ...), custom_call_target="tpu_custom_call" | custom-call | flops 4294967296 | bytes 14680064 | tf_op jit(solution)/shard_map/pallas_call | solution.py:148
  246.7 0.7 copy-done.17
  247.4 0.1 copy-done.18
  247.5 12.8 %shard_map.107 = (bf16[512,2048]{1,0:T(8,128)(2,1)}, bf16[512,2048]{1,0:T(8,128)(2,1)}, bf16[1024,512]{1,0:T(8,128)(2,1)}) custom-call(s32[14]{0:T(128)} %compare_select_fusion.7.spots, bf16[256,1024]{1,0:T(8,128)(2,1)} %copy-done.5, bf16[256,1024]{1,0:T(8,128)(2,1)} %copy-done.7, ...), custom_call_target="tpu_custom_call", output_to_operand_aliasing={{0}: (15, {}), {1}: (16, {})} | custom-call | flops 4294967296 | bytes 14680064 | tf_op jit(solution)/shard_map/pallas_call | solution.py:148
  260.3 0.1 collective-permute-start.24
  260.4 0.5 collective-permute-start.23
  260.9 6.0 %all-to-all-start.3 = ((bf16[8,128,512]{2,1,0:T(8,128)(2,1)}), bf16[8,128,512]{2,1,0:T(8,128)(2,1)S(1)}, u32[]{:S(2)}, u32[]{:S(2)}) async-start(bf16[8,128,512]{2,1,0:T(8,128)(2,1)} %bitcast.14), calls=%async_computation.3 | async-start | bytes 2097152 | tf_op jit(solution)/shard_map/all_to_all | solution.py:33
  266.9 4.3 %add_convert_fusion = bf16[2048,512]{1,0:T(8,128)(2,1)} fusion(bf16[2048,512]{1,0:T(8,128)(2,1)} %collective-permute-done.25, bf16[2048,512]{1,0:T(8,128)(2,1)} %multiply_convert_fusion), kind=kLoop, calls=%fused_computation | loop fusion | flops 4194304 | bytes 6291456 | tf_op jit(solution)/shard_map/convert_element_type | solution.py:221
  271.2 11.7 %all-to-all-done.3 = bf16[8,128,512]{2,1,0:T(8,128)(2,1)S(1)} async-done(((bf16[8,128,512]{2,1,0:T(8,128)(2,1)}), bf16[8,128,512]{2,1,0:T(8,128)(2,1)S(1)}, u32[]{:S(2)}, u32[]{:S(2)}) %all-to-all-start.3) | async-done | bytes 1048608 | tf_op jit(solution)/shard_map/all_to_all | solution.py:33
  282.8 0.8 reduce_sum.32
  283.7 3.8 %add_convert_fusion.1 = bf16[512,2048]{1,0:T(8,128)(2,1)} fusion(bf16[512,2048]{1,0:T(8,128)(2,1)} %collective-permute-done.24, bf16[512,2048]{1,0:T(8,128)(2,1)S(1)} %copy-done.1), kind=kLoop, calls=%fused_computation.2 | loop fusion | flops 4194304 | bytes 6291456 | tf_op jit(solution)/shard_map/convert_element_type | solution.py:221
  287.5 3.7 %add_convert_fusion.2 = bf16[512,2048]{1,0:T(8,128)(2,1)} fusion(bf16[512,2048]{1,0:T(8,128)(2,1)} %collective-permute-done.23, bf16[512,2048]{1,0:T(8,128)(2,1)S(1)} %copy-done), kind=kLoop, calls=%fused_computation.3 | loop fusion | flops 4194304 | bytes 6291456 | tf_op jit(solution)/shard_map/convert_element_type | solution.py:221
  (74 shorter events, 0.7 us)
Async XLA Ops:
  0.6 22.4 %copy-start.22 = (bf16[2048,512]{1,0:T(8,128)(2,1)S(1)}, bf16[2048,512]{1,0:T(8,128)(2,1)}, u32[]{:S(2)}) copy-start(bf16[2048,512]{1,0:T(8,128)(2,1)} %param.13) | copy-start | bytes 6291460
  23.0 2.6 copy-start.13
  25.7 4.6 %copy-start.15 = (bf16[128,2048]{1,0:T(8,128)(2,1)S(1)}, bf16[128,2048]{1,0:T(8,128)(2,1)}, u32[]{:S(2)}) copy-start(bf16[128,2048]{1,0:T(8,128)(2,1)} %param.9) | copy-start | bytes 1572868
  25.7 5.5 %copy-start.16 = (bf16[128,2048]{1,0:T(8,128)(2,1)S(1)}, bf16[128,2048]{1,0:T(8,128)(2,1)}, u32[]{:S(2)}) copy-start(bf16[128,2048]{1,0:T(8,128)(2,1)} %param.10) | copy-start | bytes 1572868
  25.7 32.4 %all-to-all-start.2 = ((bf16[4,256,1024]{2,1,0:T(8,128)(2,1)}), bf16[4,256,1024]{2,1,0:T(8,128)(2,1)S(1)}, u32[]{:S(2)}, u32[]{:S(2)}) async-start(bf16[4,256,1024]{2,1,0:T(8,128)(2,1)} %bitcast.10), calls=%async_computation.2 | async-start | bytes 4194304 | tf_op jit(solution)/shard_map/all_to_all | solution.py:203
  30.3 4.9 %copy-start.14 = (bf16[8,128,512]{2,1,0:T(8,128)(2,1)S(1)}, bf16[8,128,512]{2,1,0:T(8,128)(2,1)}, u32[]{:S(2)}) copy-start(bf16[8,128,512]{2,1,0:T(8,128)(2,1)} %copy-done.13) | copy-start | bytes 3145732
  32.0 48.3 %collective-permute-start.5 = (bf16[256,2048]{1,0:T(8,128)(2,1)}, bf16[256,2048]{1,0:T(8,128)(2,1)}, u32[]{:S(2)}, u32[]{:S(2)}) collective-permute-start(bf16[256,2048]{1,0:T(8,128)(2,1)} %constant_dynamic-update-slice_fusion.refs_0_.refs_2_), channel_id=1, source_target_pairs={{0,32},{32,64},{64,96},{96,0},{1,33},{33,65},{65,97},{97,1},{2,34}... | collective-permute-start | bytes 3145736 | tf_op jit(solution)/shard_map/ppermute | solution.py:25
  34.0 49.9 %collective-permute-start.9 = (bf16[256,2048]{1,0:T(8,128)(2,1)}, bf16[256,2048]{1,0:T(8,128)(2,1)S(1)}, u32[]{:S(2)}, u32[]{:S(2)}) collective-permute-start(bf16[256,2048]{1,0:T(8,128)(2,1)} %constant_dynamic-update-slice_fusion.refs_0_.refs_2_), channel_id=1, source_target_pairs={{0,96},{32,0},{64,32},{96,64},{1,97},{33,1},{65,33},{97,65},{2,98}... | collective-permute-start | bytes 3145736 | tf_op jit(solution)/shard_map/ppermute | solution.py:25
  58.0 1.3 copy-start.2
  59.4 41.2 %all-to-all-start.1 = ((bf16[4,256,1024]{2,1,0:T(8,128)(2,1)}), bf16[4,256,1024]{2,1,0:T(8,128)(2,1)}, u32[]{:S(2)}, u32[]{:S(2)}) async-start(bf16[4,256,1024]{2,1,0:T(8,128)(2,1)} %bitcast.9), calls=%async_computation.1 | async-start | bytes 4194304 | tf_op jit(solution)/shard_map/all_to_all | solution.py:203
  80.3 27.9 %collective-permute-start.7 = (bf16[256,2048]{1,0:T(8,128)(2,1)}, bf16[256,2048]{1,0:T(8,128)(2,1)}, u32[]{:S(2)}, u32[]{:S(2)}) collective-permute-start(bf16[256,2048]{1,0:T(8,128)(2,1)} %collective-permute-done.5.refs_0_.refs_2_), channel_id=1, source_target_pairs={{0,16},{16,0},{1,17},{17,1},{2,18},{18,2},{3,19},{19,3},{4,20},{20... | collective-permute-start | bytes 3145736 | tf_op jit(solution)/shard_map/ppermute | solution.py:29
  83.9 6.6 %copy-start.3 = (bf16[256,2048]{1,0:T(8,128)(2,1)}, bf16[256,2048]{1,0:T(8,128)(2,1)S(1)}, u32[]{:S(2)}) copy-start(bf16[256,2048]{1,0:T(8,128)(2,1)S(1)} %collective-permute-done.9.refs_0_.refs_2_) | copy-start | bytes 3145732
  83.9 46.8 %collective-permute-start.11 = (bf16[256,2048]{1,0:T(8,128)(2,1)S(1)}, bf16[256,2048]{1,0:T(8,128)(2,1)}, u32[]{:S(2)}, u32[]{:S(2)}) collective-permute-start(bf16[256,2048]{1,0:T(8,128)(2,1)S(1)} %collective-permute-done.9.refs_0_.refs_2_), channel_id=1, source_target_pairs={{0,16},{16,0},{1,17},{17,1},{2,18},{18,2},{3,19},{19,3},{4,20},{20... | collective-permute-start | bytes 3145736 | tf_op jit(solution)/shard_map/ppermute | solution.py:29
  84.0 93.6 %collective-permute-start.13 = (bf16[256,2048]{1,0:T(8,128)(2,1)}, bf16[256,2048]{1,0:T(8,128)(2,1)}, u32[]{:S(2)}, u32[]{:S(2)}) collective-permute-start(bf16[256,2048]{1,0:T(8,128)(2,1)} %constant_dynamic-update-slice_fusion.refs_0_.refs_2_), channel_id=1, source_target_pairs={{0,16},{16,0},{1,17},{17,1},{2,18},{18,2},{3,19},{19,3},{4,20},{20... | collective-permute-start | bytes 3145736 | tf_op jit(solution)/shard_map/ppermute | solution.py:29
  90.4 82.0 %collective-permute-start.18 = (bf16[256,1024]{1,0:T(8,128)(2,1)}, bf16[256,1024]{1,0:T(8,128)(2,1)}, u32[]{:S(2)}, u32[]{:S(2)}) collective-permute-start(bf16[256,1024]{1,0:T(8,128)(2,1)} %convert_element_type.69), channel_id=1, source_target_pairs={{0,16},{16,0},{1,17},{17,1},{2,18},{18,2},{3,19},{19,3},{4,20},{20... | collective-permute-start | bytes 1572872 | tf_op jit(solution)/shard_map/ppermute | solution.py:29
  91.3 20.5 %copy-start.21 = (bf16[128,512]{1,0:T(8,128)(2,1)S(1)}, bf16[128,512]{1,0:T(8,128)(2,1)}, u32[]{:S(2)}) copy-start(bf16[128,512]{1,0:T(8,128)(2,1)} %param.7) | copy-start | bytes 393220
  91.3 86.3 %collective-permute-start.10 = (bf16[128,2048]{1,0:T(8,128)(2,1)}, bf16[128,2048]{1,0:T(8,128)(2,1)}, u32[]{:S(2)}, u32[]{:S(2)}) collective-permute-start(bf16[128,2048]{1,0:T(8,128)(2,1)} %slice.44), channel_id=1, source_target_pairs={{0,96},{32,0},{64,32},{96,64},{1,97},{33,1},{65,33},{97,65},{2,98}... | collective-permute-start | bytes 1572872 | tf_op jit(solution)/shard_map/ppermute | solution.py:25
  108.2 69.4 %collective-permute-start = (bf16[256,1024]{1,0:T(8,128)(2,1)}, bf16[256,1024]{1,0:T(8,128)(2,1)}, u32[]{:S(2)}, u32[]{:S(2)}) collective-permute-start(bf16[256,1024]{1,0:T(8,128)(2,1)} %convert_element_type.64), channel_id=1, source_target_pairs={{0,16},{16,0},{1,17},{17,1},{2,18},{18,2},{3,19},{19,3},{4,20},{20... | collective-permute-start | bytes 1572872 | tf_op jit(solution)/shard_map/ppermute | solution.py:29
  130.7 41.6 %collective-permute-start.14 = (bf16[512,128]{1,0:T(8,128)(2,1)S(1)}, bf16[512,128]{1,0:T(8,128)(2,1)S(1)}, u32[]{:S(2)}, u32[]{:S(2)}) collective-permute-start(bf16[512,128]{1,0:T(8,128)(2,1)S(1)} %bitcast.15), channel_id=1, source_target_pairs={{0,8},{8,0},{1,9},{9,1},{2,10},{10,2},{3,11},{11,3},{4,12},{12,4},... | collective-permute-start | bytes 393224 | tf_op jit(solution)/shard_map/ppermute | solution.py:213
  172.3 16.1 %collective-permute-start.6 = (bf16[128,2048]{1,0:T(8,128)(2,1)S(1)}, bf16[128,2048]{1,0:T(8,128)(2,1)}, u32[]{:S(2)}, u32[]{:S(2)}) collective-permute-start(bf16[128,2048]{1,0:T(8,128)(2,1)S(1)} %slice.42), channel_id=1, source_target_pairs={{0,32},{32,64},{64,96},{96,0},{1,33},{33,65},{65,97},{97,1},{2,34}... | collective-permute-start | bytes 1572872 | tf_op jit(solution)/shard_map/ppermute | solution.py:25
  172.3 16.1 %collective-permute-start.12 = (bf16[128,2048]{1,0:T(8,128)(2,1)S(1)}, bf16[128,2048]{1,0:T(8,128)(2,1)}, u32[]{:S(2)}, u32[]{:S(2)}) collective-permute-start(bf16[128,2048]{1,0:T(8,128)(2,1)S(1)} %slice.45), channel_id=1, source_target_pairs={{0,96},{32,0},{64,32},{96,64},{1,97},{33,1},{65,33},{97,65},{2,98}... | collective-permute-start | bytes 1572872 | tf_op jit(solution)/shard_map/ppermute | solution.py:25
  177.5 31.7 %collective-permute-start.8 = (bf16[128,2048]{1,0:T(8,128)(2,1)}, bf16[128,2048]{1,0:T(8,128)(2,1)}, u32[]{:S(2)}, u32[]{:S(2)}) collective-permute-start(bf16[128,2048]{1,0:T(8,128)(2,1)} %slice.43), channel_id=1, source_target_pairs={{0,32},{32,64},{64,96},{96,0},{1,33},{33,65},{65,97},{97,1},{2,34}... | collective-permute-start | bytes 1572872 | tf_op jit(solution)/shard_map/ppermute | solution.py:25
  177.5 39.0 %collective-permute-start.20 = (bf16[256,1024]{1,0:T(8,128)(2,1)}, bf16[256,1024]{1,0:T(8,128)(2,1)S(1)}, u32[]{:S(2)}, u32[]{:S(2)}) collective-permute-start(bf16[256,1024]{1,0:T(8,128)(2,1)} %add_convert_fusion.3.refs_0_), channel_id=1, source_target_pairs={{0,32},{32,64},{64,96},{96,0},{1,33},{33,65},{65,97},{97,1},{2,34}... | collective-permute-start | bytes 1572872 | tf_op jit(solution)/shard_map/ppermute | solution.py:25
  177.6 40.5 %collective-permute-start.19 = (bf16[256,1024]{1,0:T(8,128)(2,1)}, bf16[256,1024]{1,0:T(8,128)(2,1)S(1)}, u32[]{:S(2)}, u32[]{:S(2)}) collective-permute-start(bf16[256,1024]{1,0:T(8,128)(2,1)} %add_convert_fusion.3.refs_0_), channel_id=1, source_target_pairs={{0,96},{32,0},{64,32},{96,64},{1,97},{33,1},{65,33},{97,65},{2,98}... | collective-permute-start | bytes 1572872 | tf_op jit(solution)/shard_map/ppermute | solution.py:25
  182.0 15.9 %copy-start.5 = (bf16[256,1024]{1,0:T(8,128)(2,1)}, bf16[256,1024]{1,0:T(8,128)(2,1)S(1)}, u32[]{:S(2)}) copy-start(bf16[256,1024]{1,0:T(8,128)(2,1)S(1)} %add_convert_fusion.4.refs_0_) | copy-start | bytes 1572868
  188.4 30.0 %collective-permute-start.2 = (bf16[256,1024]{1,0:T(8,128)(2,1)S(1)}, bf16[256,1024]{1,0:T(8,128)(2,1)S(1)}, u32[]{:S(2)}, u32[]{:S(2)}) collective-permute-start(bf16[256,1024]{1,0:T(8,128)(2,1)S(1)} %add_convert_fusion.4.refs_0_), channel_id=1, source_target_pairs={{0,32},{32,64},{64,96},{96,0},{1,33},{33,65},{65,97},{97,1},{2,34}... | collective-permute-start | bytes 1572872 | tf_op jit(solution)/shard_map/ppermute | solution.py:25
  188.4 30.1 %collective-permute-start.1 = (bf16[256,1024]{1,0:T(8,128)(2,1)S(1)}, bf16[256,1024]{1,0:T(8,128)(2,1)S(1)}, u32[]{:S(2)}, u32[]{:S(2)}) collective-permute-start(bf16[256,1024]{1,0:T(8,128)(2,1)S(1)} %add_convert_fusion.4.refs_0_), channel_id=1, source_target_pairs={{0,96},{32,0},{64,32},{96,64},{1,97},{33,1},{65,33},{97,65},{2,98}... | collective-permute-start | bytes 1572872 | tf_op jit(solution)/shard_map/ppermute | solution.py:25
  192.2 25.9 %copy-start.4 = (bf16[1024,128]{1,0:T(8,128)(2,1)}, bf16[1024,128]{1,0:T(8,128)(2,1)S(1)}, u32[]{:S(2)}) copy-start(bf16[1024,128]{1,0:T(8,128)(2,1)S(1)} %pad_maximum_fusion.refs_9_) | copy-start | bytes 786436
  209.3 19.5 %collective-permute-start.15 = (bf16[1024,128]{1,0:T(8,128)(2,1)S(1)}, bf16[1024,128]{1,0:T(8,128)(2,1)S(1)}, u32[]{:S(2)}, u32[]{:S(2)}) collective-permute-start(bf16[1024,128]{1,0:T(8,128)(2,1)S(1)} %pad_maximum_fusion.refs_9_), channel_id=1, source_target_pairs={{0,6},{2,0},{4,2},{6,4},{1,7},{3,1},{5,3},{7,5},{8,14},{10,8},{12,... | collective-permute-start | bytes 786440 | tf_op jit(solution)/shard_map/ppermute | solution.py:217
  216.6 11.5 %copy-start.8 = (bf16[256,1024]{1,0:T(8,128)(2,1)}, bf16[256,1024]{1,0:T(8,128)(2,1)S(1)}, u32[]{:S(2)}) copy-start(bf16[256,1024]{1,0:T(8,128)(2,1)S(1)} %collective-permute-done.20.refs_2_) | copy-start | bytes 1572868
  216.6 12.3 %collective-permute-start.16 = (bf16[1024,128]{1,0:T(8,128)(2,1)S(1)}, bf16[1024,128]{1,0:T(8,128)(2,1)S(1)}, u32[]{:S(2)}, u32[]{:S(2)}) collective-permute-start(bf16[1024,128]{1,0:T(8,128)(2,1)S(1)} %pad_maximum_fusion.refs_9_), channel_id=1, source_target_pairs={{0,4},{2,6},{4,0},{6,2},{1,5},{3,7},{5,1},{7,3},{8,12},{10,14},{12... | collective-permute-start | bytes 786440 | tf_op jit(solution)/shard_map/ppermute | solution.py:217
  218.2 9.9 %copy-start.9 = (bf16[256,1024]{1,0:T(8,128)(2,1)}, bf16[256,1024]{1,0:T(8,128)(2,1)S(1)}, u32[]{:S(2)}) copy-start(bf16[256,1024]{1,0:T(8,128)(2,1)S(1)} %collective-permute-done.19.refs_1_) | copy-start | bytes 1572868
  218.2 10.8 %collective-permute-start.17 = (bf16[1024,128]{1,0:T(8,128)(2,1)S(1)}, bf16[1024,128]{1,0:T(8,128)(2,1)S(1)}, u32[]{:S(2)}, u32[]{:S(2)}) collective-permute-start(bf16[1024,128]{1,0:T(8,128)(2,1)S(1)} %pad_maximum_fusion.refs_9_), channel_id=1, source_target_pairs={{0,2},{2,4},{4,6},{6,0},{1,3},{3,5},{5,7},{7,1},{8,10},{10,12},{12... | collective-permute-start | bytes 786440 | tf_op jit(solution)/shard_map/ppermute | solution.py:217
  218.5 9.6 %copy-start.6 = (bf16[256,1024]{1,0:T(8,128)(2,1)}, bf16[256,1024]{1,0:T(8,128)(2,1)S(1)}, u32[]{:S(2)}) copy-start(bf16[256,1024]{1,0:T(8,128)(2,1)S(1)} %collective-permute-done.2.refs_2_) | copy-start | bytes 1572868
  218.5 14.4 %collective-permute-start.21 = (bf16[128,1024]{1,0:T(8,128)(2,1)S(1)}, bf16[128,1024]{1,0:T(8,128)(2,1)S(1)}, u32[]{:S(2)}, u32[]{:S(2)}) collective-permute-start(bf16[128,1024]{1,0:T(8,128)(2,1)S(1)} %slice.46), channel_id=1, source_target_pairs={{0,32},{32,64},{64,96},{96,0},{1,33},{33,65},{65,97},{97,1},{2,34}... | collective-permute-start | bytes 786440 | tf_op jit(solution)/shard_map/ppermute | solution.py:25
  218.6 10.2 %copy-start.7 = (bf16[256,1024]{1,0:T(8,128)(2,1)}, bf16[256,1024]{1,0:T(8,128)(2,1)S(1)}, u32[]{:S(2)}) copy-start(bf16[256,1024]{1,0:T(8,128)(2,1)S(1)} %collective-permute-done.1.refs_1_) | copy-start | bytes 1572868
  218.6 14.3 %collective-permute-start.22 = (bf16[128,1024]{1,0:T(8,128)(2,1)S(1)}, bf16[128,1024]{1,0:T(8,128)(2,1)S(1)}, u32[]{:S(2)}, u32[]{:S(2)}) collective-permute-start(bf16[128,1024]{1,0:T(8,128)(2,1)S(1)} %slice.47), channel_id=1, source_target_pairs={{0,96},{32,0},{64,32},{96,64},{1,97},{33,1},{65,33},{97,65},{2,98}... | collective-permute-start | bytes 786440 | tf_op jit(solution)/shard_map/ppermute | solution.py:25
  228.8 5.5 %copy-start.10 = (bf16[1024,128]{1,0:T(8,128)(2,1)}, bf16[1024,128]{1,0:T(8,128)(2,1)S(1)}, u32[]{:S(2)}) copy-start(bf16[1024,128]{1,0:T(8,128)(2,1)S(1)} %collective-permute-done.15.refs_10_) | copy-start | bytes 786436
  228.8 38.1 %collective-permute-start.25 = (bf16[2048,512]{1,0:T(8,128)(2,1)}, bf16[2048,512]{1,0:T(8,128)(2,1)}, u32[]{:S(2)}, u32[]{:S(2)}) collective-permute-start(bf16[2048,512]{1,0:T(8,128)(2,1)} %multiply_convert_fusion), channel_id=1, source_target_pairs={{0,1},{1,0},{2,3},{3,2},{4,5},{5,4},{6,7},{7,6},{8,9},{9,8},{10,11... | collective-permute-start | bytes 6291464 | tf_op jit(solution)/shard_map/ppermute | solution.py:220
  228.9 5.4 %copy-start.11 = (bf16[1024,128]{1,0:T(8,128)(2,1)}, bf16[1024,128]{1,0:T(8,128)(2,1)S(1)}, u32[]{:S(2)}) copy-start(bf16[1024,128]{1,0:T(8,128)(2,1)S(1)} %collective-permute-done.16.refs_11_) | copy-start | bytes 786436
  228.9 17.8 %collective-permute-start.3 = (bf16[128,1024]{1,0:T(8,128)(2,1)}, bf16[128,1024]{1,0:T(8,128)(2,1)S(1)}, u32[]{:S(2)}, u32[]{:S(2)}) collective-permute-start(bf16[128,1024]{1,0:T(8,128)(2,1)} %slice.40), channel_id=1, source_target_pairs={{0,32},{32,64},{64,96},{96,0},{1,33},{33,65},{65,97},{97,1},{2,34}... | collective-permute-start | bytes 786440 | tf_op jit(solution)/shard_map/ppermute | solution.py:25
  229.0 0.7 copy-start.12
  229.7 17.0 %collective-permute-start.4 = (bf16[128,1024]{1,0:T(8,128)(2,1)S(1)}, bf16[128,1024]{1,0:T(8,128)(2,1)S(1)}, u32[]{:S(2)}, u32[]{:S(2)}) collective-permute-start(bf16[128,1024]{1,0:T(8,128)(2,1)S(1)} %slice.41), channel_id=1, source_target_pairs={{0,96},{32,0},{64,32},{96,64},{1,97},{33,1},{65,33},{97,65},{2,98}... | collective-permute-start | bytes 786440 | tf_op jit(solution)/shard_map/ppermute | solution.py:25
  232.9 0.7 copy-start.19
  233.6 0.7 copy-start.20
  246.7 0.7 copy-start.17
  246.7 0.8 copy-start.18
  260.3 23.4 %collective-permute-start.24 = (bf16[512,2048]{1,0:T(8,128)(2,1)}, bf16[512,2048]{1,0:T(8,128)(2,1)}, u32[]{:S(2)}, u32[]{:S(2)}) collective-permute-start(bf16[512,2048]{1,0:T(8,128)(2,1)} %get-tuple-element.38), channel_id=1, source_target_pairs={{0,1},{1,0},{2,3},{3,2},{4,5},{5,4},{6,7},{7,6},{8,9},{9,8},{10,11... | collective-permute-start | bytes 6291464 | tf_op jit(solution)/shard_map/ppermute | solution.py:220
  260.4 27.1 %collective-permute-start.23 = (bf16[512,2048]{1,0:T(8,128)(2,1)}, bf16[512,2048]{1,0:T(8,128)(2,1)}, u32[]{:S(2)}, u32[]{:S(2)}) collective-permute-start(bf16[512,2048]{1,0:T(8,128)(2,1)} %get-tuple-element.37), channel_id=1, source_target_pairs={{0,1},{1,0},{2,3},{3,2},{4,5},{5,4},{6,7},{7,6},{8,9},{9,8},{10,11... | collective-permute-start | bytes 6291464 | tf_op jit(solution)/shard_map/ppermute | solution.py:220
  260.9 21.9 %all-to-all-start.3 = ((bf16[8,128,512]{2,1,0:T(8,128)(2,1)}), bf16[8,128,512]{2,1,0:T(8,128)(2,1)S(1)}, u32[]{:S(2)}, u32[]{:S(2)}) async-start(bf16[8,128,512]{2,1,0:T(8,128)(2,1)} %bitcast.14), calls=%async_computation.3 | async-start | bytes 2097152 | tf_op jit(solution)/shard_map/all_to_all | solution.py:33
  266.9 16.8 %copy-start.1 = (bf16[512,2048]{1,0:T(8,128)(2,1)S(1)}, bf16[512,2048]{1,0:T(8,128)(2,1)}, u32[]{:S(2)}) copy-start(bf16[512,2048]{1,0:T(8,128)(2,1)} %get-tuple-element.38) | copy-start | bytes 6291460
  283.7 3.8 %copy-start = (bf16[512,2048]{1,0:T(8,128)(2,1)S(1)}, bf16[512,2048]{1,0:T(8,128)(2,1)}, u32[]{:S(2)}) copy-start(bf16[512,2048]{1,0:T(8,128)(2,1)} %get-tuple-element.37) | copy-start | bytes 6291460

commit v6 on v5

--- a/solution.py
+++ b/solution.py
@@ -100,11 +100,12 @@
     ds, refs = refs[:5], refs[5:]
     slope, active, w_gate, w_up = refs[:4]
     toks, refs = refs[4:8], refs[8:]
-    grad_gate, grad_up, back, d_gate, d_up, total, tokens = refs[-7:]
+    grad_gate, grad_up, back, both, weights, total, tokens = refs[-7:]
     c = pl.program_id(0)
 
     @pl.when(c == 0)
     def _():
+        total[...] = jnp.zeros_like(total) if first else refs[0][...]
         depth, wide = tokens.shape[0], toks[0].shape[1]
         for m in range(4):
             for j in range(2):
@@ -115,20 +116,15 @@
         d = ref[...].astype(F32)
         rows = d.shape[0]
         here = pl.ds(pl.multiple_of(spots[k] * ds[0].shape[0] + skip * rows, rows), rows)
-        d_gate[here, :] = (d * slope[here, :]).astype(BF)
-        d_up[here, :] = (d * active[here, :]).astype(BF)
-    dg, du = d_gate[...], d_up[...]
-    more = times_transposed(dg, w_gate[...]) + times_transposed(du, w_up[...])
-    grad_gate[...] = (jnp.dot(tokens[...], dg, preferred_element_type=F32) * factor).astype(BF)
-    grad_up[...] = (jnp.dot(tokens[...], du, preferred_element_type=F32) * factor).astype(BF)
-
-    @pl.when(c == 0)
-    def _():
-        total[...] = more if first else refs[0][...] + more
-
-    @pl.when(c > 0)
-    def _():
-        total[...] += more
+        both[here, :NARROW] = (d * slope[here, :]).astype(BF)
+        both[here, NARROW:] = (d * active[here, :]).astype(BF)
+    weights[:, :NARROW] = w_gate[...]
+    weights[:, NARROW:] = w_up[...]
+    both_d = both[...]
+    total[...] += times_transposed(both_d, weights[...])
+    grads = (jnp.dot(tokens[...], both_d, preferred_element_type=F32) * factor).astype(BF)
+    grad_gate[...] = grads[:, :NARROW]
+    grad_up[...] = grads[:, NARROW:]
 
     @pl.when(c == pl.num_programs(0) - 1)
     def _():
@@ -161,8 +157,8 @@
             + kept,
             out_specs=(weight, weight, whole),
             scratch_shapes=[
-                pltpu.VMEM((total, NARROW), BF),
-                pltpu.VMEM((total, NARROW), BF),
+                pltpu.VMEM((total, 2 * NARROW), BF),
+                pltpu.VMEM((depth, 2 * NARROW), BF),
                 pltpu.VMEM((total, depth), F32),
                 pltpu.VMEM((depth, total), BF),
             ],
@@ -194,7 +190,7 @@
     g2, u2 = along_y(low3, 1), along_y(high1, -1)
     paired = {k: (v, to_pair(v)) for k, v in ((0, both), (3, both3), (1, both1))}
     saved = {k: (v, v) for k, v in paired.items()}
-    saved[2] = ((g2, along_y(paired[3][1][:rows], 1)), (u2, along_y(paired[1][1][rows:], -1)))
+    saved[2] = ((g2, to_pair(g2)), (u2, to_pair(u2)))
 
     part_rows = w_down.shape[0] // 2
 

time: 293 us -> 294 us (level)
  waiting for transfers between devices: 123 us -> 132 us
  starting transfers between devices: 50.8 us -> 46.7 us
  other arithmetic: 22.2 us -> 18.8 us
    ppermute x5 -> x7, waiting for transfers between devices: 23.5 us -> 41.9 us  [to_pair(): return lax.ppermute(x, 'zh', SWAP)]
    ppermute x1, waiting for transfers between devices: 37.1 us -> 19.9 us  [local(): near = lax.ppermute(turned, 'zl', SWAP)]
    ppermute x14 -> x12, waiting for transfers between devices: 22.9 us -> 38.9 us  [along_y(): return lax.ppermute(x, 'y', ring(shift))]
    all_to_all x2, waiting for transfers between devices: 27.4 us -> 19.5 us  [gathered(): lax.all_to_all(part.reshape(4, 2 * rows, part_rows), 'y', 0, 0, tiled=True)]
    ppermute x14 -> x12, starting transfers between devices: 20.5 us -> 13.4 us  [along_y(): return lax.ppermute(x, 'y', ring(shift))]
    ppermute x5 -> x7, starting transfers between devices: 10.7 us -> 16.8 us  [to_pair(): return lax.ppermute(x, 'zh', SWAP)]
    slice x2 -> x0, local copies, waits for them, and re-layouts: 2.96 us -> none  [the longest x1 1.88 us: local(): paired[3][1][:rows]]
    unnamed x48 -> x44, local copies, waits for them, and re-layouts: 5.21 us -> 6.27 us
  transfers between devices with their start and end apart: 29 -> 29, of which waited for: 8 -> 7; matrix products, arithmetic and copies ran while one was open for 12% -> 11% of each run, Pallas kernels for 16% -> 16%
where the time goes in v6:
time: 294 us; the launch traced here: 293 us
  waiting for transfers between devices  132 us (45%)
  Pallas kernels  47.3 us (16%)
  starting transfers between devices  46.7 us (16%)
  blocking collectives  21.3 us (7%)
  other arithmetic  18.8 us (6%)
  local copies, waits for them, and re-layouts  12.8 us (4%)
  matrix products  12.6 us (4%)
    ppermute x7, waiting for transfers between devices, to_pair(): return lax.ppermute(x, 'zh', SWAP)  41.9 us
    ppermute x12, waiting for transfers between devices, along_y(): return lax.ppermute(x, 'y', ring(shift))  38.9 us
    pallas_call x2, Pallas kernels, back_of(): pl.pallas_call(functools.partial(back_kernel, factor, not before), out_sh...  24.7 us
    pallas_call x4, Pallas kernels, hidden_of(): pl.pallas_call(hidden_kernel, out_shape=(jax.ShapeDtypeStruct((total, wid...  22.7 us
    all_to_all x1, blocking collectives, across_col(): return lax.all_to_all(x, COL, 0, 0, tiled=True)  21.3 us
    ppermute x1, waiting for transfers between devices, local(): near = lax.ppermute(turned, 'zl', SWAP)  19.9 us
    all_to_all x2, waiting for transfers between devices, gathered(): lax.all_to_all(part.reshape(4, 2 * rows, part_rows), 'y', 0, 0, tiled=True)  19.5 us
    ppermute x7, starting transfers between devices, to_pair(): return lax.ppermute(x, 'zh', SWAP)  16.8 us
  transfers between devices with their start and end apart: 29, of which 7 were waited for; matrix products, arithmetic and copies ran while one was open for 11% of the time, Pallas kernels for 16%

profile of v6, /device:TPU:0, one launch (start us, length us, event | category | flops | bytes accessed | tf_op | source)
XLA Modules:
  0.0 292.5 jit_solution(13590065213737411150)
XLA Ops:
  0.6 1.1 broadcast_in_dim.24
  1.8 21.3 %all_to_all.20 = bf16[8,128,512]{2,1,0:T(8,128)(2,1)S(1)} all-to-all(bf16[8,128,512]{2,1,0:T(8,128)(2,1)S(1)} %broadcast_in_dim.24), channel_id=1, replica_groups=mesh['y'=4,'zh'=2,'zl'=2,'x'=4,'core'=2] {'zl','x'}, dimensions={0} | all-to-all | bytes 2097152 | tf_op jit(solution)/shard_map/all_to_all | solution.py:33
  23.1 2.6 convolution_convert_fusion
  25.7 4.5 %all-to-all-start.2 = ((bf16[4,256,1024]{2,1,0:T(8,128)(2,1)}), bf16[4,256,1024]{2,1,0:T(8,128)(2,1)S(1)}, u32[]{:S(2)}, u32[]{:S(2)}) async-start(bf16[4,256,1024]{2,1,0:T(8,128)(2,1)} %bitcast.10), calls=%async_computation.2 | async-start | bytes 4194304 | tf_op jit(solution)/shard_map/all_to_all | solution.py:199
  30.1 1.9 constant_dynamic-update-slice_fusion.1
  32.0 3.8 %convolution_convert_fusion.1 = bf16[1024,1024]{1,0:T(8,128)(2,1)} fusion(bf16[1024,512]{1,0:T(8,128)(2,1)S(1)} %bitcast.12, bf16[2048,512]{1,0:T(8,128)(2,1)} %param.13), kind=kOutput, calls=%fused_computation.7 | convolution fusion | flops 1074790400 | bytes 4194304 | tf_op jit(solution)/shard_map/dot_general | solution.py:47
  35.8 19.5 %all-to-all-done.2 = bf16[4,256,1024]{2,1,0:T(8,128)(2,1)S(1)} async-done(((bf16[4,256,1024]{2,1,0:T(8,128)(2,1)}), bf16[4,256,1024]{2,1,0:T(8,128)(2,1)S(1)}, u32[]{:S(2)}, u32[]{:S(2)}) %all-to-all-start.2) | async-done | bytes 2097184 | tf_op jit(solution)/shard_map/all_to_all | solution.py:199
  55.3 1.3 copy-done.2
  56.6 3.6 %all-to-all-start.1 = ((bf16[4,256,1024]{2,1,0:T(8,128)(2,1)}), bf16[4,256,1024]{2,1,0:T(8,128)(2,1)S(1)}, u32[]{:S(2)}, u32[]{:S(2)}) async-start(bf16[4,256,1024]{2,1,0:T(8,128)(2,1)} %bitcast.9), calls=%async_computation.1 | async-start | bytes 4194304 | tf_op jit(solution)/shard_map/all_to_all | solution.py:199
  60.3 0.8 constant_dynamic-update-slice_fusion.refs_0_.refs_2_
  61.1 2.0 collective-permute-start.5
  63.1 1.3 collective-permute-start.8
  64.3 3.6 %collective-permute-start.13 = (bf16[256,2048]{1,0:T(8,128)(2,1)}, bf16[256,2048]{1,0:T(8,128)(2,1)}, u32[]{:S(2)}, u32[]{:S(2)}) collective-permute-start(bf16[256,2048]{1,0:T(8,128)(2,1)} %constant_dynamic-update-slice_fusion.refs_0_.refs_2_), channel_id=1, source_target_pairs={{0,16},{16,0},{1,17},{17,1},{2,18},{18,2},{3,19},{19,3},{4,20},{20... | collective-permute-start | bytes 3145736 | tf_op jit(solution)/shard_map/ppermute | solution.py:29
  67.9 38.9 %collective-permute-done.5.refs_0_.refs_2_ = bf16[256,2048]{1,0:T(8,128)(2,1)} collective-permute-done((bf16[256,2048]{1,0:T(8,128)(2,1)}, bf16[256,2048]{1,0:T(8,128)(2,1)}, u32[]{:S(2)}, u32[]{:S(2)}) %collective-permute-start.5) | collective-permute-done | bytes 1048608 | tf_op jit(solution)/shard_map/ppermute | solution.py:25
  106.8 3.6 %collective-permute-start.12 = (bf16[256,2048]{1,0:T(8,128)(2,1)}, bf16[256,2048]{1,0:T(8,128)(2,1)}, u32[]{:S(2)}, u32[]{:S(2)}) collective-permute-start(bf16[256,2048]{1,0:T(8,128)(2,1)} %collective-permute-done.5.refs_0_.refs_2_), channel_id=1, source_target_pairs={{0,16},{16,0},{1,17},{17,1},{2,18},{18,2},{3,19},{19,3},{4,20},{20... | collective-permute-start | bytes 3145736 | tf_op jit(solution)/shard_map/ppermute | solution.py:29
  110.4 1.9 slice.35
  112.3 0.9 collective-permute-start.9
  113.2 0.1 copy.22
  113.4 2.1 convert_reduce_fusion
  115.5 0.9 convert_element_type.69
  116.4 1.1 collective-permute-start.18
  117.5 19.9 %collective-permute-done.14 = bf16[512,128]{1,0:T(8,128)(2,1)S(1)} collective-permute-done((bf16[512,128]{1,0:T(8,128)(2,1)S(1)}, bf16[512,128]{1,0:T(8,128)(2,1)S(1)}, u32[]{:S(2)}, u32[]{:S(2)}) %collective-permute-start.14) | collective-permute-done | bytes 131104 | tf_op jit(solution)/shard_map/ppermute | solution.py:209
  137.4 1.2 collective-permute-start.11
  138.6 1.9 slice.34
  140.5 0.4 convert_reduce_fusion.1
  140.9 2.5 collective-permute-start
  143.4 5.4 %collective-permute-done.18 = bf16[256,1024]{1,0:T(8,128)(2,1)} collective-permute-done((bf16[256,1024]{1,0:T(8,128)(2,1)}, bf16[256,1024]{1,0:T(8,128)(2,1)}, u32[]{:S(2)}, u32[]{:S(2)}) %collective-permute-start.18) | collective-permute-done | bytes 524320 | tf_op jit(solution)/shard_map/ppermute | solution.py:29
  148.8 3.5 %collective-permute-start.10 = (bf16[128,2048]{1,0:T(8,128)(2,1)}, bf16[128,2048]{1,0:T(8,128)(2,1)}, u32[]{:S(2)}, u32[]{:S(2)}) collective-permute-start(bf16[128,2048]{1,0:T(8,128)(2,1)} %collective-permute-done.9.refs_2_), channel_id=1, source_target_pairs={{0,16},{16,0},{1,17},{17,1},{2,18},{18,2},{3,19},{19,3},{4,20},{20... | collective-permute-start | bytes 1572872 | tf_op jit(solution)/shard_map/ppermute | solution.py:29
  152.3 1.2 add_convert_fusion.3.refs_0_
  153.5 1.4 collective-permute-start.7
  155.0 27.4 %collective-permute-done = bf16[256,1024]{1,0:T(8,128)(2,1)S(1)} collective-permute-done((bf16[256,1024]{1,0:T(8,128)(2,1)S(1)}, bf16[256,1024]{1,0:T(8,128)(2,1)S(1)}, u32[]{:S(2)}, u32[]{:S(2)}) %collective-permute-start) | collective-permute-done | bytes 524320 | tf_op jit(solution)/shard_map/ppermute | solution.py:29
  182.4 0.9 collective-permute-start.19
  183.3 0.2 add_convert_fusion.4.refs_0_
  183.5 1.2 collective-permute-start.2
  184.7 9.0 %collective-permute-done.10.refs_3_ = bf16[128,2048]{1,0:T(8,128)(2,1)} collective-permute-done((bf16[128,2048]{1,0:T(8,128)(2,1)}, bf16[128,2048]{1,0:T(8,128)(2,1)}, u32[]{:S(2)}, u32[]{:S(2)}) %collective-permute-start.10) | collective-permute-done | bytes 524320 | tf_op jit(solution)/shard_map/ppermute | solution.py:29
  193.7 0.9 collective-permute-start.1
  194.6 0.5 compare_select_fusion.7.spots
  195.2 0.9 pad_maximum_fusion.refs_9_
  196.1 5.7 %shard_map.102 = (bf16[1024,2048]{1,0:T(8,128)(2,1)}, f32[1024,2048]{1,0:T(8,128)}, f32[1024,2048]{1,0:T(8,128)}) custom-call(s32[14]{0:T(128)} %compare_select_fusion.7.spots, bf16[256,2048]{1,0:T(8,128)(2,1)} %constant_dynamic-update-slice_fusion.refs_0_.refs_2_, bf16[256,2048]{1,0:T(8,128)(2,1)} %collective-permute-done.13.refs_1_.refs_3_, ...), custom_call_target="tpu_custom_call" | custom-call | flops 5242880 | bytes 7340032 | tf_op jit(solution)/shard_map/pallas_call | solution.py:79
  201.8 5.6 %shard_map.103 = (bf16[1024,2048]{1,0:T(8,128)(2,1)}, f32[1024,2048]{1,0:T(8,128)}, f32[1024,2048]{1,0:T(8,128)}) custom-call(s32[14]{0:T(128)} %compare_select_fusion.7.spots, bf16[256,2048]{1,0:T(8,128)(2,1)} %collective-permute-done.5.refs_0_.refs_2_, ...), custom_call_target="tpu_custom_call", output_to_operand_aliasing={{0}: (5, {}), {1}: (6, {}), {2}: (7, {})} | custom-call | flops 5242880 | bytes 7340032 | tf_op jit(solution)/shard_map/pallas_call | solution.py:79
  207.5 5.7 %shard_map.104 = (bf16[1024,2048]{1,0:T(8,128)(2,1)}, f32[1024,2048]{1,0:T(8,128)}, f32[1024,2048]{1,0:T(8,128)}) custom-call(s32[14]{0:T(128)} %compare_select_fusion.7.spots, bf16[256,2048]{1,0:T(8,128)(2,1)} %collective-permute-done.8.refs_0_.refs_2_, ...), custom_call_target="tpu_custom_call", output_to_operand_aliasing={{0}: (5, {}), {1}: (6, {}), {2}: (7, {})} | custom-call | flops 5242880 | bytes 7340032 | tf_op jit(solution)/shard_map/pallas_call | solution.py:79
  213.1 0.6 collective-permute-start.15
  213.7 5.7 %shard_map.105 = (bf16[1024,2048]{1,0:T(8,128)(2,1)}, f32[1024,2048]{1,0:T(8,128)}, f32[1024,2048]{1,0:T(8,128)}) custom-call(s32[14]{0:T(128)} %compare_select_fusion.7.spots, bf16[128,2048]{1,0:T(8,128)(2,1)} %collective-permute-done.6.refs_0_, ...), custom_call_target="tpu_custom_call", output_to_operand_aliasing={{0}: (5, {}), {1}: (6, {}), {2}: (7, {})} | custom-call | flops 5242880 | bytes 7340032 | tf_op jit(solution)/shard_map/pallas_call | solution.py:79
  219.4 2.6 collective-permute-start.16
  222.2 1.4 collective-permute-start.21
  223.5 2.1 collective-permute-start.22
  225.7 6.2 %multiply_convert_fusion = bf16[2048,512]{1,0:T(8,128)(2,1)} fusion(bf16[1024,2048]{1,0:T(8,128)(2,1)} %get-tuple-element.39, bf16[1024,512]{1,0:T(8,128)(2,1)} %bitcast.13), kind=kOutput, calls=%fused_computation.1 | convolution fusion | flops 2149580800 | bytes 7340032 | tf_op jit(solution)/shard_map/dot_general | solution.py:43
  231.9 0.7 slice.32
  232.9 0.6 copy-done.10
  233.5 2.7 collective-permute-start.4
  236.2 0.7 copy-done.16
  236.9 0.7 copy-done.17
  237.6 12.1 %shard_map.106 = (bf16[512,2048]{1,0:T(8,128)(2,1)}, bf16[512,2048]{1,0:T(8,128)(2,1)}, f32[1024,512]{1,0:T(8,128)}) custom-call(s32[14]{0:T(128)} %compare_select_fusion.7.spots, bf16[256,1024]{1,0:T(8,128)(2,1)} %copy-done.5, bf16[256,1024]{1,0:T(8,128)(2,1)} %copy-done.9, bf16[256,1024]{1,0:T(8,128)(2,1)} %copy-done.8, bf16[128,1024]{1,0:T(8,128)(2,1)} %copy-done.16, ...), custom_call_target="tpu_custom_call" | custom-call | flops 4294967296 | bytes 14680064 | tf_op jit(solution)/shard_map/pallas_call | solution.py:144
  249.8 0.7 copy-done.14
  250.5 0.1 copy-done.15
  250.6 12.5 %shard_map.107 = (bf16[512,2048]{1,0:T(8,128)(2,1)}, bf16[512,2048]{1,0:T(8,128)(2,1)}, bf16[1024,512]{1,0:T(8,128)(2,1)}) custom-call(s32[14]{0:T(128)} %compare_select_fusion.7.spots, bf16[256,1024]{1,0:T(8,128)(2,1)} %copy-done.4, bf16[256,1024]{1,0:T(8,128)(2,1)} %copy-done.7, ...), custom_call_target="tpu_custom_call", output_to_operand_aliasing={{0}: (15, {}), {1}: (16, {})} | custom-call | flops 4294967296 | bytes 14680064 | tf_op jit(solution)/shard_map/pallas_call | solution.py:144
  263.1 0.1 collective-permute-start.24
  263.2 0.5 collective-permute-start.23
  263.7 4.5 %all-to-all-start.3 = ((bf16[8,128,512]{2,1,0:T(8,128)(2,1)}), bf16[8,128,512]{2,1,0:T(8,128)(2,1)S(1)}, u32[]{:S(2)}, u32[]{:S(2)}) async-start(bf16[8,128,512]{2,1,0:T(8,128)(2,1)} %bitcast.14), calls=%async_computation.3 | async-start | bytes 2097152 | tf_op jit(solution)/shard_map/all_to_all | solution.py:33
  268.2 4.3 %add_convert_fusion = bf16[2048,512]{1,0:T(8,128)(2,1)} fusion(bf16[2048,512]{1,0:T(8,128)(2,1)} %collective-permute-done.25, bf16[2048,512]{1,0:T(8,128)(2,1)} %multiply_convert_fusion), kind=kLoop, calls=%fused_computation | loop fusion | flops 4194304 | bytes 6291456 | tf_op jit(solution)/shard_map/convert_element_type | solution.py:217
  272.5 11.7 %all-to-all-done.3 = bf16[8,128,512]{2,1,0:T(8,128)(2,1)S(1)} async-done(((bf16[8,128,512]{2,1,0:T(8,128)(2,1)}), bf16[8,128,512]{2,1,0:T(8,128)(2,1)S(1)}, u32[]{:S(2)}, u32[]{:S(2)}) %all-to-all-start.3) | async-done | bytes 1048608 | tf_op jit(solution)/shard_map/all_to_all | solution.py:33
  284.2 0.8 reduce_sum.32
  285.0 3.8 %add_convert_fusion.1 = bf16[512,2048]{1,0:T(8,128)(2,1)} fusion(bf16[512,2048]{1,0:T(8,128)(2,1)} %collective-permute-done.24, bf16[512,2048]{1,0:T(8,128)(2,1)S(1)} %copy-done.1), kind=kLoop, calls=%fused_computation.2 | loop fusion | flops 4194304 | bytes 6291456 | tf_op jit(solution)/shard_map/convert_element_type | solution.py:217
  288.8 3.7 %add_convert_fusion.2 = bf16[512,2048]{1,0:T(8,128)(2,1)} fusion(bf16[512,2048]{1,0:T(8,128)(2,1)} %collective-permute-done.23, bf16[512,2048]{1,0:T(8,128)(2,1)S(1)} %copy-done), kind=kLoop, calls=%fused_computation.3 | loop fusion | flops 4194304 | bytes 6291456 | tf_op jit(solution)/shard_map/convert_element_type | solution.py:217
  (68 shorter events, 0.6 us)
Async XLA Ops:
  0.6 22.4 %copy-start.20 = (bf16[2048,512]{1,0:T(8,128)(2,1)S(1)}, bf16[2048,512]{1,0:T(8,128)(2,1)}, u32[]{:S(2)}) copy-start(bf16[2048,512]{1,0:T(8,128)(2,1)} %param.13) | copy-start | bytes 6291460
  23.0 9.0 %copy-start.12 = (bf16[8,128,512]{2,1,0:T(8,128)(2,1)}, bf16[8,128,512]{2,1,0:T(8,128)(2,1)S(1)}, u32[]{:S(2)}) copy-start(bf16[8,128,512]{2,1,0:T(8,128)(2,1)S(1)} %all_to_all.20) | copy-start | bytes 3145732
  25.7 29.7 %all-to-all-start.2 = ((bf16[4,256,1024]{2,1,0:T(8,128)(2,1)}), bf16[4,256,1024]{2,1,0:T(8,128)(2,1)S(1)}, u32[]{:S(2)}, u32[]{:S(2)}) async-start(bf16[4,256,1024]{2,1,0:T(8,128)(2,1)} %bitcast.10), calls=%async_computation.2 | async-start | bytes 4194304 | tf_op jit(solution)/shard_map/all_to_all | solution.py:199
  55.3 1.3 copy-start.2
  55.3 4.9 %copy-start.13 = (bf16[128,2048]{1,0:T(8,128)(2,1)S(1)}, bf16[128,2048]{1,0:T(8,128)(2,1)}, u32[]{:S(2)}) copy-start(bf16[128,2048]{1,0:T(8,128)(2,1)} %param.10) | copy-start | bytes 1572868
  56.6 83.8 %all-to-all-start.1 = ((bf16[4,256,1024]{2,1,0:T(8,128)(2,1)}), bf16[4,256,1024]{2,1,0:T(8,128)(2,1)S(1)}, u32[]{:S(2)}, u32[]{:S(2)}) async-start(bf16[4,256,1024]{2,1,0:T(8,128)(2,1)} %bitcast.9), calls=%async_computation.1 | async-start | bytes 4194304 | tf_op jit(solution)/shard_map/all_to_all | solution.py:199
  60.3 53.0 %copy-start.18 = (bf16[128,512]{1,0:T(8,128)(2,1)S(1)}, bf16[128,512]{1,0:T(8,128)(2,1)}, u32[]{:S(2)}) copy-start(bf16[128,512]{1,0:T(8,128)(2,1)} %param.7) | copy-start | bytes 393220
  61.1 45.7 %collective-permute-start.5 = (bf16[256,2048]{1,0:T(8,128)(2,1)}, bf16[256,2048]{1,0:T(8,128)(2,1)}, u32[]{:S(2)}, u32[]{:S(2)}) collective-permute-start(bf16[256,2048]{1,0:T(8,128)(2,1)} %constant_dynamic-update-slice_fusion.refs_0_.refs_2_), channel_id=1, source_target_pairs={{0,32},{32,64},{64,96},{96,0},{1,33},{33,65},{65,97},{97,1},{2,34}... | collective-permute-start | bytes 3145736 | tf_op jit(solution)/shard_map/ppermute | solution.py:25
  63.1 47.4 %collective-permute-start.8 = (bf16[256,2048]{1,0:T(8,128)(2,1)}, bf16[256,2048]{1,0:T(8,128)(2,1)}, u32[]{:S(2)}, u32[]{:S(2)}) collective-permute-start(bf16[256,2048]{1,0:T(8,128)(2,1)} %constant_dynamic-update-slice_fusion.refs_0_.refs_2_), channel_id=1, source_target_pairs={{0,96},{32,0},{64,32},{96,64},{1,97},{33,1},{65,33},{97,65},{2,98}... | collective-permute-start | bytes 3145736 | tf_op jit(solution)/shard_map/ppermute | solution.py:25
  64.3 76.1 %collective-permute-start.13 = (bf16[256,2048]{1,0:T(8,128)(2,1)}, bf16[256,2048]{1,0:T(8,128)(2,1)}, u32[]{:S(2)}, u32[]{:S(2)}) collective-permute-start(bf16[256,2048]{1,0:T(8,128)(2,1)} %constant_dynamic-update-slice_fusion.refs_0_.refs_2_), channel_id=1, source_target_pairs={{0,16},{16,0},{1,17},{17,1},{2,18},{18,2},{3,19},{19,3},{4,20},{20... | collective-permute-start | bytes 3145736 | tf_op jit(solution)/shard_map/ppermute | solution.py:29
  106.8 48.1 %collective-permute-start.12 = (bf16[256,2048]{1,0:T(8,128)(2,1)}, bf16[256,2048]{1,0:T(8,128)(2,1)}, u32[]{:S(2)}, u32[]{:S(2)}) collective-permute-start(bf16[256,2048]{1,0:T(8,128)(2,1)} %collective-permute-done.5.refs_0_.refs_2_), channel_id=1, source_target_pairs={{0,16},{16,0},{1,17},{17,1},{2,18},{18,2},{3,19},{19,3},{4,20},{20... | collective-permute-start | bytes 3145736 | tf_op jit(solution)/shard_map/ppermute | solution.py:29
  112.3 28.6 %collective-permute-start.9 = (bf16[128,2048]{1,0:T(8,128)(2,1)}, bf16[128,2048]{1,0:T(8,128)(2,1)}, u32[]{:S(2)}, u32[]{:S(2)}) collective-permute-start(bf16[128,2048]{1,0:T(8,128)(2,1)} %slice.35), channel_id=1, source_target_pairs={{0,96},{32,0},{64,32},{96,64},{1,97},{33,1},{65,33},{97,65},{2,98}... | collective-permute-start | bytes 1572872 | tf_op jit(solution)/shard_map/ppermute | solution.py:25
  113.3 24.1 %collective-permute-start.14 = (bf16[512,128]{1,0:T(8,128)(2,1)S(1)}, bf16[512,128]{1,0:T(8,128)(2,1)S(1)}, u32[]{:S(2)}, u32[]{:S(2)}) collective-permute-start(bf16[512,128]{1,0:T(8,128)(2,1)S(1)} %bitcast.15), channel_id=1, source_target_pairs={{0,8},{8,0},{1,9},{9,1},{2,10},{10,2},{3,11},{11,3},{4,12},{12,4},... | collective-permute-start | bytes 393224 | tf_op jit(solution)/shard_map/ppermute | solution.py:209
  116.4 32.4 %collective-permute-start.18 = (bf16[256,1024]{1,0:T(8,128)(2,1)}, bf16[256,1024]{1,0:T(8,128)(2,1)}, u32[]{:S(2)}, u32[]{:S(2)}) collective-permute-start(bf16[256,1024]{1,0:T(8,128)(2,1)} %convert_element_type.69), channel_id=1, source_target_pairs={{0,16},{16,0},{1,17},{17,1},{2,18},{18,2},{3,19},{19,3},{4,20},{20... | collective-permute-start | bytes 1572872 | tf_op jit(solution)/shard_map/ppermute | solution.py:29
  137.4 3.4 %copy-start.19 = (bf16[512,128]{1,0:T(8,128)(2,1)}, bf16[512,128]{1,0:T(8,128)(2,1)S(1)}, u32[]{:S(2)}) copy-start(bf16[512,128]{1,0:T(8,128)(2,1)S(1)} %collective-permute-done.14) | copy-start | bytes 393220
  137.4 46.1 %collective-permute-start.11 = (bf16[256,2048]{1,0:T(8,128)(2,1)}, bf16[256,2048]{1,0:T(8,128)(2,1)}, u32[]{:S(2)}, u32[]{:S(2)}) collective-permute-start(bf16[256,2048]{1,0:T(8,128)(2,1)} %collective-permute-done.8.refs_0_.refs_2_), channel_id=1, source_target_pairs={{0,16},{16,0},{1,17},{17,1},{2,18},{18,2},{3,19},{19,3},{4,20},{20... | collective-permute-start | bytes 3145736 | tf_op jit(solution)/shard_map/ppermute | solution.py:29
  140.4 13.1 %collective-permute-start.6 = (bf16[128,2048]{1,0:T(8,128)(2,1)}, bf16[128,2048]{1,0:T(8,128)(2,1)}, u32[]{:S(2)}, u32[]{:S(2)}) collective-permute-start(bf16[128,2048]{1,0:T(8,128)(2,1)} %slice.34), channel_id=1, source_target_pairs={{0,32},{32,64},{64,96},{96,0},{1,33},{33,65},{65,97},{97,1},{2,34}... | collective-permute-start | bytes 1572872 | tf_op jit(solution)/shard_map/ppermute | solution.py:25
  140.9 41.5 %collective-permute-start = (bf16[256,1024]{1,0:T(8,128)(2,1)S(1)}, bf16[256,1024]{1,0:T(8,128)(2,1)S(1)}, u32[]{:S(2)}, u32[]{:S(2)}) collective-permute-start(bf16[256,1024]{1,0:T(8,128)(2,1)S(1)} %convert_element_type.64), channel_id=1, source_target_pairs={{0,16},{16,0},{1,17},{17,1},{2,18},{18,2},{3,19},{19,3},{4,20},{20... | collective-permute-start | bytes 1572872 | tf_op jit(solution)/shard_map/ppermute | solution.py:29
  148.8 44.9 %collective-permute-start.10 = (bf16[128,2048]{1,0:T(8,128)(2,1)}, bf16[128,2048]{1,0:T(8,128)(2,1)}, u32[]{:S(2)}, u32[]{:S(2)}) collective-permute-start(bf16[128,2048]{1,0:T(8,128)(2,1)} %collective-permute-done.9.refs_2_), channel_id=1, source_target_pairs={{0,16},{16,0},{1,17},{17,1},{2,18},{18,2},{3,19},{19,3},{4,20},{20... | collective-permute-start | bytes 1572872 | tf_op jit(solution)/shard_map/ppermute | solution.py:29
  153.5 48.3 %copy-start.5 = (bf16[256,1024]{1,0:T(8,128)(2,1)}, bf16[256,1024]{1,0:T(8,128)(2,1)S(1)}, u32[]{:S(2)}) copy-start(bf16[256,1024]{1,0:T(8,128)(2,1)S(1)} %add_convert_fusion.3.refs_0_) | copy-start | bytes 1572868
  153.5 59.6 %collective-permute-start.7 = (bf16[128,2048]{1,0:T(8,128)(2,1)}, bf16[128,2048]{1,0:T(8,128)(2,1)}, u32[]{:S(2)}, u32[]{:S(2)}) collective-permute-start(bf16[128,2048]{1,0:T(8,128)(2,1)} %collective-permute-done.6.refs_0_), channel_id=1, source_target_pairs={{0,16},{16,0},{1,17},{17,1},{2,18},{18,2},{3,19},{19,3},{4,20},{20... | collective-permute-start | bytes 1572872 | tf_op jit(solution)/shard_map/ppermute | solution.py:29
  155.0 64.4 %collective-permute-start.20 = (bf16[256,1024]{1,0:T(8,128)(2,1)S(1)}, bf16[256,1024]{1,0:T(8,128)(2,1)S(1)}, u32[]{:S(2)}, u32[]{:S(2)}) collective-permute-start(bf16[256,1024]{1,0:T(8,128)(2,1)S(1)} %add_convert_fusion.3.refs_0_), channel_id=1, source_target_pairs={{0,32},{32,64},{64,96},{96,0},{1,33},{33,65},{65,97},{97,1},{2,34}... | collective-permute-start | bytes 1572872 | tf_op jit(solution)/shard_map/ppermute | solution.py:25
  182.4 39.6 %collective-permute-start.19 = (bf16[256,1024]{1,0:T(8,128)(2,1)S(1)}, bf16[256,1024]{1,0:T(8,128)(2,1)S(1)}, u32[]{:S(2)}, u32[]{:S(2)}) collective-permute-start(bf16[256,1024]{1,0:T(8,128)(2,1)S(1)} %add_convert_fusion.3.refs_0_), channel_id=1, source_target_pairs={{0,96},{32,0},{64,32},{96,64},{1,97},{33,1},{65,33},{97,65},{2,98}... | collective-permute-start | bytes 1572872 | tf_op jit(solution)/shard_map/ppermute | solution.py:25
  183.5 18.3 %copy-start.4 = (bf16[256,1024]{1,0:T(8,128)(2,1)}, bf16[256,1024]{1,0:T(8,128)(2,1)S(1)}, u32[]{:S(2)}) copy-start(bf16[256,1024]{1,0:T(8,128)(2,1)S(1)} %add_convert_fusion.4.refs_0_) | copy-start | bytes 1572868
  183.5 38.7 %collective-permute-start.2 = (bf16[256,1024]{1,0:T(8,128)(2,1)S(1)}, bf16[256,1024]{1,0:T(8,128)(2,1)S(1)}, u32[]{:S(2)}, u32[]{:S(2)}) collective-permute-start(bf16[256,1024]{1,0:T(8,128)(2,1)S(1)} %add_convert_fusion.4.refs_0_), channel_id=1, source_target_pairs={{0,32},{32,64},{64,96},{96,0},{1,33},{33,65},{65,97},{97,1},{2,34}... | collective-permute-start | bytes 1572872 | tf_op jit(solution)/shard_map/ppermute | solution.py:25
  193.7 29.8 %collective-permute-start.1 = (bf16[256,1024]{1,0:T(8,128)(2,1)S(1)}, bf16[256,1024]{1,0:T(8,128)(2,1)S(1)}, u32[]{:S(2)}, u32[]{:S(2)}) collective-permute-start(bf16[256,1024]{1,0:T(8,128)(2,1)S(1)} %add_convert_fusion.4.refs_0_), channel_id=1, source_target_pairs={{0,96},{32,0},{64,32},{96,64},{1,97},{33,1},{65,33},{97,65},{2,98}... | collective-permute-start | bytes 1572872 | tf_op jit(solution)/shard_map/ppermute | solution.py:25
  196.1 25.9 %copy-start.3 = (bf16[1024,128]{1,0:T(8,128)(2,1)}, bf16[1024,128]{1,0:T(8,128)(2,1)S(1)}, u32[]{:S(2)}) copy-start(bf16[1024,128]{1,0:T(8,128)(2,1)S(1)} %pad_maximum_fusion.refs_9_) | copy-start | bytes 786436
  213.1 19.5 %collective-permute-start.15 = (bf16[1024,128]{1,0:T(8,128)(2,1)S(1)}, bf16[1024,128]{1,0:T(8,128)(2,1)}, u32[]{:S(2)}, u32[]{:S(2)}) collective-permute-start(bf16[1024,128]{1,0:T(8,128)(2,1)S(1)} %pad_maximum_fusion.refs_9_), channel_id=1, source_target_pairs={{0,6},{2,0},{4,2},{6,4},{1,7},{3,1},{5,3},{7,5},{8,14},{10,8},{12,... | collective-permute-start | bytes 786440 | tf_op jit(solution)/shard_map/ppermute | solution.py:213
  219.4 12.5 %copy-start.8 = (bf16[256,1024]{1,0:T(8,128)(2,1)}, bf16[256,1024]{1,0:T(8,128)(2,1)S(1)}, u32[]{:S(2)}) copy-start(bf16[256,1024]{1,0:T(8,128)(2,1)S(1)} %collective-permute-done.20.refs_2_) | copy-start | bytes 1572868
  219.4 13.4 %collective-permute-start.16 = (bf16[1024,128]{1,0:T(8,128)(2,1)S(1)}, bf16[1024,128]{1,0:T(8,128)(2,1)S(1)}, u32[]{:S(2)}, u32[]{:S(2)}) collective-permute-start(bf16[1024,128]{1,0:T(8,128)(2,1)S(1)} %pad_maximum_fusion.refs_9_), channel_id=1, source_target_pairs={{0,4},{2,6},{4,0},{6,2},{1,5},{3,7},{5,1},{7,3},{8,12},{10,14},{12... | collective-permute-start | bytes 786440 | tf_op jit(solution)/shard_map/ppermute | solution.py:213
  222.0 9.9 %copy-start.9 = (bf16[256,1024]{1,0:T(8,128)(2,1)}, bf16[256,1024]{1,0:T(8,128)(2,1)S(1)}, u32[]{:S(2)}) copy-start(bf16[256,1024]{1,0:T(8,128)(2,1)S(1)} %collective-permute-done.19.refs_1_) | copy-start | bytes 1572868
  222.0 10.8 %collective-permute-start.17 = (bf16[1024,128]{1,0:T(8,128)(2,1)S(1)}, bf16[1024,128]{1,0:T(8,128)(2,1)S(1)}, u32[]{:S(2)}, u32[]{:S(2)}) collective-permute-start(bf16[1024,128]{1,0:T(8,128)(2,1)S(1)} %pad_maximum_fusion.refs_9_), channel_id=1, source_target_pairs={{0,2},{2,4},{4,6},{6,0},{1,3},{3,5},{5,7},{7,1},{8,10},{10,12},{12... | collective-permute-start | bytes 786440 | tf_op jit(solution)/shard_map/ppermute | solution.py:213
  222.2 9.7 %copy-start.6 = (bf16[256,1024]{1,0:T(8,128)(2,1)}, bf16[256,1024]{1,0:T(8,128)(2,1)S(1)}, u32[]{:S(2)}) copy-start(bf16[256,1024]{1,0:T(8,128)(2,1)S(1)} %collective-permute-done.2.refs_2_) | copy-start | bytes 1572868
  222.2 14.0 %collective-permute-start.21 = (bf16[128,1024]{1,0:T(8,128)(2,1)S(1)}, bf16[128,1024]{1,0:T(8,128)(2,1)S(1)}, u32[]{:S(2)}, u32[]{:S(2)}) collective-permute-start(bf16[128,1024]{1,0:T(8,128)(2,1)S(1)} %slice.36), channel_id=1, source_target_pairs={{0,32},{32,64},{64,96},{96,0},{1,33},{33,65},{65,97},{97,1},{2,34}... | collective-permute-start | bytes 786440 | tf_op jit(solution)/shard_map/ppermute | solution.py:25
  223.5 9.1 %copy-start.7 = (bf16[256,1024]{1,0:T(8,128)(2,1)}, bf16[256,1024]{1,0:T(8,128)(2,1)S(1)}, u32[]{:S(2)}) copy-start(bf16[256,1024]{1,0:T(8,128)(2,1)S(1)} %collective-permute-done.1.refs_1_) | copy-start | bytes 1572868
  223.5 12.6 %collective-permute-start.22 = (bf16[128,1024]{1,0:T(8,128)(2,1)S(1)}, bf16[128,1024]{1,0:T(8,128)(2,1)S(1)}, u32[]{:S(2)}, u32[]{:S(2)}) collective-permute-start(bf16[128,1024]{1,0:T(8,128)(2,1)S(1)} %slice.37), channel_id=1, source_target_pairs={{0,96},{32,0},{64,32},{96,64},{1,97},{33,1},{65,33},{97,65},{2,98}... | collective-permute-start | bytes 786440 | tf_op jit(solution)/shard_map/ppermute | solution.py:25
  232.7 35.6 %collective-permute-start.25 = (bf16[2048,512]{1,0:T(8,128)(2,1)}, bf16[2048,512]{1,0:T(8,128)(2,1)}, u32[]{:S(2)}, u32[]{:S(2)}) collective-permute-start(bf16[2048,512]{1,0:T(8,128)(2,1)} %multiply_convert_fusion), channel_id=1, source_target_pairs={{0,1},{1,0},{2,3},{3,2},{4,5},{5,4},{6,7},{7,6},{8,9},{9,8},{10,11... | collective-permute-start | bytes 6291464 | tf_op jit(solution)/shard_map/ppermute | solution.py:216
  232.8 0.7 copy-start.10
  232.8 17.0 %collective-permute-start.3 = (bf16[128,1024]{1,0:T(8,128)(2,1)}, bf16[128,1024]{1,0:T(8,128)(2,1)S(1)}, u32[]{:S(2)}, u32[]{:S(2)}) collective-permute-start(bf16[128,1024]{1,0:T(8,128)(2,1)} %slice.32), channel_id=1, source_target_pairs={{0,32},{32,64},{64,96},{96,0},{1,33},{33,65},{65,97},{97,1},{2,34}... | collective-permute-start | bytes 786440 | tf_op jit(solution)/shard_map/ppermute | solution.py:25
  233.5 4.1 %copy-start.11 = (bf16[1024,128]{1,0:T(8,128)(2,1)}, bf16[1024,128]{1,0:T(8,128)(2,1)S(1)}, u32[]{:S(2)}) copy-start(bf16[1024,128]{1,0:T(8,128)(2,1)S(1)} %collective-permute-done.17.refs_12_) | copy-start | bytes 786436
  233.5 16.3 %collective-permute-start.4 = (bf16[128,1024]{1,0:T(8,128)(2,1)S(1)}, bf16[128,1024]{1,0:T(8,128)(2,1)S(1)}, u32[]{:S(2)}, u32[]{:S(2)}) collective-permute-start(bf16[128,1024]{1,0:T(8,128)(2,1)S(1)} %slice.33), channel_id=1, source_target_pairs={{0,96},{32,0},{64,32},{96,64},{1,97},{33,1},{65,33},{97,65},{2,98}... | collective-permute-start | bytes 786440 | tf_op jit(solution)/shard_map/ppermute | solution.py:25
  236.2 0.7 copy-start.16
  236.9 0.7 copy-start.17
  249.8 0.7 copy-start.14
  249.8 0.8 copy-start.15
  263.1 21.9 %collective-permute-start.24 = (bf16[512,2048]{1,0:T(8,128)(2,1)}, bf16[512,2048]{1,0:T(8,128)(2,1)}, u32[]{:S(2)}, u32[]{:S(2)}) collective-permute-start(bf16[512,2048]{1,0:T(8,128)(2,1)} %get-tuple-element.38), channel_id=1, source_target_pairs={{0,1},{1,0},{2,3},{3,2},{4,5},{5,4},{6,7},{7,6},{8,9},{9,8},{10,11... | collective-permute-start | bytes 6291464 | tf_op jit(solution)/shard_map/ppermute | solution.py:216
  263.2 25.6 %collective-permute-start.23 = (bf16[512,2048]{1,0:T(8,128)(2,1)}, bf16[512,2048]{1,0:T(8,128)(2,1)}, u32[]{:S(2)}, u32[]{:S(2)}) collective-permute-start(bf16[512,2048]{1,0:T(8,128)(2,1)} %get-tuple-element.37), channel_id=1, source_target_pairs={{0,1},{1,0},{2,3},{3,2},{4,5},{5,4},{6,7},{7,6},{8,9},{9,8},{10,11... | collective-permute-start | bytes 6291464 | tf_op jit(solution)/shard_map/ppermute | solution.py:216
  263.7 20.5 %all-to-all-start.3 = ((bf16[8,128,512]{2,1,0:T(8,128)(2,1)}), bf16[8,128,512]{2,1,0:T(8,128)(2,1)S(1)}, u32[]{:S(2)}, u32[]{:S(2)}) async-start(bf16[8,128,512]{2,1,0:T(8,128)(2,1)} %bitcast.14), calls=%async_computation.3 | async-start | bytes 2097152 | tf_op jit(solution)/shard_map/all_to_all | solution.py:33
  268.2 16.8 %copy-start.1 = (bf16[512,2048]{1,0:T(8,128)(2,1)S(1)}, bf16[512,2048]{1,0:T(8,128)(2,1)}, u32[]{:S(2)}) copy-start(bf16[512,2048]{1,0:T(8,128)(2,1)} %get-tuple-element.38) | copy-start | bytes 6291460
  285.0 3.8 %copy-start = (bf16[512,2048]{1,0:T(8,128)(2,1)S(1)}, bf16[512,2048]{1,0:T(8,128)(2,1)}, u32[]{:S(2)}) copy-start(bf16[512,2048]{1,0:T(8,128)(2,1)} %get-tuple-element.37) | copy-start | bytes 6291460

commit v7 on v6

--- a/solution.py
+++ b/solution.py
@@ -96,28 +96,39 @@
     )(spots, *gates, *ups, *before)
 
 
-def back_kernel(factor, first, spots, *refs):
-    ds, refs = refs[:5], refs[5:]
+def back_kernel(factor, far, *refs):
+    ds, refs = refs[:10], refs[10:]
     slope, active, w_gate, w_up = refs[:4]
     toks, refs = refs[4:8], refs[8:]
-    grad_gate, grad_up, back, both, weights, total, tokens = refs[-7:]
+    grad_gate, grad_up, back, both, weights, total, tokens = refs
     c = pl.program_id(0)
+    half = pl.num_programs(0) // 2
 
     @pl.when(c == 0)
     def _():
-        total[...] = jnp.zeros_like(total) if first else refs[0][...]
+        total[...] = jnp.zeros_like(total)
         depth, wide = tokens.shape[0], toks[0].shape[1]
         for m in range(4):
             for j in range(2):
-                here = pl.ds(pl.multiple_of(spots[6 + 2 * m + j] * wide, wide), wide)
+                here = pl.ds(pl.multiple_of(far[2 * m + j] * wide, wide), wide)
                 tokens[:, here] = toks[m][j * depth : (j + 1) * depth, :]
 
-    for ref, k, skip in zip(ds, (0, 1, 3, 2, 2), (0, 0, 0, 0, 1)):
-        d = ref[...].astype(F32)
-        rows = d.shape[0]
-        here = pl.ds(pl.multiple_of(spots[k] * ds[0].shape[0] + skip * rows, rows), rows)
-        both[here, :NARROW] = (d * slope[here, :]).astype(BF)
-        both[here, NARROW:] = (d * active[here, :]).astype(BF)
+    def scaled(parts):
+        for ref, k, skip in zip(parts, (0, 1, 3, 2, 2), (0, 0, 0, 0, 1)):
+            d = ref[...].astype(F32)
+            rows = d.shape[0]
+            here = pl.ds(pl.multiple_of(far[8 + k] * parts[0].shape[0] + skip * rows, rows), rows)
+            both[here, :NARROW] = (d * slope[here, :]).astype(BF)
+            both[here, NARROW:] = (d * active[here, :]).astype(BF)
+
+    @pl.when(c < half)
+    def _():
+        scaled(ds[:5])
+
+    @pl.when(c >= half)
+    def _():
+        scaled(ds[5:])
+
     weights[:, :NARROW] = w_gate[...]
     weights[:, NARROW:] = w_up[...]
     both_d = both[...]
@@ -131,30 +142,30 @@
         back[...] = total[...].astype(back.dtype)
 
 
-def back_of(spots, half, ds, slope, active, w_gate, w_up, toks, factor, before):
-    rows, part = ds[0].shape
+def back_of(far, halves, slope, active, w_gate, w_up, toks, factor):
     depth, width = w_gate.shape
-    total = 4 * rows
-    steps = part // NARROW
-    pieces = [pl.BlockSpec((d.shape[0], NARROW), lambda c, w: (0, c)) for d in ds]
-    weight = pl.BlockSpec((depth, NARROW), lambda c, w: (0, c + half * steps))
-    full = pl.BlockSpec((total, NARROW), lambda c, w: (0, c + half * steps))
+    total = slope.shape[0]
+    steps = width // NARROW
+    half = steps // 2
+    early = [pl.BlockSpec((d.shape[0], NARROW), lambda c, w: (0, jnp.minimum(c, half - 1))) for d in halves[0]]
+    late = [pl.BlockSpec((d.shape[0], NARROW), lambda c, w: (0, jnp.maximum(c - half, 0))) for d in halves[1]]
+    weight = pl.BlockSpec((depth, NARROW), lambda c, w: (0, c))
+    full = pl.BlockSpec((total, NARROW), lambda c, w: (0, c))
     whole = pl.BlockSpec((total, depth), lambda c, w: (0, 0))
-    kept = [whole] + [pl.BlockSpec(memory_space=pl.ANY)] * 2 if before else []
     return pl.pallas_call(
-        functools.partial(back_kernel, factor, not before),
+        functools.partial(back_kernel, factor),
         out_shape=(
             jax.ShapeDtypeStruct((depth, width), BF),
             jax.ShapeDtypeStruct((depth, width), BF),
-            jax.ShapeDtypeStruct((total, depth), BF if before else F32),
+            jax.ShapeDtypeStruct((total, depth), BF),
         ),
         grid_spec=pltpu.PrefetchScalarGridSpec(
             num_scalar_prefetch=1,
             grid=(steps,),
-            in_specs=pieces
+            in_specs=early
+            + late
             + [full, full, weight, weight]
-            + [pl.BlockSpec(t.shape, lambda c, w: (0, 0)) for t in toks]
-            + kept,
+            + [pl.BlockSpec(t.shape, lambda c, w: (0, 0)) for t in toks],
             out_specs=(weight, weight, whole),
             scratch_shapes=[
                 pltpu.VMEM((total, 2 * NARROW), BF),
@@ -163,11 +174,10 @@
                 pltpu.VMEM((depth, total), BF),
             ],
         ),
-        input_output_aliases={15: 0, 16: 1} if before else {},
         cost_estimate=pl.CostEstimate(
-            flops=8 * total * part * depth, bytes_accessed=total * part * 14, transcendentals=0
-        ),
-    )(spots, *ds, slope, active, w_gate, w_up, *toks, *before)
+            flops=8 * total * width * depth, bytes_accessed=total * width * 14, transcendentals=0
+        ),
+    )(far, *halves[0], *halves[1], slope, active, w_gate, w_up, *toks)
 
 
 def local(tokens, grad_out, gate_pre, up_pre, w_gate, w_up, w_down):
@@ -175,11 +185,11 @@
     factor = float(1.0 / np.sqrt(np.float32(16 * rows)))
     y, zh = lax.axis_index("y"), lax.axis_index("zh")
     x, zl = lax.axis_index("x"), lax.axis_index("zl")
-    p = lax.iota(jnp.int32, 14)
+    p = lax.iota(jnp.int32, 6)
     spots = jnp.where(p < 4, lax.rem(y + p, 4), jnp.where(p == 4, zh, 1 - zh))
-    m = p - 6
+    m = lax.iota(jnp.int32, 12)
     far = jnp.where(lax.rem(m, 2) == 0, zl, 1 - zl) * 4 + lax.rem(x + m // 2, 4)
-    spots = jnp.where(p < 6, spots, far)
+    far = jnp.where(m < 8, far, lax.rem(y + m, 4))
 
     out_all = gather_col(grad_out)
 
@@ -222,10 +232,7 @@
     hidden, slope, active = kept
     down = (inner_rows(hidden, out_all) * factor).astype(BF)
     grad_down = both_cores(down)
-    before = ()
-    for h in (0, 1):
-        gate, up, back = back_of(spots, h, halves[h], slope, active, w_gate, w_up, toks, factor, before)
-        before = (back, gate, up)
+    gate, up, back = back_of(far, halves, slope, active, w_gate, w_up, toks, factor)
     back_recv = across_col(back.reshape(8, rows, width))
     grad_gate = both_cores(gate)
     grad_up = both_cores(up)

time: 294 us -> 296 us (level)
  waiting for transfers between devices: 132 us -> 142 us
  Pallas kernels: 47.3 us -> 41.4 us
    ppermute x7, waiting for transfers between devices: 41.9 us -> 51 us  [to_pair(): return lax.ppermute(x, 'zh', SWAP)]
    pallas_call x2 -> x1, Pallas kernels: 24.7 us -> 18.6 us  [back_of(): pl.pallas_call(functools.partial(back_kernel, factor), out_shape=(jax.Sha...]
    unnamed x44 -> x42, local copies, waits for them, and re-layouts: 6.27 us -> 5.64 us
  transfers between devices with their start and end apart: 29 -> 29, of which waited for: 7 -> 8; matrix products, arithmetic and copies ran while one was open for 11% -> 11% of each run, Pallas kernels for 16% -> 14%
where the time goes in v7:
time: 296 us; the launch traced here: 294 us
  waiting for transfers between devices  142 us (48%)
  starting transfers between devices  46.3 us (16%)
  Pallas kernels  41.4 us (14%)
  blocking collectives  21.3 us (7%)
  other arithmetic  18.4 us (6%)
  local copies, waits for them, and re-layouts  13.5 us (5%)
  matrix products  11 us (4%)
    ppermute x7, waiting for transfers between devices, to_pair(): return lax.ppermute(x, 'zh', SWAP)  51 us
    ppermute x12, waiting for transfers between devices, along_y(): return lax.ppermute(x, 'y', ring(shift))  38.9 us
    pallas_call x4, Pallas kernels, hidden_of(): pl.pallas_call(hidden_kernel, out_shape=(jax.ShapeDtypeStruct((total, wid...  22.8 us
    all_to_all x1, blocking collectives, across_col(): return lax.all_to_all(x, COL, 0, 0, tiled=True)  21.3 us
    all_to_all x2, waiting for transfers between devices, gathered(): lax.all_to_all(part.reshape(4, 2 * rows, part_rows), 'y', 0, 0, tiled=True)  19.5 us
    ppermute x1, waiting for transfers between devices, local(): near = lax.ppermute(turned, 'zl', SWAP)  19.4 us
    pallas_call x1, Pallas kernels, back_of(): pl.pallas_call(functools.partial(back_kernel, factor), out_shape=(jax.Sha...  18.6 us
    ppermute x7, starting transfers between devices, to_pair(): return lax.ppermute(x, 'zh', SWAP)  14.4 us
  transfers between devices with their start and end apart: 29, of which 8 were waited for; matrix products, arithmetic and copies ran while one was open for 11% of the time, Pallas kernels for 14%

profile of v7, /device:TPU:0, one launch (start us, length us, event | category | flops | bytes accessed | tf_op | source)
XLA Modules:
  0.0 294.5 jit_solution(5295144951364951584)
XLA Ops:
  0.6 1.1 broadcast_in_dim.24
  1.8 21.3 %all_to_all.20 = bf16[8,128,512]{2,1,0:T(8,128)(2,1)S(1)} all-to-all(bf16[8,128,512]{2,1,0:T(8,128)(2,1)S(1)} %broadcast_in_dim.24), channel_id=1, replica_groups=mesh['y'=4,'zh'=2,'zl'=2,'x'=4,'core'=2] {'zl','x'}, dimensions={0} | all-to-all | bytes 2097152 | tf_op jit(solution)/shard_map/all_to_all | solution.py:33
  23.1 2.6 convolution_convert_fusion
  25.7 4.5 %all-to-all-start.2 = ((bf16[4,256,1024]{2,1,0:T(8,128)(2,1)}), bf16[4,256,1024]{2,1,0:T(8,128)(2,1)S(1)}, u32[]{:S(2)}, u32[]{:S(2)}) async-start(bf16[4,256,1024]{2,1,0:T(8,128)(2,1)} %bitcast.10), calls=%async_computation.2 | async-start | bytes 4194304 | tf_op jit(solution)/shard_map/all_to_all | solution.py:209
  30.1 1.9 constant_dynamic-update-slice_fusion.1
  32.0 3.8 %convolution_convert_fusion.1 = bf16[1024,1024]{1,0:T(8,128)(2,1)} fusion(bf16[1024,512]{1,0:T(8,128)(2,1)S(1)} %bitcast.12, bf16[2048,512]{1,0:T(8,128)(2,1)} %param.13), kind=kOutput, calls=%fused_computation.7 | convolution fusion | flops 1074790400 | bytes 4194304 | tf_op jit(solution)/shard_map/dot_general | solution.py:47
  35.8 19.5 %all-to-all-done.2 = bf16[4,256,1024]{2,1,0:T(8,128)(2,1)S(1)} async-done(((bf16[4,256,1024]{2,1,0:T(8,128)(2,1)}), bf16[4,256,1024]{2,1,0:T(8,128)(2,1)S(1)}, u32[]{:S(2)}, u32[]{:S(2)}) %all-to-all-start.2) | async-done | bytes 2097184 | tf_op jit(solution)/shard_map/all_to_all | solution.py:209
  55.3 1.3 copy-done
  56.6 3.6 %all-to-all-start.1 = ((bf16[4,256,1024]{2,1,0:T(8,128)(2,1)}), bf16[4,256,1024]{2,1,0:T(8,128)(2,1)S(1)}, u32[]{:S(2)}, u32[]{:S(2)}) async-start(bf16[4,256,1024]{2,1,0:T(8,128)(2,1)} %bitcast.9), calls=%async_computation.1 | async-start | bytes 4194304 | tf_op jit(solution)/shard_map/all_to_all | solution.py:209
  60.3 0.8 constant_dynamic-update-slice_fusion.refs_0_.refs_2_
  61.1 2.0 collective-permute-start.10
  63.1 1.3 collective-permute-start.13
  64.3 3.6 %collective-permute-start.18 = (bf16[256,2048]{1,0:T(8,128)(2,1)}, bf16[256,2048]{1,0:T(8,128)(2,1)}, u32[]{:S(2)}, u32[]{:S(2)}) collective-permute-start(bf16[256,2048]{1,0:T(8,128)(2,1)} %constant_dynamic-update-slice_fusion.refs_0_.refs_2_), channel_id=1, source_target_pairs={{0,16},{16,0},{1,17},{17,1},{2,18},{18,2},{3,19},{19,3},{4,20},{20... | collective-permute-start | bytes 3145736 | tf_op jit(solution)/shard_map/ppermute | solution.py:29
  67.9 38.9 %collective-permute-done.10.refs_0_.refs_2_ = bf16[256,2048]{1,0:T(8,128)(2,1)} collective-permute-done((bf16[256,2048]{1,0:T(8,128)(2,1)}, bf16[256,2048]{1,0:T(8,128)(2,1)}, u32[]{:S(2)}, u32[]{:S(2)}) %collective-permute-start.10) | collective-permute-done | bytes 1048608 | tf_op jit(solution)/shard_map/ppermute | solution.py:25
  106.8 3.6 %collective-permute-start.17 = (bf16[256,2048]{1,0:T(8,128)(2,1)}, bf16[256,2048]{1,0:T(8,128)(2,1)}, u32[]{:S(2)}, u32[]{:S(2)}) collective-permute-start(bf16[256,2048]{1,0:T(8,128)(2,1)} %collective-permute-done.10.refs_0_.refs_2_), channel_id=1, source_target_pairs={{0,16},{16,0},{1,17},{17,1},{2,18},{18,2},{3,19},{19,3},{4,20},{20... | collective-permute-start | bytes 3145736 | tf_op jit(solution)/shard_map/ppermute | solution.py:29
  110.4 1.9 slice.36
  112.3 0.1 copy.20
  112.5 0.1 collective-permute-start.19
  112.6 2.1 convert_reduce_fusion
  114.6 0.9 convert_element_type.69
  115.5 19.4 %collective-permute-done.19 = bf16[512,128]{1,0:T(8,128)(2,1)S(1)} collective-permute-done((bf16[512,128]{1,0:T(8,128)(2,1)S(1)}, bf16[512,128]{1,0:T(8,128)(2,1)S(1)}, u32[]{:S(2)}, u32[]{:S(2)}) %collective-permute-start.19) | collective-permute-done | bytes 131104 | tf_op jit(solution)/shard_map/ppermute | solution.py:219
  134.9 3.5 %collective-permute-start.16 = (bf16[256,2048]{1,0:T(8,128)(2,1)}, bf16[256,2048]{1,0:T(8,128)(2,1)}, u32[]{:S(2)}, u32[]{:S(2)}) collective-permute-start(bf16[256,2048]{1,0:T(8,128)(2,1)} %collective-permute-done.13.refs_0_.refs_2_), channel_id=1, source_target_pairs={{0,16},{16,0},{1,17},{17,1},{2,18},{18,2},{3,19},{19,3},{4,20},{20... | collective-permute-start | bytes 3145736 | tf_op jit(solution)/shard_map/ppermute | solution.py:29
  138.4 1.9 slice.37
  140.3 0.9 collective-permute-start.14
  141.2 0.4 convert_reduce_fusion.1
  141.7 0.1 collective-permute-start
  141.8 9.7 %collective-permute-done.5 = bf16[256,1024]{1,0:T(8,128)(2,1)} collective-permute-done((bf16[256,1024]{1,0:T(8,128)(2,1)}, bf16[256,1024]{1,0:T(8,128)(2,1)}, u32[]{:S(2)}, u32[]{:S(2)}) %collective-permute-start.5) | collective-permute-done | bytes 524320 | tf_op jit(solution)/shard_map/ppermute | solution.py:29
  151.5 1.2 add_convert_fusion.3.refs_5_
  152.7 3.6 %collective-permute-start.15 = (bf16[128,2048]{1,0:T(8,128)(2,1)}, bf16[128,2048]{1,0:T(8,128)(2,1)S(1)}, u32[]{:S(2)}, u32[]{:S(2)}) collective-permute-start(bf16[128,2048]{1,0:T(8,128)(2,1)} %collective-permute-done.14.refs_2_), channel_id=1, source_target_pairs={{0,16},{16,0},{1,17},{17,1},{2,18},{18,2},{3,19},{19,3},{4,20},{20... | collective-permute-start | bytes 1572872 | tf_op jit(solution)/shard_map/ppermute | solution.py:29
  156.3 28.8 %collective-permute-done = bf16[256,1024]{1,0:T(8,128)(2,1)S(1)} collective-permute-done((bf16[256,1024]{1,0:T(8,128)(2,1)S(1)}, bf16[256,1024]{1,0:T(8,128)(2,1)S(1)}, u32[]{:S(2)}, u32[]{:S(2)}) %collective-permute-start) | collective-permute-done | bytes 524320 | tf_op jit(solution)/shard_map/ppermute | solution.py:29
  185.1 0.9 collective-permute-start.6
  186.0 0.2 add_convert_fusion.4.refs_0_
  186.2 1.2 collective-permute-start.2
  187.4 7.9 %collective-permute-done.12.refs_1_ = bf16[128,2048]{1,0:T(8,128)(2,1)S(1)} collective-permute-done((bf16[128,2048]{1,0:T(8,128)(2,1)}, bf16[128,2048]{1,0:T(8,128)(2,1)S(1)}, u32[]{:S(2)}, u32[]{:S(2)}) %collective-permute-start.12) | collective-permute-done | bytes 524320 | tf_op jit(solution)/shard_map/ppermute | solution.py:29
  195.3 0.9 collective-permute-start.1
  196.2 4.7 %collective-permute-done.15.refs_3_ = bf16[128,2048]{1,0:T(8,128)(2,1)S(1)} collective-permute-done((bf16[128,2048]{1,0:T(8,128)(2,1)}, bf16[128,2048]{1,0:T(8,128)(2,1)S(1)}, u32[]{:S(2)}, u32[]{:S(2)}) %collective-permute-start.15) | collective-permute-done | bytes 524320 | tf_op jit(solution)/shard_map/ppermute | solution.py:29
  200.9 1.5 collective-permute-start.20
  202.4 0.8 copy-done.10
  203.2 1.5 collective-permute-start.21
  204.7 0.5 compare_select_fusion.7.spots
  205.3 0.5 compare_select_fusion.9.far
  205.8 5.7 %shard_map.102 = (bf16[1024,2048]{1,0:T(8,128)(2,1)}, f32[1024,2048]{1,0:T(8,128)}, f32[1024,2048]{1,0:T(8,128)}) custom-call(s32[6]{0:T(128)} %compare_select_fusion.7.spots, bf16[256,2048]{1,0:T(8,128)(2,1)} %constant_dynamic-update-slice_fusion.refs_0_.refs_2_, bf16[256,2048]{1,0:T(8,128)(2,1)} %collective-permute-done.18.refs_1_.refs_3_, ...), custom_call_target="tpu_custom_call" | custom-call | flops 5242880 | bytes 7340032 | tf_op jit(solution)/shard_map/pallas_call | solution.py:79
  211.5 5.7 %shard_map.103 = (bf16[1024,2048]{1,0:T(8,128)(2,1)}, f32[1024,2048]{1,0:T(8,128)}, f32[1024,2048]{1,0:T(8,128)}) custom-call(s32[6]{0:T(128)} %compare_select_fusion.7.spots, bf16[256,2048]{1,0:T(8,128)(2,1)} %collective-permute-done.10.refs_0_.refs_2_, ...), custom_call_target="tpu_custom_call", output_to_operand_aliasing={{0}: (5, {}), {1}: (6, {}), {2}: (7, {})} | custom-call | flops 5242880 | bytes 7340032 | tf_op jit(solution)/shard_map/pallas_call | solution.py:79
  217.2 5.7 %shard_map.104 = (bf16[1024,2048]{1,0:T(8,128)(2,1)}, f32[1024,2048]{1,0:T(8,128)}, f32[1024,2048]{1,0:T(8,128)}) custom-call(s32[6]{0:T(128)} %compare_select_fusion.7.spots, bf16[256,2048]{1,0:T(8,128)(2,1)} %collective-permute-done.13.refs_0_.refs_2_, ...), custom_call_target="tpu_custom_call", output_to_operand_aliasing={{0}: (5, {}), {1}: (6, {}), {2}: (7, {})} | custom-call | flops 5242880 | bytes 7340032 | tf_op jit(solution)/shard_map/pallas_call | solution.py:79
  222.9 5.8 %shard_map.105 = (bf16[1024,2048]{1,0:T(8,128)(2,1)}, f32[1024,2048]{1,0:T(8,128)}, f32[1024,2048]{1,0:T(8,128)}) custom-call(s32[6]{0:T(128)} %compare_select_fusion.7.spots, bf16[128,2048]{1,0:T(8,128)(2,1)} %collective-permute-done.11.refs_0_, bf16[128,2048]{1,0:T(8,128)(2,1)} %copy-done.4, ...), custom_call_target="tpu_custom_call", output_to_operand_aliasing={{0}: (5, {}), {1}: (6, {}), {2}: (7, {})} | custom-call | flops 5242880 | bytes 7340032 | tf_op jit(solution)/shard_map/pallas_call | solution.py:79
  228.7 0.1 collective-permute-start.22
  228.8 0.3 collective-permute-start.8
  229.1 1.0 slice.32
  230.1 3.2 %collective-permute-start.9 = (bf16[128,1024]{1,0:T(8,128)(2,1)S(1)}, bf16[128,1024]{1,0:T(8,128)(2,1)S(1)}, u32[]{:S(2)}, u32[]{:S(2)}) collective-permute-start(bf16[128,1024]{1,0:T(8,128)(2,1)S(1)} %slice.35), channel_id=1, source_target_pairs={{0,96},{32,0},{64,32},{96,64},{1,97},{33,1},{65,33},{97,65},{2,98}... | collective-permute-start | bytes 786440 | tf_op jit(solution)/shard_map/ppermute | solution.py:25
  233.4 1.0 slice.33
  234.4 3.2 %collective-permute-start.4 = (bf16[128,1024]{1,0:T(8,128)(2,1)S(1)}, bf16[128,1024]{1,0:T(8,128)(2,1)S(1)}, u32[]{:S(2)}, u32[]{:S(2)}) collective-permute-start(bf16[128,1024]{1,0:T(8,128)(2,1)S(1)} %slice.33), channel_id=1, source_target_pairs={{0,96},{32,0},{64,32},{96,64},{1,97},{33,1},{65,33},{97,65},{2,98}... | collective-permute-start | bytes 786440 | tf_op jit(solution)/shard_map/ppermute | solution.py:25
  237.7 4.6 %multiply_convert_fusion = bf16[2048,512]{1,0:T(8,128)(2,1)S(1)} fusion(bf16[1024,2048]{1,0:T(8,128)(2,1)} %get-tuple-element.33, bf16[1024,512]{1,0:T(8,128)(2,1)S(1)} %bitcast.13), kind=kOutput, calls=%fused_computation.1 | convolution fusion | flops 2149580800 | bytes 7340032 | tf_op jit(solution)/shard_map/dot_general | solution.py:43
  242.3 0.1 collective-permute-start.25
  242.4 0.7 copy-done.18
  243.2 0.7 copy-done.19
  243.9 18.6 %shard_map.106 = (bf16[512,2048]{1,0:T(8,128)(2,1)}, bf16[512,2048]{1,0:T(8,128)(2,1)}, bf16[1024,512]{1,0:T(8,128)(2,1)}) custom-call(s32[12]{0:T(128)} %compare_select_fusion.9.far, bf16[256,1024]{1,0:T(8,128)(2,1)} %copy-done.8, bf16[256,1024]{1,0:T(8,128)(2,1)} %collective-permute-done.1.refs_1_, bf16[256,1024]{1,0:T(8,128)(2,1)} %collective-permute-done.2.refs_2_, ...), custom_call_target="tpu_custom_call" | custom-call | flops 8589934592 | bytes 29360128 | tf_op jit(solution)/shard_map/pallas_call | solution.py:155
  262.5 0.6 collective-permute-start.24
  263.0 0.1 collective-permute-start.23
  263.1 5.9 %all-to-all-start.3 = ((bf16[8,128,512]{2,1,0:T(8,128)(2,1)}), bf16[8,128,512]{2,1,0:T(8,128)(2,1)S(1)}, u32[]{:S(2)}, u32[]{:S(2)}) async-start(bf16[8,128,512]{2,1,0:T(8,128)(2,1)} %bitcast.14), calls=%async_computation.3 | async-start | bytes 2097152 | tf_op jit(solution)/shard_map/all_to_all | solution.py:33
  269.1 3.5 %add_convert_fusion = bf16[2048,512]{1,0:T(8,128)(2,1)} fusion(bf16[2048,512]{1,0:T(8,128)(2,1)} %collective-permute-done.25, bf16[2048,512]{1,0:T(8,128)(2,1)S(1)} %multiply_convert_fusion), kind=kLoop, calls=%fused_computation | loop fusion | flops 4194304 | bytes 6291456 | tf_op jit(solution)/shard_map/convert_element_type | solution.py:227
  272.6 12.8 %all-to-all-done.3 = bf16[8,128,512]{2,1,0:T(8,128)(2,1)S(1)} async-done(((bf16[8,128,512]{2,1,0:T(8,128)(2,1)}), bf16[8,128,512]{2,1,0:T(8,128)(2,1)S(1)}, u32[]{:S(2)}, u32[]{:S(2)}) %all-to-all-start.3) | async-done | bytes 1048608 | tf_op jit(solution)/shard_map/all_to_all | solution.py:33
  285.3 0.8 reduce_sum.32
  286.2 4.6 %add_convert_fusion.1 = bf16[512,2048]{1,0:T(8,128)(2,1)} fusion(bf16[512,2048]{1,0:T(8,128)(2,1)} %collective-permute-done.24, bf16[512,2048]{1,0:T(8,128)(2,1)} %get-tuple-element.32), kind=kLoop, calls=%fused_computation.2 | loop fusion | flops 4194304 | bytes 6291456 | tf_op jit(solution)/shard_map/convert_element_type | solution.py:227
  290.8 3.7 %add_convert_fusion.2 = bf16[512,2048]{1,0:T(8,128)(2,1)} fusion(bf16[512,2048]{1,0:T(8,128)(2,1)} %collective-permute-done.23, bf16[512,2048]{1,0:T(8,128)(2,1)S(1)} %copy-done.1), kind=kLoop, calls=%fused_computation.3 | loop fusion | flops 4194304 | bytes 6291456 | tf_op jit(solution)/shard_map/convert_element_type | solution.py:227
  (66 shorter events, 0.3 us)
Async XLA Ops:
  0.6 22.4 %copy-start.14 = (bf16[2048,512]{1,0:T(8,128)(2,1)S(1)}, bf16[2048,512]{1,0:T(8,128)(2,1)}, u32[]{:S(2)}) copy-start(bf16[2048,512]{1,0:T(8,128)(2,1)} %param.13) | copy-start | bytes 6291460
  23.0 9.0 %copy-start.2 = (bf16[8,128,512]{2,1,0:T(8,128)(2,1)}, bf16[8,128,512]{2,1,0:T(8,128)(2,1)S(1)}, u32[]{:S(2)}) copy-start(bf16[8,128,512]{2,1,0:T(8,128)(2,1)S(1)} %all_to_all.20) | copy-start | bytes 3145732
  25.7 29.7 %all-to-all-start.2 = ((bf16[4,256,1024]{2,1,0:T(8,128)(2,1)}), bf16[4,256,1024]{2,1,0:T(8,128)(2,1)S(1)}, u32[]{:S(2)}, u32[]{:S(2)}) async-start(bf16[4,256,1024]{2,1,0:T(8,128)(2,1)} %bitcast.10), calls=%async_computation.2 | async-start | bytes 4194304 | tf_op jit(solution)/shard_map/all_to_all | solution.py:209
  55.3 1.3 copy-start
  55.3 4.9 %copy-start.6 = (bf16[128,2048]{1,0:T(8,128)(2,1)S(1)}, bf16[128,2048]{1,0:T(8,128)(2,1)}, u32[]{:S(2)}) copy-start(bf16[128,2048]{1,0:T(8,128)(2,1)} %param.10) | copy-start | bytes 1572868
  56.6 84.6 %all-to-all-start.1 = ((bf16[4,256,1024]{2,1,0:T(8,128)(2,1)}), bf16[4,256,1024]{2,1,0:T(8,128)(2,1)S(1)}, u32[]{:S(2)}, u32[]{:S(2)}) async-start(bf16[4,256,1024]{2,1,0:T(8,128)(2,1)} %bitcast.9), calls=%async_computation.1 | async-start | bytes 4194304 | tf_op jit(solution)/shard_map/all_to_all | solution.py:209
  60.3 52.1 %copy-start.13 = (bf16[128,512]{1,0:T(8,128)(2,1)S(1)}, bf16[128,512]{1,0:T(8,128)(2,1)}, u32[]{:S(2)}) copy-start(bf16[128,512]{1,0:T(8,128)(2,1)} %param.7) | copy-start | bytes 393220
  61.1 45.7 %collective-permute-start.10 = (bf16[256,2048]{1,0:T(8,128)(2,1)}, bf16[256,2048]{1,0:T(8,128)(2,1)}, u32[]{:S(2)}, u32[]{:S(2)}) collective-permute-start(bf16[256,2048]{1,0:T(8,128)(2,1)} %constant_dynamic-update-slice_fusion.refs_0_.refs_2_), channel_id=1, source_target_pairs={{0,32},{32,64},{64,96},{96,0},{1,33},{33,65},{65,97},{97,1},{2,34}... | collective-permute-start | bytes 3145736 | tf_op jit(solution)/shard_map/ppermute | solution.py:25
  63.1 71.8 %collective-permute-start.13 = (bf16[256,2048]{1,0:T(8,128)(2,1)}, bf16[256,2048]{1,0:T(8,128)(2,1)}, u32[]{:S(2)}, u32[]{:S(2)}) collective-permute-start(bf16[256,2048]{1,0:T(8,128)(2,1)} %constant_dynamic-update-slice_fusion.refs_0_.refs_2_), channel_id=1, source_target_pairs={{0,96},{32,0},{64,32},{96,64},{1,97},{33,1},{65,33},{97,65},{2,98}... | collective-permute-start | bytes 3145736 | tf_op jit(solution)/shard_map/ppermute | solution.py:25
  64.3 76.0 %collective-permute-start.18 = (bf16[256,2048]{1,0:T(8,128)(2,1)}, bf16[256,2048]{1,0:T(8,128)(2,1)}, u32[]{:S(2)}, u32[]{:S(2)}) collective-permute-start(bf16[256,2048]{1,0:T(8,128)(2,1)} %constant_dynamic-update-slice_fusion.refs_0_.refs_2_), channel_id=1, source_target_pairs={{0,16},{16,0},{1,17},{17,1},{2,18},{18,2},{3,19},{19,3},{4,20},{20... | collective-permute-start | bytes 3145736 | tf_op jit(solution)/shard_map/ppermute | solution.py:29
  106.8 49.5 %collective-permute-start.17 = (bf16[256,2048]{1,0:T(8,128)(2,1)}, bf16[256,2048]{1,0:T(8,128)(2,1)}, u32[]{:S(2)}, u32[]{:S(2)}) collective-permute-start(bf16[256,2048]{1,0:T(8,128)(2,1)} %collective-permute-done.10.refs_0_.refs_2_), channel_id=1, source_target_pairs={{0,16},{16,0},{1,17},{17,1},{2,18},{18,2},{3,19},{19,3},{4,20},{20... | collective-permute-start | bytes 3145736 | tf_op jit(solution)/shard_map/ppermute | solution.py:29
  112.3 29.4 %collective-permute-start.11 = (bf16[128,2048]{1,0:T(8,128)(2,1)}, bf16[128,2048]{1,0:T(8,128)(2,1)}, u32[]{:S(2)}, u32[]{:S(2)}) collective-permute-start(bf16[128,2048]{1,0:T(8,128)(2,1)} %slice.36), channel_id=1, source_target_pairs={{0,32},{32,64},{64,96},{96,0},{1,33},{33,65},{65,97},{97,1},{2,34}... | collective-permute-start | bytes 1572872 | tf_op jit(solution)/shard_map/ppermute | solution.py:25
  112.5 22.4 %collective-permute-start.19 = (bf16[512,128]{1,0:T(8,128)(2,1)S(1)}, bf16[512,128]{1,0:T(8,128)(2,1)S(1)}, u32[]{:S(2)}, u32[]{:S(2)}) collective-permute-start(bf16[512,128]{1,0:T(8,128)(2,1)S(1)} %bitcast.15), channel_id=1, source_target_pairs={{0,8},{8,0},{1,9},{9,1},{2,10},{10,2},{3,11},{11,3},{4,12},{12,4},... | collective-permute-start | bytes 393224 | tf_op jit(solution)/shard_map/ppermute | solution.py:219
  134.9 16.6 %collective-permute-start.5 = (bf16[256,1024]{1,0:T(8,128)(2,1)}, bf16[256,1024]{1,0:T(8,128)(2,1)}, u32[]{:S(2)}, u32[]{:S(2)}) collective-permute-start(bf16[256,1024]{1,0:T(8,128)(2,1)} %convert_element_type.69), channel_id=1, source_target_pairs={{0,16},{16,0},{1,17},{17,1},{2,18},{18,2},{3,19},{19,3},{4,20},{20... | collective-permute-start | bytes 1572872 | tf_op jit(solution)/shard_map/ppermute | solution.py:29
  134.9 51.3 %collective-permute-start.16 = (bf16[256,2048]{1,0:T(8,128)(2,1)}, bf16[256,2048]{1,0:T(8,128)(2,1)}, u32[]{:S(2)}, u32[]{:S(2)}) collective-permute-start(bf16[256,2048]{1,0:T(8,128)(2,1)} %collective-permute-done.13.refs_0_.refs_2_), channel_id=1, source_target_pairs={{0,16},{16,0},{1,17},{17,1},{2,18},{18,2},{3,19},{19,3},{4,20},{20... | collective-permute-start | bytes 3145736 | tf_op jit(solution)/shard_map/ppermute | solution.py:29
  140.3 12.4 %collective-permute-start.14 = (bf16[128,2048]{1,0:T(8,128)(2,1)}, bf16[128,2048]{1,0:T(8,128)(2,1)}, u32[]{:S(2)}, u32[]{:S(2)}) collective-permute-start(bf16[128,2048]{1,0:T(8,128)(2,1)} %slice.37), channel_id=1, source_target_pairs={{0,96},{32,0},{64,32},{96,64},{1,97},{33,1},{65,33},{97,65},{2,98}... | collective-permute-start | bytes 1572872 | tf_op jit(solution)/shard_map/ppermute | solution.py:25
  141.7 43.4 %collective-permute-start = (bf16[256,1024]{1,0:T(8,128)(2,1)S(1)}, bf16[256,1024]{1,0:T(8,128)(2,1)S(1)}, u32[]{:S(2)}, u32[]{:S(2)}) collective-permute-start(bf16[256,1024]{1,0:T(8,128)(2,1)S(1)} %convert_element_type.64), channel_id=1, source_target_pairs={{0,16},{16,0},{1,17},{17,1},{2,18},{18,2},{3,19},{19,3},{4,20},{20... | collective-permute-start | bytes 1572872 | tf_op jit(solution)/shard_map/ppermute | solution.py:29
  151.5 43.8 %collective-permute-start.12 = (bf16[128,2048]{1,0:T(8,128)(2,1)}, bf16[128,2048]{1,0:T(8,128)(2,1)S(1)}, u32[]{:S(2)}, u32[]{:S(2)}) collective-permute-start(bf16[128,2048]{1,0:T(8,128)(2,1)} %collective-permute-done.11.refs_0_), channel_id=1, source_target_pairs={{0,16},{16,0},{1,17},{17,1},{2,18},{18,2},{3,19},{19,3},{4,20},{20... | collective-permute-start | bytes 1572872 | tf_op jit(solution)/shard_map/ppermute | solution.py:29
  152.7 58.8 %copy-start.7 = (bf16[256,1024]{1,0:T(8,128)(2,1)}, bf16[256,1024]{1,0:T(8,128)(2,1)S(1)}, u32[]{:S(2)}) copy-start(bf16[256,1024]{1,0:T(8,128)(2,1)S(1)} %add_convert_fusion.3.refs_5_) | copy-start | bytes 1572868
  152.7 48.2 %collective-permute-start.15 = (bf16[128,2048]{1,0:T(8,128)(2,1)}, bf16[128,2048]{1,0:T(8,128)(2,1)S(1)}, u32[]{:S(2)}, u32[]{:S(2)}) collective-permute-start(bf16[128,2048]{1,0:T(8,128)(2,1)} %collective-permute-done.14.refs_2_), channel_id=1, source_target_pairs={{0,16},{16,0},{1,17},{17,1},{2,18},{18,2},{3,19},{19,3},{4,20},{20... | collective-permute-start | bytes 1572872 | tf_op jit(solution)/shard_map/ppermute | solution.py:29
  156.3 46.1 %collective-permute-start.7 = (bf16[256,1024]{1,0:T(8,128)(2,1)S(1)}, bf16[256,1024]{1,0:T(8,128)(2,1)S(1)}, u32[]{:S(2)}, u32[]{:S(2)}) collective-permute-start(bf16[256,1024]{1,0:T(8,128)(2,1)S(1)} %add_convert_fusion.3.refs_5_), channel_id=1, source_target_pairs={{0,32},{32,64},{64,96},{96,0},{1,33},{33,65},{65,97},{97,1},{2,34}... | collective-permute-start | bytes 1572872 | tf_op jit(solution)/shard_map/ppermute | solution.py:25
  185.1 43.6 %collective-permute-start.6 = (bf16[256,1024]{1,0:T(8,128)(2,1)S(1)}, bf16[256,1024]{1,0:T(8,128)(2,1)S(1)}, u32[]{:S(2)}, u32[]{:S(2)}) collective-permute-start(bf16[256,1024]{1,0:T(8,128)(2,1)S(1)} %add_convert_fusion.3.refs_5_), channel_id=1, source_target_pairs={{0,96},{32,0},{64,32},{96,64},{1,97},{33,1},{65,33},{97,65},{2,98}... | collective-permute-start | bytes 1572872 | tf_op jit(solution)/shard_map/ppermute | solution.py:25
  186.2 25.3 %copy-start.8 = (bf16[256,1024]{1,0:T(8,128)(2,1)}, bf16[256,1024]{1,0:T(8,128)(2,1)S(1)}, u32[]{:S(2)}) copy-start(bf16[256,1024]{1,0:T(8,128)(2,1)S(1)} %add_convert_fusion.4.refs_0_) | copy-start | bytes 1572868
  186.2 42.6 %collective-permute-start.2 = (bf16[256,1024]{1,0:T(8,128)(2,1)S(1)}, bf16[256,1024]{1,0:T(8,128)(2,1)}, u32[]{:S(2)}, u32[]{:S(2)}) collective-permute-start(bf16[256,1024]{1,0:T(8,128)(2,1)S(1)} %add_convert_fusion.4.refs_0_), channel_id=1, source_target_pairs={{0,32},{32,64},{64,96},{96,0},{1,33},{33,65},{65,97},{97,1},{2,34}... | collective-permute-start | bytes 1572872 | tf_op jit(solution)/shard_map/ppermute | solution.py:25
  195.3 16.2 %copy-start.4 = (bf16[128,2048]{1,0:T(8,128)(2,1)}, bf16[128,2048]{1,0:T(8,128)(2,1)S(1)}, u32[]{:S(2)}) copy-start(bf16[128,2048]{1,0:T(8,128)(2,1)S(1)} %collective-permute-done.12.refs_1_) | copy-start | bytes 1572868
  195.3 34.9 %collective-permute-start.1 = (bf16[256,1024]{1,0:T(8,128)(2,1)S(1)}, bf16[256,1024]{1,0:T(8,128)(2,1)}, u32[]{:S(2)}, u32[]{:S(2)}) collective-permute-start(bf16[256,1024]{1,0:T(8,128)(2,1)S(1)} %add_convert_fusion.4.refs_0_), channel_id=1, source_target_pairs={{0,96},{32,0},{64,32},{96,64},{1,97},{33,1},{65,33},{97,65},{2,98}... | collective-permute-start | bytes 1572872 | tf_op jit(solution)/shard_map/ppermute | solution.py:25
  196.2 32.5 %copy-start.9 = (bf16[1024,128]{1,0:T(8,128)(2,1)}, bf16[1024,128]{1,0:T(8,128)(2,1)S(1)}, u32[]{:S(2)}) copy-start(bf16[1024,128]{1,0:T(8,128)(2,1)S(1)} %pad_maximum_fusion.refs_14_) | copy-start | bytes 786436
  200.9 10.6 %copy-start.5 = (bf16[128,2048]{1,0:T(8,128)(2,1)}, bf16[128,2048]{1,0:T(8,128)(2,1)S(1)}, u32[]{:S(2)}) copy-start(bf16[128,2048]{1,0:T(8,128)(2,1)S(1)} %collective-permute-done.15.refs_3_) | copy-start | bytes 1572868
  200.9 33.5 %collective-permute-start.20 = (bf16[1024,128]{1,0:T(8,128)(2,1)S(1)}, bf16[1024,128]{1,0:T(8,128)(2,1)}, u32[]{:S(2)}, u32[]{:S(2)}) collective-permute-start(bf16[1024,128]{1,0:T(8,128)(2,1)S(1)} %pad_maximum_fusion.refs_14_), channel_id=1, source_target_pairs={{0,6},{2,0},{4,2},{6,4},{1,7},{3,1},{5,3},{7,5},{8,14},{10,8},{12,... | collective-permute-start | bytes 786440 | tf_op jit(solution)/shard_map/ppermute | solution.py:223
  202.4 0.8 copy-start.10
  203.2 31.2 %collective-permute-start.21 = (bf16[1024,128]{1,0:T(8,128)(2,1)S(1)}, bf16[1024,128]{1,0:T(8,128)(2,1)}, u32[]{:S(2)}, u32[]{:S(2)}) collective-permute-start(bf16[1024,128]{1,0:T(8,128)(2,1)S(1)} %pad_maximum_fusion.refs_14_), channel_id=1, source_target_pairs={{0,4},{2,6},{4,0},{6,2},{1,5},{3,7},{5,1},{7,3},{8,12},{10,14},{12... | collective-permute-start | bytes 786440 | tf_op jit(solution)/shard_map/ppermute | solution.py:223
  222.9 5.8 %copy-start.11 = (bf16[256,1024]{1,0:T(8,128)(2,1)S(1)}, bf16[256,1024]{1,0:T(8,128)(2,1)}, u32[]{:S(2)}) copy-start(bf16[256,1024]{1,0:T(8,128)(2,1)} %copy-done.10) | copy-start | bytes 1572868
  228.6 9.0 %copy-start.3 = (bf16[8,128,512]{2,1,0:T(8,128)(2,1)S(1)}, bf16[8,128,512]{2,1,0:T(8,128)(2,1)}, u32[]{:S(2)}) copy-start(bf16[8,128,512]{2,1,0:T(8,128)(2,1)} %copy-done.2) | copy-start | bytes 3145732
  228.7 9.0 %copy-start.12 = (bf16[256,1024]{1,0:T(8,128)(2,1)}, bf16[256,1024]{1,0:T(8,128)(2,1)S(1)}, u32[]{:S(2)}) copy-start(bf16[256,1024]{1,0:T(8,128)(2,1)S(1)} %collective-permute-done.6.refs_6_) | copy-start | bytes 1572868
  228.7 13.6 %collective-permute-start.22 = (bf16[1024,128]{1,0:T(8,128)(2,1)S(1)}, bf16[1024,128]{1,0:T(8,128)(2,1)S(1)}, u32[]{:S(2)}, u32[]{:S(2)}) collective-permute-start(bf16[1024,128]{1,0:T(8,128)(2,1)S(1)} %pad_maximum_fusion.refs_14_), channel_id=1, source_target_pairs={{0,2},{2,4},{4,6},{6,0},{1,3},{3,5},{5,7},{7,1},{8,10},{10,12},{12... | collective-permute-start | bytes 786440 | tf_op jit(solution)/shard_map/ppermute | solution.py:223
  228.8 13.5 %collective-permute-start.8 = (bf16[128,1024]{1,0:T(8,128)(2,1)S(1)}, bf16[128,1024]{1,0:T(8,128)(2,1)S(1)}, u32[]{:S(2)}, u32[]{:S(2)}) collective-permute-start(bf16[128,1024]{1,0:T(8,128)(2,1)S(1)} %slice.34), channel_id=1, source_target_pairs={{0,32},{32,64},{64,96},{96,0},{1,33},{33,65},{65,97},{97,1},{2,34}... | collective-permute-start | bytes 786440 | tf_op jit(solution)/shard_map/ppermute | solution.py:25
  230.1 12.3 %collective-permute-start.9 = (bf16[128,1024]{1,0:T(8,128)(2,1)S(1)}, bf16[128,1024]{1,0:T(8,128)(2,1)S(1)}, u32[]{:S(2)}, u32[]{:S(2)}) collective-permute-start(bf16[128,1024]{1,0:T(8,128)(2,1)S(1)} %slice.35), channel_id=1, source_target_pairs={{0,96},{32,0},{64,32},{96,64},{1,97},{33,1},{65,33},{97,65},{2,98}... | collective-permute-start | bytes 786440 | tf_op jit(solution)/shard_map/ppermute | solution.py:25
  234.3 8.1 %collective-permute-start.3 = (bf16[128,1024]{1,0:T(8,128)(2,1)S(1)}, bf16[128,1024]{1,0:T(8,128)(2,1)S(1)}, u32[]{:S(2)}, u32[]{:S(2)}) collective-permute-start(bf16[128,1024]{1,0:T(8,128)(2,1)S(1)} %slice.32), channel_id=1, source_target_pairs={{0,32},{32,64},{64,96},{96,0},{1,33},{33,65},{65,97},{97,1},{2,34}... | collective-permute-start | bytes 786440 | tf_op jit(solution)/shard_map/ppermute | solution.py:25
  234.4 8.0 %collective-permute-start.4 = (bf16[128,1024]{1,0:T(8,128)(2,1)S(1)}, bf16[128,1024]{1,0:T(8,128)(2,1)S(1)}, u32[]{:S(2)}, u32[]{:S(2)}) collective-permute-start(bf16[128,1024]{1,0:T(8,128)(2,1)S(1)} %slice.33), channel_id=1, source_target_pairs={{0,96},{32,0},{64,32},{96,64},{1,97},{33,1},{65,33},{97,65},{2,98}... | collective-permute-start | bytes 786440 | tf_op jit(solution)/shard_map/ppermute | solution.py:25
  242.3 1.6 copy-start.15
  242.3 26.8 %collective-permute-start.25 = (bf16[2048,512]{1,0:T(8,128)(2,1)S(1)}, bf16[2048,512]{1,0:T(8,128)(2,1)}, u32[]{:S(2)}, u32[]{:S(2)}) collective-permute-start(bf16[2048,512]{1,0:T(8,128)(2,1)S(1)} %multiply_convert_fusion), channel_id=1, source_target_pairs={{0,1},{1,0},{2,3},{3,2},{4,5},{5,4},{6,7},{7,6},{8,9},{9,8},{10,11... | collective-permute-start | bytes 6291464 | tf_op jit(solution)/shard_map/ppermute | solution.py:226
  242.4 1.5 copy-start.16
  242.4 1.5 copy-start.17
  242.4 0.7 copy-start.18
  243.2 0.7 copy-start.19
  262.5 23.7 %collective-permute-start.24 = (bf16[512,2048]{1,0:T(8,128)(2,1)}, bf16[512,2048]{1,0:T(8,128)(2,1)}, u32[]{:S(2)}, u32[]{:S(2)}) collective-permute-start(bf16[512,2048]{1,0:T(8,128)(2,1)} %get-tuple-element.32), channel_id=1, source_target_pairs={{0,1},{1,0},{2,3},{3,2},{4,5},{5,4},{6,7},{7,6},{8,9},{9,8},{10,11... | collective-permute-start | bytes 6291464 | tf_op jit(solution)/shard_map/ppermute | solution.py:226
  263.0 27.7 %collective-permute-start.23 = (bf16[512,2048]{1,0:T(8,128)(2,1)}, bf16[512,2048]{1,0:T(8,128)(2,1)}, u32[]{:S(2)}, u32[]{:S(2)}) collective-permute-start(bf16[512,2048]{1,0:T(8,128)(2,1)} %get-tuple-element.31), channel_id=1, source_target_pairs={{0,1},{1,0},{2,3},{3,2},{4,5},{5,4},{6,7},{7,6},{8,9},{9,8},{10,11... | collective-permute-start | bytes 6291464 | tf_op jit(solution)/shard_map/ppermute | solution.py:226
  263.1 22.2 %all-to-all-start.3 = ((bf16[8,128,512]{2,1,0:T(8,128)(2,1)}), bf16[8,128,512]{2,1,0:T(8,128)(2,1)S(1)}, u32[]{:S(2)}, u32[]{:S(2)}) async-start(bf16[8,128,512]{2,1,0:T(8,128)(2,1)} %bitcast.14), calls=%async_computation.3 | async-start | bytes 2097152 | tf_op jit(solution)/shard_map/all_to_all | solution.py:33
  286.2 4.6 %copy-start.1 = (bf16[512,2048]{1,0:T(8,128)(2,1)S(1)}, bf16[512,2048]{1,0:T(8,128)(2,1)}, u32[]{:S(2)}) copy-start(bf16[512,2048]{1,0:T(8,128)(2,1)} %get-tuple-element.31) | copy-start | bytes 6291460

commit v8 on v7

--- a/solution.py
+++ b/solution.py
@@ -14,7 +14,7 @@
 F32 = jnp.float32
 SWAP = [(0, 1), (1, 0)]
 STEP = 512
-NARROW = 256
+NARROW = 512
 
 
 def ring(shift):
@@ -200,7 +200,8 @@
     g2, u2 = along_y(low3, 1), along_y(high1, -1)
     paired = {k: (v, to_pair(v)) for k, v in ((0, both), (3, both3), (1, both1))}
     saved = {k: (v, v) for k, v in paired.items()}
-    saved[2] = ((g2, to_pair(g2)), (u2, to_pair(u2)))
+    low3p = paired[3][1][:rows]
+    saved[2] = ((g2, along_y(low3p, 1)), (u2, to_pair(u2)))
 
     part_rows = w_down.shape[0] // 2
 

time: 296 us -> 277 us (0.936)
  waiting for transfers between devices: 142 us -> 120 us
    ppermute x7 -> x6, waiting for transfers between devices: 51 us -> 32 us  [to_pair(): return lax.ppermute(x, 'zh', SWAP)]
    ppermute x12 -> x13, starting transfers between devices: 13.9 us -> 15.6 us  [along_y(): return lax.ppermute(x, 'y', ring(shift))]
    ppermute x12 -> x13, waiting for transfers between devices: 38.9 us -> 40.3 us  [along_y(): return lax.ppermute(x, 'y', ring(shift))]
    ppermute x7 -> x6, starting transfers between devices: 14.4 us -> 14.3 us  [to_pair(): return lax.ppermute(x, 'zh', SWAP)]
  transfers between devices with their start and end apart: 29 -> 29, of which waited for: 8 -> 9; matrix products, arithmetic and copies ran while one was open for 11% -> 13% of each run, Pallas kernels for 14% -> 15%
where the time goes in v8:
time: 277 us; the launch traced here: 275 us
  waiting for transfers between devices  120 us (43%)
  starting transfers between devices  47.1 us (17%)
  Pallas kernels  40.1 us (14%)
  blocking collectives  21.3 us (8%)
  other arithmetic  19.2 us (7%)
  local copies, waits for them, and re-layouts  16 us (6%)
  matrix products  11 us (4%)
    ppermute x13, waiting for transfers between devices, along_y(): return lax.ppermute(x, 'y', ring(shift))  40.3 us
    ppermute x6, waiting for transfers between devices, to_pair(): return lax.ppermute(x, 'zh', SWAP)  32 us
    pallas_call x4, Pallas kernels, hidden_of(): pl.pallas_call(hidden_kernel, out_shape=(jax.ShapeDtypeStruct((total, wid...  22.6 us
    all_to_all x1, blocking collectives, across_col(): return lax.all_to_all(x, COL, 0, 0, tiled=True)  21.3 us
    all_to_all x2, waiting for transfers between devices, gathered(): lax.all_to_all(part.reshape(4, 2 * rows, part_rows), 'y', 0, 0, tiled=True)  18.2 us
    pallas_call x1, Pallas kernels, back_of(): pl.pallas_call(functools.partial(back_kernel, factor), out_shape=(jax.Sha...  17.4 us
    ppermute x1, waiting for transfers between devices, local(): near = lax.ppermute(turned, 'zl', SWAP)  16.5 us
    ppermute x13, starting transfers between devices, along_y(): return lax.ppermute(x, 'y', ring(shift))  15.6 us
  transfers between devices with their start and end apart: 29, of which 9 were waited for; matrix products, arithmetic and copies ran while one was open for 13% of the time, Pallas kernels for 15%

profile of v8, /device:TPU:0, one launch (start us, length us, event | category | flops | bytes accessed | tf_op | source)
XLA Modules:
  0.0 275.3 jit_solution(12691028201452239877)
XLA Ops:
  0.6 1.1 broadcast_in_dim.24
  1.8 21.3 %all_to_all.20 = bf16[8,128,512]{2,1,0:T(8,128)(2,1)S(1)} all-to-all(bf16[8,128,512]{2,1,0:T(8,128)(2,1)S(1)} %broadcast_in_dim.24), channel_id=1, replica_groups=mesh['y'=4,'zh'=2,'zl'=2,'x'=4,'core'=2] {'zl','x'}, dimensions={0} | all-to-all | bytes 2097152 | tf_op jit(solution)/shard_map/all_to_all | solution.py:33
  23.1 2.6 convolution_convert_fusion
  25.7 4.5 %all-to-all-start.2 = ((bf16[4,256,1024]{2,1,0:T(8,128)(2,1)}), bf16[4,256,1024]{2,1,0:T(8,128)(2,1)S(1)}, u32[]{:S(2)}, u32[]{:S(2)}) async-start(bf16[4,256,1024]{2,1,0:T(8,128)(2,1)} %bitcast.10), calls=%async_computation.2 | async-start | bytes 4194304 | tf_op jit(solution)/shard_map/all_to_all | solution.py:210
  30.1 1.9 constant_dynamic-update-slice_fusion.1
  32.0 1.9 constant_dynamic-update-slice_fusion.refs_0_.refs_2_
  33.9 2.0 collective-permute-start.10
  35.9 3.8 %convolution_convert_fusion.1 = bf16[1024,1024]{1,0:T(8,128)(2,1)} fusion(bf16[1024,512]{1,0:T(8,128)(2,1)S(1)} %bitcast.12, bf16[2048,512]{1,0:T(8,128)(2,1)} %param.13), kind=kOutput, calls=%fused_computation.7 | convolution fusion | flops 1074790400 | bytes 4194304 | tf_op jit(solution)/shard_map/dot_general | solution.py:47
  39.7 18.2 %all-to-all-done.2 = bf16[4,256,1024]{2,1,0:T(8,128)(2,1)S(1)} async-done(((bf16[4,256,1024]{2,1,0:T(8,128)(2,1)}), bf16[4,256,1024]{2,1,0:T(8,128)(2,1)S(1)}, u32[]{:S(2)}, u32[]{:S(2)}) %all-to-all-start.2) | async-done | bytes 2097184 | tf_op jit(solution)/shard_map/all_to_all | solution.py:210
  57.9 1.3 copy-done
  59.2 3.6 %all-to-all-start.1 = ((bf16[4,256,1024]{2,1,0:T(8,128)(2,1)}), bf16[4,256,1024]{2,1,0:T(8,128)(2,1)S(1)}, u32[]{:S(2)}, u32[]{:S(2)}) async-start(bf16[4,256,1024]{2,1,0:T(8,128)(2,1)} %bitcast.9), calls=%async_computation.1 | async-start | bytes 4194304 | tf_op jit(solution)/shard_map/all_to_all | solution.py:210
  62.8 3.2 %collective-permute-start.14 = (bf16[256,2048]{1,0:T(8,128)(2,1)}, bf16[256,2048]{1,0:T(8,128)(2,1)}, u32[]{:S(2)}, u32[]{:S(2)}) collective-permute-start(bf16[256,2048]{1,0:T(8,128)(2,1)} %constant_dynamic-update-slice_fusion.refs_0_.refs_2_), channel_id=1, source_target_pairs={{0,96},{32,0},{64,32},{96,64},{1,97},{33,1},{65,33},{97,65},{2,98}... | collective-permute-start | bytes 3145736 | tf_op jit(solution)/shard_map/ppermute | solution.py:25
  66.0 14.1 %collective-permute-done.10.refs_0_.refs_2_ = bf16[256,2048]{1,0:T(8,128)(2,1)} collective-permute-done((bf16[256,2048]{1,0:T(8,128)(2,1)}, bf16[256,2048]{1,0:T(8,128)(2,1)}, u32[]{:S(2)}, u32[]{:S(2)}) %collective-permute-start.10) | collective-permute-done | bytes 1048608 | tf_op jit(solution)/shard_map/ppermute | solution.py:25
  80.1 3.6 %collective-permute-start.12 = (bf16[256,2048]{1,0:T(8,128)(2,1)}, bf16[256,2048]{1,0:T(8,128)(2,1)}, u32[]{:S(2)}, u32[]{:S(2)}) collective-permute-start(bf16[256,2048]{1,0:T(8,128)(2,1)} %collective-permute-done.10.refs_0_.refs_2_), channel_id=1, source_target_pairs={{0,16},{16,0},{1,17},{17,1},{2,18},{18,2},{3,19},{19,3},{4,20},{20... | collective-permute-start | bytes 3145736 | tf_op jit(solution)/shard_map/ppermute | solution.py:29
  83.8 23.0 %collective-permute-done.14.refs_0_.refs_2_ = bf16[256,2048]{1,0:T(8,128)(2,1)} collective-permute-done((bf16[256,2048]{1,0:T(8,128)(2,1)}, bf16[256,2048]{1,0:T(8,128)(2,1)}, u32[]{:S(2)}, u32[]{:S(2)}) %collective-permute-start.14) | collective-permute-done | bytes 1048608 | tf_op jit(solution)/shard_map/ppermute | solution.py:25
  106.7 1.9 slice.42
  108.6 0.8 collective-permute-start.15
  109.5 0.6 collective-permute-start.19
  110.1 2.1 convert_reduce_fusion
  112.2 0.9 convert_element_type.69
  113.1 3.6 %collective-permute-start.5 = (bf16[256,1024]{1,0:T(8,128)(2,1)}, bf16[256,1024]{1,0:T(8,128)(2,1)}, u32[]{:S(2)}, u32[]{:S(2)}) collective-permute-start(bf16[256,1024]{1,0:T(8,128)(2,1)} %convert_element_type.69), channel_id=1, source_target_pairs={{0,16},{16,0},{1,17},{17,1},{2,18},{18,2},{3,19},{19,3},{4,20},{20... | collective-permute-start | bytes 1572872 | tf_op jit(solution)/shard_map/ppermute | solution.py:29
  116.7 16.5 %collective-permute-done.19 = bf16[512,128]{1,0:T(8,128)(2,1)S(1)} collective-permute-done((bf16[512,128]{1,0:T(8,128)(2,1)S(1)}, bf16[512,128]{1,0:T(8,128)(2,1)S(1)}, u32[]{:S(2)}, u32[]{:S(2)}) %collective-permute-start.19) | collective-permute-done | bytes 131104 | tf_op jit(solution)/shard_map/ppermute | solution.py:220
  133.2 1.2 collective-permute-start.17
  134.3 1.9 slice.40
  136.2 0.4 convert_reduce_fusion.1
  136.7 0.6 copy-done.7
  137.3 2.4 collective-permute-start
  139.6 1.1 slice.41
  140.7 3.8 %collective-permute-done.5 = bf16[256,1024]{1,0:T(8,128)(2,1)} collective-permute-done((bf16[256,1024]{1,0:T(8,128)(2,1)}, bf16[256,1024]{1,0:T(8,128)(2,1)}, u32[]{:S(2)}, u32[]{:S(2)}) %collective-permute-start.5) | collective-permute-done | bytes 524320 | tf_op jit(solution)/shard_map/ppermute | solution.py:29
  144.6 3.5 %collective-permute-start.16 = (bf16[128,2048]{1,0:T(8,128)(2,1)}, bf16[128,2048]{1,0:T(8,128)(2,1)S(1)}, u32[]{:S(2)}, u32[]{:S(2)}) collective-permute-start(bf16[128,2048]{1,0:T(8,128)(2,1)} %collective-permute-done.15.refs_2_), channel_id=1, source_target_pairs={{0,16},{16,0},{1,17},{17,1},{2,18},{18,2},{3,19},{19,3},{4,20},{20... | collective-permute-start | bytes 1572872 | tf_op jit(solution)/shard_map/ppermute | solution.py:29
  148.1 2.0 add_convert_fusion.3.refs_5_
  150.1 3.2 %collective-permute-done.11.refs_0_ = bf16[128,2048]{1,0:T(8,128)(2,1)S(1)} collective-permute-done((bf16[128,2048]{1,0:T(8,128)(2,1)S(1)}, bf16[128,2048]{1,0:T(8,128)(2,1)S(1)}, u32[]{:S(2)}, u32[]{:S(2)}) %collective-permute-start.11) | collective-permute-done | bytes 524320 | tf_op jit(solution)/shard_map/ppermute | solution.py:25
  153.3 24.8 %collective-permute-done = bf16[256,1024]{1,0:T(8,128)(2,1)S(1)} collective-permute-done((bf16[256,1024]{1,0:T(8,128)(2,1)S(1)}, bf16[256,1024]{1,0:T(8,128)(2,1)S(1)}, u32[]{:S(2)}, u32[]{:S(2)}) %collective-permute-start) | collective-permute-done | bytes 524320 | tf_op jit(solution)/shard_map/ppermute | solution.py:29
  178.1 0.9 collective-permute-start.6
  179.2 1.2 collective-permute-start.2
  180.4 3.3 %collective-permute-done.16.refs_3_ = bf16[128,2048]{1,0:T(8,128)(2,1)S(1)} collective-permute-done((bf16[128,2048]{1,0:T(8,128)(2,1)}, bf16[128,2048]{1,0:T(8,128)(2,1)S(1)}, u32[]{:S(2)}, u32[]{:S(2)}) %collective-permute-start.16) | collective-permute-done | bytes 524320 | tf_op jit(solution)/shard_map/ppermute | solution.py:29
  183.7 0.9 collective-permute-start.1
  184.7 0.6 collective-permute-start.20
  185.2 2.5 collective-permute-start.21
  187.8 0.6 compare_select_fusion.7.spots
  188.4 0.5 compare_select_fusion.9.far
  188.9 5.7 %shard_map.102 = (bf16[1024,2048]{1,0:T(8,128)(2,1)}, f32[1024,2048]{1,0:T(8,128)}, f32[1024,2048]{1,0:T(8,128)}) custom-call(s32[6]{0:T(128)} %compare_select_fusion.7.spots, bf16[256,2048]{1,0:T(8,128)(2,1)} %constant_dynamic-update-slice_fusion.refs_0_.refs_2_, bf16[256,2048]{1,0:T(8,128)(2,1)} %collective-permute-done.18.refs_1_.refs_3_, ...), custom_call_target="tpu_custom_call" | custom-call | flops 5242880 | bytes 7340032 | tf_op jit(solution)/shard_map/pallas_call | solution.py:79
  194.6 5.7 %shard_map.103 = (bf16[1024,2048]{1,0:T(8,128)(2,1)}, f32[1024,2048]{1,0:T(8,128)}, f32[1024,2048]{1,0:T(8,128)}) custom-call(s32[6]{0:T(128)} %compare_select_fusion.7.spots, bf16[256,2048]{1,0:T(8,128)(2,1)} %collective-permute-done.10.refs_0_.refs_2_, ...), custom_call_target="tpu_custom_call", output_to_operand_aliasing={{0}: (5, {}), {1}: (6, {}), {2}: (7, {})} | custom-call | flops 5242880 | bytes 7340032 | tf_op jit(solution)/shard_map/pallas_call | solution.py:79
  200.3 5.7 %shard_map.104 = (bf16[1024,2048]{1,0:T(8,128)(2,1)}, f32[1024,2048]{1,0:T(8,128)}, f32[1024,2048]{1,0:T(8,128)}) custom-call(s32[6]{0:T(128)} %compare_select_fusion.7.spots, bf16[256,2048]{1,0:T(8,128)(2,1)} %collective-permute-done.14.refs_0_.refs_2_, ...), custom_call_target="tpu_custom_call", output_to_operand_aliasing={{0}: (5, {}), {1}: (6, {}), {2}: (7, {})} | custom-call | flops 5242880 | bytes 7340032 | tf_op jit(solution)/shard_map/pallas_call | solution.py:79
  205.9 5.6 %shard_map.105 = (bf16[1024,2048]{1,0:T(8,128)(2,1)}, f32[1024,2048]{1,0:T(8,128)}, f32[1024,2048]{1,0:T(8,128)}) custom-call(s32[6]{0:T(128)} %compare_select_fusion.7.spots, bf16[128,2048]{1,0:T(8,128)(2,1)} %copy-done.4, bf16[128,2048]{1,0:T(8,128)(2,1)} %copy-done.6, ...), custom_call_target="tpu_custom_call", output_to_operand_aliasing={{0}: (5, {}), {1}: (6, {}), {2}: (7, {})} | custom-call | flops 5242880 | bytes 7340032 | tf_op jit(solution)/shard_map/pallas_call | solution.py:79
  211.6 1.1 slice.38
  212.7 0.3 collective-permute-start.22
  213.0 1.2 collective-permute-start.8
  214.2 1.0 slice.36
  215.1 2.2 collective-permute-start.9
  217.3 1.0 slice.37
  218.4 3.2 %collective-permute-start.4 = (bf16[128,1024]{1,0:T(8,128)(2,1)S(1)}, bf16[128,1024]{1,0:T(8,128)(2,1)S(1)}, u32[]{:S(2)}, u32[]{:S(2)}) collective-permute-start(bf16[128,1024]{1,0:T(8,128)(2,1)S(1)} %slice.37), channel_id=1, source_target_pairs={{0,96},{32,0},{64,32},{96,64},{1,97},{33,1},{65,33},{97,65},{2,98}... | collective-permute-start | bytes 786440 | tf_op jit(solution)/shard_map/ppermute | solution.py:25
  221.6 4.6 %multiply_convert_fusion = bf16[2048,512]{1,0:T(8,128)(2,1)S(1)} fusion(bf16[1024,2048]{1,0:T(8,128)(2,1)} %get-tuple-element.33, bf16[1024,512]{1,0:T(8,128)(2,1)S(1)} %bitcast.13), kind=kOutput, calls=%fused_computation.1 | convolution fusion | flops 2149580800 | bytes 7340032 | tf_op jit(solution)/shard_map/dot_general | solution.py:43
  226.4 0.5 copy-done.15
  227.2 0.5 copy-done.19
  227.7 17.4 %shard_map.106 = (bf16[512,2048]{1,0:T(8,128)(2,1)}, bf16[512,2048]{1,0:T(8,128)(2,1)}, bf16[1024,512]{1,0:T(8,128)(2,1)}) custom-call(s32[12]{0:T(128)} %compare_select_fusion.9.far, bf16[256,1024]{1,0:T(8,128)(2,1)} %copy-done.8, bf16[256,1024]{1,0:T(8,128)(2,1)} %collective-permute-done.1.refs_1_, bf16[256,1024]{1,0:T(8,128)(2,1)} %collective-permute-done.2.refs_2_, ...), custom_call_target="tpu_custom_call" | custom-call | flops 8589934592 | bytes 29360128 | tf_op jit(solution)/shard_map/pallas_call | solution.py:155
  245.1 0.3 collective-permute-start.24
  245.4 0.3 collective-permute-start.23
  245.7 4.5 %all-to-all-start.3 = ((bf16[8,128,512]{2,1,0:T(8,128)(2,1)}), bf16[8,128,512]{2,1,0:T(8,128)(2,1)S(1)}, u32[]{:S(2)}, u32[]{:S(2)}) async-start(bf16[8,128,512]{2,1,0:T(8,128)(2,1)} %bitcast.14), calls=%async_computation.3 | async-start | bytes 2097152 | tf_op jit(solution)/shard_map/all_to_all | solution.py:33
  250.2 3.5 %add_convert_fusion = bf16[2048,512]{1,0:T(8,128)(2,1)} fusion(bf16[2048,512]{1,0:T(8,128)(2,1)} %collective-permute-done.25, bf16[2048,512]{1,0:T(8,128)(2,1)S(1)} %multiply_convert_fusion), kind=kLoop, calls=%fused_computation | loop fusion | flops 4194304 | bytes 6291456 | tf_op jit(solution)/shard_map/convert_element_type | solution.py:228
  253.7 12.5 %all-to-all-done.3 = bf16[8,128,512]{2,1,0:T(8,128)(2,1)S(1)} async-done(((bf16[8,128,512]{2,1,0:T(8,128)(2,1)}), bf16[8,128,512]{2,1,0:T(8,128)(2,1)S(1)}, u32[]{:S(2)}, u32[]{:S(2)}) %all-to-all-start.3) | async-done | bytes 1048608 | tf_op jit(solution)/shard_map/all_to_all | solution.py:33
  266.2 0.8 reduce_sum.32
  267.0 4.6 %add_convert_fusion.1 = bf16[512,2048]{1,0:T(8,128)(2,1)} fusion(bf16[512,2048]{1,0:T(8,128)(2,1)} %collective-permute-done.24, bf16[512,2048]{1,0:T(8,128)(2,1)} %get-tuple-element.32), kind=kLoop, calls=%fused_computation.2 | loop fusion | flops 4194304 | bytes 6291456 | tf_op jit(solution)/shard_map/convert_element_type | solution.py:228
  271.6 3.7 %add_convert_fusion.2 = bf16[512,2048]{1,0:T(8,128)(2,1)} fusion(bf16[512,2048]{1,0:T(8,128)(2,1)} %collective-permute-done.23, bf16[512,2048]{1,0:T(8,128)(2,1)S(1)} %copy-done.1), kind=kLoop, calls=%fused_computation.3 | loop fusion | flops 4194304 | bytes 6291456 | tf_op jit(solution)/shard_map/convert_element_type | solution.py:228
  (67 shorter events, 0.9 us)
Async XLA Ops:
  0.6 22.4 %copy-start.12 = (bf16[2048,512]{1,0:T(8,128)(2,1)S(1)}, bf16[2048,512]{1,0:T(8,128)(2,1)}, u32[]{:S(2)}) copy-start(bf16[2048,512]{1,0:T(8,128)(2,1)} %param.13) | copy-start | bytes 6291460
  23.0 12.9 %copy-start.2 = (bf16[8,128,512]{2,1,0:T(8,128)(2,1)}, bf16[8,128,512]{2,1,0:T(8,128)(2,1)S(1)}, u32[]{:S(2)}) copy-start(bf16[8,128,512]{2,1,0:T(8,128)(2,1)S(1)} %all_to_all.20) | copy-start | bytes 3145732
  25.7 32.3 %all-to-all-start.2 = ((bf16[4,256,1024]{2,1,0:T(8,128)(2,1)}), bf16[4,256,1024]{2,1,0:T(8,128)(2,1)S(1)}, u32[]{:S(2)}, u32[]{:S(2)}) async-start(bf16[4,256,1024]{2,1,0:T(8,128)(2,1)} %bitcast.10), calls=%async_computation.2 | async-start | bytes 4194304 | tf_op jit(solution)/shard_map/all_to_all | solution.py:210
  33.9 46.3 %collective-permute-start.10 = (bf16[256,2048]{1,0:T(8,128)(2,1)}, bf16[256,2048]{1,0:T(8,128)(2,1)}, u32[]{:S(2)}, u32[]{:S(2)}) collective-permute-start(bf16[256,2048]{1,0:T(8,128)(2,1)} %constant_dynamic-update-slice_fusion.refs_0_.refs_2_), channel_id=1, source_target_pairs={{0,32},{32,64},{64,96},{96,0},{1,33},{33,65},{65,97},{97,1},{2,34}... | collective-permute-start | bytes 3145736 | tf_op jit(solution)/shard_map/ppermute | solution.py:25
  57.9 1.3 copy-start
  57.9 51.4 %copy-start.11 = (bf16[128,512]{1,0:T(8,128)(2,1)S(1)}, bf16[128,512]{1,0:T(8,128)(2,1)}, u32[]{:S(2)}) copy-start(bf16[128,512]{1,0:T(8,128)(2,1)} %param.7) | copy-start | bytes 393220
  59.2 77.0 %all-to-all-start.1 = ((bf16[4,256,1024]{2,1,0:T(8,128)(2,1)}), bf16[4,256,1024]{2,1,0:T(8,128)(2,1)S(1)}, u32[]{:S(2)}, u32[]{:S(2)}) async-start(bf16[4,256,1024]{2,1,0:T(8,128)(2,1)} %bitcast.9), calls=%async_computation.1 | async-start | bytes 4194304 | tf_op jit(solution)/shard_map/all_to_all | solution.py:210
  62.8 43.9 %collective-permute-start.14 = (bf16[256,2048]{1,0:T(8,128)(2,1)}, bf16[256,2048]{1,0:T(8,128)(2,1)}, u32[]{:S(2)}, u32[]{:S(2)}) collective-permute-start(bf16[256,2048]{1,0:T(8,128)(2,1)} %constant_dynamic-update-slice_fusion.refs_0_.refs_2_), channel_id=1, source_target_pairs={{0,96},{32,0},{64,32},{96,64},{1,97},{33,1},{65,33},{97,65},{2,98}... | collective-permute-start | bytes 3145736 | tf_op jit(solution)/shard_map/ppermute | solution.py:25
  80.1 57.1 %collective-permute-start.12 = (bf16[256,2048]{1,0:T(8,128)(2,1)}, bf16[256,2048]{1,0:T(8,128)(2,1)}, u32[]{:S(2)}, u32[]{:S(2)}) collective-permute-start(bf16[256,2048]{1,0:T(8,128)(2,1)} %collective-permute-done.10.refs_0_.refs_2_), channel_id=1, source_target_pairs={{0,16},{16,0},{1,17},{17,1},{2,18},{18,2},{3,19},{19,3},{4,20},{20... | collective-permute-start | bytes 3145736 | tf_op jit(solution)/shard_map/ppermute | solution.py:29
  83.7 66.4 %collective-permute-start.18 = (bf16[256,2048]{1,0:T(8,128)(2,1)}, bf16[256,2048]{1,0:T(8,128)(2,1)}, u32[]{:S(2)}, u32[]{:S(2)}) collective-permute-start(bf16[256,2048]{1,0:T(8,128)(2,1)} %constant_dynamic-update-slice_fusion.refs_0_.refs_2_), channel_id=1, source_target_pairs={{0,16},{16,0},{1,17},{17,1},{2,18},{18,2},{3,19},{19,3},{4,20},{20... | collective-permute-start | bytes 3145736 | tf_op jit(solution)/shard_map/ppermute | solution.py:29
  108.6 28.1 %collective-permute-start.15 = (bf16[128,2048]{1,0:T(8,128)(2,1)}, bf16[128,2048]{1,0:T(8,128)(2,1)}, u32[]{:S(2)}, u32[]{:S(2)}) collective-permute-start(bf16[128,2048]{1,0:T(8,128)(2,1)} %slice.42), channel_id=1, source_target_pairs={{0,96},{32,0},{64,32},{96,64},{1,97},{33,1},{65,33},{97,65},{2,98}... | collective-permute-start | bytes 1572872 | tf_op jit(solution)/shard_map/ppermute | solution.py:25
  109.5 23.7 %collective-permute-start.19 = (bf16[512,128]{1,0:T(8,128)(2,1)S(1)}, bf16[512,128]{1,0:T(8,128)(2,1)S(1)}, u32[]{:S(2)}, u32[]{:S(2)}) collective-permute-start(bf16[512,128]{1,0:T(8,128)(2,1)S(1)} %bitcast.15), channel_id=1, source_target_pairs={{0,8},{8,0},{1,9},{9,1},{2,10},{10,2},{3,11},{11,3},{4,12},{12,4},... | collective-permute-start | bytes 393224 | tf_op jit(solution)/shard_map/ppermute | solution.py:220
  113.1 31.5 %collective-permute-start.5 = (bf16[256,1024]{1,0:T(8,128)(2,1)}, bf16[256,1024]{1,0:T(8,128)(2,1)}, u32[]{:S(2)}, u32[]{:S(2)}) collective-permute-start(bf16[256,1024]{1,0:T(8,128)(2,1)} %convert_element_type.69), channel_id=1, source_target_pairs={{0,16},{16,0},{1,17},{17,1},{2,18},{18,2},{3,19},{19,3},{4,20},{20... | collective-permute-start | bytes 1572872 | tf_op jit(solution)/shard_map/ppermute | solution.py:29
  133.2 46.0 %collective-permute-start.17 = (bf16[256,2048]{1,0:T(8,128)(2,1)}, bf16[256,2048]{1,0:T(8,128)(2,1)}, u32[]{:S(2)}, u32[]{:S(2)}) collective-permute-start(bf16[256,2048]{1,0:T(8,128)(2,1)} %collective-permute-done.14.refs_0_.refs_2_), channel_id=1, source_target_pairs={{0,16},{16,0},{1,17},{17,1},{2,18},{18,2},{3,19},{19,3},{4,20},{20... | collective-permute-start | bytes 3145736 | tf_op jit(solution)/shard_map/ppermute | solution.py:29
  136.2 1.0 copy-start.7
  137.3 16.0 %collective-permute-start.11 = (bf16[128,2048]{1,0:T(8,128)(2,1)S(1)}, bf16[128,2048]{1,0:T(8,128)(2,1)S(1)}, u32[]{:S(2)}, u32[]{:S(2)}) collective-permute-start(bf16[128,2048]{1,0:T(8,128)(2,1)S(1)} %copy-done.7), channel_id=1, source_target_pairs={{0,32},{32,64},{64,96},{96,0},{1,33},{33,65},{65,97},{97,1},{2,34}... | collective-permute-start | bytes 1572872 | tf_op jit(solution)/shard_map/ppermute | solution.py:25
  137.3 40.8 %collective-permute-start = (bf16[256,1024]{1,0:T(8,128)(2,1)S(1)}, bf16[256,1024]{1,0:T(8,128)(2,1)S(1)}, u32[]{:S(2)}, u32[]{:S(2)}) collective-permute-start(bf16[256,1024]{1,0:T(8,128)(2,1)S(1)} %convert_element_type.64), channel_id=1, source_target_pairs={{0,16},{16,0},{1,17},{17,1},{2,18},{18,2},{3,19},{19,3},{4,20},{20... | collective-permute-start | bytes 1572872 | tf_op jit(solution)/shard_map/ppermute | solution.py:29
  144.6 39.2 %collective-permute-start.16 = (bf16[128,2048]{1,0:T(8,128)(2,1)}, bf16[128,2048]{1,0:T(8,128)(2,1)S(1)}, u32[]{:S(2)}, u32[]{:S(2)}) collective-permute-start(bf16[128,2048]{1,0:T(8,128)(2,1)} %collective-permute-done.15.refs_2_), channel_id=1, source_target_pairs={{0,16},{16,0},{1,17},{17,1},{2,18},{18,2},{3,19},{19,3},{4,20},{20... | collective-permute-start | bytes 1572872 | tf_op jit(solution)/shard_map/ppermute | solution.py:29
  150.1 34.6 %collective-permute-start.13 = (bf16[128,2048]{1,0:T(8,128)(2,1)S(1)}, bf16[128,2048]{1,0:T(8,128)(2,1)S(1)}, u32[]{:S(2)}, u32[]{:S(2)}) collective-permute-start(bf16[128,2048]{1,0:T(8,128)(2,1)S(1)} %slice.41), channel_id=1, source_target_pairs={{0,32},{32,64},{64,96},{96,0},{1,33},{33,65},{65,97},{97,1},{2,34}... | collective-permute-start | bytes 1572872 | tf_op jit(solution)/shard_map/ppermute | solution.py:25
  153.3 41.3 %copy-start.4 = (bf16[128,2048]{1,0:T(8,128)(2,1)}, bf16[128,2048]{1,0:T(8,128)(2,1)S(1)}, u32[]{:S(2)}) copy-start(bf16[128,2048]{1,0:T(8,128)(2,1)S(1)} %collective-permute-done.11.refs_0_) | copy-start | bytes 1572868
  153.3 32.0 %collective-permute-start.7 = (bf16[256,1024]{1,0:T(8,128)(2,1)}, bf16[256,1024]{1,0:T(8,128)(2,1)}, u32[]{:S(2)}, u32[]{:S(2)}) collective-permute-start(bf16[256,1024]{1,0:T(8,128)(2,1)} %add_convert_fusion.3.refs_5_), channel_id=1, source_target_pairs={{0,32},{32,64},{64,96},{96,0},{1,33},{33,65},{65,97},{97,1},{2,34}... | collective-permute-start | bytes 1572872 | tf_op jit(solution)/shard_map/ppermute | solution.py:25
  178.1 34.5 %collective-permute-start.6 = (bf16[256,1024]{1,0:T(8,128)(2,1)}, bf16[256,1024]{1,0:T(8,128)(2,1)S(1)}, u32[]{:S(2)}, u32[]{:S(2)}) collective-permute-start(bf16[256,1024]{1,0:T(8,128)(2,1)} %add_convert_fusion.3.refs_5_), channel_id=1, source_target_pairs={{0,96},{32,0},{64,32},{96,64},{1,97},{33,1},{65,33},{97,65},{2,98}... | collective-permute-start | bytes 1572872 | tf_op jit(solution)/shard_map/ppermute | solution.py:25
  179.2 15.4 %copy-start.8 = (bf16[256,1024]{1,0:T(8,128)(2,1)}, bf16[256,1024]{1,0:T(8,128)(2,1)S(1)}, u32[]{:S(2)}) copy-start(bf16[256,1024]{1,0:T(8,128)(2,1)S(1)} %add_convert_fusion.4.refs_0_) | copy-start | bytes 1572868
  179.2 33.7 %collective-permute-start.2 = (bf16[256,1024]{1,0:T(8,128)(2,1)S(1)}, bf16[256,1024]{1,0:T(8,128)(2,1)}, u32[]{:S(2)}, u32[]{:S(2)}) collective-permute-start(bf16[256,1024]{1,0:T(8,128)(2,1)S(1)} %add_convert_fusion.4.refs_0_), channel_id=1, source_target_pairs={{0,32},{32,64},{64,96},{96,0},{1,33},{33,65},{65,97},{97,1},{2,34}... | collective-permute-start | bytes 1572872 | tf_op jit(solution)/shard_map/ppermute | solution.py:25
  183.7 10.8 %copy-start.5 = (bf16[128,2048]{1,0:T(8,128)(2,1)}, bf16[128,2048]{1,0:T(8,128)(2,1)S(1)}, u32[]{:S(2)}) copy-start(bf16[128,2048]{1,0:T(8,128)(2,1)S(1)} %collective-permute-done.16.refs_3_) | copy-start | bytes 1572868
  183.7 31.4 %collective-permute-start.1 = (bf16[256,1024]{1,0:T(8,128)(2,1)S(1)}, bf16[256,1024]{1,0:T(8,128)(2,1)}, u32[]{:S(2)}, u32[]{:S(2)}) collective-permute-start(bf16[256,1024]{1,0:T(8,128)(2,1)S(1)} %add_convert_fusion.4.refs_0_), channel_id=1, source_target_pairs={{0,96},{32,0},{64,32},{96,64},{1,97},{33,1},{65,33},{97,65},{2,98}... | collective-permute-start | bytes 1572872 | tf_op jit(solution)/shard_map/ppermute | solution.py:25
  184.7 28.0 %copy-start.9 = (bf16[1024,128]{1,0:T(8,128)(2,1)}, bf16[1024,128]{1,0:T(8,128)(2,1)S(1)}, u32[]{:S(2)}) copy-start(bf16[1024,128]{1,0:T(8,128)(2,1)S(1)} %pad_maximum_fusion.refs_14_) | copy-start | bytes 786436
  184.7 9.9 %copy-start.6 = (bf16[128,2048]{1,0:T(8,128)(2,1)}, bf16[128,2048]{1,0:T(8,128)(2,1)S(1)}, u32[]{:S(2)}) copy-start(bf16[128,2048]{1,0:T(8,128)(2,1)S(1)} %collective-permute-done.13.refs_1_) | copy-start | bytes 1572868
  184.7 33.6 %collective-permute-start.20 = (bf16[1024,128]{1,0:T(8,128)(2,1)S(1)}, bf16[1024,128]{1,0:T(8,128)(2,1)S(1)}, u32[]{:S(2)}, u32[]{:S(2)}) collective-permute-start(bf16[1024,128]{1,0:T(8,128)(2,1)S(1)} %pad_maximum_fusion.refs_14_), channel_id=1, source_target_pairs={{0,6},{2,0},{4,2},{6,4},{1,7},{3,1},{5,3},{7,5},{8,14},{10,8},{12,... | collective-permute-start | bytes 786440 | tf_op jit(solution)/shard_map/ppermute | solution.py:224
  185.2 33.1 %collective-permute-start.21 = (bf16[1024,128]{1,0:T(8,128)(2,1)S(1)}, bf16[1024,128]{1,0:T(8,128)(2,1)S(1)}, u32[]{:S(2)}, u32[]{:S(2)}) collective-permute-start(bf16[1024,128]{1,0:T(8,128)(2,1)S(1)} %pad_maximum_fusion.refs_14_), channel_id=1, source_target_pairs={{0,4},{2,6},{4,0},{6,2},{1,5},{3,7},{5,1},{7,3},{8,12},{10,14},{12... | collective-permute-start | bytes 786440 | tf_op jit(solution)/shard_map/ppermute | solution.py:224
  211.6 10.1 %copy-start.3 = (bf16[8,128,512]{2,1,0:T(8,128)(2,1)S(1)}, bf16[8,128,512]{2,1,0:T(8,128)(2,1)}, u32[]{:S(2)}) copy-start(bf16[8,128,512]{2,1,0:T(8,128)(2,1)} %copy-done.2) | copy-start | bytes 3145732
  212.6 9.0 %copy-start.10 = (bf16[256,1024]{1,0:T(8,128)(2,1)}, bf16[256,1024]{1,0:T(8,128)(2,1)S(1)}, u32[]{:S(2)}) copy-start(bf16[256,1024]{1,0:T(8,128)(2,1)S(1)} %collective-permute-done.6.refs_6_) | copy-start | bytes 1572868
  212.7 13.6 %collective-permute-start.22 = (bf16[1024,128]{1,0:T(8,128)(2,1)S(1)}, bf16[1024,128]{1,0:T(8,128)(2,1)S(1)}, u32[]{:S(2)}, u32[]{:S(2)}) collective-permute-start(bf16[1024,128]{1,0:T(8,128)(2,1)S(1)} %pad_maximum_fusion.refs_14_), channel_id=1, source_target_pairs={{0,2},{2,4},{4,6},{6,0},{1,3},{3,5},{5,7},{7,1},{8,10},{10,12},{12... | collective-permute-start | bytes 786440 | tf_op jit(solution)/shard_map/ppermute | solution.py:224
  213.0 13.4 %collective-permute-start.8 = (bf16[128,1024]{1,0:T(8,128)(2,1)S(1)}, bf16[128,1024]{1,0:T(8,128)(2,1)S(1)}, u32[]{:S(2)}, u32[]{:S(2)}) collective-permute-start(bf16[128,1024]{1,0:T(8,128)(2,1)S(1)} %slice.38), channel_id=1, source_target_pairs={{0,32},{32,64},{64,96},{96,0},{1,33},{33,65},{65,97},{97,1},{2,34}... | collective-permute-start | bytes 786440 | tf_op jit(solution)/shard_map/ppermute | solution.py:25
  215.1 11.2 %collective-permute-start.9 = (bf16[128,1024]{1,0:T(8,128)(2,1)S(1)}, bf16[128,1024]{1,0:T(8,128)(2,1)S(1)}, u32[]{:S(2)}, u32[]{:S(2)}) collective-permute-start(bf16[128,1024]{1,0:T(8,128)(2,1)S(1)} %slice.39), channel_id=1, source_target_pairs={{0,96},{32,0},{64,32},{96,64},{1,97},{33,1},{65,33},{97,65},{2,98}... | collective-permute-start | bytes 786440 | tf_op jit(solution)/shard_map/ppermute | solution.py:25
  218.3 7.9 %copy-start.13 = (bf16[1024,128]{1,0:T(8,128)(2,1)}, bf16[1024,128]{1,0:T(8,128)(2,1)S(1)}, u32[]{:S(2)}) copy-start(bf16[1024,128]{1,0:T(8,128)(2,1)S(1)} %collective-permute-done.20.refs_15_) | copy-start | bytes 786436
  218.3 8.1 %collective-permute-start.3 = (bf16[128,1024]{1,0:T(8,128)(2,1)S(1)}, bf16[128,1024]{1,0:T(8,128)(2,1)S(1)}, u32[]{:S(2)}, u32[]{:S(2)}) collective-permute-start(bf16[128,1024]{1,0:T(8,128)(2,1)S(1)} %slice.36), channel_id=1, source_target_pairs={{0,32},{32,64},{64,96},{96,0},{1,33},{33,65},{65,97},{97,1},{2,34}... | collective-permute-start | bytes 786440 | tf_op jit(solution)/shard_map/ppermute | solution.py:25
  218.4 7.8 %copy-start.14 = (bf16[1024,128]{1,0:T(8,128)(2,1)}, bf16[1024,128]{1,0:T(8,128)(2,1)S(1)}, u32[]{:S(2)}) copy-start(bf16[1024,128]{1,0:T(8,128)(2,1)S(1)} %collective-permute-done.21.refs_16_) | copy-start | bytes 786436
  218.4 8.0 %collective-permute-start.4 = (bf16[128,1024]{1,0:T(8,128)(2,1)S(1)}, bf16[128,1024]{1,0:T(8,128)(2,1)S(1)}, u32[]{:S(2)}, u32[]{:S(2)}) collective-permute-start(bf16[128,1024]{1,0:T(8,128)(2,1)S(1)} %slice.37), channel_id=1, source_target_pairs={{0,96},{32,0},{64,32},{96,64},{1,97},{33,1},{65,33},{97,65},{2,98}... | collective-permute-start | bytes 786440 | tf_op jit(solution)/shard_map/ppermute | solution.py:25
  226.3 0.7 copy-start.15
  226.3 23.9 %collective-permute-start.25 = (bf16[2048,512]{1,0:T(8,128)(2,1)S(1)}, bf16[2048,512]{1,0:T(8,128)(2,1)}, u32[]{:S(2)}, u32[]{:S(2)}) collective-permute-start(bf16[2048,512]{1,0:T(8,128)(2,1)S(1)} %multiply_convert_fusion), channel_id=1, source_target_pairs={{0,1},{1,0},{2,3},{3,2},{4,5},{5,4},{6,7},{7,6},{8,9},{9,8},{10,11... | collective-permute-start | bytes 6291464 | tf_op jit(solution)/shard_map/ppermute | solution.py:227
  226.4 0.7 copy-start.16
  226.4 1.3 copy-start.17
  226.4 0.7 copy-start.18
  226.9 0.7 copy-start.19
  245.1 22.0 %collective-permute-start.24 = (bf16[512,2048]{1,0:T(8,128)(2,1)}, bf16[512,2048]{1,0:T(8,128)(2,1)}, u32[]{:S(2)}, u32[]{:S(2)}) collective-permute-start(bf16[512,2048]{1,0:T(8,128)(2,1)} %get-tuple-element.32), channel_id=1, source_target_pairs={{0,1},{1,0},{2,3},{3,2},{4,5},{5,4},{6,7},{7,6},{8,9},{9,8},{10,11... | collective-permute-start | bytes 6291464 | tf_op jit(solution)/shard_map/ppermute | solution.py:227
  245.4 26.3 %collective-permute-start.23 = (bf16[512,2048]{1,0:T(8,128)(2,1)}, bf16[512,2048]{1,0:T(8,128)(2,1)}, u32[]{:S(2)}, u32[]{:S(2)}) collective-permute-start(bf16[512,2048]{1,0:T(8,128)(2,1)} %get-tuple-element.31), channel_id=1, source_target_pairs={{0,1},{1,0},{2,3},{3,2},{4,5},{5,4},{6,7},{7,6},{8,9},{9,8},{10,11... | collective-permute-start | bytes 6291464 | tf_op jit(solution)/shard_map/ppermute | solution.py:227
  245.7 20.6 %all-to-all-start.3 = ((bf16[8,128,512]{2,1,0:T(8,128)(2,1)}), bf16[8,128,512]{2,1,0:T(8,128)(2,1)S(1)}, u32[]{:S(2)}, u32[]{:S(2)}) async-start(bf16[8,128,512]{2,1,0:T(8,128)(2,1)} %bitcast.14), calls=%async_computation.3 | async-start | bytes 2097152 | tf_op jit(solution)/shard_map/all_to_all | solution.py:33
  267.0 4.6 %copy-start.1 = (bf16[512,2048]{1,0:T(8,128)(2,1)S(1)}, bf16[512,2048]{1,0:T(8,128)(2,1)}, u32[]{:S(2)}) copy-start(bf16[512,2048]{1,0:T(8,128)(2,1)} %get-tuple-element.31) | copy-start | bytes 6291460
